TPU v7x, 32 devices: a whole 2x2x4 slice. The times are simulated.
32 devices in a mesh: rec: 4 (over y, core), tm: 8 (over z, x).
Axes of the slice: x: 2, y: 2, z: 4, core: 2. Of those that a mesh axis runs over, the one named last changes fastest.
Arguments:
- frames: bfloat16 [4, 4096, 1024], P('rec', 'tm'), may hold values from -6 to 6
- lengths: int32 [4], P('rec'), may hold values from 1024 to 4096, as said below
- norm_gain: float32 [1024], replicated, may hold values from 0.1 to 1.9
- memory_gain: float32 [1024], replicated, may hold values from 0.1 to 1.9
- qkv_weight: bfloat16 [3, 1024, 1024], P(None, None, 'tm'), may hold values from -3.75 to 3.75
- out_weight: bfloat16 [1024, 1024], P(None, 'tm'), may hold values from -0.1875 to 0.1875
- segment_ids: int32 [4, 8, 512], P('rec', 'tm'), may hold values from 0 to 127, never falling along the last dimension, each value on 1 to 12 neighbouring positions
- owners: int32 [4, 8, 128, 1], P('rec', 'tm'), may hold values from 0 to 7; in each aligned block of 128 rows (0 to 127, 128 to 255, ..., all dimensions but the last counted through in order) at most 32 rows name the same one
- language_weight: bfloat16 [1024, 2048], P(None, 'rec'), may hold values from -0.1875 to 0.1875
Outputs:
- encoded: bfloat16 [4, 4096, 1024], P('rec', 'tm')
- lm_rows: bfloat16 [4, 8, 256, 2048], P('rec', 'tm')
Inputs may be any that keep to these rules, and one draw needn't show every extreme that they name: `lengths`: one recording has exactly 4096 live frames. `segment_ids`: in each block, token numbers never fall and each of the 128 tokens has 1 to 12 frames, one exactly 12. `owners`: within the 128 tokens of one block no owner is named more than 32 times, a bound that some block reaches.
All inputs are finite; a program needn't handle non-finite values.
Results may differ from a plain program's by a relative error of at most 0.035.
Values may be sent and summed in bfloat16 or wider, within the bound.
No kernel may reach another device: no remote copies, remote signals or barrier semaphores. Data moves between devices by JAX's collectives and lax.ppermute only.
A program may use at most 64 MiB of HBM per device.

v0:
```python
import functools

import jax
import jax.numpy as jnp
from jax import lax
from jax.experimental import pallas as pl
from jax.experimental.pallas import tpu as pltpu
from jax.sharding import PartitionSpec as P


H = 16
C = 32
RC = 8


EPS_NORM = 1e-05
EPS_MEMORY = 1e-06
NEG_BIG = -1e30
LANES = 128


def shifted(block, axis, distance):
    devices = range(lax.axis_size(axis))
    route = [(i - distance, i) for i in devices if i - distance in devices]
    return lax.ppermute(block, axis, route)


def layer_norm(values_in, gain):
    values_in = values_in.astype(jnp.float32)
    centre = jnp.mean(values_in, axis=-1, keepdims=True)
    centred = values_in - centre
    spread = jnp.mean(centred * centred, axis=-1, keepdims=True)
    return centred * lax.rsqrt(spread + EPS_NORM) * gain


def span_memory(normed, live_mask, gain, span_len):
    model_width = normed.shape[1]
    masked = jnp.where(live_mask[:, None], normed.astype(jnp.float32), jnp.float32(0.0))
    owner_sums = masked.reshape(-1, span_len, model_width).sum(axis=1)
    counts = live_mask.reshape(-1, span_len).astype(jnp.float32).sum(axis=1)
    means = owner_sums / jnp.maximum(counts, 1.0)[:, None]
    power = jnp.mean(means * means, axis=-1, keepdims=True)
    return (means * lax.rsqrt(power + EPS_MEMORY) * gain).astype(jnp.bfloat16)


def block_size():
    return 256


def local_part(query, keys, values, first_frame, length, head_count, span_len, right_len):
    frame_count, model_width = query.shape
    head_size = model_width // head_count
    group_rows = 4 * span_len
    group_count = frame_count // group_rows
    block_rows = block_size()
    query_blocks = query.reshape(group_count, group_rows, head_count, head_size)
    key_blocks = keys[:frame_count].reshape(group_count, group_rows, head_count, head_size)
    value_blocks = values[:frame_count].reshape(group_count, group_rows, head_count, head_size)
    key_tail = keys[frame_count:].reshape(1, right_len, head_count, head_size)
    value_tail = values[frame_count:].reshape(1, right_len, head_count, head_size)
    key_all = jnp.concatenate(
        [key_blocks, jnp.concatenate([key_blocks[1:, :right_len], key_tail], axis=0)], axis=1
    )
    value_all = jnp.concatenate(
        [value_blocks, jnp.concatenate([value_blocks[1:, :right_len], value_tail], axis=0)], axis=1
    )
    start_offsets = jnp.arange(group_count, dtype=jnp.int32)[:, None] * group_rows
    query_pos = first_frame + start_offsets + jnp.arange(group_rows, dtype=jnp.int32)[None, :]
    key_pos = first_frame + jnp.concatenate(
        [
            start_offsets + jnp.arange(group_rows, dtype=jnp.int32)[None, :],
            start_offsets + group_rows + jnp.arange(right_len, dtype=jnp.int32)[None, :],
        ],
        axis=1,
    )
    query_span = query_pos // span_len
    span_end = (query_span + 1) * span_len
    same = (key_pos // span_len)[:, None, :] == query_span[:, :, None]
    ahead = (key_pos[:, None, :] >= span_end[:, :, None]) & (
        key_pos[:, None, :] < span_end[:, :, None] + right_len
    )
    allowed = (same | ahead) & (key_pos < length)[:, None, :]
    scores = jnp.einsum(
        "gqhd,gkhd->ghqk", query_blocks, key_all, preferred_element_type=jnp.float32
    ) * head_size ** (-0.5)
    scores = jnp.where(allowed[:, None], scores, NEG_BIG)
    row_peak = jnp.max(scores, axis=-1)
    weights = jnp.where(allowed[:, None], jnp.exp(scores - row_peak[..., None]), jnp.float32(0.0))
    row_total = jnp.sum(weights, axis=-1)
    accum = jnp.einsum(
        "ghqk,gkhd->ghqd",
        weights.astype(jnp.bfloat16),
        value_all,
        preferred_element_type=jnp.float32,
    )
    block_count = frame_count // block_rows
    row_peak = (
        row_peak.transpose(1, 0, 2).reshape(head_count, block_count, block_rows).transpose(1, 0, 2)
    )
    row_total = (
        row_total.transpose(1, 0, 2).reshape(head_count, block_count, block_rows).transpose(1, 0, 2)
    )
    accum = (
        accum.transpose(1, 0, 2, 3)
        .reshape(head_count, block_count, block_rows, head_size)
        .transpose(1, 0, 2, 3)
    )
    return (row_peak, row_total, accum)


def memory_update(
    carry, memory_keys, memory_values, query, first_frame, length, head_count, span_len
):
    row_peak, row_total, accum = carry
    block_count, _, block_rows = row_peak.shape
    row_count, model_width = memory_keys.shape
    head_size = model_width // head_count
    mem_keys = memory_keys.reshape(row_count, head_count, head_size)
    mem_values = memory_values.reshape(row_count, head_count, head_size)
    mem_index = jnp.arange(row_count, dtype=jnp.int32)
    mem_live = mem_index * span_len < length
    query_blocks = query.reshape(block_count, block_rows, head_count, head_size)
    positions = first_frame + jnp.arange(block_count * block_rows, dtype=jnp.int32).reshape(
        block_count, block_rows
    )

    def one_block(packed):
        query_now, pos_now, peak_now, total_now, accum_now = packed
        scores = jnp.einsum(
            "qhd,khd->hqk", query_now, mem_keys, preferred_element_type=jnp.float32
        ) * head_size ** (-0.5)
        allowed = (mem_index[None, :] < (pos_now // span_len)[:, None]) & mem_live[None, :]
        scores = jnp.where(allowed[None], scores, NEG_BIG)
        new_peak = jnp.maximum(peak_now, jnp.max(scores, axis=-1))
        weights = jnp.where(allowed[None], jnp.exp(scores - new_peak[..., None]), jnp.float32(0.0))
        factor = jnp.exp(peak_now - new_peak)
        total_next = total_now * factor + jnp.sum(weights, axis=-1)
        accum_next = accum_now * factor[..., None] + jnp.einsum(
            "hqk,khd->hqd",
            weights.astype(jnp.bfloat16),
            mem_values,
            preferred_element_type=jnp.float32,
        )
        return (new_peak, total_next, accum_next)

    return lax.map(one_block, (query_blocks, positions, row_peak, row_total, accum))


def finish(carry, frame_count, model_width):
    _, row_total, accum = carry
    result = accum / row_total[..., None]
    return result.transpose(0, 2, 1, 3).reshape(frame_count, model_width).astype(jnp.bfloat16)


def dispatch_matrix(owner_ids, owner_count, capacity):
    choose = (owner_ids[:, None] == jnp.arange(owner_count, dtype=jnp.int32)[None, :]).astype(
        jnp.int32
    )
    before = jnp.cumsum(choose, axis=0) - choose
    slot_index = jnp.sum(before * choose, axis=1)
    target = owner_ids * capacity + slot_index
    slot_rows = jnp.arange(owner_count * capacity, dtype=jnp.int32)
    return (slot_rows[:, None] == target[None, :]).astype(jnp.bfloat16)


def plain_device(
    frames,
    lengths,
    norm_gain,
    memory_gain,
    qkv_weight,
    out_weight,
    segment_ids,
    owners,
    language_weight,
):
    local_frames = frames[0]
    frame_count, model_width = local_frames.shape
    head_count = H
    time_count = lax.axis_size("tm")
    first_frame = lax.axis_index("tm") * frame_count
    length = lengths[0]
    live_mask = first_frame + jnp.arange(frame_count, dtype=jnp.int32) < length
    right_frames = shifted(local_frames[:RC], "tm", -1)
    normed = layer_norm(local_frames, norm_gain).astype(jnp.bfloat16)
    normed_right = layer_norm(right_frames, norm_gain).astype(jnp.bfloat16)
    memory = span_memory(normed, live_mask, memory_gain, C)
    stacked_rows = jnp.concatenate([normed, normed_right, memory], axis=0)
    projected = jnp.einsum(
        "fd,kdw->kfw",
        stacked_rows,
        lax.all_gather(qkv_weight, "tm", axis=2, tiled=True),
        preferred_element_type=jnp.float32,
    ).astype(jnp.bfloat16)
    split_at = frame_count + RC
    query = projected[0, :frame_count]
    keys = projected[1, :split_at]
    values = projected[2, :split_at]
    memory_keys = projected[1, split_at:]
    memory_values = projected[2, split_at:]
    carry = local_part(query, keys, values, first_frame, length, head_count, C, RC)
    carry = memory_update(
        carry,
        lax.all_gather(memory_keys, "tm", axis=0, tiled=True),
        lax.all_gather(memory_values, "tm", axis=0, tiled=True),
        query,
        first_frame,
        length,
        head_count,
        C,
    )
    attended = finish(carry, frame_count, model_width)
    output_proj = jnp.dot(
        attended,
        lax.all_gather(out_weight, "tm", axis=1, tiled=True),
        preferred_element_type=jnp.float32,
    )
    encoded = jnp.where(
        live_mask[:, None], local_frames.astype(jnp.float32) + output_proj, jnp.float32(0.0)
    ).astype(jnp.bfloat16)
    token_count = owners.shape[2]
    segments = segment_ids[0, 0]
    owner_indicator = (
        segments[None, :] == jnp.arange(token_count, dtype=jnp.int32)[:, None]
    ).astype(jnp.bfloat16)
    owner_sums = jnp.dot(owner_indicator, encoded, preferred_element_type=jnp.float32)
    counts = jnp.sum(owner_indicator.astype(jnp.float32), axis=1)
    pooled_rows = (owner_sums / counts[:, None]).astype(jnp.bfloat16)
    slot_count = 2 * token_count
    capacity = slot_count // time_count
    route_matrix = dispatch_matrix(owners[0, 0, :, 0], time_count, capacity)
    sent_rows = jnp.dot(route_matrix, pooled_rows, preferred_element_type=jnp.float32).astype(
        jnp.bfloat16
    )
    received = lax.all_to_all(
        sent_rows.reshape(time_count, capacity, model_width),
        "tm",
        split_axis=0,
        concat_axis=0,
        tiled=True,
    )
    received = received.reshape(slot_count, model_width)
    lm_out = jnp.dot(
        received,
        lax.all_gather(language_weight, "rec", axis=1, tiled=True),
        preferred_element_type=jnp.float32,
    ).astype(jnp.bfloat16)
    return (encoded[None], lm_out[None, None])


def vmem_spec():
    return pl.BlockSpec(memory_space=pltpu.VMEM)


def smem_spec():
    return pl.BlockSpec(memory_space=pltpu.SMEM)


def local_call(kernel, out_shapes, operands, scratch=(), flops=0, moved=0):
    return pl.pallas_call(
        kernel,
        out_shape=out_shapes,
        in_specs=[smem_spec()] + [vmem_spec()] * (len(operands) - 1),
        out_specs=jax.tree.map(lambda _: vmem_spec(), out_shapes),
        scratch_shapes=list(scratch),
        cost_estimate=pl.CostEstimate(flops=flops, bytes_accessed=moved, transcendentals=0),
    )(*operands)


def shape_of(*dims, dtype=jnp.bfloat16):
    return jax.ShapeDtypeStruct(dims, dtype)


def normalise_kernel(span_len, scalars, frames, gain, memory_gain, normed_out, memory_out):
    first_frame, length = scalars[0], scalars[1]
    frame_count, _ = frames.shape
    span_count = frame_count // span_len
    values = frames[...].astype(jnp.float32)
    centre = jnp.mean(values, axis=-1, keepdims=True)
    centred = values - centre
    spread = jnp.mean(centred * centred, axis=-1, keepdims=True)
    normed = (centred * lax.rsqrt(spread + EPS_NORM) * gain[...]).astype(jnp.bfloat16)
    normed_out[...] = normed
    spans = lax.broadcasted_iota(jnp.int32, (span_count, frame_count), 0)
    places = lax.broadcasted_iota(jnp.int32, (span_count, frame_count), 1)
    member = (places >= spans * span_len) & (places < (spans + 1) * span_len)
    member = member & (places < length - first_frame)
    sums = jnp.dot(
        member.astype(jnp.bfloat16), normed, preferred_element_type=jnp.float32
    )
    counts = jnp.sum(member.astype(jnp.float32), axis=-1, keepdims=True)
    means = sums / jnp.maximum(counts, 1.0)
    power = jnp.mean(means * means, axis=-1, keepdims=True)
    memory_out[...] = (
        means * lax.rsqrt(power + EPS_MEMORY) * memory_gain[...]
    ).astype(jnp.bfloat16)


def attend_kernel(span_len, right_len, head_size, scalars, *refs):
    (rows_0, extra_0, rows_1, extra_1) = refs[:4]
    pieces = refs[4:12]
    out_0, out_1, projection, weight, query, key, value, bias = refs[12:]
    first_frame, core, y_half = scalars[0], scalars[3], scalars[4]
    frame_count, model_width = rows_0.shape
    half = model_width // 2
    width = out_0.shape[1]
    heads = width // head_size
    block = 2 * span_len
    pad = key.shape[0] - frame_count
    near = block + pad
    memory_count = extra_0.shape[0] - pad
    lanes = heads * block

    places = (y_half * half, (1 - y_half) * half)
    for side in range(2):
        place = pl.ds(pl.multiple_of(places[side], half), half)
        for shard in range(2):
            mine_0, mine_1 = pieces[4 * shard + 2 * side], pieces[4 * shard + 2 * side + 1]
            shard_width = mine_0.shape[2]
            columns = slice(shard * shard_width, (shard + 1) * shard_width)
            for part in range(4):
                chosen = jnp.where(core == 0, mine_0[part], mine_1[part])
                if part < 3:
                    weight[part, place, columns] = chosen
                else:
                    projection[place, columns] = chosen

    rows = lax.broadcasted_iota(jnp.int32, (near, lanes), 0)
    spans = (lax.broadcasted_iota(jnp.int32, (near, lanes), 1) % block) // span_len
    same = (rows >= spans * span_len) & (rows < (spans + 1) * span_len + right_len)
    bias[...] = jnp.where(same, jnp.float32(0.0), jnp.float32(NEG_BIG))
    lane_spans = (lax.broadcasted_iota(jnp.int32, (1, lanes), 1) % block) // span_len
    memory_rows = lax.broadcasted_iota(jnp.int32, (memory_count, lanes), 0)
    feature_head = lax.broadcasted_iota(jnp.int32, (1, width), 1) // head_size
    head_masks = [(feature_head == h).astype(jnp.float32) for h in range(heads)]
    head_masks_16 = [m.astype(jnp.bfloat16) for m in head_masks]

    for rec, (own, extra, out) in enumerate(((rows_0, extra_0, out_0), (rows_1, extra_1, out_1))):
        length = scalars[1 + rec]
        scale = head_size ** (-0.5)
        query[...] = (
            jnp.dot(own[...], weight[0], preferred_element_type=jnp.float32) * scale
        ).astype(jnp.bfloat16)
        key[:frame_count] = jnp.dot(
            own[...], weight[1], preferred_element_type=jnp.float32
        ).astype(jnp.bfloat16)
        value[:frame_count] = jnp.dot(
            own[...], weight[2], preferred_element_type=jnp.float32
        ).astype(jnp.bfloat16)
        extra_key = jnp.dot(extra[...], weight[1], preferred_element_type=jnp.float32).astype(
            jnp.bfloat16
        )
        extra_value = jnp.dot(extra[...], weight[2], preferred_element_type=jnp.float32).astype(
            jnp.bfloat16
        )
        key[frame_count:] = extra_key[:pad]
        value[frame_count:] = extra_value[:pad]
        memory_key, memory_value = extra_key[pad:], extra_value[pad:]
        live_spans = (length + span_len - 1) // span_len

        def one_block(b, _):
            start = pl.multiple_of(b * block, block)
            q_now = query[pl.ds(start, block), :]
            stacked = jnp.concatenate([q_now * m for m in head_masks_16], axis=0)
            keys = jnp.concatenate([key[pl.ds(start, near), :], memory_key], axis=0)
            values = jnp.concatenate([value[pl.ds(start, near), :], memory_value], axis=0)
            scores = lax.dot_general(
                keys, stacked, (((1,), (1,)), ((), ())), preferred_element_type=jnp.float32
            )
            limit = length - first_frame - start
            local = jnp.where(rows < limit, scores[:near] + bias[...], NEG_BIG)
            span_limit = jnp.minimum(first_frame // span_len + 2 * b + lane_spans, live_spans)
            memory = jnp.where(memory_rows < span_limit, scores[near:], NEG_BIG)
            peak = jnp.maximum(
                jnp.max(local, axis=0, keepdims=True), jnp.max(memory, axis=0, keepdims=True)
            )
            local = jnp.exp(local - peak)
            memory = jnp.exp(memory - peak)
            total = jnp.sum(local, axis=0, keepdims=True) + jnp.sum(memory, axis=0, keepdims=True)
            inverse = 1.0 / total
            weights = jnp.concatenate([local * inverse, memory * inverse], axis=0).astype(
                jnp.bfloat16
            )
            mixed = lax.dot_general(
                weights, values, (((0,), (0,)), ((), ())), preferred_element_type=jnp.float32
            )
            picked = mixed[:block] * head_masks[0]
            for h in range(1, heads):
                picked = picked + mixed[h * block : (h + 1) * block] * head_masks[h]
            out[pl.ds(start, block), :] = picked.astype(jnp.bfloat16)
            return 0

        lax.fori_loop(0, frame_count // block, one_block, 0, unroll=2)


def encode_kernel(scalars, *refs):
    attended = refs[:4]
    projections = refs[4:8]
    frames, segments, owners_row, owners_col = refs[8:12]
    encoded_out, sent_out, gathered = refs[12:]
    first_frame, length, capacity = (scalars[i] for i in range(3))
    frame_count, _ = frames.shape
    token_count = owners_row.shape[1]
    offsets = [
        [pl.multiple_of(scalars[3 + 2 * i + s], LANES) for s in range(2)] for i in range(4)
    ]
    shard = attended[0].shape[1] // 2
    for i in range(4):
        for s in range(2):
            gathered[:, pl.ds(offsets[i][s], shard)] = attended[i][:, s * shard : (s + 1) * shard]
    tokens = lax.broadcasted_iota(jnp.int32, (token_count, frame_count), 0)
    indicator = segments[...] == tokens
    counts = jnp.sum(indicator.astype(jnp.float32), axis=1, keepdims=True)
    indicator = indicator.astype(jnp.bfloat16)
    earlier = lax.broadcasted_iota(jnp.int32, (token_count, token_count), 0)
    later = lax.broadcasted_iota(jnp.int32, (token_count, token_count), 1)
    clash = (owners_col[...] == owners_row[...]) & (earlier < later)
    slot = jnp.sum(clash.astype(jnp.int32), axis=0, keepdims=True)
    target = owners_row[...] * capacity + slot
    slots = lax.broadcasted_iota(jnp.int32, (sent_out.shape[0], token_count), 0)
    route = (slots == target).astype(jnp.bfloat16)
    live = (
        first_frame + lax.broadcasted_iota(jnp.int32, (frame_count, 1), 0) < length
    )
    for i in range(4):
        mixed = jnp.dot(
            gathered[...], projections[i][...], preferred_element_type=jnp.float32
        )
        base = jnp.concatenate(
            [frames[:, pl.ds(offsets[i][s], shard)] for s in range(2)], axis=1
        ).astype(jnp.float32)
        encoded = jnp.where(live, base + mixed, 0.0).astype(jnp.bfloat16)
        pooled = (
            jnp.dot(indicator, encoded, preferred_element_type=jnp.float32) / counts
        ).astype(jnp.bfloat16)
        sent = jnp.dot(route, pooled, preferred_element_type=jnp.float32).astype(jnp.bfloat16)
        for s in range(2):
            encoded_out[:, pl.ds(offsets[i][s], shard)] = encoded[:, s * shard : (s + 1) * shard]
            sent_out[:, pl.ds(offsets[i][s], shard)] = sent[:, s * shard : (s + 1) * shard]


def language_kernel(scalars, received, *refs):
    weights, out = refs[:-1], refs[-1]
    half = received.shape[1] // 2
    for i in range(len(weights) // 2):
        upper, lower = weights[2 * i], weights[2 * i + 1]
        width = upper.shape[1]
        place = pl.multiple_of(scalars[i], LANES)
        out[:, pl.ds(place, width)] = (
            jnp.dot(received[:, :half], upper[...], preferred_element_type=jnp.float32)
            + jnp.dot(received[:, half:], lower[...], preferred_element_type=jnp.float32)
        ).astype(jnp.bfloat16)


def along_x(r, j, _):
    return r, j ^ 1


def along_y(r, j, _):
    return r ^ 2, j


def other_core(r, j, _):
    return r ^ 1, j


def z_up(r, j, count):
    return r, (j + 2) % count


def z_down(r, j, count):
    return r, (j - 2) % count


def relocate(value, core_0, core_1):
    rec_count, time_count = lax.axis_size("rec"), lax.axis_size("tm")
    pairs = []
    for r in range(rec_count):
        for j in range(time_count):
            route = (core_0, core_1)[r % 2]
            if route is not None:
                to_r, to_j = route(r, j, time_count)
                pairs.append((r * time_count + j, to_r * time_count + to_j))
    return lax.ppermute(value, ("rec", "tm"), pairs)


def swap_cores(value):
    return relocate(value, other_core, other_core)


def exchange_blocks(blocks):
    return lax.all_to_all(blocks, "tm", split_axis=0, concat_axis=0, tiled=True)


def per_device(
    frames,
    lengths,
    norm_gain,
    memory_gain,
    qkv_weight,
    out_weight,
    segment_ids,
    owners,
    language_weight,
):
    local_frames = frames[0]
    frame_count, model_width = local_frames.shape
    shard = out_weight.shape[1]
    half = model_width // 2
    time_count = lax.axis_size("tm")
    rec_count = lax.axis_size("rec")
    rec, time = lax.axis_index("rec"), lax.axis_index("tm")
    core, y_half = rec % 2, (rec // 2) % 2
    x, z = time % 2, time // 2
    z_count = time_count // 2
    first_frame = time * frame_count
    length = lengths[0]
    head_size = model_width // H
    bf16 = jnp.bfloat16

    own = jnp.concatenate([qkv_weight, out_weight[None]], axis=0)
    own_a = lax.dynamic_slice_in_dim(own, y_half * half, half, 1)
    own_b = lax.dynamic_slice_in_dim(own, (1 - y_half) * half, half, 1)

    def pick(for_core_0, for_core_1):
        return jnp.where(core == 0, for_core_0, for_core_1)

    m1 = relocate(own_a, along_x, z_up)
    m2 = relocate(pick(own_a, own_b), z_down, z_up)
    language_half = language_weight.shape[0] // 2
    l1a = relocate(language_weight[:language_half], along_y, along_y)
    l1b = relocate(language_weight[language_half:], along_y, along_y)

    normed, memory = local_call(
        functools.partial(normalise_kernel, C),
        (shape_of(frame_count, model_width), shape_of(frame_count // C, model_width)),
        (
            jnp.stack([first_frame, length]).astype(jnp.int32),
            local_frames,
            norm_gain[None],
            memory_gain[None],
        ),
        flops=10 * frame_count * model_width,
        moved=4 * frame_count * model_width,
    )
    other_length = swap_cores(lengths)[0]
    other_normed = swap_cores(normed)
    ahead = shifted(normed[:RC], "tm", -1)
    memories = exchange_blocks(
        jnp.broadcast_to(memory[None], (time_count,) + memory.shape)
    ).reshape(-1, model_width)
    extra = jnp.concatenate([ahead, jnp.zeros_like(ahead), memories], axis=0)
    other_extra = swap_cores(extra)

    m3 = relocate(m1, along_y, along_x)
    m4 = relocate(m1, None, z_up)
    m5 = relocate(m2, along_x, z_up)
    m6 = relocate(pick(m2, m3), along_y, along_y)
    m7 = relocate(m4, None, along_x)
    m8 = relocate(m5, along_y, along_x)

    slot_pieces = (
        ((own_a, m1), (own_b, m2), (m1, m3), (m3, m6)),
        ((m2, m4), (m6, m5), (m5, m7), (m8, m8)),
    )
    scalars = jnp.stack([first_frame, length, other_length, core, y_half]).astype(jnp.int32)
    pad = 2 * RC
    block = 2 * C
    width = 2 * shard
    attended, outs = [], []
    for pieces in slot_pieces:
        flat = [p for pair in pieces for p in pair]
        *pair, out_piece = local_call(
            functools.partial(attend_kernel, C, RC, head_size),
            (
                shape_of(frame_count, width),
                shape_of(frame_count, width),
                shape_of(model_width, width),
            ),
            (scalars, normed, extra, other_normed, other_extra, *flat),
            scratch=(
                pltpu.VMEM((3, model_width, width), bf16),
                pltpu.VMEM((frame_count, width), bf16),
                pltpu.VMEM((frame_count + pad, width), bf16),
                pltpu.VMEM((frame_count + pad, width), bf16),
                pltpu.VMEM((block + pad, width // head_size * block), jnp.float32),
            ),
            flops=12 * frame_count * model_width * width,
            moved=8 * frame_count * model_width,
        )
        attended.append(pair)
        outs.append(out_piece)
    other_outs = [swap_cores(w) for w in outs]
    other_attended = [swap_cores(for_other) for _, for_other in attended]

    def group_of(of_core, slot):
        return jnp.where(of_core == 0, z + slot, z - slot - 1) % z_count

    offsets = []
    for of_core in (core, 1 - core):
        for slot in range(2):
            group = group_of(of_core, slot)
            offsets += [(2 * group + x) * shard, (2 * group + 1 - x) * shard]
    token_count = owners.shape[2]
    slot_count = 2 * token_count
    capacity = slot_count // time_count
    owners_col = owners[0, 0]
    encoded, sent_rows = local_call(
        encode_kernel,
        (shape_of(frame_count, model_width), shape_of(slot_count, model_width)),
        (
            jnp.stack([first_frame, length, capacity] + offsets).astype(jnp.int32),
            attended[0][0],
            attended[1][0],
            *other_attended,
            *outs,
            *other_outs,
            local_frames,
            segment_ids[0],
            owners_col.reshape(1, token_count),
            owners_col,
        ),
        scratch=(pltpu.VMEM((frame_count, model_width), bf16),),
        flops=2 * frame_count * model_width * model_width,
        moved=6 * frame_count * model_width,
    )
    received = exchange_blocks(
        sent_rows.reshape(time_count, capacity, model_width)
    ).reshape(slot_count, model_width)
    language_shard = language_weight.shape[1]
    places = [(rec ^ i) * language_shard for i in range(rec_count)]
    lm_out = local_call(
        language_kernel,
        shape_of(slot_count, rec_count * language_shard),
        (
            jnp.stack(places).astype(jnp.int32),
            received,
            *[language_weight[:language_half], language_weight[language_half:]],
            *[swap_cores(language_weight[:language_half])],
            *[swap_cores(language_weight[language_half:])],
            *[l1a, l1b],
            *[swap_cores(l1a), swap_cores(l1b)],
        ),
        flops=2 * slot_count * model_width * rec_count * language_shard,
        moved=2 * model_width * rec_count * language_shard,
    )
    return (encoded[None], lm_out[None, None])


def solution(mesh):
    in_specs = (
        P("rec", "tm", None),
        P("rec"),
        P(),
        P(),
        P(None, None, "tm"),
        P(None, "tm"),
        P("rec", "tm", None),
        P("rec", "tm", None, None),
        P(None, "rec"),
    )
    out_specs = (P("rec", "tm", None), P("rec", "tm", None, None))
    rec_count, time_count = mesh.shape["rec"], mesh.shape["tm"]
    paired = shard_map_of(mesh, in_specs, out_specs, per_device)
    plain = shard_map_of(mesh, in_specs, out_specs, plain_device)

    def run(*arrays):
        shard = arrays[5].shape[1] // time_count
        fits = rec_count == 4 and time_count == 8 and shard % LANES == 0
        return (paired if fits else plain)(*arrays)

    return run


def shard_map_of(mesh, in_specs, out_specs, body):
    return jax.shard_map(
        body, mesh=mesh, in_specs=in_specs, out_specs=out_specs, check_vma=False
    )
```

profile of v0, /device:TPU:0, one launch (start us, length us, event | category | flops | bytes accessed | tf_op | source)
XLA Modules:
  0.0 125.3 jit_solution(18143844628520814175)
XLA Ops:
  0.7 2.3 %broadcast_select_fusion.1 = (bf16[4,512,128]{2,1,0:T(8,128)(2,1)S(1)}, bf16[4,512,128]{2,1,0:T(8,128)(2,1)}, bf16[4,512,128]{2,1,0:T(8,128)(2,1)S(1)}) fusion(pred[]{:T(512)S(6)} %eq.18, s32[]{:T(128)S(6)} %select_n.82, bf16[1,1024,128]{2,1,0:T(8,128)(2,1)} %bitcast.33, bf16[3,1024,128]{2,1,0:T(8,128)(2,1)} %param.13, s32[]{:T(128)S(6)} %select_n.81), kind=kLoop, calls=%fused_computation.7 | loop fusion | flops 2359296 | bytes 2621449 | tf_op jit(solution)/shard_map/jit(_where)/select_n | solution.py:526
  3.0 3.0 %collective-permute-start.4 = (bf16[4,512,128]{2,1,0:T(8,128)(2,1)S(1)}, bf16[4,512,128]{2,1,0:T(8,128)(2,1)S(1)}, u32[]{:S(2)}, u32[]{:S(2)}) collective-permute-start(bf16[4,512,128]{2,1,0:T(8,128)(2,1)S(1)} %get-tuple-element.24.refs_4_), channel_id=1, source_target_pairs={{0,1},{1,0},{2,3},{3,2},{4,5},{5,4},{6,7},{7,6},{8,10},{9,11},{10,... | collective-permute-start | bytes 1572872 | tf_op jit(solution)/shard_map/ppermute | solution.py:484
  6.0 3.6 %collective-permute-start.5 = (bf16[4,512,128]{2,1,0:T(8,128)(2,1)S(1)}, bf16[4,512,128]{2,1,0:T(8,128)(2,1)S(1)}, u32[]{:S(2)}, u32[]{:S(2)}) collective-permute-start(bf16[4,512,128]{2,1,0:T(8,128)(2,1)S(1)} %get-tuple-element.22), channel_id=1, source_target_pairs={{0,6},{1,7},{2,0},{3,1},{4,2},{5,3},{6,4},{7,5},{8,10},{9,11},{10,... | collective-permute-start | bytes 1572872 | tf_op jit(solution)/shard_map/ppermute | solution.py:484
  9.6 3.6 %collective-permute-done.4.refs_5_.refs_8_ = bf16[4,512,128]{2,1,0:T(8,128)(2,1)S(1)} collective-permute-done((bf16[4,512,128]{2,1,0:T(8,128)(2,1)S(1)}, bf16[4,512,128]{2,1,0:T(8,128)(2,1)S(1)}, u32[]{:S(2)}, u32[]{:S(2)}) %collective-permute-start.4) | collective-permute-done | bytes 524320 | tf_op jit(solution)/shard_map/ppermute | solution.py:484
  13.1 2.1 %collective-permute-start.6 = (bf16[4,512,128]{2,1,0:T(8,128)(2,1)S(1)}, bf16[4,512,128]{2,1,0:T(8,128)(2,1)S(1)}, u32[]{:S(2)}, u32[]{:S(2)}) collective-permute-start(bf16[4,512,128]{2,1,0:T(8,128)(2,1)S(1)} %collective-permute-done.4.refs_5_.refs_8_), channel_id=1, source_target_pairs={{0,16},{1,17},{2,18},{3,19},{4,20},{5,21},{6,22},{7,23},{8,9},{9,8... | collective-permute-start | bytes 1572872 | tf_op jit(solution)/shard_map/ppermute | solution.py:484
  15.9 1.5 %collective-permute-start.8 = (bf16[4,512,128]{2,1,0:T(8,128)(2,1)S(1)}, bf16[4,512,128]{2,1,0:T(8,128)(2,1)}, u32[]{:S(2)}, u32[]{:S(2)}) collective-permute-start(bf16[4,512,128]{2,1,0:T(8,128)(2,1)S(1)} %collective-permute-done.4.refs_5_.refs_8_), channel_id=1, source_target_pairs={{8,10},{9,11},{10,12},{11,13},{12,14},{13,15},{14,8},{15,9},{24,26... | collective-permute-start | bytes 1572872 | tf_op jit(solution)/shard_map/ppermute | solution.py:484
  17.3 5.5 %collective-permute-done.5.refs_7_.refs_4_ = bf16[4,512,128]{2,1,0:T(8,128)(2,1)S(1)} collective-permute-done((bf16[4,512,128]{2,1,0:T(8,128)(2,1)S(1)}, bf16[4,512,128]{2,1,0:T(8,128)(2,1)S(1)}, u32[]{:S(2)}, u32[]{:S(2)}) %collective-permute-start.5) | collective-permute-done | bytes 524320 | tf_op jit(solution)/shard_map/ppermute | solution.py:484
  22.8 0.7 pad_add_fusion.scalars
  23.5 2.9 %shard_map.104 = (bf16[512,1024]{1,0:T(8,128)(2,1)}, bf16[16,1024]{1,0:T(8,128)(2,1)}) custom-call(s32[2]{0:T(128)} %pad_add_fusion.scalars, bf16[512,1024]{1,0:T(8,128)(2,1)} %bitcast.27, f32[1,1024]{1,0:T(1,128)} %bitcast.34, f32[1,1024]{1,0:T(1,128)} %bitcast.35), custom_call_target="tpu_custom_call" | custom-call | flops 5242880 | bytes 2097152 | tf_op jit(solution)/shard_map/pallas_call | solution.py:260
  26.5 2.7 %collective-permute-start.2 = (bf16[512,1024]{1,0:T(8,128)(2,1)}, bf16[512,1024]{1,0:T(8,128)(2,1)S(1)}, u32[]{:S(2)}, u32[]{:S(2)}) collective-permute-start(bf16[512,1024]{1,0:T(8,128)(2,1)} %get-tuple-element.12.refs_0_), channel_id=1, source_target_pairs={{0,8},{1,9},{2,10},{3,11},{4,12},{5,13},{6,14},{7,15},{8,0},{9,1},... | collective-permute-start | bytes 3145736 | tf_op jit(solution)/shard_map/ppermute | solution.py:484
  29.2 1.5 %broadcast_in_dim.27 = bf16[8,16,1024]{2,1,0:T(8,128)(2,1)} broadcast(bf16[16,1024]{1,0:T(8,128)(2,1)} %get-tuple-element.13), dimensions={1,2} | broadcast | bytes 294912 | tf_op jit(solution)/shard_map/broadcast_in_dim | solution.py:550
  30.6 5.7 %all-to-all-start = ((bf16[8,16,1024]{2,1,0:T(8,128)(2,1)}), bf16[8,16,1024]{2,1,0:T(8,128)(2,1)S(1)}, u32[]{:S(2)}, u32[]{:S(2)}) async-start(bf16[8,16,1024]{2,1,0:T(8,128)(2,1)} %broadcast_in_dim.27), calls=%async_computation | async-start | bytes 524288 | tf_op jit(solution)/shard_map/all_to_all | solution.py:492
  36.3 0.7 slice.6
  37.0 0.1 pad.7.clone
  37.1 1.3 %collective-permute-start.1 = (bf16[8,1024]{1,0:T(8,128)(2,1)S(1)}, bf16[8,1024]{1,0:T(8,128)(2,1)S(1)}, u32[]{:S(2)}, u32[]{:S(2)}) collective-permute-start(bf16[8,1024]{1,0:T(8,128)(2,1)S(1)} %slice.6), channel_id=1, source_target_pairs={{1,0},{2,1},{3,2},{4,3},{5,4},{6,5},{7,6},{9,8},{10,9},{11,10},{12... | collective-permute-start | bytes 49160 | tf_op jit(solution)/shard_map/ppermute | solution.py:25
  38.5 4.4 %collective-permute-done.1 = bf16[8,1024]{1,0:T(8,128)(2,1)S(1)} collective-permute-done((bf16[8,1024]{1,0:T(8,128)(2,1)S(1)}, bf16[8,1024]{1,0:T(8,128)(2,1)S(1)}, u32[]{:S(2)}, u32[]{:S(2)}) %collective-permute-start.1) | collective-permute-done | bytes 16416 | tf_op jit(solution)/shard_map/ppermute | solution.py:25
  42.9 1.5 %collective-permute-start.7 = (bf16[4,512,128]{2,1,0:T(8,128)(2,1)S(1)}, bf16[4,512,128]{2,1,0:T(8,128)(2,1)S(1)}, u32[]{:S(2)}, u32[]{:S(2)}) collective-permute-start(bf16[4,512,128]{2,1,0:T(8,128)(2,1)S(1)} %broadcast_select_fusion), channel_id=1, source_target_pairs={{0,16},{1,17},{2,18},{3,19},{4,20},{5,21},{6,22},{7,23},{8,24},{9,... | collective-permute-start | bytes 1572872 | tf_op jit(solution)/shard_map/ppermute | solution.py:484
  44.4 1.4 %collective-permute-start.10 = (bf16[4,512,128]{2,1,0:T(8,128)(2,1)}, bf16[4,512,128]{2,1,0:T(8,128)(2,1)}, u32[]{:S(2)}, u32[]{:S(2)}) collective-permute-start(bf16[4,512,128]{2,1,0:T(8,128)(2,1)} %collective-permute-done.8.refs_5_), channel_id=1, source_target_pairs={{8,9},{9,8},{10,11},{11,10},{12,13},{13,12},{14,15},{15,14},{24,25... | collective-permute-start | bytes 1572872 | tf_op jit(solution)/shard_map/ppermute | solution.py:484
  45.8 0.5 collective-permute-start.11
  46.3 0.1 pad_maximum_fusion.refs_1_
  46.5 2.9 %collective-permute-start.3 = (bf16[144,1024]{1,0:T(8,128)(2,1)S(1)}, bf16[144,1024]{1,0:T(8,128)(2,1)S(1)}, u32[]{:S(2)}, u32[]{:S(2)}) collective-permute-start(bf16[144,1024]{1,0:T(8,128)(2,1)S(1)} %pad_maximum_fusion.refs_1_), channel_id=1, source_target_pairs={{0,8},{1,9},{2,10},{3,11},{4,12},{5,13},{6,14},{7,15},{8,0},{9,1},... | collective-permute-start | bytes 884744 | tf_op jit(solution)/shard_map/ppermute | solution.py:484
  49.3 1.3 %stack.71.scalars = s32[5]{0:T(128)} concatenate(s32[1]{0:T(128)} %bitcast, s32[1]{0:T(128)S(6)} %copy.12, s32[1]{0:T(128)} %collective-permute-done, s32[1]{0:T(128)} %bitcast.9, s32[1]{0:T(128)} %bitcast.10), dimensions={0} | concatenate | bytes 40 | tf_op jit(solution)/shard_map/stack | solution.py:566
  50.7 5.8 %collective-permute-done.7.refs_11_.refs_6_ = bf16[4,512,128]{2,1,0:T(8,128)(2,1)S(1)} collective-permute-done((bf16[4,512,128]{2,1,0:T(8,128)(2,1)S(1)}, bf16[4,512,128]{2,1,0:T(8,128)(2,1)S(1)}, u32[]{:S(2)}, u32[]{:S(2)}) %collective-permute-start.7) | collective-permute-done | bytes 524320 | tf_op jit(solution)/shard_map/ppermute | solution.py:484
  56.5 0.8 copy-done.9
  57.3 13.8 %shard_map.105 = (bf16[512,256]{1,0:T(8,128)(2,1)}, bf16[512,256]{1,0:T(8,128)(2,1)}, bf16[1024,256]{1,0:T(8,128)(2,1)}) custom-call(s32[5]{0:T(128)} %stack.71.scalars, bf16[512,1024]{1,0:T(8,128)(2,1)} %get-tuple-element.12.refs_0_, bf16[144,1024]{1,0:T(8,128)(2,1)} %copy-done.3, bf16[512,1024]{1,0:T(8,128)(2,1)} %copy-done.2, ...), custom_call_target="tpu_custom_call" | custom-call | flops 1610612736 | bytes 4194304 | tf_op jit(solution)/shard_map/pallas_call | solution.py:260
  71.1 0.1 collective-permute-start.14
  71.2 0.8 copy-done.10
  72.0 13.7 %shard_map.106 = (bf16[512,256]{1,0:T(8,128)(2,1)}, bf16[512,256]{1,0:T(8,128)(2,1)}, bf16[1024,256]{1,0:T(8,128)(2,1)}) custom-call(s32[5]{0:T(128)} %stack.71.scalars, bf16[512,1024]{1,0:T(8,128)(2,1)} %get-tuple-element.12.refs_0_, bf16[144,1024]{1,0:T(8,128)(2,1)} %copy-done.3, bf16[512,1024]{1,0:T(8,128)(2,1)} %copy-done.2, ...), custom_call_target="tpu_custom_call" | custom-call | flops 1610612736 | bytes 4194304 | tf_op jit(solution)/shard_map/pallas_call | solution.py:260
  85.7 0.5 collective-permute-start.15
  86.2 0.1 collective-permute-start.12
  86.2 0.4 collective-permute-start.13
  86.8 1.6 %collective-permute-start.18 = (bf16[512,512]{1,0:T(8,128)(2,1)S(1)}, bf16[512,512]{1,0:T(8,128)(2,1)S(1)}, u32[]{:S(2)}, u32[]{:S(2)}) collective-permute-start(bf16[512,512]{1,0:T(8,128)(2,1)S(1)} %get-tuple-element.26.refs_0_), channel_id=1, source_target_pairs={{0,16},{1,17},{2,18},{3,19},{4,20},{5,21},{6,22},{7,23},{8,24},{9,... | collective-permute-start | bytes 1572872 | tf_op jit(solution)/shard_map/ppermute | solution.py:484
  88.4 1.4 %collective-permute-start.19 = (bf16[512,512]{1,0:T(8,128)(2,1)S(1)}, bf16[512,512]{1,0:T(8,128)(2,1)S(1)}, u32[]{:S(2)}, u32[]{:S(2)}) collective-permute-start(bf16[512,512]{1,0:T(8,128)(2,1)S(1)} %get-tuple-element.25.refs_1_), channel_id=1, source_target_pairs={{0,16},{1,17},{2,18},{3,19},{4,20},{5,21},{6,22},{7,23},{8,24},{9,... | collective-permute-start | bytes 1572872 | tf_op jit(solution)/shard_map/ppermute | solution.py:484
  89.8 0.7 copy-done.18
  90.5 0.7 copy.11.refs_11_
  91.2 0.6 stack.68.scalars
  91.8 0.8 copy-done.15
  92.6 7.2 %shard_map.107 = (bf16[512,1024]{1,0:T(8,128)(2,1)}, bf16[256,1024]{1,0:T(8,128)(2,1)}) custom-call(s32[11]{0:T(128)} %stack.68.scalars, bf16[512,256]{1,0:T(8,128)(2,1)} %get-tuple-element.14.refs_0_, bf16[512,256]{1,0:T(8,128)(2,1)} %get-tuple-element.15.refs_1_, bf16[512,256]{1,0:T(8,128)(2,1)} %copy-done.17, ...), custom_call_target="tpu_custom_call" | custom-call | flops 1073741824 | bytes 3145728 | tf_op jit(solution)/shard_map/pallas_call | solution.py:260
  99.8 5.4 %all-to-all-start.1 = ((bf16[8,32,1024]{2,1,0:T(8,128)(2,1)}), bf16[8,32,1024]{2,1,0:T(8,128)(2,1)S(1)}, u32[]{:S(2)}, u32[]{:S(2)}) async-start(bf16[8,32,1024]{2,1,0:T(8,128)(2,1)} %bitcast.32), calls=%async_computation.1 | async-start | bytes 1048576 | tf_op jit(solution)/shard_map/all_to_all | solution.py:492
  105.3 0.1 collective-permute-start.16
  105.3 0.5 collective-permute-start.17
  105.8 0.1 collective-permute-start.20
  105.9 6.1 %collective-permute-done.19.refs_5_ = bf16[512,512]{1,0:T(8,128)(2,1)S(1)} collective-permute-done((bf16[512,512]{1,0:T(8,128)(2,1)S(1)}, bf16[512,512]{1,0:T(8,128)(2,1)S(1)}, u32[]{:S(2)}, u32[]{:S(2)}) %collective-permute-start.19) | collective-permute-done | bytes 524320 | tf_op jit(solution)/shard_map/ppermute | solution.py:484
  112.0 0.8 pad_add_fusion.1.scalars
  112.8 1.2 collective-permute-done.21.refs_7_
  114.0 6.0 %all-to-all-done.1 = bf16[8,32,1024]{2,1,0:T(8,128)(2,1)S(1)} async-done(((bf16[8,32,1024]{2,1,0:T(8,128)(2,1)}), bf16[8,32,1024]{2,1,0:T(8,128)(2,1)S(1)}, u32[]{:S(2)}, u32[]{:S(2)}) %all-to-all-start.1) | async-done | bytes 524320 | tf_op jit(solution)/shard_map/all_to_all | solution.py:492
  120.0 0.8 copy-done.4
  120.8 4.5 %shard_map.108 = bf16[256,2048]{1,0:T(8,128)(2,1)} custom-call(s32[4]{0:T(128)} %pad_add_fusion.1.scalars, bf16[256,1024]{1,0:T(8,128)(2,1)} %bitcast.29, bf16[512,512]{1,0:T(8,128)(2,1)} %copy-done.6, bf16[512,512]{1,0:T(8,128)(2,1)} %copy-done.5, bf16[512,512]{1,0:T(8,128)(2,1)} %copy-done.16, bf16[512,512]{1,0:T(8,128)(2,1)} %collective-permute-done.17.refs_3_, ...), custom_call_target="tpu_custom_call" | custom-call | flops 1073741824 | bytes 4194304 | tf_op jit(solution)/shard_map/pallas_call | solution.py:260
  (58 shorter events, 0.3 us)
Async XLA Ops:
  3.0 23.4 %copy-start.7 = (bf16[4,512,128]{2,1,0:T(8,128)(2,1)}, bf16[4,512,128]{2,1,0:T(8,128)(2,1)S(1)}, u32[]{:S(2)}) copy-start(bf16[4,512,128]{2,1,0:T(8,128)(2,1)S(1)} %get-tuple-element.24.refs_4_) | copy-start | bytes 1572868
  3.0 10.1 %collective-permute-start.4 = (bf16[4,512,128]{2,1,0:T(8,128)(2,1)S(1)}, bf16[4,512,128]{2,1,0:T(8,128)(2,1)S(1)}, u32[]{:S(2)}, u32[]{:S(2)}) collective-permute-start(bf16[4,512,128]{2,1,0:T(8,128)(2,1)S(1)} %get-tuple-element.24.refs_4_), channel_id=1, source_target_pairs={{0,1},{1,0},{2,3},{3,2},{4,5},{5,4},{6,7},{7,6},{8,10},{9,11},{10,... | collective-permute-start | bytes 1572872 | tf_op jit(solution)/shard_map/ppermute | solution.py:484
  6.0 16.8 %collective-permute-start.5 = (bf16[4,512,128]{2,1,0:T(8,128)(2,1)S(1)}, bf16[4,512,128]{2,1,0:T(8,128)(2,1)S(1)}, u32[]{:S(2)}, u32[]{:S(2)}) collective-permute-start(bf16[4,512,128]{2,1,0:T(8,128)(2,1)S(1)} %get-tuple-element.22), channel_id=1, source_target_pairs={{0,6},{1,7},{2,0},{3,1},{4,2},{5,3},{6,4},{7,5},{8,10},{9,11},{10,... | collective-permute-start | bytes 1572872 | tf_op jit(solution)/shard_map/ppermute | solution.py:484
  13.1 13.3 %copy-start.8 = (bf16[4,512,128]{2,1,0:T(8,128)(2,1)}, bf16[4,512,128]{2,1,0:T(8,128)(2,1)S(1)}, u32[]{:S(2)}) copy-start(bf16[4,512,128]{2,1,0:T(8,128)(2,1)S(1)} %collective-permute-done.4.refs_5_.refs_8_) | copy-start | bytes 1572868
  13.1 24.0 %collective-permute-start.6 = (bf16[4,512,128]{2,1,0:T(8,128)(2,1)S(1)}, bf16[4,512,128]{2,1,0:T(8,128)(2,1)S(1)}, u32[]{:S(2)}, u32[]{:S(2)}) collective-permute-start(bf16[4,512,128]{2,1,0:T(8,128)(2,1)S(1)} %collective-permute-done.4.refs_5_.refs_8_), channel_id=1, source_target_pairs={{0,16},{1,17},{2,18},{3,19},{4,20},{5,21},{6,22},{7,23},{8,9},{9,8... | collective-permute-start | bytes 1572872 | tf_op jit(solution)/shard_map/ppermute | solution.py:484
  15.9 28.5 %collective-permute-start.8 = (bf16[4,512,128]{2,1,0:T(8,128)(2,1)S(1)}, bf16[4,512,128]{2,1,0:T(8,128)(2,1)}, u32[]{:S(2)}, u32[]{:S(2)}) collective-permute-start(bf16[4,512,128]{2,1,0:T(8,128)(2,1)S(1)} %collective-permute-done.4.refs_5_.refs_8_), channel_id=1, source_target_pairs={{8,10},{9,11},{10,12},{11,13},{12,14},{13,15},{14,8},{15,9},{24,26... | collective-permute-start | bytes 1572872 | tf_op jit(solution)/shard_map/ppermute | solution.py:484
  22.8 15.6 %copy-start = (bf16[4,512,128]{2,1,0:T(8,128)(2,1)}, bf16[4,512,128]{2,1,0:T(8,128)(2,1)S(1)}, u32[]{:S(2)}) copy-start(bf16[4,512,128]{2,1,0:T(8,128)(2,1)S(1)} %collective-permute-done.5.refs_7_.refs_4_) | copy-start | bytes 1572868
  22.8 23.0 %collective-permute-start.9 = (bf16[4,512,128]{2,1,0:T(8,128)(2,1)S(1)}, bf16[4,512,128]{2,1,0:T(8,128)(2,1)}, u32[]{:S(2)}, u32[]{:S(2)}) collective-permute-start(bf16[4,512,128]{2,1,0:T(8,128)(2,1)S(1)} %collective-permute-done.5.refs_7_.refs_4_), channel_id=1, source_target_pairs={{0,1},{1,0},{2,3},{3,2},{4,5},{5,4},{6,7},{7,6},{8,10},{9,11},{10,... | collective-permute-start | bytes 1572872 | tf_op jit(solution)/shard_map/ppermute | solution.py:484
  26.5 24.2 %collective-permute-start.2 = (bf16[512,1024]{1,0:T(8,128)(2,1)}, bf16[512,1024]{1,0:T(8,128)(2,1)S(1)}, u32[]{:S(2)}, u32[]{:S(2)}) collective-permute-start(bf16[512,1024]{1,0:T(8,128)(2,1)} %get-tuple-element.12.refs_0_), channel_id=1, source_target_pairs={{0,8},{1,9},{2,10},{3,11},{4,12},{5,13},{6,14},{7,15},{8,0},{9,1},... | collective-permute-start | bytes 3145736 | tf_op jit(solution)/shard_map/ppermute | solution.py:484
  30.6 15.7 %all-to-all-start = ((bf16[8,16,1024]{2,1,0:T(8,128)(2,1)}), bf16[8,16,1024]{2,1,0:T(8,128)(2,1)S(1)}, u32[]{:S(2)}, u32[]{:S(2)}) async-start(bf16[8,16,1024]{2,1,0:T(8,128)(2,1)} %broadcast_in_dim.27), calls=%async_computation | async-start | bytes 524288 | tf_op jit(solution)/shard_map/all_to_all | solution.py:492
  36.3 10.2 %collective-permute-start = (s32[1]{0:T(128)}, s32[1]{0:T(128)}, u32[]{:S(2)}, u32[]{:S(2)}) collective-permute-start(s32[1]{0:T(128)} %param.10), channel_id=1, source_target_pairs={{0,8},{1,9},{2,10},{3,11},{4,12},{5,13},{6,14},{7,15},{8,0},{9,1},... | collective-permute-start | bytes 20 | tf_op jit(solution)/shard_map/ppermute | solution.py:484
  37.1 1.4 %copy-start.1 = (bf16[4,512,128]{2,1,0:T(8,128)(2,1)}, bf16[4,512,128]{2,1,0:T(8,128)(2,1)S(1)}, u32[]{:S(2)}) copy-start(bf16[4,512,128]{2,1,0:T(8,128)(2,1)S(1)} %collective-permute-done.6.refs_9_.refs_10_) | copy-start | bytes 1572868
  37.1 5.7 %collective-permute-start.1 = (bf16[8,1024]{1,0:T(8,128)(2,1)S(1)}, bf16[8,1024]{1,0:T(8,128)(2,1)S(1)}, u32[]{:S(2)}, u32[]{:S(2)}) collective-permute-start(bf16[8,1024]{1,0:T(8,128)(2,1)S(1)} %slice.6), channel_id=1, source_target_pairs={{1,0},{2,1},{3,2},{4,3},{5,4},{6,5},{7,6},{9,8},{10,9},{11,10},{12... | collective-permute-start | bytes 49160 | tf_op jit(solution)/shard_map/ppermute | solution.py:25
  42.9 13.6 %collective-permute-start.7 = (bf16[4,512,128]{2,1,0:T(8,128)(2,1)S(1)}, bf16[4,512,128]{2,1,0:T(8,128)(2,1)S(1)}, u32[]{:S(2)}, u32[]{:S(2)}) collective-permute-start(bf16[4,512,128]{2,1,0:T(8,128)(2,1)S(1)} %broadcast_select_fusion), channel_id=1, source_target_pairs={{0,16},{1,17},{2,18},{3,19},{4,20},{5,21},{6,22},{7,23},{8,24},{9,... | collective-permute-start | bytes 1572872 | tf_op jit(solution)/shard_map/ppermute | solution.py:484
  44.4 26.8 %collective-permute-start.10 = (bf16[4,512,128]{2,1,0:T(8,128)(2,1)}, bf16[4,512,128]{2,1,0:T(8,128)(2,1)}, u32[]{:S(2)}, u32[]{:S(2)}) collective-permute-start(bf16[4,512,128]{2,1,0:T(8,128)(2,1)} %collective-permute-done.8.refs_5_), channel_id=1, source_target_pairs={{8,9},{9,8},{10,11},{11,10},{12,13},{13,12},{14,15},{15,14},{24,25... | collective-permute-start | bytes 1572872 | tf_op jit(solution)/shard_map/ppermute | solution.py:484
  45.8 25.3 %collective-permute-start.11 = (bf16[4,512,128]{2,1,0:T(8,128)(2,1)}, bf16[4,512,128]{2,1,0:T(8,128)(2,1)S(1)}, u32[]{:S(2)}, u32[]{:S(2)}) collective-permute-start(bf16[4,512,128]{2,1,0:T(8,128)(2,1)} %collective-permute-done.9.refs_7_.refs_8_), channel_id=1, source_target_pairs={{0,16},{1,17},{2,18},{3,19},{4,20},{5,21},{6,22},{7,23},{8,9},{9,8... | collective-permute-start | bytes 1572872 | tf_op jit(solution)/shard_map/ppermute | solution.py:484
  46.5 10.0 %copy-start.3 = (bf16[144,1024]{1,0:T(8,128)(2,1)}, bf16[144,1024]{1,0:T(8,128)(2,1)S(1)}, u32[]{:S(2)}) copy-start(bf16[144,1024]{1,0:T(8,128)(2,1)S(1)} %pad_maximum_fusion.refs_1_) | copy-start | bytes 884740
  46.5 4.2 %collective-permute-start.3 = (bf16[144,1024]{1,0:T(8,128)(2,1)S(1)}, bf16[144,1024]{1,0:T(8,128)(2,1)S(1)}, u32[]{:S(2)}, u32[]{:S(2)}) collective-permute-start(bf16[144,1024]{1,0:T(8,128)(2,1)S(1)} %pad_maximum_fusion.refs_1_), channel_id=1, source_target_pairs={{0,8},{1,9},{2,10},{3,11},{4,12},{5,13},{6,14},{7,15},{8,0},{9,1},... | collective-permute-start | bytes 884744 | tf_op jit(solution)/shard_map/ppermute | solution.py:484
  50.7 5.8 %copy-start.11 = (bf16[144,1024]{1,0:T(8,128)(2,1)}, bf16[144,1024]{1,0:T(8,128)(2,1)S(1)}, u32[]{:S(2)}) copy-start(bf16[144,1024]{1,0:T(8,128)(2,1)S(1)} %collective-permute-done.3.refs_3_) | copy-start | bytes 884740
  50.7 5.8 %copy-start.2 = (bf16[512,1024]{1,0:T(8,128)(2,1)}, bf16[512,1024]{1,0:T(8,128)(2,1)S(1)}, u32[]{:S(2)}) copy-start(bf16[512,1024]{1,0:T(8,128)(2,1)S(1)} %collective-permute-done.2.refs_2_) | copy-start | bytes 3145732
  56.5 0.8 copy-start.9
  71.1 15.1 %copy-start.19 = (bf16[512,256]{1,0:T(8,128)(2,1)S(1)}, bf16[512,256]{1,0:T(8,128)(2,1)}, u32[]{:S(2)}) copy-start(bf16[512,256]{1,0:T(8,128)(2,1)} %get-tuple-element.16) | copy-start | bytes 786436
  71.1 15.6 %copy-start.12 = (bf16[1024,512]{1,0:T(8,128)(2,1)S(1)}, bf16[1024,512]{1,0:T(8,128)(2,1)}, u32[]{:S(2)}) copy-start(bf16[1024,512]{1,0:T(8,128)(2,1)} %param.17) | copy-start | bytes 3145732
  71.1 20.8 %collective-permute-start.14 = (bf16[1024,256]{1,0:T(8,128)(2,1)}, bf16[1024,256]{1,0:T(8,128)(2,1)S(1)}, u32[]{:S(2)}, u32[]{:S(2)}) collective-permute-start(bf16[1024,256]{1,0:T(8,128)(2,1)} %get-tuple-element.18.refs_4_), channel_id=1, source_target_pairs={{0,8},{1,9},{2,10},{3,11},{4,12},{5,13},{6,14},{7,15},{8,0},{9,1},... | collective-permute-start | bytes 1572872 | tf_op jit(solution)/shard_map/ppermute | solution.py:484
  71.2 0.8 copy-start.10
  85.7 6.1 %collective-permute-start.15 = (bf16[1024,256]{1,0:T(8,128)(2,1)}, bf16[1024,256]{1,0:T(8,128)(2,1)}, u32[]{:S(2)}, u32[]{:S(2)}) collective-permute-start(bf16[1024,256]{1,0:T(8,128)(2,1)} %get-tuple-element.19.refs_5_), channel_id=1, source_target_pairs={{0,8},{1,9},{2,10},{3,11},{4,12},{5,13},{6,14},{7,15},{8,0},{9,1},... | collective-permute-start | bytes 1572872 | tf_op jit(solution)/shard_map/ppermute | solution.py:484
  86.2 2.2 %collective-permute-start.12 = (bf16[512,256]{1,0:T(8,128)(2,1)S(1)}, bf16[512,256]{1,0:T(8,128)(2,1)S(1)}, u32[]{:S(2)}, u32[]{:S(2)}) collective-permute-start(bf16[512,256]{1,0:T(8,128)(2,1)S(1)} %copy-done.19), channel_id=1, source_target_pairs={{0,8},{1,9},{2,10},{3,11},{4,12},{5,13},{6,14},{7,15},{8,0},{9,1},... | collective-permute-start | bytes 786440 | tf_op jit(solution)/shard_map/ppermute | solution.py:484
  86.2 5.6 %collective-permute-start.13 = (bf16[512,256]{1,0:T(8,128)(2,1)}, bf16[512,256]{1,0:T(8,128)(2,1)}, u32[]{:S(2)}, u32[]{:S(2)}) collective-permute-start(bf16[512,256]{1,0:T(8,128)(2,1)} %get-tuple-element.17), channel_id=1, source_target_pairs={{0,8},{1,9},{2,10},{3,11},{4,12},{5,13},{6,14},{7,15},{8,0},{9,1},... | collective-permute-start | bytes 786440 | tf_op jit(solution)/shard_map/ppermute | solution.py:484
  86.8 18.5 %copy-start.6 = (bf16[512,512]{1,0:T(8,128)(2,1)}, bf16[512,512]{1,0:T(8,128)(2,1)S(1)}, u32[]{:S(2)}) copy-start(bf16[512,512]{1,0:T(8,128)(2,1)S(1)} %get-tuple-element.26.refs_0_) | copy-start | bytes 1572868
  86.8 18.6 %copy-start.5 = (bf16[512,512]{1,0:T(8,128)(2,1)}, bf16[512,512]{1,0:T(8,128)(2,1)S(1)}, u32[]{:S(2)}) copy-start(bf16[512,512]{1,0:T(8,128)(2,1)S(1)} %get-tuple-element.25.refs_1_) | copy-start | bytes 1572868
  86.8 19.1 %collective-permute-start.18 = (bf16[512,512]{1,0:T(8,128)(2,1)S(1)}, bf16[512,512]{1,0:T(8,128)(2,1)S(1)}, u32[]{:S(2)}, u32[]{:S(2)}) collective-permute-start(bf16[512,512]{1,0:T(8,128)(2,1)S(1)} %get-tuple-element.26.refs_0_), channel_id=1, source_target_pairs={{0,16},{1,17},{2,18},{3,19},{4,20},{5,21},{6,22},{7,23},{8,24},{9,... | collective-permute-start | bytes 1572872 | tf_op jit(solution)/shard_map/ppermute | solution.py:484
  88.4 3.5 %copy-start.17 = (bf16[512,256]{1,0:T(8,128)(2,1)}, bf16[512,256]{1,0:T(8,128)(2,1)S(1)}, u32[]{:S(2)}) copy-start(bf16[512,256]{1,0:T(8,128)(2,1)S(1)} %collective-permute-done.12.refs_2_) | copy-start | bytes 786436
  88.4 23.6 %collective-permute-start.19 = (bf16[512,512]{1,0:T(8,128)(2,1)S(1)}, bf16[512,512]{1,0:T(8,128)(2,1)S(1)}, u32[]{:S(2)}, u32[]{:S(2)}) collective-permute-start(bf16[512,512]{1,0:T(8,128)(2,1)S(1)} %get-tuple-element.25.refs_1_), channel_id=1, source_target_pairs={{0,16},{1,17},{2,18},{3,19},{4,20},{5,21},{6,22},{7,23},{8,24},{9,... | collective-permute-start | bytes 1572872 | tf_op jit(solution)/shard_map/ppermute | solution.py:484
  89.8 0.7 copy-start.18
  91.8 0.8 copy-start.15
  99.8 20.1 %all-to-all-start.1 = ((bf16[8,32,1024]{2,1,0:T(8,128)(2,1)}), bf16[8,32,1024]{2,1,0:T(8,128)(2,1)S(1)}, u32[]{:S(2)}, u32[]{:S(2)}) async-start(bf16[8,32,1024]{2,1,0:T(8,128)(2,1)} %bitcast.32), calls=%async_computation.1 | async-start | bytes 1048576 | tf_op jit(solution)/shard_map/all_to_all | solution.py:492
  105.3 7.5 %collective-permute-start.16 = (bf16[512,512]{1,0:T(8,128)(2,1)S(1)}, bf16[512,512]{1,0:T(8,128)(2,1)S(1)}, u32[]{:S(2)}, u32[]{:S(2)}) collective-permute-start(bf16[512,512]{1,0:T(8,128)(2,1)S(1)} %get-tuple-element.26.refs_0_), channel_id=1, source_target_pairs={{0,8},{1,9},{2,10},{3,11},{4,12},{5,13},{6,14},{7,15},{8,0},{9,1},... | collective-permute-start | bytes 1572872 | tf_op jit(solution)/shard_map/ppermute | solution.py:484
  105.3 7.4 %collective-permute-start.17 = (bf16[512,512]{1,0:T(8,128)(2,1)S(1)}, bf16[512,512]{1,0:T(8,128)(2,1)}, u32[]{:S(2)}, u32[]{:S(2)}) collective-permute-start(bf16[512,512]{1,0:T(8,128)(2,1)S(1)} %get-tuple-element.25.refs_1_), channel_id=1, source_target_pairs={{0,8},{1,9},{2,10},{3,11},{4,12},{5,13},{6,14},{7,15},{8,0},{9,1},... | collective-permute-start | bytes 1572872 | tf_op jit(solution)/shard_map/ppermute | solution.py:484
  105.8 14.2 %copy-start.13 = (bf16[512,512]{1,0:T(8,128)(2,1)}, bf16[512,512]{1,0:T(8,128)(2,1)S(1)}, u32[]{:S(2)}) copy-start(bf16[512,512]{1,0:T(8,128)(2,1)S(1)} %collective-permute-done.18.refs_4_) | copy-start | bytes 1572868
  105.8 6.9 %collective-permute-start.20 = (bf16[512,512]{1,0:T(8,128)(2,1)S(1)}, bf16[512,512]{1,0:T(8,128)(2,1)}, u32[]{:S(2)}, u32[]{:S(2)}) collective-permute-start(bf16[512,512]{1,0:T(8,128)(2,1)S(1)} %collective-permute-done.18.refs_4_), channel_id=1, source_target_pairs={{0,8},{1,9},{2,10},{3,11},{4,12},{5,13},{6,14},{7,15},{8,0},{9,1},... | collective-permute-start | bytes 1572872 | tf_op jit(solution)/shard_map/ppermute | solution.py:484
  112.0 8.0 %copy-start.14 = (bf16[512,512]{1,0:T(8,128)(2,1)}, bf16[512,512]{1,0:T(8,128)(2,1)S(1)}, u32[]{:S(2)}) copy-start(bf16[512,512]{1,0:T(8,128)(2,1)S(1)} %collective-permute-done.19.refs_5_) | copy-start | bytes 1572868
  112.0 2.0 %collective-permute-start.21 = (bf16[512,512]{1,0:T(8,128)(2,1)S(1)}, bf16[512,512]{1,0:T(8,128)(2,1)}, u32[]{:S(2)}, u32[]{:S(2)}) collective-permute-start(bf16[512,512]{1,0:T(8,128)(2,1)S(1)} %collective-permute-done.19.refs_5_), channel_id=1, source_target_pairs={{0,8},{1,9},{2,10},{3,11},{4,12},{5,13},{6,14},{7,15},{8,0},{9,1},... | collective-permute-start | bytes 1572872 | tf_op jit(solution)/shard_map/ppermute | solution.py:484
  112.8 7.2 %copy-start.16 = (bf16[512,512]{1,0:T(8,128)(2,1)}, bf16[512,512]{1,0:T(8,128)(2,1)S(1)}, u32[]{:S(2)}) copy-start(bf16[512,512]{1,0:T(8,128)(2,1)S(1)} %collective-permute-done.16.refs_2_) | copy-start | bytes 1572868
  120.0 0.8 copy-start.4
where the time goes:
time: 126 us; the launch traced here: 125 us
  Pallas kernels  42.2 us (33%)
  starting transfers between devices  36.2 us (29%)
  waiting for transfers between devices  32.5 us (26%)
  local copies, waits for them, and re-layouts  8.85 us (7%)
  other arithmetic  3.96 us (3%)
  between operations  1.56 us (1%)
    pallas_call x5, Pallas kernels, local_call(): pl.pallas_call(kernel, out_shape=out_shapes, in_specs=[smem_spec()] + [vm...  42.2 us
    ppermute x21, starting transfers between devices, relocate(): return lax.ppermute(value, ('rec', 'tm'), pairs)  23.9 us
    ppermute x21, waiting for transfers between devices, relocate(): return lax.ppermute(value, ('rec', 'tm'), pairs)  22.2 us
    all_to_all x2, starting transfers between devices, exchange_blocks(): return lax.all_to_all(blocks, 'tm', split_axis=0, concat_axis=0, tiled=True)  11.1 us
    all_to_all x2, waiting for transfers between devices, exchange_blocks(): return lax.all_to_all(blocks, 'tm', split_axis=0, concat_axis=0, tiled=True)  5.97 us
    ppermute x1, waiting for transfers between devices, shifted(): return lax.ppermute(block, axis, route)  4.36 us
    unnamed x40, local copies, waits for them, and re-layouts  3.84 us
  transfers between devices with their start and end apart: 24, of which 7 were waited for; matrix products, arithmetic and copies ran while one was open for 5% of the time, Pallas kernels for 30%

commit v1 on v0

--- a/solution.py
+++ b/solution.py
@@ -17,6 +17,7 @@
 EPS_MEMORY = 1e-06
 NEG_BIG = -1e30
 LANES = 128
+LOG2_E = 1.4426950408889634
 
 
 def shifted(block, axis, distance):
@@ -256,15 +257,18 @@
     return pl.BlockSpec(memory_space=pltpu.SMEM)
 
 
-def local_call(kernel, out_shapes, operands, scratch=(), flops=0, moved=0):
+def local_call(kernel, out_shapes, scalars, operands, scratch=(), in_place=0, flops=0, moved=0):
+    whole = len(operands) - in_place
     return pl.pallas_call(
         kernel,
         out_shape=out_shapes,
-        in_specs=[smem_spec()] + [vmem_spec()] * (len(operands) - 1),
+        in_specs=[smem_spec()] * len(scalars)
+        + [vmem_spec()] * whole
+        + [pl.BlockSpec(memory_space=pl.ANY)] * in_place,
         out_specs=jax.tree.map(lambda _: vmem_spec(), out_shapes),
         scratch_shapes=list(scratch),
         cost_estimate=pl.CostEstimate(flops=flops, bytes_accessed=moved, transcendentals=0),
-    )(*operands)
+    )(*scalars, *operands)
 
 
 def shape_of(*dims, dtype=jnp.bfloat16):
@@ -296,34 +300,72 @@
     ).astype(jnp.bfloat16)
 
 
-def attend_kernel(span_len, right_len, head_size, scalars, *refs):
-    (rows_0, extra_0, rows_1, extra_1) = refs[:4]
-    pieces = refs[4:12]
-    out_0, out_1, projection, weight, query, key, value, bias = refs[12:]
-    first_frame, core, y_half = scalars[0], scalars[3], scalars[4]
-    frame_count, model_width = rows_0.shape
+def attend_kernel(span_len, right_len, head_size, scalars, other_length, *refs):
+    sources, pieces = refs[:4], refs[4:12]
+    out_0, out_1, projection = refs[12:15]
+    rows_in, weight, query, key, value, bias, scores, peaks, weights, sems = refs[15:]
+    first_frame, core, y_half = scalars[0], scalars[2], scalars[3]
+    frame_count, model_width = sources[0].shape
     half = model_width // 2
     width = out_0.shape[1]
     heads = width // head_size
     block = 2 * span_len
-    pad = key.shape[0] - frame_count
-    near = block + pad
-    memory_count = extra_0.shape[0] - pad
+    blocks = frame_count // block
+    near = bias.shape[0]
+    pad = near - block
+    row_count = rows_in.shape[1]
+    memory_count = row_count - frame_count - pad
+    memory_at = frame_count + pad
     lanes = heads * block
 
-    places = (y_half * half, (1 - y_half) * half)
-    for side in range(2):
-        place = pl.ds(pl.multiple_of(places[side], half), half)
-        for shard in range(2):
-            mine_0, mine_1 = pieces[4 * shard + 2 * side], pieces[4 * shard + 2 * side + 1]
-            shard_width = mine_0.shape[2]
-            columns = slice(shard * shard_width, (shard + 1) * shard_width)
-            for part in range(4):
-                chosen = jnp.where(core == 0, mine_0[part], mine_1[part])
-                if part < 3:
-                    weight[part, place, columns] = chosen
+    def piece_copies(of_core, projected):
+        places = (y_half * half, (1 - y_half) * half)
+        copies = []
+        for side in range(2):
+            place = pl.ds(pl.multiple_of(places[side], half), half)
+            for shard in range(2):
+                piece = pieces[4 * shard + 2 * side + of_core]
+                columns = pl.ds(shard * piece.shape[2], piece.shape[2])
+                index = 2 * side + shard
+                if projected:
+                    ends = piece.at[3], projection.at[place, columns], sems.at[4 + index]
                 else:
-                    projection[place, columns] = chosen
+                    ends = piece.at[0:3], weight.at[:, place, columns], sems.at[index]
+                copies.append(pltpu.make_async_copy(*ends))
+        return copies
+
+    row_copies = []
+    for rec in range(2):
+        row_copies.append(
+            [
+                pltpu.make_async_copy(
+                    sources[2 * rec], rows_in.at[rec, 0:frame_count], sems.at[8 + 2 * rec]
+                ),
+                pltpu.make_async_copy(
+                    sources[2 * rec + 1],
+                    rows_in.at[rec, frame_count:row_count],
+                    sems.at[9 + 2 * rec],
+                ),
+            ]
+        )
+
+    for of_core in range(2):
+
+        @pl.when(core == of_core)
+        def _():
+            for copy in piece_copies(of_core, False):
+                copy.start()
+
+    for copies in row_copies:
+        for copy in copies:
+            copy.start()
+
+    for of_core in range(2):
+
+        @pl.when(core == of_core)
+        def _():
+            for copy in piece_copies(of_core, True):
+                copy.start()
 
     rows = lax.broadcasted_iota(jnp.int32, (near, lanes), 0)
     spans = (lax.broadcasted_iota(jnp.int32, (near, lanes), 1) % block) // span_len
@@ -332,86 +374,115 @@
     lane_spans = (lax.broadcasted_iota(jnp.int32, (1, lanes), 1) % block) // span_len
     memory_rows = lax.broadcasted_iota(jnp.int32, (memory_count, lanes), 0)
     feature_head = lax.broadcasted_iota(jnp.int32, (1, width), 1) // head_size
-    head_masks = [(feature_head == h).astype(jnp.float32) for h in range(heads)]
-    head_masks_16 = [m.astype(jnp.bfloat16) for m in head_masks]
-
-    for rec, (own, extra, out) in enumerate(((rows_0, extra_0, out_0), (rows_1, extra_1, out_1))):
-        length = scalars[1 + rec]
-        scale = head_size ** (-0.5)
-        query[...] = (
-            jnp.dot(own[...], weight[0], preferred_element_type=jnp.float32) * scale
+    head_masks = [(feature_head == h).astype(jnp.bfloat16) for h in range(heads)]
+    scale = head_size ** (-0.5) * LOG2_E
+
+    for copy in piece_copies(0, False):
+        copy.wait()
+    for rec in range(2):
+        for copy in row_copies[rec]:
+            copy.wait()
+        query[rec] = (
+            jnp.dot(
+                rows_in[rec, 0:frame_count], weight[0], preferred_element_type=jnp.float32
+            )
+            * scale
         ).astype(jnp.bfloat16)
-        key[:frame_count] = jnp.dot(
-            own[...], weight[1], preferred_element_type=jnp.float32
+        key[rec] = jnp.dot(
+            rows_in[rec], weight[1], preferred_element_type=jnp.float32
         ).astype(jnp.bfloat16)
-        value[:frame_count] = jnp.dot(
-            own[...], weight[2], preferred_element_type=jnp.float32
+        value[rec] = jnp.dot(
+            rows_in[rec], weight[2], preferred_element_type=jnp.float32
         ).astype(jnp.bfloat16)
-        extra_key = jnp.dot(extra[...], weight[1], preferred_element_type=jnp.float32).astype(
-            jnp.bfloat16
+
+    def score_block(i, _):
+        rec = i // blocks
+        b = i - rec * blocks
+        length = jnp.where(rec == 0, scalars[1], other_length[0])
+        start = pl.multiple_of(b * block, block)
+        q_now = query[rec, pl.ds(start, block), :]
+        stacked = jnp.concatenate([q_now * m for m in head_masks], axis=0)
+        keys = jnp.concatenate(
+            [key[rec, pl.ds(start, near), :], key[rec, memory_at:row_count, :]], axis=0
         )
-        extra_value = jnp.dot(extra[...], weight[2], preferred_element_type=jnp.float32).astype(
-            jnp.bfloat16
+        raw = lax.dot_general(
+            keys, stacked, (((1,), (1,)), ((), ())), preferred_element_type=jnp.float32
         )
-        key[frame_count:] = extra_key[:pad]
-        value[frame_count:] = extra_value[:pad]
-        memory_key, memory_value = extra_key[pad:], extra_value[pad:]
+        limit = length - first_frame - start
+        local = jnp.where(rows < limit, raw[:near] + bias[...], NEG_BIG)
         live_spans = (length + span_len - 1) // span_len
-
-        def one_block(b, _):
+        span_limit = jnp.minimum(first_frame // span_len + 2 * b + lane_spans, live_spans)
+        memory = jnp.where(memory_rows < span_limit, raw[near:], NEG_BIG)
+        scores[i, 0:near, :] = local
+        scores[i, near:, :] = memory
+        peaks[i] = jnp.maximum(
+            jnp.max(local, axis=0, keepdims=True), jnp.max(memory, axis=0, keepdims=True)
+        )
+        return 0
+
+    def weigh_block(i, _):
+        weights[i] = jnp.exp2(scores[i] - peaks[i]).astype(jnp.bfloat16)
+        return 0
+
+    ones = jnp.ones((near + memory_count, LANES), jnp.bfloat16)
+    first_of_pair = lax.broadcasted_iota(jnp.int32, (1, 2 * LANES), 1) % LANES < head_size
+
+    def mix_block(rec, out):
+        def body(b, _):
             start = pl.multiple_of(b * block, block)
-            q_now = query[pl.ds(start, block), :]
-            stacked = jnp.concatenate([q_now * m for m in head_masks_16], axis=0)
-            keys = jnp.concatenate([key[pl.ds(start, near), :], memory_key], axis=0)
-            values = jnp.concatenate([value[pl.ds(start, near), :], memory_value], axis=0)
-            scores = lax.dot_general(
-                keys, stacked, (((1,), (1,)), ((), ())), preferred_element_type=jnp.float32
+            values = jnp.concatenate(
+                [value[rec, pl.ds(start, near), :], value[rec, memory_at:row_count, :]], axis=0
             )
-            limit = length - first_frame - start
-            local = jnp.where(rows < limit, scores[:near] + bias[...], NEG_BIG)
-            span_limit = jnp.minimum(first_frame // span_len + 2 * b + lane_spans, live_spans)
-            memory = jnp.where(memory_rows < span_limit, scores[near:], NEG_BIG)
-            peak = jnp.maximum(
-                jnp.max(local, axis=0, keepdims=True), jnp.max(memory, axis=0, keepdims=True)
-            )
-            local = jnp.exp(local - peak)
-            memory = jnp.exp(memory - peak)
-            total = jnp.sum(local, axis=0, keepdims=True) + jnp.sum(memory, axis=0, keepdims=True)
-            inverse = 1.0 / total
-            weights = jnp.concatenate([local * inverse, memory * inverse], axis=0).astype(
-                jnp.bfloat16
-            )
-            mixed = lax.dot_general(
-                weights, values, (((0,), (0,)), ((), ())), preferred_element_type=jnp.float32
-            )
-            picked = mixed[:block] * head_masks[0]
-            for h in range(1, heads):
-                picked = picked + mixed[h * block : (h + 1) * block] * head_masks[h]
-            out[pl.ds(start, block), :] = picked.astype(jnp.bfloat16)
+            for pair in range(width // LANES):
+                columns = slice(pair * LANES, (pair + 1) * LANES)
+                pair_rows = slice(pair * 2 * block, (pair + 1) * 2 * block)
+                mixed = lax.dot_general(
+                    weights[rec * blocks + b, :, pair_rows],
+                    jnp.concatenate([values[:, columns], ones], axis=1),
+                    (((0,), (0,)), ((), ())),
+                    preferred_element_type=jnp.float32,
+                )
+                picked = jnp.where(first_of_pair, mixed[:block], mixed[block:])
+                out[pl.ds(start, block), columns] = (
+                    picked[:, :LANES] / picked[:, LANES:]
+                ).astype(jnp.bfloat16)
             return 0
 
-        lax.fori_loop(0, frame_count // block, one_block, 0, unroll=2)
-
-
-def encode_kernel(scalars, *refs):
-    attended = refs[:4]
-    projections = refs[4:8]
-    frames, segments, owners_row, owners_col = refs[8:12]
-    encoded_out, sent_out, gathered = refs[12:]
-    first_frame, length, capacity = (scalars[i] for i in range(3))
-    frame_count, _ = frames.shape
-    token_count = owners_row.shape[1]
+        return body
+
+    lax.fori_loop(0, 2 * blocks, score_block, 0, unroll=2)
+    lax.fori_loop(0, 2 * blocks, weigh_block, 0, unroll=2)
+    for rec, out in enumerate((out_0, out_1)):
+        lax.fori_loop(0, blocks, mix_block(rec, out), 0, unroll=2)
+    for copy in piece_copies(0, True):
+        copy.wait()
+
+
+def assemble(scalars, offsets_at, attended, gathered):
+    shard = attended[0].shape[1] // 2
     offsets = [
-        [pl.multiple_of(scalars[3 + 2 * i + s], LANES) for s in range(2)] for i in range(4)
+        [pl.multiple_of(scalars[offsets_at + 2 * i + s], LANES) for s in range(2)]
+        for i in range(4)
     ]
-    shard = attended[0].shape[1] // 2
     for i in range(4):
         for s in range(2):
             gathered[:, pl.ds(offsets[i][s], shard)] = attended[i][:, s * shard : (s + 1) * shard]
+    return offsets, shard
+
+
+def pool_kernel(offsets_at, scalars, *refs):
+    attended, projections = refs[:4], refs[4:8]
+    frames, segments, owners_row, owners_col = refs[8:12]
+    sent_out, gathered = refs[12:]
+    first_frame, length, capacity = scalars[0], scalars[1], scalars[4]
+    frame_count, _ = frames.shape
+    offsets, shard = assemble(scalars, offsets_at, attended, gathered)
+    token_count = owners_row.shape[1]
     tokens = lax.broadcasted_iota(jnp.int32, (token_count, frame_count), 0)
-    indicator = segments[...] == tokens
-    counts = jnp.sum(indicator.astype(jnp.float32), axis=1, keepdims=True)
-    indicator = indicator.astype(jnp.bfloat16)
+    places = first_frame + lax.broadcasted_iota(jnp.int32, (token_count, frame_count), 1)
+    member = (segments[...] == tokens).astype(jnp.float32)
+    counts = jnp.sum(member, axis=1, keepdims=True)
+    live_member = jnp.where(places < length, member, 0.0).astype(jnp.bfloat16)
     earlier = lax.broadcasted_iota(jnp.int32, (token_count, token_count), 0)
     later = lax.broadcasted_iota(jnp.int32, (token_count, token_count), 1)
     clash = (owners_col[...] == owners_row[...]) & (earlier < later)
@@ -419,36 +490,58 @@
     target = owners_row[...] * capacity + slot
     slots = lax.broadcasted_iota(jnp.int32, (sent_out.shape[0], token_count), 0)
     route = (slots == target).astype(jnp.bfloat16)
+    mean_attended = (
+        jnp.dot(live_member, gathered[...], preferred_element_type=jnp.float32) / counts
+    ).astype(jnp.bfloat16)
+    for i in range(4):
+        mixed = jnp.dot(mean_attended, projections[i][...], preferred_element_type=jnp.float32)
+        for s in range(2):
+            columns = pl.ds(offsets[i][s], shard)
+            base = jnp.dot(live_member, frames[:, columns], preferred_element_type=jnp.float32)
+            pooled = (base / counts + mixed[:, s * shard : (s + 1) * shard]).astype(jnp.bfloat16)
+            sent_out[:, columns] = jnp.dot(
+                route, pooled, preferred_element_type=jnp.float32
+            ).astype(jnp.bfloat16)
+
+
+def encode_kernel(offsets_at, scalars, *refs):
+    attended, projections, frames = refs[:4], refs[4:8], refs[8]
+    encoded_out, gathered = refs[9:]
+    first_frame, length = scalars[0], scalars[1]
+    frame_count, _ = frames.shape
+    offsets, shard = assemble(scalars, offsets_at, attended, gathered)
     live = (
         first_frame + lax.broadcasted_iota(jnp.int32, (frame_count, 1), 0) < length
-    )
+    ).astype(jnp.float32)
     for i in range(4):
         mixed = jnp.dot(
             gathered[...], projections[i][...], preferred_element_type=jnp.float32
         )
-        base = jnp.concatenate(
-            [frames[:, pl.ds(offsets[i][s], shard)] for s in range(2)], axis=1
-        ).astype(jnp.float32)
-        encoded = jnp.where(live, base + mixed, 0.0).astype(jnp.bfloat16)
-        pooled = (
-            jnp.dot(indicator, encoded, preferred_element_type=jnp.float32) / counts
-        ).astype(jnp.bfloat16)
-        sent = jnp.dot(route, pooled, preferred_element_type=jnp.float32).astype(jnp.bfloat16)
         for s in range(2):
-            encoded_out[:, pl.ds(offsets[i][s], shard)] = encoded[:, s * shard : (s + 1) * shard]
-            sent_out[:, pl.ds(offsets[i][s], shard)] = sent[:, s * shard : (s + 1) * shard]
-
-
-def language_kernel(scalars, received, *refs):
-    weights, out = refs[:-1], refs[-1]
-    half = received.shape[1] // 2
-    for i in range(len(weights) // 2):
-        upper, lower = weights[2 * i], weights[2 * i + 1]
-        width = upper.shape[1]
-        place = pl.multiple_of(scalars[i], LANES)
-        out[:, pl.ds(place, width)] = (
-            jnp.dot(received[:, :half], upper[...], preferred_element_type=jnp.float32)
-            + jnp.dot(received[:, half:], lower[...], preferred_element_type=jnp.float32)
+            columns = pl.ds(offsets[i][s], shard)
+            base = frames[:, columns].astype(jnp.float32)
+            encoded_out[:, columns] = (
+                (base + mixed[:, s * shard : (s + 1) * shard]) * live
+            ).astype(jnp.bfloat16)
+
+
+def language_kernel(places_at, scalars, received, *refs):
+    pieces, out, weights, sems = refs[:-3], refs[-3], refs[-2], refs[-1]
+    half, width = pieces[0].shape
+    copies = [
+        pltpu.make_async_copy(
+            piece, weights.at[i // 2, pl.ds((i % 2) * half, half)], sems.at[i]
+        )
+        for i, piece in enumerate(pieces)
+    ]
+    for copy in copies:
+        copy.start()
+    for i in range(len(pieces) // 2):
+        copies[2 * i].wait()
+        copies[2 * i + 1].wait()
+        place = pl.multiple_of(scalars[places_at + i], LANES)
+        out[:, pl.ds(place, width)] = jnp.dot(
+            received[...], weights[i], preferred_element_type=jnp.float32
         ).astype(jnp.bfloat16)
 
 
@@ -525,25 +618,40 @@
     def pick(for_core_0, for_core_1):
         return jnp.where(core == 0, for_core_0, for_core_1)
 
+    token_count = owners.shape[2]
+    slot_count = 2 * token_count
+    capacity = slot_count // time_count
+    language_shard = language_weight.shape[1]
+
+    def group_of(of_core, slot):
+        return jnp.where(of_core == 0, z + slot, z - slot - 1) % z_count
+
+    numbers = [first_frame, length, core, y_half, capacity]
+    offsets_at = len(numbers)
+    for of_core in (core, 1 - core):
+        for slot in range(2):
+            group = group_of(of_core, slot)
+            numbers += [(2 * group + x) * shard, (2 * group + 1 - x) * shard]
+    places_at = len(numbers)
+    numbers += [(rec ^ i) * language_shard for i in range(rec_count)]
+    scalars = jnp.stack(numbers).astype(jnp.int32)
+
     m1 = relocate(own_a, along_x, z_up)
     m2 = relocate(pick(own_a, own_b), z_down, z_up)
     language_half = language_weight.shape[0] // 2
-    l1a = relocate(language_weight[:language_half], along_y, along_y)
-    l1b = relocate(language_weight[language_half:], along_y, along_y)
+    upper, lower = language_weight[:language_half], language_weight[language_half:]
+    l1a = relocate(upper, along_y, along_y)
+    l1b = relocate(lower, along_y, along_y)
 
     normed, memory = local_call(
         functools.partial(normalise_kernel, C),
         (shape_of(frame_count, model_width), shape_of(frame_count // C, model_width)),
-        (
-            jnp.stack([first_frame, length]).astype(jnp.int32),
-            local_frames,
-            norm_gain[None],
-            memory_gain[None],
-        ),
+        (scalars,),
+        (local_frames, norm_gain[None], memory_gain[None]),
         flops=10 * frame_count * model_width,
         moved=4 * frame_count * model_width,
     )
-    other_length = swap_cores(lengths)[0]
+    other_length = swap_cores(lengths)
     other_normed = swap_cores(normed)
     ahead = shifted(normed[:RC], "tm", -1)
     memories = exchange_blocks(
@@ -555,18 +663,22 @@
     m3 = relocate(m1, along_y, along_x)
     m4 = relocate(m1, None, z_up)
     m5 = relocate(m2, along_x, z_up)
-    m6 = relocate(pick(m2, m3), along_y, along_y)
+    m6 = relocate(m3, None, along_y)
+    m6b = relocate(m2, along_y, None)
     m7 = relocate(m4, None, along_x)
     m8 = relocate(m5, along_y, along_x)
 
     slot_pieces = (
         ((own_a, m1), (own_b, m2), (m1, m3), (m3, m6)),
-        ((m2, m4), (m6, m5), (m5, m7), (m8, m8)),
-    )
-    scalars = jnp.stack([first_frame, length, other_length, core, y_half]).astype(jnp.int32)
+        ((m2, m4), (m6b, m5), (m5, m7), (m8, m8)),
+    )
     pad = 2 * RC
     block = 2 * C
     width = 2 * shard
+    row_count = frame_count + extra.shape[0]
+    keys_seen = block + extra.shape[0]
+    lanes = width // head_size * block
+    block_count = 2 * (frame_count // block)
     attended, outs = [], []
     for pieces in slot_pieces:
         flat = [p for pair in pieces for p in pair]
@@ -577,13 +689,20 @@
                 shape_of(frame_count, width),
                 shape_of(model_width, width),
             ),
-            (scalars, normed, extra, other_normed, other_extra, *flat),
+            (scalars, other_length),
+            (normed, extra, other_normed, other_extra, *flat),
+            in_place=4 + len(flat),
             scratch=(
+                pltpu.VMEM((2, row_count, model_width), bf16),
                 pltpu.VMEM((3, model_width, width), bf16),
-                pltpu.VMEM((frame_count, width), bf16),
-                pltpu.VMEM((frame_count + pad, width), bf16),
-                pltpu.VMEM((frame_count + pad, width), bf16),
-                pltpu.VMEM((block + pad, width // head_size * block), jnp.float32),
+                pltpu.VMEM((2, frame_count, width), bf16),
+                pltpu.VMEM((2, row_count, width), bf16),
+                pltpu.VMEM((2, row_count, width), bf16),
+                pltpu.VMEM((block + pad, lanes), jnp.float32),
+                pltpu.VMEM((block_count, keys_seen, lanes), jnp.float32),
+                pltpu.VMEM((block_count, 1, lanes), jnp.float32),
+                pltpu.VMEM((block_count, keys_seen, lanes), bf16),
+                pltpu.SemaphoreType.DMA((12,)),
             ),
             flops=12 * frame_count * model_width * width,
             moved=8 * frame_count * model_width,
@@ -593,53 +712,48 @@
     other_outs = [swap_cores(w) for w in outs]
     other_attended = [swap_cores(for_other) for _, for_other in attended]
 
-    def group_of(of_core, slot):
-        return jnp.where(of_core == 0, z + slot, z - slot - 1) % z_count
-
-    offsets = []
-    for of_core in (core, 1 - core):
-        for slot in range(2):
-            group = group_of(of_core, slot)
-            offsets += [(2 * group + x) * shard, (2 * group + 1 - x) * shard]
-    token_count = owners.shape[2]
-    slot_count = 2 * token_count
-    capacity = slot_count // time_count
     owners_col = owners[0, 0]
-    encoded, sent_rows = local_call(
-        encode_kernel,
-        (shape_of(frame_count, model_width), shape_of(slot_count, model_width)),
-        (
-            jnp.stack([first_frame, length, capacity] + offsets).astype(jnp.int32),
-            attended[0][0],
-            attended[1][0],
-            *other_attended,
-            *outs,
-            *other_outs,
-            local_frames,
-            segment_ids[0],
-            owners_col.reshape(1, token_count),
-            owners_col,
-        ),
+    features = (attended[0][0], attended[1][0], *other_attended, *outs, *other_outs, local_frames)
+    sent_rows = local_call(
+        functools.partial(pool_kernel, offsets_at),
+        shape_of(slot_count, model_width),
+        (scalars,),
+        (*features, segment_ids[0], owners_col.reshape(1, token_count), owners_col),
+        scratch=(pltpu.VMEM((frame_count, model_width), bf16),),
+        flops=4 * token_count * model_width * model_width,
+        moved=6 * frame_count * model_width,
+    )
+    received = exchange_blocks(
+        sent_rows.reshape(time_count, capacity, model_width)
+    ).reshape(slot_count, model_width)
+    encoded = local_call(
+        functools.partial(encode_kernel, offsets_at),
+        shape_of(frame_count, model_width),
+        (scalars,),
+        features,
         scratch=(pltpu.VMEM((frame_count, model_width), bf16),),
         flops=2 * frame_count * model_width * model_width,
         moved=6 * frame_count * model_width,
     )
-    received = exchange_blocks(
-        sent_rows.reshape(time_count, capacity, model_width)
-    ).reshape(slot_count, model_width)
-    language_shard = language_weight.shape[1]
-    places = [(rec ^ i) * language_shard for i in range(rec_count)]
+    language_pieces = (
+        upper,
+        lower,
+        swap_cores(upper),
+        swap_cores(lower),
+        l1a,
+        l1b,
+        swap_cores(l1a),
+        swap_cores(l1b),
+    )
     lm_out = local_call(
-        language_kernel,
+        functools.partial(language_kernel, places_at),
         shape_of(slot_count, rec_count * language_shard),
-        (
-            jnp.stack(places).astype(jnp.int32),
-            received,
-            *[language_weight[:language_half], language_weight[language_half:]],
-            *[swap_cores(language_weight[:language_half])],
-            *[swap_cores(language_weight[language_half:])],
-            *[l1a, l1b],
-            *[swap_cores(l1a), swap_cores(l1b)],
+        (scalars,),
+        (received, *language_pieces),
+        in_place=len(language_pieces),
+        scratch=(
+            pltpu.VMEM((rec_count, model_width, language_shard), bf16),
+            pltpu.SemaphoreType.DMA((len(language_pieces),)),
         ),
         flops=2 * slot_count * model_width * rec_count * language_shard,
         moved=2 * model_width * rec_count * language_shard,

time: 126 us -> 115 us (0.913)
  waiting for transfers between devices: 32.5 us -> 16.4 us
  starting transfers between devices: 36.2 us -> 41.6 us
    ppermute x21 -> x22, waiting for transfers between devices: 22.2 us -> 12.5 us  [relocate(): return lax.ppermute(value, ('rec', 'tm'), pairs)]
    ppermute x21 -> x22, starting transfers between devices: 23.9 us -> 33.2 us  [relocate(): return lax.ppermute(value, ('rec', 'tm'), pairs)]
    all_to_all x2, waiting for transfers between devices: 5.97 us -> 0.01 us  [exchange_blocks(): return lax.all_to_all(blocks, 'tm', split_axis=0, concat_axis=0, tiled=True)]
    all_to_all x2, starting transfers between devices: 11.1 us -> 7.08 us  [exchange_blocks(): return lax.all_to_all(blocks, 'tm', split_axis=0, concat_axis=0, tiled=True)]
    another operation x2 -> x0, other arithmetic: 1.45 us -> none  [the longest x1 0.78 us: per_device(): jnp.stack(places).astype(jnp.int32)]
    pallas_call x5 -> x6, Pallas kernels: 42.2 us -> 42.5 us  [local_call(): pl.pallas_call(kernel, out_shape=out_shapes, in_specs=[smem_spec()] * len...]
    unnamed x40 -> x44, local copies, waits for them, and re-layouts: 3.84 us -> 4.07 us
  transfers between devices with their start and end apart: 24 -> 25, of which waited for: 7 -> 4; matrix products, arithmetic and copies ran while one was open for 5% -> 5% of each run, Pallas kernels for 30% -> 33%
where the time goes in v1:
time: 115 us
  Pallas kernels  42.5 us (37%)
  starting transfers between devices  41.6 us (36%)
  waiting for transfers between devices  16.4 us (14%)
  local copies, waits for them, and re-layouts  9.04 us (8%)
  other arithmetic  3.39 us (3%)
  between operations  1.81 us (2%)
    pallas_call x6, Pallas kernels, local_call(): pl.pallas_call(kernel, out_shape=out_shapes, in_specs=[smem_spec()] * len...  42.5 us
    ppermute x22, starting transfers between devices, relocate(): return lax.ppermute(value, ('rec', 'tm'), pairs)  33.2 us
    ppermute x22, waiting for transfers between devices, relocate(): return lax.ppermute(value, ('rec', 'tm'), pairs)  12.5 us
    all_to_all x2, starting transfers between devices, exchange_blocks(): return lax.all_to_all(blocks, 'tm', split_axis=0, concat_axis=0, tiled=True)  7.08 us
    unnamed x44, local copies, waits for them, and re-layouts  4.07 us
    ppermute x1, waiting for transfers between devices, shifted(): return lax.ppermute(block, axis, route)  3.89 us
    select_n x1, other arithmetic, pick(): return jnp.where(core == 0, for_core_0, for_core_1)  2.33 us
  transfers between devices with their start and end apart: 25, of which 4 were waited for; matrix products, arithmetic and copies ran while one was open for 5% of the time, Pallas kernels for 33%

profile of v1, /device:TPU:0, one launch (start us, length us, event | category | flops | bytes accessed | tf_op | source)
XLA Modules:
  0.0 114.7 jit_solution(451684140240388587)
XLA Ops:
  0.7 2.3 %broadcast_select_fusion = (bf16[4,512,128]{2,1,0:T(8,128)(2,1)S(1)}, bf16[4,512,128]{2,1,0:T(8,128)(2,1)}, bf16[4,512,128]{2,1,0:T(8,128)(2,1)S(1)}) fusion(pred[]{:T(512)S(6)} %eq.17, s32[]{:T(128)S(6)} %select_n.78, bf16[1,1024,128]{2,1,0:T(8,128)(2,1)} %bitcast.35, bf16[3,1024,128]{2,1,0:T(8,128)(2,1)} %param.13, s32[]{:T(128)S(6)} %select_n.77), kind=kLoop, calls=%fused_computation.6 | loop fusion | flops 2359296 | bytes 2621449 | tf_op jit(solution)/shard_map/jit(_where)/select_n | solution.py:619
  3.0 3.0 %collective-permute-start.4 = (bf16[4,512,128]{2,1,0:T(8,128)(2,1)S(1)}, bf16[4,512,128]{2,1,0:T(8,128)(2,1)S(1)}, u32[]{:S(2)}, u32[]{:S(2)}) collective-permute-start(bf16[4,512,128]{2,1,0:T(8,128)(2,1)S(1)} %get-tuple-element.20.refs_4_), channel_id=1, source_target_pairs={{0,1},{1,0},{2,3},{3,2},{4,5},{5,4},{6,7},{7,6},{8,10},{9,11},{10,... | collective-permute-start | bytes 1572872 | tf_op jit(solution)/shard_map/ppermute | solution.py:577
  6.0 3.6 %collective-permute-start.5 = (bf16[4,512,128]{2,1,0:T(8,128)(2,1)S(1)}, bf16[4,512,128]{2,1,0:T(8,128)(2,1)S(1)}, u32[]{:S(2)}, u32[]{:S(2)}) collective-permute-start(bf16[4,512,128]{2,1,0:T(8,128)(2,1)S(1)} %get-tuple-element.18), channel_id=1, source_target_pairs={{0,6},{1,7},{2,0},{3,1},{4,2},{5,3},{6,4},{7,5},{8,10},{9,11},{10,... | collective-permute-start | bytes 1572872 | tf_op jit(solution)/shard_map/ppermute | solution.py:577
  10.2 0.7 stack.63.scalars
  10.9 2.9 %shard_map.104 = (bf16[512,1024]{1,0:T(8,128)(2,1)}, bf16[16,1024]{1,0:T(8,128)(2,1)}) custom-call(s32[17]{0:T(128)} %stack.63.scalars, bf16[512,1024]{1,0:T(8,128)(2,1)} %bitcast.27, f32[1,1024]{1,0:T(1,128)} %bitcast.36, f32[1,1024]{1,0:T(1,128)} %bitcast.37), custom_call_target="tpu_custom_call" | custom-call | flops 5242880 | bytes 2097152 | tf_op jit(solution)/shard_map/pallas_call | solution.py:262
  13.9 1.5 %broadcast_in_dim.27 = bf16[8,16,1024]{2,1,0:T(8,128)(2,1)} broadcast(bf16[16,1024]{1,0:T(8,128)(2,1)} %get-tuple-element.11), dimensions={1,2} | broadcast | bytes 294912 | tf_op jit(solution)/shard_map/broadcast_in_dim | solution.py:658
  15.3 3.4 %all-to-all-start = ((bf16[8,16,1024]{2,1,0:T(8,128)(2,1)}), bf16[8,16,1024]{2,1,0:T(8,128)(2,1)S(1)}, u32[]{:S(2)}, u32[]{:S(2)}) async-start(bf16[8,16,1024]{2,1,0:T(8,128)(2,1)} %broadcast_in_dim.27), calls=%async_computation | async-start | bytes 524288 | tf_op jit(solution)/shard_map/all_to_all | solution.py:585
  18.9 1.6 %collective-permute-start.6 = (bf16[4,512,128]{2,1,0:T(8,128)(2,1)S(1)}, bf16[4,512,128]{2,1,0:T(8,128)(2,1)S(1)}, u32[]{:S(2)}, u32[]{:S(2)}) collective-permute-start(bf16[4,512,128]{2,1,0:T(8,128)(2,1)S(1)} %collective-permute-done.4.refs_5_.refs_8_), channel_id=1, source_target_pairs={{0,16},{1,17},{2,18},{3,19},{4,20},{5,21},{6,22},{7,23},{8,9},{9,8... | collective-permute-start | bytes 1572872 | tf_op jit(solution)/shard_map/ppermute | solution.py:577
  20.5 0.7 slice.9
  21.2 1.3 %collective-permute-start.1 = (bf16[8,1024]{1,0:T(8,128)(2,1)S(1)}, bf16[8,1024]{1,0:T(8,128)(2,1)S(1)}, u32[]{:S(2)}, u32[]{:S(2)}) collective-permute-start(bf16[8,1024]{1,0:T(8,128)(2,1)S(1)} %slice.9), channel_id=1, source_target_pairs={{1,0},{2,1},{3,2},{4,3},{5,4},{6,5},{7,6},{9,8},{10,9},{11,10},{12... | collective-permute-start | bytes 49160 | tf_op jit(solution)/shard_map/ppermute | solution.py:26
  22.5 0.5 collective-permute-start
  23.1 3.9 %collective-permute-done.1 = bf16[8,1024]{1,0:T(8,128)(2,1)S(1)} collective-permute-done((bf16[8,1024]{1,0:T(8,128)(2,1)S(1)}, bf16[8,1024]{1,0:T(8,128)(2,1)S(1)}, u32[]{:S(2)}, u32[]{:S(2)}) %collective-permute-start.1) | collective-permute-done | bytes 16416 | tf_op jit(solution)/shard_map/ppermute | solution.py:26
  27.0 1.5 %collective-permute-start.8 = (bf16[4,512,128]{2,1,0:T(8,128)(2,1)S(1)}, bf16[4,512,128]{2,1,0:T(8,128)(2,1)}, u32[]{:S(2)}, u32[]{:S(2)}) collective-permute-start(bf16[4,512,128]{2,1,0:T(8,128)(2,1)S(1)} %collective-permute-done.4.refs_5_.refs_8_), channel_id=1, source_target_pairs={{8,10},{9,11},{10,12},{11,13},{12,14},{13,15},{14,8},{15,9},{24,26... | collective-permute-start | bytes 1572872 | tf_op jit(solution)/shard_map/ppermute | solution.py:577
  28.4 3.9 %collective-permute-start.10 = (bf16[4,512,128]{2,1,0:T(8,128)(2,1)S(1)}, bf16[4,512,128]{2,1,0:T(8,128)(2,1)S(1)}, u32[]{:S(2)}, u32[]{:S(2)}) collective-permute-start(bf16[4,512,128]{2,1,0:T(8,128)(2,1)S(1)} %collective-permute-done.5.refs_7_.refs_4_), channel_id=1, source_target_pairs={{0,1},{1,0},{2,3},{3,2},{4,5},{5,4},{6,7},{7,6},{8,10},{9,11},{10,... | collective-permute-start | bytes 1572872 | tf_op jit(solution)/shard_map/ppermute | solution.py:577
  32.4 0.7 copy-done.13
  33.1 1.1 pad_maximum_fusion.refs_1_
  34.2 2.6 %collective-permute-start.3 = (bf16[144,1024]{1,0:T(8,128)(2,1)S(1)}, bf16[144,1024]{1,0:T(8,128)(2,1)S(1)}, u32[]{:S(2)}, u32[]{:S(2)}) collective-permute-start(bf16[144,1024]{1,0:T(8,128)(2,1)S(1)} %pad_maximum_fusion.refs_1_), channel_id=1, source_target_pairs={{0,8},{1,9},{2,10},{3,11},{4,12},{5,13},{6,14},{7,15},{8,0},{9,1},... | collective-permute-start | bytes 884744 | tf_op jit(solution)/shard_map/ppermute | solution.py:577
  36.8 0.7 collective-permute-start.7
  37.5 0.5 collective-permute-done.3.refs_3_
  38.0 3.4 %collective-permute-start.9 = (bf16[4,512,128]{2,1,0:T(8,128)(2,1)S(1)}, bf16[4,512,128]{2,1,0:T(8,128)(2,1)}, u32[]{:S(2)}, u32[]{:S(2)}) collective-permute-start(bf16[4,512,128]{2,1,0:T(8,128)(2,1)S(1)} %collective-permute-done.5.refs_7_.refs_4_), channel_id=1, source_target_pairs={{0,16},{1,17},{2,18},{3,19},{4,20},{5,21},{6,22},{7,23},{16,0},{17... | collective-permute-start | bytes 1572872 | tf_op jit(solution)/shard_map/ppermute | solution.py:577
  41.5 1.5 %collective-permute-start.11 = (bf16[4,512,128]{2,1,0:T(8,128)(2,1)}, bf16[4,512,128]{2,1,0:T(8,128)(2,1)}, u32[]{:S(2)}, u32[]{:S(2)}) collective-permute-start(bf16[4,512,128]{2,1,0:T(8,128)(2,1)} %collective-permute-done.8.refs_5_), channel_id=1, source_target_pairs={{8,9},{9,8},{10,11},{11,10},{12,13},{13,12},{14,15},{15,14},{24,25... | collective-permute-start | bytes 1572872 | tf_op jit(solution)/shard_map/ppermute | solution.py:577
  42.9 0.5 collective-permute-start.12
  43.5 0.8 copy-done.19
  44.3 0.3 copy-done
  44.6 12.0 %shard_map.105 = (bf16[512,256]{1,0:T(8,128)(2,1)}, bf16[512,256]{1,0:T(8,128)(2,1)}, bf16[1024,256]{1,0:T(8,128)(2,1)}) custom-call(s32[17]{0:T(128)} %stack.63.scalars, s32[1]{0:T(128)} %collective-permute-done.other_length, bf16[512,1024]{1,0:T(8,128)(2,1)} %get-tuple-element.10.refs_0_, bf16[144,1024]{1,0:T(8,128)(2,1)} %copy-done.1, ...), custom_call_target="tpu_custom_call" | custom-call | flops 1610612736 | bytes 4194304 | tf_op jit(solution)/shard_map/pallas_call | solution.py:262
  56.6 7.0 %collective-permute-start.15 = (bf16[1024,256]{1,0:T(8,128)(2,1)}, bf16[1024,256]{1,0:T(8,128)(2,1)S(1)}, u32[]{:S(2)}, u32[]{:S(2)}) collective-permute-start(bf16[1024,256]{1,0:T(8,128)(2,1)} %get-tuple-element.16.refs_4_), channel_id=1, source_target_pairs={{0,8},{1,9},{2,10},{3,11},{4,12},{5,13},{6,14},{7,15},{8,0},{9,1},... | collective-permute-start | bytes 1572872 | tf_op jit(solution)/shard_map/ppermute | solution.py:577
  63.6 12.0 %shard_map.106 = (bf16[512,256]{1,0:T(8,128)(2,1)}, bf16[512,256]{1,0:T(8,128)(2,1)}, bf16[1024,256]{1,0:T(8,128)(2,1)}) custom-call(s32[17]{0:T(128)} %stack.63.scalars, s32[1]{0:T(128)} %collective-permute-done.other_length, bf16[512,1024]{1,0:T(8,128)(2,1)} %get-tuple-element.10.refs_0_, bf16[144,1024]{1,0:T(8,128)(2,1)} %copy-done.1, ...), custom_call_target="tpu_custom_call" | custom-call | flops 1610612736 | bytes 4194304 | tf_op jit(solution)/shard_map/pallas_call | solution.py:262
  75.6 0.1 collective-permute-start.16
  75.8 0.5 collective-permute-start.13
  76.3 1.3 %fusion.4 = (bf16[512,512]{1,0:T(8,128)(2,1)S(1)}, bf16[512,512]{1,0:T(8,128)(2,1)S(1)}) fusion(bf16[1024,512]{1,0:T(8,128)(2,1)} %param.17), kind=kLoop, calls=%fused_computation.8 | loop fusion | bytes 2097152 | tf_op jit(solution)/shard_map/slice | solution.py:642
  77.6 1.6 %collective-permute-start.19 = (bf16[512,512]{1,0:T(8,128)(2,1)S(1)}, bf16[512,512]{1,0:T(8,128)(2,1)S(1)}, u32[]{:S(2)}, u32[]{:S(2)}) collective-permute-start(bf16[512,512]{1,0:T(8,128)(2,1)S(1)} %get-tuple-element.22.refs_0_), channel_id=1, source_target_pairs={{0,16},{1,17},{2,18},{3,19},{4,20},{5,21},{6,22},{7,23},{8,24},{9,... | collective-permute-start | bytes 1572872 | tf_op jit(solution)/shard_map/ppermute | solution.py:577
  79.2 0.5 collective-permute-start.20
  79.7 0.1 copy-done.20
  79.8 0.7 copy.11.refs_11_
  80.6 0.7 copy-done.15
  81.3 0.2 copy-done.10
  81.5 0.2 copy-done.11
  81.7 5.4 %shard_map.108 = bf16[256,1024]{1,0:T(8,128)(2,1)} custom-call(s32[17]{0:T(128)} %stack.63.scalars, bf16[512,256]{1,0:T(8,128)(2,1)} %get-tuple-element.12.refs_0_, bf16[512,256]{1,0:T(8,128)(2,1)} %get-tuple-element.13.refs_1_, bf16[512,256]{1,0:T(8,128)(2,1)} %copy-done.14, bf16[512,256]{1,0:T(8,128)(2,1)} %copy-done.15, ...), custom_call_target="tpu_custom_call" | custom-call | flops 536870912 | bytes 3145728 | tf_op jit(solution)/shard_map/pallas_call | solution.py:262
  87.1 3.7 %all-to-all-start.1 = ((bf16[8,32,1024]{2,1,0:T(8,128)(2,1)}), bf16[8,32,1024]{2,1,0:T(8,128)(2,1)S(1)}, u32[]{:S(2)}, u32[]{:S(2)}) async-start(bf16[8,32,1024]{2,1,0:T(8,128)(2,1)} %bitcast.31), calls=%async_computation.1 | async-start | bytes 1048576 | tf_op jit(solution)/shard_map/all_to_all | solution.py:585
  90.7 0.2 collective-permute-start.17
  91.0 0.4 collective-permute-start.18
  91.3 1.1 collective-permute-done.19.refs_4_
  92.5 10.8 %collective-permute-done.20.refs_5_ = bf16[512,512]{1,0:T(8,128)(2,1)} collective-permute-done((bf16[512,512]{1,0:T(8,128)(2,1)S(1)}, bf16[512,512]{1,0:T(8,128)(2,1)}, u32[]{:S(2)}, u32[]{:S(2)}) %collective-permute-start.20) | collective-permute-done | bytes 524320 | tf_op jit(solution)/shard_map/ppermute | solution.py:577
  103.3 5.1 %shard_map.107 = bf16[512,1024]{1,0:T(8,128)(2,1)} custom-call(s32[17]{0:T(128)} %stack.63.scalars, bf16[512,256]{1,0:T(8,128)(2,1)} %get-tuple-element.12.refs_0_, bf16[512,256]{1,0:T(8,128)(2,1)} %get-tuple-element.13.refs_1_, bf16[512,256]{1,0:T(8,128)(2,1)} %copy-done.14, bf16[512,256]{1,0:T(8,128)(2,1)} %copy-done.15, ...), custom_call_target="tpu_custom_call" | custom-call | flops 1073741824 | bytes 3145728 | tf_op jit(solution)/shard_map/pallas_call | solution.py:262
  108.4 0.7 copy-done.17
  109.1 0.2 copy-done.18
  109.3 0.2 copy-done.6
  109.5 5.0 %shard_map.109 = bf16[256,2048]{1,0:T(8,128)(2,1)} custom-call(s32[17]{0:T(128)} %stack.63.scalars, bf16[256,1024]{1,0:T(8,128)(2,1)} %bitcast.30, bf16[512,512]{1,0:T(8,128)(2,1)} %copy-done.9, bf16[512,512]{1,0:T(8,128)(2,1)} %copy-done.8, bf16[512,512]{1,0:T(8,128)(2,1)} %copy-done.17, bf16[512,512]{1,0:T(8,128)(2,1)} %copy-done.18, ...), custom_call_target="tpu_custom_call" | custom-call | flops 1073741824 | bytes 4194304 | tf_op jit(solution)/shard_map/pallas_call | solution.py:262
  (61 shorter events, 0.4 us)
Async XLA Ops:
  3.0 10.9 %copy-start.7 = (bf16[4,512,128]{2,1,0:T(8,128)(2,1)}, bf16[4,512,128]{2,1,0:T(8,128)(2,1)S(1)}, u32[]{:S(2)}) copy-start(bf16[4,512,128]{2,1,0:T(8,128)(2,1)S(1)} %get-tuple-element.20.refs_4_) | copy-start | bytes 1572868
  3.0 15.8 %collective-permute-start.4 = (bf16[4,512,128]{2,1,0:T(8,128)(2,1)S(1)}, bf16[4,512,128]{2,1,0:T(8,128)(2,1)S(1)}, u32[]{:S(2)}, u32[]{:S(2)}) collective-permute-start(bf16[4,512,128]{2,1,0:T(8,128)(2,1)S(1)} %get-tuple-element.20.refs_4_), channel_id=1, source_target_pairs={{0,1},{1,0},{2,3},{3,2},{4,5},{5,4},{6,7},{7,6},{8,10},{9,11},{10,... | collective-permute-start | bytes 1572872 | tf_op jit(solution)/shard_map/ppermute | solution.py:577
  6.0 22.4 %collective-permute-start.5 = (bf16[4,512,128]{2,1,0:T(8,128)(2,1)S(1)}, bf16[4,512,128]{2,1,0:T(8,128)(2,1)S(1)}, u32[]{:S(2)}, u32[]{:S(2)}) collective-permute-start(bf16[4,512,128]{2,1,0:T(8,128)(2,1)S(1)} %get-tuple-element.18), channel_id=1, source_target_pairs={{0,6},{1,7},{2,0},{3,1},{4,2},{5,3},{6,4},{7,5},{8,10},{9,11},{10,... | collective-permute-start | bytes 1572872 | tf_op jit(solution)/shard_map/ppermute | solution.py:577
  15.3 17.0 %all-to-all-start = ((bf16[8,16,1024]{2,1,0:T(8,128)(2,1)}), bf16[8,16,1024]{2,1,0:T(8,128)(2,1)S(1)}, u32[]{:S(2)}, u32[]{:S(2)}) async-start(bf16[8,16,1024]{2,1,0:T(8,128)(2,1)} %broadcast_in_dim.27), calls=%async_computation | async-start | bytes 524288 | tf_op jit(solution)/shard_map/all_to_all | solution.py:585
  18.8 24.7 %collective-permute-start.2 = (bf16[512,1024]{1,0:T(8,128)(2,1)}, bf16[512,1024]{1,0:T(8,128)(2,1)S(1)}, u32[]{:S(2)}, u32[]{:S(2)}) collective-permute-start(bf16[512,1024]{1,0:T(8,128)(2,1)} %get-tuple-element.10.refs_0_), channel_id=1, source_target_pairs={{0,8},{1,9},{2,10},{3,11},{4,12},{5,13},{6,14},{7,15},{8,0},{9,1},... | collective-permute-start | bytes 3145736 | tf_op jit(solution)/shard_map/ppermute | solution.py:577
  18.9 25.5 %copy-start.3 = (bf16[4,512,128]{2,1,0:T(8,128)(2,1)}, bf16[4,512,128]{2,1,0:T(8,128)(2,1)S(1)}, u32[]{:S(2)}) copy-start(bf16[4,512,128]{2,1,0:T(8,128)(2,1)S(1)} %collective-permute-done.4.refs_5_.refs_8_) | copy-start | bytes 1572868
  18.9 17.9 %collective-permute-start.6 = (bf16[4,512,128]{2,1,0:T(8,128)(2,1)S(1)}, bf16[4,512,128]{2,1,0:T(8,128)(2,1)S(1)}, u32[]{:S(2)}, u32[]{:S(2)}) collective-permute-start(bf16[4,512,128]{2,1,0:T(8,128)(2,1)S(1)} %collective-permute-done.4.refs_5_.refs_8_), channel_id=1, source_target_pairs={{0,16},{1,17},{2,18},{3,19},{4,20},{5,21},{6,22},{7,23},{8,9},{9,8... | collective-permute-start | bytes 1572872 | tf_op jit(solution)/shard_map/ppermute | solution.py:577
  21.2 5.8 %collective-permute-start.1 = (bf16[8,1024]{1,0:T(8,128)(2,1)S(1)}, bf16[8,1024]{1,0:T(8,128)(2,1)S(1)}, u32[]{:S(2)}, u32[]{:S(2)}) collective-permute-start(bf16[8,1024]{1,0:T(8,128)(2,1)S(1)} %slice.9), channel_id=1, source_target_pairs={{1,0},{2,1},{3,2},{4,3},{5,4},{6,5},{7,6},{9,8},{10,9},{11,10},{12... | collective-permute-start | bytes 49160 | tf_op jit(solution)/shard_map/ppermute | solution.py:26
  22.5 11.7 %collective-permute-start = (s32[1]{0:T(128)}, s32[1]{0:T(128)}, u32[]{:S(2)}, u32[]{:S(2)}) collective-permute-start(s32[1]{0:T(128)} %param.10), channel_id=1, source_target_pairs={{0,8},{1,9},{2,10},{3,11},{4,12},{5,13},{6,14},{7,15},{8,0},{9,1},... | collective-permute-start | bytes 20 | tf_op jit(solution)/shard_map/ppermute | solution.py:577
  27.0 14.5 %collective-permute-start.8 = (bf16[4,512,128]{2,1,0:T(8,128)(2,1)S(1)}, bf16[4,512,128]{2,1,0:T(8,128)(2,1)}, u32[]{:S(2)}, u32[]{:S(2)}) collective-permute-start(bf16[4,512,128]{2,1,0:T(8,128)(2,1)S(1)} %collective-permute-done.4.refs_5_.refs_8_), channel_id=1, source_target_pairs={{8,10},{9,11},{10,12},{11,13},{12,14},{13,15},{14,8},{15,9},{24,26... | collective-permute-start | bytes 1572872 | tf_op jit(solution)/shard_map/ppermute | solution.py:577
  28.4 15.9 %copy-start.2 = (bf16[4,512,128]{2,1,0:T(8,128)(2,1)}, bf16[4,512,128]{2,1,0:T(8,128)(2,1)S(1)}, u32[]{:S(2)}) copy-start(bf16[4,512,128]{2,1,0:T(8,128)(2,1)S(1)} %collective-permute-done.5.refs_7_.refs_4_) | copy-start | bytes 1572868
  28.4 14.5 %collective-permute-start.10 = (bf16[4,512,128]{2,1,0:T(8,128)(2,1)S(1)}, bf16[4,512,128]{2,1,0:T(8,128)(2,1)S(1)}, u32[]{:S(2)}, u32[]{:S(2)}) collective-permute-start(bf16[4,512,128]{2,1,0:T(8,128)(2,1)S(1)} %collective-permute-done.5.refs_7_.refs_4_), channel_id=1, source_target_pairs={{0,1},{1,0},{2,3},{3,2},{4,5},{5,4},{6,7},{7,6},{8,10},{9,11},{10,... | collective-permute-start | bytes 1572872 | tf_op jit(solution)/shard_map/ppermute | solution.py:577
  32.4 0.7 copy-start.13
  34.2 10.2 %copy-start.1 = (bf16[144,1024]{1,0:T(8,128)(2,1)}, bf16[144,1024]{1,0:T(8,128)(2,1)S(1)}, u32[]{:S(2)}) copy-start(bf16[144,1024]{1,0:T(8,128)(2,1)S(1)} %pad_maximum_fusion.refs_1_) | copy-start | bytes 884740
  34.2 3.8 %collective-permute-start.3 = (bf16[144,1024]{1,0:T(8,128)(2,1)S(1)}, bf16[144,1024]{1,0:T(8,128)(2,1)S(1)}, u32[]{:S(2)}, u32[]{:S(2)}) collective-permute-start(bf16[144,1024]{1,0:T(8,128)(2,1)S(1)} %pad_maximum_fusion.refs_1_), channel_id=1, source_target_pairs={{0,8},{1,9},{2,10},{3,11},{4,12},{5,13},{6,14},{7,15},{8,0},{9,1},... | collective-permute-start | bytes 884744 | tf_op jit(solution)/shard_map/ppermute | solution.py:577
  36.8 7.5 %copy-start.4 = (bf16[4,512,128]{2,1,0:T(8,128)(2,1)}, bf16[4,512,128]{2,1,0:T(8,128)(2,1)S(1)}, u32[]{:S(2)}) copy-start(bf16[4,512,128]{2,1,0:T(8,128)(2,1)S(1)} %collective-permute-done.6.refs_9_.refs_10_) | copy-start | bytes 1572868
  36.8 6.6 %collective-permute-start.7 = (bf16[4,512,128]{2,1,0:T(8,128)(2,1)S(1)}, bf16[4,512,128]{2,1,0:T(8,128)(2,1)S(1)}, u32[]{:S(2)}, u32[]{:S(2)}) collective-permute-start(bf16[4,512,128]{2,1,0:T(8,128)(2,1)S(1)} %collective-permute-done.6.refs_9_.refs_10_), channel_id=1, source_target_pairs={{8,24},{9,25},{10,26},{11,27},{12,28},{13,29},{14,30},{15,31},{24,... | collective-permute-start | bytes 1572872 | tf_op jit(solution)/shard_map/ppermute | solution.py:577
  38.0 5.4 %copy-start.12 = (bf16[144,1024]{1,0:T(8,128)(2,1)}, bf16[144,1024]{1,0:T(8,128)(2,1)S(1)}, u32[]{:S(2)}) copy-start(bf16[144,1024]{1,0:T(8,128)(2,1)S(1)} %collective-permute-done.3.refs_3_) | copy-start | bytes 884740
  38.0 25.6 %collective-permute-start.9 = (bf16[4,512,128]{2,1,0:T(8,128)(2,1)S(1)}, bf16[4,512,128]{2,1,0:T(8,128)(2,1)}, u32[]{:S(2)}, u32[]{:S(2)}) collective-permute-start(bf16[4,512,128]{2,1,0:T(8,128)(2,1)S(1)} %collective-permute-done.5.refs_7_.refs_4_), channel_id=1, source_target_pairs={{0,16},{1,17},{2,18},{3,19},{4,20},{5,21},{6,22},{7,23},{16,0},{17... | collective-permute-start | bytes 1572872 | tf_op jit(solution)/shard_map/ppermute | solution.py:577
  41.5 22.1 %collective-permute-start.11 = (bf16[4,512,128]{2,1,0:T(8,128)(2,1)}, bf16[4,512,128]{2,1,0:T(8,128)(2,1)}, u32[]{:S(2)}, u32[]{:S(2)}) collective-permute-start(bf16[4,512,128]{2,1,0:T(8,128)(2,1)} %collective-permute-done.8.refs_5_), channel_id=1, source_target_pairs={{8,9},{9,8},{10,11},{11,10},{12,13},{13,12},{14,15},{15,14},{24,25... | collective-permute-start | bytes 1572872 | tf_op jit(solution)/shard_map/ppermute | solution.py:577
  42.9 13.7 %copy-start.5 = (bf16[4,512,128]{2,1,0:T(8,128)(2,1)}, bf16[4,512,128]{2,1,0:T(8,128)(2,1)S(1)}, u32[]{:S(2)}) copy-start(bf16[4,512,128]{2,1,0:T(8,128)(2,1)S(1)} %collective-permute-done.10.refs_7_.refs_8_) | copy-start | bytes 1572868
  42.9 20.7 %collective-permute-start.12 = (bf16[4,512,128]{2,1,0:T(8,128)(2,1)S(1)}, bf16[4,512,128]{2,1,0:T(8,128)(2,1)}, u32[]{:S(2)}, u32[]{:S(2)}) collective-permute-start(bf16[4,512,128]{2,1,0:T(8,128)(2,1)S(1)} %collective-permute-done.10.refs_7_.refs_8_), channel_id=1, source_target_pairs={{0,16},{1,17},{2,18},{3,19},{4,20},{5,21},{6,22},{7,23},{8,9},{9,8... | collective-permute-start | bytes 1572872 | tf_op jit(solution)/shard_map/ppermute | solution.py:577
  43.4 1.1 copy-start
  43.5 0.9 copy-start.19
  56.6 19.1 %copy-start.21 = (bf16[512,256]{1,0:T(8,128)(2,1)S(1)}, bf16[512,256]{1,0:T(8,128)(2,1)}, u32[]{:S(2)}) copy-start(bf16[512,256]{1,0:T(8,128)(2,1)} %get-tuple-element.14) | copy-start | bytes 786436
  56.6 24.0 %collective-permute-start.15 = (bf16[1024,256]{1,0:T(8,128)(2,1)}, bf16[1024,256]{1,0:T(8,128)(2,1)S(1)}, u32[]{:S(2)}, u32[]{:S(2)}) collective-permute-start(bf16[1024,256]{1,0:T(8,128)(2,1)} %get-tuple-element.16.refs_4_), channel_id=1, source_target_pairs={{0,8},{1,9},{2,10},{3,11},{4,12},{5,13},{6,14},{7,15},{8,0},{9,1},... | collective-permute-start | bytes 1572872 | tf_op jit(solution)/shard_map/ppermute | solution.py:577
  75.6 5.0 %collective-permute-start.16 = (bf16[1024,256]{1,0:T(8,128)(2,1)}, bf16[1024,256]{1,0:T(8,128)(2,1)S(1)}, u32[]{:S(2)}, u32[]{:S(2)}) collective-permute-start(bf16[1024,256]{1,0:T(8,128)(2,1)} %get-tuple-element.17.refs_5_), channel_id=1, source_target_pairs={{0,8},{1,9},{2,10},{3,11},{4,12},{5,13},{6,14},{7,15},{8,0},{9,1},... | collective-permute-start | bytes 1572872 | tf_op jit(solution)/shard_map/ppermute | solution.py:577
  75.8 3.4 %collective-permute-start.13 = (bf16[512,256]{1,0:T(8,128)(2,1)S(1)}, bf16[512,256]{1,0:T(8,128)(2,1)S(1)}, u32[]{:S(2)}, u32[]{:S(2)}) collective-permute-start(bf16[512,256]{1,0:T(8,128)(2,1)S(1)} %copy-done.21), channel_id=1, source_target_pairs={{0,8},{1,9},{2,10},{3,11},{4,12},{5,13},{6,14},{7,15},{8,0},{9,1},... | collective-permute-start | bytes 786440 | tf_op jit(solution)/shard_map/ppermute | solution.py:577
  76.2 4.4 %collective-permute-start.14 = (bf16[512,256]{1,0:T(8,128)(2,1)}, bf16[512,256]{1,0:T(8,128)(2,1)S(1)}, u32[]{:S(2)}, u32[]{:S(2)}) collective-permute-start(bf16[512,256]{1,0:T(8,128)(2,1)} %get-tuple-element.15), channel_id=1, source_target_pairs={{0,8},{1,9},{2,10},{3,11},{4,12},{5,13},{6,14},{7,15},{8,0},{9,1},... | collective-permute-start | bytes 786440 | tf_op jit(solution)/shard_map/ppermute | solution.py:577
  77.6 13.2 %copy-start.9 = (bf16[512,512]{1,0:T(8,128)(2,1)}, bf16[512,512]{1,0:T(8,128)(2,1)S(1)}, u32[]{:S(2)}) copy-start(bf16[512,512]{1,0:T(8,128)(2,1)S(1)} %get-tuple-element.22.refs_0_) | copy-start | bytes 1572868
  77.6 13.4 %copy-start.8 = (bf16[512,512]{1,0:T(8,128)(2,1)}, bf16[512,512]{1,0:T(8,128)(2,1)S(1)}, u32[]{:S(2)}) copy-start(bf16[512,512]{1,0:T(8,128)(2,1)S(1)} %get-tuple-element.21.refs_1_) | copy-start | bytes 1572868
  77.6 14.9 %collective-permute-start.19 = (bf16[512,512]{1,0:T(8,128)(2,1)S(1)}, bf16[512,512]{1,0:T(8,128)(2,1)S(1)}, u32[]{:S(2)}, u32[]{:S(2)}) collective-permute-start(bf16[512,512]{1,0:T(8,128)(2,1)S(1)} %get-tuple-element.22.refs_0_), channel_id=1, source_target_pairs={{0,16},{1,17},{2,18},{3,19},{4,20},{5,21},{6,22},{7,23},{8,24},{9,... | collective-permute-start | bytes 1572872 | tf_op jit(solution)/shard_map/ppermute | solution.py:577
  79.2 1.4 %copy-start.14 = (bf16[512,256]{1,0:T(8,128)(2,1)}, bf16[512,256]{1,0:T(8,128)(2,1)S(1)}, u32[]{:S(2)}) copy-start(bf16[512,256]{1,0:T(8,128)(2,1)S(1)} %collective-permute-done.13.refs_2_) | copy-start | bytes 786436
  79.2 0.7 copy-start.20
  79.2 24.1 %collective-permute-start.20 = (bf16[512,512]{1,0:T(8,128)(2,1)S(1)}, bf16[512,512]{1,0:T(8,128)(2,1)}, u32[]{:S(2)}, u32[]{:S(2)}) collective-permute-start(bf16[512,512]{1,0:T(8,128)(2,1)S(1)} %get-tuple-element.21.refs_1_), channel_id=1, source_target_pairs={{0,16},{1,17},{2,18},{3,19},{4,20},{5,21},{6,22},{7,23},{8,24},{9,... | collective-permute-start | bytes 1572872 | tf_op jit(solution)/shard_map/ppermute | solution.py:577
  80.6 0.7 copy-start.15
  80.6 0.9 copy-start.10
  80.6 1.0 copy-start.11
  87.1 21.3 %all-to-all-start.1 = ((bf16[8,32,1024]{2,1,0:T(8,128)(2,1)}), bf16[8,32,1024]{2,1,0:T(8,128)(2,1)S(1)}, u32[]{:S(2)}, u32[]{:S(2)}) async-start(bf16[8,32,1024]{2,1,0:T(8,128)(2,1)} %bitcast.31), calls=%async_computation.1 | async-start | bytes 1048576 | tf_op jit(solution)/shard_map/all_to_all | solution.py:585
  90.7 17.6 %collective-permute-start.17 = (bf16[512,512]{1,0:T(8,128)(2,1)S(1)}, bf16[512,512]{1,0:T(8,128)(2,1)S(1)}, u32[]{:S(2)}, u32[]{:S(2)}) collective-permute-start(bf16[512,512]{1,0:T(8,128)(2,1)S(1)} %get-tuple-element.22.refs_0_), channel_id=1, source_target_pairs={{0,8},{1,9},{2,10},{3,11},{4,12},{5,13},{6,14},{7,15},{8,0},{9,1},... | collective-permute-start | bytes 1572872 | tf_op jit(solution)/shard_map/ppermute | solution.py:577
  91.0 17.4 %collective-permute-start.18 = (bf16[512,512]{1,0:T(8,128)(2,1)S(1)}, bf16[512,512]{1,0:T(8,128)(2,1)S(1)}, u32[]{:S(2)}, u32[]{:S(2)}) collective-permute-start(bf16[512,512]{1,0:T(8,128)(2,1)S(1)} %get-tuple-element.21.refs_1_), channel_id=1, source_target_pairs={{0,8},{1,9},{2,10},{3,11},{4,12},{5,13},{6,14},{7,15},{8,0},{9,1},... | collective-permute-start | bytes 1572872 | tf_op jit(solution)/shard_map/ppermute | solution.py:577
  92.5 15.9 %copy-start.16 = (bf16[512,512]{1,0:T(8,128)(2,1)}, bf16[512,512]{1,0:T(8,128)(2,1)S(1)}, u32[]{:S(2)}) copy-start(bf16[512,512]{1,0:T(8,128)(2,1)S(1)} %collective-permute-done.19.refs_4_) | copy-start | bytes 1572868
  92.5 15.9 %collective-permute-start.21 = (bf16[512,512]{1,0:T(8,128)(2,1)S(1)}, bf16[512,512]{1,0:T(8,128)(2,1)}, u32[]{:S(2)}, u32[]{:S(2)}) collective-permute-start(bf16[512,512]{1,0:T(8,128)(2,1)S(1)} %collective-permute-done.19.refs_4_), channel_id=1, source_target_pairs={{0,8},{1,9},{2,10},{3,11},{4,12},{5,13},{6,14},{7,15},{8,0},{9,1},... | collective-permute-start | bytes 1572872 | tf_op jit(solution)/shard_map/ppermute | solution.py:577
  103.3 5.1 %collective-permute-start.22 = (bf16[512,512]{1,0:T(8,128)(2,1)}, bf16[512,512]{1,0:T(8,128)(2,1)}, u32[]{:S(2)}, u32[]{:S(2)}) collective-permute-start(bf16[512,512]{1,0:T(8,128)(2,1)} %collective-permute-done.20.refs_5_), channel_id=1, source_target_pairs={{0,8},{1,9},{2,10},{3,11},{4,12},{5,13},{6,14},{7,15},{8,0},{9,1},... | collective-permute-start | bytes 1572872 | tf_op jit(solution)/shard_map/ppermute | solution.py:577
  108.3 0.8 copy-start.17
  108.4 1.0 copy-start.18
  108.4 1.1 copy-start.6

commit v2 on v1

--- a/solution.py
+++ b/solution.py
@@ -257,7 +257,7 @@
     return pl.BlockSpec(memory_space=pltpu.SMEM)
 
 
-def local_call(kernel, out_shapes, scalars, operands, scratch=(), in_place=0, flops=0, moved=0):
+def local_call(kernel, out_shapes, scalars, operands, scratch=(), in_place=0, out_in_place=False, vmem_mib=16, flops=0, moved=0):
     whole = len(operands) - in_place
     return pl.pallas_call(
         kernel,
@@ -265,7 +265,10 @@
         in_specs=[smem_spec()] * len(scalars)
         + [vmem_spec()] * whole
         + [pl.BlockSpec(memory_space=pl.ANY)] * in_place,
-        out_specs=jax.tree.map(lambda _: vmem_spec(), out_shapes),
+        out_specs=jax.tree.map(
+            lambda _: pl.BlockSpec(memory_space=pl.ANY) if out_in_place else vmem_spec(), out_shapes
+        ),
+        compiler_params=pltpu.CompilerParams(vmem_limit_bytes=vmem_mib << 20),
         scratch_shapes=list(scratch),
         cost_estimate=pl.CostEstimate(flops=flops, bytes_accessed=moved, transcendentals=0),
     )(*scalars, *operands)
@@ -275,7 +278,9 @@
     return jax.ShapeDtypeStruct(dims, dtype)
 
 
-def normalise_kernel(span_len, scalars, frames, gain, memory_gain, normed_out, memory_out):
+def normalise_kernel(
+    span_len, scalars, frames, gain, memory_gain, normed_out, ahead_out, memory_out
+):
     first_frame, length = scalars[0], scalars[1]
     frame_count, _ = frames.shape
     span_count = frame_count // span_len
@@ -285,6 +290,7 @@
     spread = jnp.mean(centred * centred, axis=-1, keepdims=True)
     normed = (centred * lax.rsqrt(spread + EPS_NORM) * gain[...]).astype(jnp.bfloat16)
     normed_out[...] = normed
+    ahead_out[...] = normed[: ahead_out.shape[0]]
     spans = lax.broadcasted_iota(jnp.int32, (span_count, frame_count), 0)
     places = lax.broadcasted_iota(jnp.int32, (span_count, frame_count), 1)
     member = (places >= spans * span_len) & (places < (spans + 1) * span_len)
@@ -295,27 +301,48 @@
     counts = jnp.sum(member.astype(jnp.float32), axis=-1, keepdims=True)
     means = sums / jnp.maximum(counts, 1.0)
     power = jnp.mean(means * means, axis=-1, keepdims=True)
-    memory_out[...] = (
-        means * lax.rsqrt(power + EPS_MEMORY) * memory_gain[...]
-    ).astype(jnp.bfloat16)
+    memory = (means * lax.rsqrt(power + EPS_MEMORY) * memory_gain[...]).astype(jnp.bfloat16)
+    for copy in range(memory_out.shape[0]):
+        memory_out[copy] = memory
+
+
+def prepare_kernel(scalars, frames, segments, owners_row, owners_col, base_out, member_out, count_out, route_out):
+    first_frame, length, capacity = scalars[0], scalars[1], scalars[4]
+    token_count, frame_count = member_out.shape
+    tokens = lax.broadcasted_iota(jnp.int32, (token_count, frame_count), 0)
+    places = first_frame + lax.broadcasted_iota(jnp.int32, (token_count, frame_count), 1)
+    member = (segments[...] == tokens).astype(jnp.float32)
+    counts = jnp.sum(member, axis=1, keepdims=True)
+    live_member = jnp.where(places < length, member, 0.0).astype(jnp.bfloat16)
+    earlier = lax.broadcasted_iota(jnp.int32, (token_count, token_count), 0)
+    later = lax.broadcasted_iota(jnp.int32, (token_count, token_count), 1)
+    clash = (owners_col[...] == owners_row[...]) & (earlier < later)
+    slot = jnp.sum(clash.astype(jnp.int32), axis=0, keepdims=True)
+    target = owners_row[...] * capacity + slot
+    slots = lax.broadcasted_iota(jnp.int32, route_out.shape, 0)
+    route_out[...] = (slots == target).astype(jnp.bfloat16)
+    member_out[...] = live_member
+    count_out[...] = jnp.broadcast_to(1.0 / counts, count_out.shape)
+    base_out[...] = (
+        jnp.dot(live_member, frames[...], preferred_element_type=jnp.float32) / counts
+    )
 
 
 def attend_kernel(span_len, right_len, head_size, scalars, other_length, *refs):
-    sources, pieces = refs[:4], refs[4:12]
-    out_0, out_1, projection = refs[12:15]
-    rows_in, weight, query, key, value, bias, scores, peaks, weights, sems = refs[15:]
+    sources, pieces = refs[:6], refs[6:14]
+    outs, projection = refs[14:16], refs[16]
+    rows_in, weight, query, key, value, bias, scores, peaks, weights, sems = refs[17:]
     first_frame, core, y_half = scalars[0], scalars[2], scalars[3]
     frame_count, model_width = sources[0].shape
     half = model_width // 2
-    width = out_0.shape[1]
+    width = outs[0].shape[1]
     heads = width // head_size
     block = 2 * span_len
     blocks = frame_count // block
     near = bias.shape[0]
-    pad = near - block
-    row_count = rows_in.shape[1]
-    memory_count = row_count - frame_count - pad
-    memory_at = frame_count + pad
+    memory_at = frame_count + near - block
+    row_count = rows_in.shape[0] // 2
+    memory_count = row_count - memory_at
     lanes = heads * block
 
     def piece_copies(of_core, projected):
@@ -325,46 +352,38 @@
             place = pl.ds(pl.multiple_of(places[side], half), half)
             for shard in range(2):
                 piece = pieces[4 * shard + 2 * side + of_core]
-                columns = pl.ds(shard * piece.shape[2], piece.shape[2])
                 index = 2 * side + shard
-                if projected:
-                    ends = piece.at[3], projection.at[place, columns], sems.at[4 + index]
-                else:
-                    ends = piece.at[0:3], weight.at[:, place, columns], sems.at[index]
-                copies.append(pltpu.make_async_copy(*ends))
+                for part in (3,) if projected else (0, 1, 2):
+                    target = projection if projected else weight
+                    start = shard * piece.shape[2] + (0 if projected else part * width)
+                    copies.append(
+                        pltpu.make_async_copy(
+                            piece.at[part],
+                            target.at[place, pl.ds(start, piece.shape[2])],
+                            sems.at[4 * part + index],
+                        )
+                    )
         return copies
 
     row_copies = []
     for rec in range(2):
-        row_copies.append(
-            [
+        at = rec * row_count
+        for i, (start, size) in enumerate(
+            ((0, frame_count), (frame_count, near - block), (memory_at, memory_count))
+        ):
+            row_copies.append(
                 pltpu.make_async_copy(
-                    sources[2 * rec], rows_in.at[rec, 0:frame_count], sems.at[8 + 2 * rec]
-                ),
-                pltpu.make_async_copy(
-                    sources[2 * rec + 1],
-                    rows_in.at[rec, frame_count:row_count],
-                    sems.at[9 + 2 * rec],
-                ),
-            ]
-        )
-
+                    sources[3 * rec + i], rows_in.at[pl.ds(at + start, size)], sems.at[16 + 3 * rec + i]
+                )
+            )
+
+    for copy in row_copies:
+        copy.start()
     for of_core in range(2):
 
         @pl.when(core == of_core)
         def _():
-            for copy in piece_copies(of_core, False):
-                copy.start()
-
-    for copies in row_copies:
-        for copy in copies:
-            copy.start()
-
-    for of_core in range(2):
-
-        @pl.when(core == of_core)
-        def _():
-            for copy in piece_copies(of_core, True):
+            for copy in piece_copies(of_core, False) + piece_copies(of_core, True):
                 copy.start()
 
     rows = lax.broadcasted_iota(jnp.int32, (near, lanes), 0)
@@ -377,33 +396,21 @@
     head_masks = [(feature_head == h).astype(jnp.bfloat16) for h in range(heads)]
     scale = head_size ** (-0.5) * LOG2_E
 
-    for copy in piece_copies(0, False):
+    for copy in row_copies + piece_copies(0, False):
         copy.wait()
-    for rec in range(2):
-        for copy in row_copies[rec]:
-            copy.wait()
-        query[rec] = (
-            jnp.dot(
-                rows_in[rec, 0:frame_count], weight[0], preferred_element_type=jnp.float32
-            )
-            * scale
-        ).astype(jnp.bfloat16)
-        key[rec] = jnp.dot(
-            rows_in[rec], weight[1], preferred_element_type=jnp.float32
-        ).astype(jnp.bfloat16)
-        value[rec] = jnp.dot(
-            rows_in[rec], weight[2], preferred_element_type=jnp.float32
-        ).astype(jnp.bfloat16)
-
-    def score_block(i, _):
-        rec = i // blocks
-        b = i - rec * blocks
-        length = jnp.where(rec == 0, scalars[1], other_length[0])
-        start = pl.multiple_of(b * block, block)
-        q_now = query[rec, pl.ds(start, block), :]
+    mixed = jnp.dot(rows_in[...], weight[...], preferred_element_type=jnp.float32)
+    query[...] = (mixed[:, :width] * scale).astype(jnp.bfloat16)
+    key[...] = mixed[:, width : 2 * width].astype(jnp.bfloat16)
+    value[...] = mixed[:, 2 * width :].astype(jnp.bfloat16)
+
+    def score_block(i):
+        rec, b = divmod(i, blocks)
+        at, start = rec * row_count, b * block
+        length = scalars[1] if rec == 0 else other_length[0]
+        q_now = query[at + start : at + start + block]
         stacked = jnp.concatenate([q_now * m for m in head_masks], axis=0)
         keys = jnp.concatenate(
-            [key[rec, pl.ds(start, near), :], key[rec, memory_at:row_count, :]], axis=0
+            [key[at + start : at + start + near], key[at + memory_at : at + row_count]], axis=0
         )
         raw = lax.dot_general(
             keys, stacked, (((1,), (1,)), ((), ())), preferred_element_type=jnp.float32
@@ -418,42 +425,41 @@
         peaks[i] = jnp.maximum(
             jnp.max(local, axis=0, keepdims=True), jnp.max(memory, axis=0, keepdims=True)
         )
-        return 0
-
-    def weigh_block(i, _):
+
+    def weigh_block(i):
         weights[i] = jnp.exp2(scores[i] - peaks[i]).astype(jnp.bfloat16)
-        return 0
 
     ones = jnp.ones((near + memory_count, LANES), jnp.bfloat16)
     first_of_pair = lax.broadcasted_iota(jnp.int32, (1, 2 * LANES), 1) % LANES < head_size
 
-    def mix_block(rec, out):
-        def body(b, _):
-            start = pl.multiple_of(b * block, block)
-            values = jnp.concatenate(
-                [value[rec, pl.ds(start, near), :], value[rec, memory_at:row_count, :]], axis=0
+    def mix_block(i):
+        rec, b = divmod(i, blocks)
+        at, start = rec * row_count, b * block
+        values = jnp.concatenate(
+            [value[at + start : at + start + near], value[at + memory_at : at + row_count]], axis=0
+        )
+        for pair in range(width // LANES):
+            columns = slice(pair * LANES, (pair + 1) * LANES)
+            pair_rows = slice(pair * 2 * block, (pair + 1) * 2 * block)
+            sums = lax.dot_general(
+                weights[i, :, pair_rows],
+                jnp.concatenate([values[:, columns], ones], axis=1),
+                (((0,), (0,)), ((), ())),
+                preferred_element_type=jnp.float32,
             )
-            for pair in range(width // LANES):
-                columns = slice(pair * LANES, (pair + 1) * LANES)
-                pair_rows = slice(pair * 2 * block, (pair + 1) * 2 * block)
-                mixed = lax.dot_general(
-                    weights[rec * blocks + b, :, pair_rows],
-                    jnp.concatenate([values[:, columns], ones], axis=1),
-                    (((0,), (0,)), ((), ())),
-                    preferred_element_type=jnp.float32,
-                )
-                picked = jnp.where(first_of_pair, mixed[:block], mixed[block:])
-                out[pl.ds(start, block), columns] = (
-                    picked[:, :LANES] / picked[:, LANES:]
-                ).astype(jnp.bfloat16)
-            return 0
-
-        return body
-
-    lax.fori_loop(0, 2 * blocks, score_block, 0, unroll=2)
-    lax.fori_loop(0, 2 * blocks, weigh_block, 0, unroll=2)
-    for rec, out in enumerate((out_0, out_1)):
-        lax.fori_loop(0, blocks, mix_block(rec, out), 0, unroll=2)
+            picked = jnp.where(first_of_pair, sums[:block], sums[block:])
+            outs[rec][start : start + block, columns] = (
+                picked[:, :LANES] / picked[:, LANES:]
+            ).astype(jnp.bfloat16)
+
+    count = 2 * blocks
+    for step in range(count + 2):
+        if step >= 2:
+            mix_block(step - 2)
+        if 1 <= step <= count:
+            weigh_block(step - 1)
+        if step < count:
+            score_block(step)
     for copy in piece_copies(0, True):
         copy.wait()
 
@@ -470,38 +476,47 @@
     return offsets, shard
 
 
-def pool_kernel(offsets_at, scalars, *refs):
+def pool_kernel(offsets_at, scalars, base, member, inverse, route, *refs):
     attended, projections = refs[:4], refs[4:8]
-    frames, segments, owners_row, owners_col = refs[8:12]
-    sent_out, gathered = refs[12:]
-    first_frame, length, capacity = scalars[0], scalars[1], scalars[4]
-    frame_count, _ = frames.shape
-    offsets, shard = assemble(scalars, offsets_at, attended, gathered)
-    token_count = owners_row.shape[1]
-    tokens = lax.broadcasted_iota(jnp.int32, (token_count, frame_count), 0)
-    places = first_frame + lax.broadcasted_iota(jnp.int32, (token_count, frame_count), 1)
-    member = (segments[...] == tokens).astype(jnp.float32)
-    counts = jnp.sum(member, axis=1, keepdims=True)
-    live_member = jnp.where(places < length, member, 0.0).astype(jnp.bfloat16)
-    earlier = lax.broadcasted_iota(jnp.int32, (token_count, token_count), 0)
-    later = lax.broadcasted_iota(jnp.int32, (token_count, token_count), 1)
-    clash = (owners_col[...] == owners_row[...]) & (earlier < later)
-    slot = jnp.sum(clash.astype(jnp.int32), axis=0, keepdims=True)
-    target = owners_row[...] * capacity + slot
-    slots = lax.broadcasted_iota(jnp.int32, (sent_out.shape[0], token_count), 0)
-    route = (slots == target).astype(jnp.bfloat16)
-    mean_attended = (
-        jnp.dot(live_member, gathered[...], preferred_element_type=jnp.float32) / counts
-    ).astype(jnp.bfloat16)
+    sent_out, gathered, weight, pooled, sems = refs[8:]
+    shard = attended[0].shape[1] // 2
+    offsets = [
+        [pl.multiple_of(scalars[offsets_at + 2 * i + s], LANES) for s in range(2)]
+        for i in range(4)
+    ]
+    row_copies, weight_copies = [], []
     for i in range(4):
-        mixed = jnp.dot(mean_attended, projections[i][...], preferred_element_type=jnp.float32)
+        for s in range(2):
+            row_copies.append(
+                pltpu.make_async_copy(
+                    attended[i].at[:, pl.ds(s * shard, shard)],
+                    gathered.at[:, pl.ds(offsets[i][s], shard)],
+                    sems.at[2 * i + s],
+                )
+            )
+        weight_copies.append(
+            pltpu.make_async_copy(projections[i], weight.at[i], sems.at[8 + i])
+        )
+    for copy in row_copies + weight_copies:
+        copy.start()
+    for copy in row_copies:
+        copy.wait()
+    means = jnp.dot(member[...], gathered[...], preferred_element_type=jnp.float32)
+    model_width = means.shape[1]
+    means = (means * jnp.concatenate([inverse[...]] * (model_width // LANES), axis=1)).astype(
+        jnp.bfloat16
+    )
+    for i in range(4):
+        weight_copies[i].wait()
+        mixed = jnp.dot(means, weight[i], preferred_element_type=jnp.float32)
         for s in range(2):
             columns = pl.ds(offsets[i][s], shard)
-            base = jnp.dot(live_member, frames[:, columns], preferred_element_type=jnp.float32)
-            pooled = (base / counts + mixed[:, s * shard : (s + 1) * shard]).astype(jnp.bfloat16)
-            sent_out[:, columns] = jnp.dot(
-                route, pooled, preferred_element_type=jnp.float32
+            pooled[:, columns] = (
+                base[:, columns] + mixed[:, s * shard : (s + 1) * shard]
             ).astype(jnp.bfloat16)
+    sent_out[...] = jnp.dot(
+        route[...], pooled[...], preferred_element_type=jnp.float32
+    ).astype(jnp.bfloat16)
 
 
 def encode_kernel(offsets_at, scalars, *refs):
@@ -525,24 +540,31 @@
             ).astype(jnp.bfloat16)
 
 
-def language_kernel(places_at, scalars, received, *refs):
-    pieces, out, weights, sems = refs[:-3], refs[-3], refs[-2], refs[-1]
-    half, width = pieces[0].shape
+def language_kernel(places_at, scalars, *refs):
+    received, pieces, out = refs[0], refs[1:-6], refs[-6]
+    rows, weights, product, sems, out_sems = refs[-5:]
+    count, width = len(pieces), pieces[0].shape[1]
+    row_copy = pltpu.make_async_copy(received, rows, sems.at[count])
+    row_copy.start()
     copies = [
-        pltpu.make_async_copy(
-            piece, weights.at[i // 2, pl.ds((i % 2) * half, half)], sems.at[i]
-        )
-        for i, piece in enumerate(pieces)
+        pltpu.make_async_copy(piece, weights.at[i], sems.at[i]) for i, piece in enumerate(pieces)
     ]
     for copy in copies:
         copy.start()
-    for i in range(len(pieces) // 2):
-        copies[2 * i].wait()
-        copies[2 * i + 1].wait()
+    row_copy.wait()
+    out_copies = []
+    for i in range(count):
+        copies[i].wait()
+        product[i] = jnp.dot(
+            rows[...], weights[i], preferred_element_type=jnp.float32
+        ).astype(jnp.bfloat16)
         place = pl.multiple_of(scalars[places_at + i], LANES)
-        out[:, pl.ds(place, width)] = jnp.dot(
-            received[...], weights[i], preferred_element_type=jnp.float32
-        ).astype(jnp.bfloat16)
+        out_copies.append(
+            pltpu.make_async_copy(product.at[i], out.at[:, pl.ds(place, width)], out_sems.at[i])
+        )
+        out_copies[-1].start()
+    for copy in out_copies:
+        copy.wait()
 
 
 def along_x(r, j, _):
@@ -638,14 +660,16 @@
 
     m1 = relocate(own_a, along_x, z_up)
     m2 = relocate(pick(own_a, own_b), z_down, z_up)
-    language_half = language_weight.shape[0] // 2
-    upper, lower = language_weight[:language_half], language_weight[language_half:]
-    l1a = relocate(upper, along_y, along_y)
-    l1b = relocate(lower, along_y, along_y)
-
-    normed, memory = local_call(
+    l1 = relocate(language_weight, along_y, along_y)
+
+    pad = 2 * RC
+    normed, start_rows, memory = local_call(
         functools.partial(normalise_kernel, C),
-        (shape_of(frame_count, model_width), shape_of(frame_count // C, model_width)),
+        (
+            shape_of(frame_count, model_width),
+            shape_of(pad, model_width),
+            shape_of(time_count, frame_count // C, model_width),
+        ),
         (scalars,),
         (local_frames, norm_gain[None], memory_gain[None]),
         flops=10 * frame_count * model_width,
@@ -653,30 +677,40 @@
     )
     other_length = swap_cores(lengths)
     other_normed = swap_cores(normed)
-    ahead = shifted(normed[:RC], "tm", -1)
-    memories = exchange_blocks(
-        jnp.broadcast_to(memory[None], (time_count,) + memory.shape)
-    ).reshape(-1, model_width)
-    extra = jnp.concatenate([ahead, jnp.zeros_like(ahead), memories], axis=0)
-    other_extra = swap_cores(extra)
+    ahead = shifted(start_rows, "tm", -1)
+    memories = exchange_blocks(memory).reshape(-1, model_width)
+    owners_col = owners[0, 0]
+    prepared = local_call(
+        prepare_kernel,
+        (
+            shape_of(token_count, model_width, dtype=jnp.float32),
+            shape_of(token_count, frame_count),
+            shape_of(token_count, LANES, dtype=jnp.float32),
+            shape_of(slot_count, token_count),
+        ),
+        (scalars,),
+        (local_frames, segment_ids[0], owners_col.reshape(1, token_count), owners_col),
+        flops=2 * token_count * frame_count * model_width,
+        moved=2 * frame_count * model_width,
+    )
+    other_ahead = swap_cores(ahead)
+    other_memories = swap_cores(memories)
 
     m3 = relocate(m1, along_y, along_x)
     m4 = relocate(m1, None, z_up)
     m5 = relocate(m2, along_x, z_up)
-    m6 = relocate(m3, None, along_y)
-    m6b = relocate(m2, along_y, None)
+    m6 = relocate(pick(m2, m3), along_y, along_y)
     m7 = relocate(m4, None, along_x)
     m8 = relocate(m5, along_y, along_x)
 
     slot_pieces = (
         ((own_a, m1), (own_b, m2), (m1, m3), (m3, m6)),
-        ((m2, m4), (m6b, m5), (m5, m7), (m8, m8)),
-    )
-    pad = 2 * RC
+        ((m2, m4), (m6, m5), (m5, m7), (m8, m8)),
+    )
     block = 2 * C
     width = 2 * shard
-    row_count = frame_count + extra.shape[0]
-    keys_seen = block + extra.shape[0]
+    row_count = frame_count + pad + memories.shape[0]
+    keys_seen = block + pad + memories.shape[0]
     lanes = width // head_size * block
     block_count = 2 * (frame_count // block)
     attended, outs = [], []
@@ -690,20 +724,21 @@
                 shape_of(model_width, width),
             ),
             (scalars, other_length),
-            (normed, extra, other_normed, other_extra, *flat),
-            in_place=4 + len(flat),
+            (normed, ahead, memories, other_normed, other_ahead, other_memories, *flat),
+            in_place=6 + len(flat),
             scratch=(
-                pltpu.VMEM((2, row_count, model_width), bf16),
-                pltpu.VMEM((3, model_width, width), bf16),
-                pltpu.VMEM((2, frame_count, width), bf16),
-                pltpu.VMEM((2, row_count, width), bf16),
-                pltpu.VMEM((2, row_count, width), bf16),
+                pltpu.VMEM((2 * row_count, model_width), bf16),
+                pltpu.VMEM((model_width, 3 * width), bf16),
+                pltpu.VMEM((2 * row_count, width), bf16),
+                pltpu.VMEM((2 * row_count, width), bf16),
+                pltpu.VMEM((2 * row_count, width), bf16),
                 pltpu.VMEM((block + pad, lanes), jnp.float32),
                 pltpu.VMEM((block_count, keys_seen, lanes), jnp.float32),
                 pltpu.VMEM((block_count, 1, lanes), jnp.float32),
                 pltpu.VMEM((block_count, keys_seen, lanes), bf16),
-                pltpu.SemaphoreType.DMA((12,)),
+                pltpu.SemaphoreType.DMA((22,)),
             ),
+            vmem_mib=32,
             flops=12 * frame_count * model_width * width,
             moved=8 * frame_count * model_width,
         )
@@ -712,14 +747,19 @@
     other_outs = [swap_cores(w) for w in outs]
     other_attended = [swap_cores(for_other) for _, for_other in attended]
 
-    owners_col = owners[0, 0]
-    features = (attended[0][0], attended[1][0], *other_attended, *outs, *other_outs, local_frames)
+    features = (attended[0][0], attended[1][0], *other_attended, *outs, *other_outs)
     sent_rows = local_call(
         functools.partial(pool_kernel, offsets_at),
         shape_of(slot_count, model_width),
         (scalars,),
-        (*features, segment_ids[0], owners_col.reshape(1, token_count), owners_col),
-        scratch=(pltpu.VMEM((frame_count, model_width), bf16),),
+        (*prepared, *features),
+        in_place=len(features),
+        scratch=(
+            pltpu.VMEM((frame_count, model_width), bf16),
+            pltpu.VMEM((4, model_width, width), bf16),
+            pltpu.VMEM((token_count, model_width), bf16),
+            pltpu.SemaphoreType.DMA((12,)),
+        ),
         flops=4 * token_count * model_width * model_width,
         moved=6 * frame_count * model_width,
     )
@@ -730,30 +770,25 @@
         functools.partial(encode_kernel, offsets_at),
         shape_of(frame_count, model_width),
         (scalars,),
-        features,
+        (*features, local_frames),
         scratch=(pltpu.VMEM((frame_count, model_width), bf16),),
         flops=2 * frame_count * model_width * model_width,
         moved=6 * frame_count * model_width,
     )
-    language_pieces = (
-        upper,
-        lower,
-        swap_cores(upper),
-        swap_cores(lower),
-        l1a,
-        l1b,
-        swap_cores(l1a),
-        swap_cores(l1b),
-    )
+    language_pieces = (language_weight, swap_cores(language_weight), l1, swap_cores(l1))
     lm_out = local_call(
         functools.partial(language_kernel, places_at),
         shape_of(slot_count, rec_count * language_shard),
         (scalars,),
         (received, *language_pieces),
-        in_place=len(language_pieces),
+        in_place=1 + rec_count,
+        out_in_place=True,
         scratch=(
+            pltpu.VMEM((slot_count, model_width), bf16),
             pltpu.VMEM((rec_count, model_width, language_shard), bf16),
-            pltpu.SemaphoreType.DMA((len(language_pieces),)),
+            pltpu.VMEM((rec_count, slot_count, language_shard), bf16),
+            pltpu.SemaphoreType.DMA((rec_count + 1,)),
+            pltpu.SemaphoreType.DMA((rec_count,)),
         ),
         flops=2 * slot_count * model_width * rec_count * language_shard,
         moved=2 * model_width * rec_count * language_shard,

time: 115 us -> 119 us (1.035)
  waiting for transfers between devices: 16.4 us -> 46.9 us
  starting transfers between devices: 41.6 us -> 29.6 us
  Pallas kernels: 42.5 us -> 33 us
  local copies, waits for them, and re-layouts: 9.04 us -> 4.84 us
    all_to_all x2, waiting for transfers between devices: 0.01 us -> 17.7 us  [exchange_blocks(): return lax.all_to_all(blocks, 'tm', split_axis=0, concat_axis=0, tiled=True)]
    ppermute x22 -> x19, starting transfers between devices: 33.2 us -> 18.8 us  [relocate(): return lax.ppermute(value, ('rec', 'tm'), pairs)]
    ppermute x22 -> x19, waiting for transfers between devices: 12.5 us -> 23.6 us  [relocate(): return lax.ppermute(value, ('rec', 'tm'), pairs)]
    pallas_call x6 -> x7, Pallas kernels: 42.5 us -> 33 us  [local_call(): pl.pallas_call(kernel, out_shape=out_shapes, in_specs=[smem_spec()] * len...]
    all_to_all x2, starting transfers between devices: 7.08 us -> 9.53 us  [exchange_blocks(): return lax.all_to_all(blocks, 'tm', split_axis=0, concat_axis=0, tiled=True)]
    slice x2 -> x0, local copies, waits for them, and re-layouts: 1.99 us -> none  [the longest x1 1.27 us: per_device(): language_weight[language_half:]]
    ppermute x1, waiting for transfers between devices: 3.89 us -> 5.56 us  [shifted(): return lax.ppermute(block, axis, route)]
    broadcast_in_dim x2 -> x0, local copies, waits for them, and re-layouts: 1.49 us -> none  [the longest x1 1.49 us: per_device(): jnp.broadcast_to(memory[None], (time_count,) + memory.shape)]
  transfers between devices with their start and end apart: 25 -> 22, of which waited for: 4 -> 8; matrix products, arithmetic and copies ran while one was open for 5% -> 0% of each run, Pallas kernels for 33% -> 24%
where the time goes in v2:
time: 119 us
  waiting for transfers between devices  46.9 us (39%)
  Pallas kernels  33 us (28%)
  starting transfers between devices  29.6 us (25%)
  local copies, waits for them, and re-layouts  4.84 us (4%)
  other arithmetic  2.64 us (2%)
  between operations  1.75 us (1%)
    pallas_call x7, Pallas kernels, local_call(): pl.pallas_call(kernel, out_shape=out_shapes, in_specs=[smem_spec()] * len...  33 us
    ppermute x19, waiting for transfers between devices, relocate(): return lax.ppermute(value, ('rec', 'tm'), pairs)  23.6 us
    ppermute x19, starting transfers between devices, relocate(): return lax.ppermute(value, ('rec', 'tm'), pairs)  18.8 us
    all_to_all x2, waiting for transfers between devices, exchange_blocks(): return lax.all_to_all(blocks, 'tm', split_axis=0, concat_axis=0, tiled=True)  17.7 us
    all_to_all x2, starting transfers between devices, exchange_blocks(): return lax.all_to_all(blocks, 'tm', split_axis=0, concat_axis=0, tiled=True)  9.53 us
    ppermute x1, waiting for transfers between devices, shifted(): return lax.ppermute(block, axis, route)  5.56 us
    unnamed x30, local copies, waits for them, and re-layouts  4.63 us
    select_n x2, other arithmetic, pick(): return jnp.where(core == 0, for_core_0, for_core_1)  2.64 us
  transfers between devices with their start and end apart: 22, of which 8 were waited for; matrix products, arithmetic and copies ran while one was open for 0% of the time, Pallas kernels for 24%

profile of v2, /device:TPU:0, one launch (start us, length us, event | category | flops | bytes accessed | tf_op | source)
XLA Modules:
  0.0 118.7 jit_solution(18362128738912548145)
XLA Ops:
  0.7 2.6 %broadcast_select_fusion.1 = (bf16[4,512,128]{2,1,0:T(8,128)(2,1)}, bf16[4,512,128]{2,1,0:T(8,128)(2,1)}, bf16[4,512,128]{2,1,0:T(8,128)(2,1)S(1)}) fusion(pred[]{:T(512)S(6)} %eq.18, s32[]{:T(128)S(6)} %select_n.82, bf16[1,1024,128]{2,1,0:T(8,128)(2,1)} %bitcast.41, bf16[3,1024,128]{2,1,0:T(8,128)(2,1)} %param.13, s32[]{:T(128)S(6)} %select_n.81), kind=kLoop, calls=%fused_computation.7 | loop fusion | flops 2359296 | bytes 2621449 | tf_op jit(solution)/shard_map/jit(_where)/select_n | solution.py:641
  3.3 3.0 %collective-permute-start.5 = (bf16[4,512,128]{2,1,0:T(8,128)(2,1)S(1)}, bf16[4,512,128]{2,1,0:T(8,128)(2,1)}, u32[]{:S(2)}, u32[]{:S(2)}) collective-permute-start(bf16[4,512,128]{2,1,0:T(8,128)(2,1)S(1)} %get-tuple-element.30.refs_6_), channel_id=1, source_target_pairs={{0,1},{1,0},{2,3},{3,2},{4,5},{5,4},{6,7},{7,6},{8,10},{9,11},{10,... | collective-permute-start | bytes 1572872 | tf_op jit(solution)/shard_map/ppermute | solution.py:599
  6.2 0.8 copy-done.2
  7.1 3.6 %collective-permute-start.6 = (bf16[4,512,128]{2,1,0:T(8,128)(2,1)}, bf16[4,512,128]{2,1,0:T(8,128)(2,1)S(1)}, u32[]{:S(2)}, u32[]{:S(2)}) collective-permute-start(bf16[4,512,128]{2,1,0:T(8,128)(2,1)} %get-tuple-element.28), channel_id=1, source_target_pairs={{0,6},{1,7},{2,0},{3,1},{4,2},{5,3},{6,4},{7,5},{8,10},{9,11},{10,... | collective-permute-start | bytes 1572872 | tf_op jit(solution)/shard_map/ppermute | solution.py:599
  10.7 2.8 %collective-permute-done.5.refs_7_.refs_10_ = bf16[4,512,128]{2,1,0:T(8,128)(2,1)} collective-permute-done((bf16[4,512,128]{2,1,0:T(8,128)(2,1)S(1)}, bf16[4,512,128]{2,1,0:T(8,128)(2,1)}, u32[]{:S(2)}, u32[]{:S(2)}) %collective-permute-start.5) | collective-permute-done | bytes 524320 | tf_op jit(solution)/shard_map/ppermute | solution.py:599
  13.5 2.1 %collective-permute-start.7 = (bf16[4,512,128]{2,1,0:T(8,128)(2,1)}, bf16[4,512,128]{2,1,0:T(8,128)(2,1)S(1)}, u32[]{:S(2)}, u32[]{:S(2)}) collective-permute-start(bf16[4,512,128]{2,1,0:T(8,128)(2,1)} %collective-permute-done.5.refs_7_.refs_10_), channel_id=1, source_target_pairs={{0,16},{1,17},{2,18},{3,19},{4,20},{5,21},{6,22},{7,23},{8,9},{9,8... | collective-permute-start | bytes 1572872 | tf_op jit(solution)/shard_map/ppermute | solution.py:599
  16.2 0.1 stack.63.scalars
  16.3 0.0 copy-start.11
  16.3 0.6 copy-done.12
  16.9 0.1 copy-done.11
  17.0 1.5 %shard_map.104 = (bf16[512,1024]{1,0:T(8,128)(2,1)S(1)}, bf16[16,1024]{1,0:T(8,128)(2,1)S(1)}, bf16[8,16,1024]{2,1,0:T(8,128)(2,1)S(1)}) custom-call(s32[17]{0:T(128)S(1)} %stack.63.scalars, bf16[512,1024]{1,0:T(8,128)(2,1)S(1)} %bitcast.27, f32[1,1024]{1,0:T(1,128)S(1)} %bitcast.34, f32[1,1024]{1,0:T(1,128)S(1)} %bitcast.35), custom_call_target="tpu_custom_call" | custom-call | flops 5242880 | bytes 2097152 | tf_op jit(solution)/shard_map/pallas_call | solution.py:262
  18.5 0.7 copy-done.10
  19.2 5.8 %all-to-all-start = ((bf16[8,16,1024]{2,1,0:T(8,128)(2,1)}), bf16[8,16,1024]{2,1,0:T(8,128)(2,1)S(1)}, u32[]{:S(2)}, u32[]{:S(2)}) async-start(bf16[8,16,1024]{2,1,0:T(8,128)(2,1)} %copy-done.10), calls=%async_computation | async-start | bytes 524288 | tf_op jit(solution)/shard_map/all_to_all | solution.py:607
  25.0 0.7 collective-permute-start.2
  25.7 1.5 %collective-permute-start.9 = (bf16[4,512,128]{2,1,0:T(8,128)(2,1)}, bf16[4,512,128]{2,1,0:T(8,128)(2,1)}, u32[]{:S(2)}, u32[]{:S(2)}) collective-permute-start(bf16[4,512,128]{2,1,0:T(8,128)(2,1)} %collective-permute-done.5.refs_7_.refs_10_), channel_id=1, source_target_pairs={{8,10},{9,11},{10,12},{11,13},{12,14},{13,15},{14,8},{15,9},{24,26... | collective-permute-start | bytes 1572872 | tf_op jit(solution)/shard_map/ppermute | solution.py:599
  27.1 1.6 %collective-permute-start.10 = (bf16[4,512,128]{2,1,0:T(8,128)(2,1)S(1)}, bf16[4,512,128]{2,1,0:T(8,128)(2,1)}, u32[]{:S(2)}, u32[]{:S(2)}) collective-permute-start(bf16[4,512,128]{2,1,0:T(8,128)(2,1)S(1)} %collective-permute-done.6.refs_9_.refs_6_), channel_id=1, source_target_pairs={{0,1},{1,0},{2,3},{3,2},{4,5},{5,4},{6,7},{7,6},{8,10},{9,11},{10,... | collective-permute-start | bytes 1572872 | tf_op jit(solution)/shard_map/ppermute | solution.py:599
  28.7 1.7 %collective-permute-start = (s32[1]{0:T(128)}, s32[1]{0:T(128)}, u32[]{:S(2)}, u32[]{:S(2)}) collective-permute-start(s32[1]{0:T(128)} %param.10), channel_id=1, source_target_pairs={{0,8},{1,9},{2,10},{3,11},{4,12},{5,13},{6,14},{7,15},{8,0},{9,1},... | collective-permute-start | bytes 20 | tf_op jit(solution)/shard_map/ppermute | solution.py:599
  30.4 1.1 collective-permute-done.other_length
  31.5 1.3 %collective-permute-start.1 = (bf16[16,1024]{1,0:T(8,128)(2,1)S(1)}, bf16[16,1024]{1,0:T(8,128)(2,1)S(1)}, u32[]{:S(2)}, u32[]{:S(2)}) collective-permute-start(bf16[16,1024]{1,0:T(8,128)(2,1)S(1)} %get-tuple-element.16), channel_id=1, source_target_pairs={{1,0},{2,1},{3,2},{4,3},{5,4},{6,5},{7,6},{9,8},{10,9},{11,10},{12... | collective-permute-start | bytes 98312 | tf_op jit(solution)/shard_map/ppermute | solution.py:26
  32.8 5.6 %collective-permute-done.1.refs_1_ = bf16[16,1024]{1,0:T(8,128)(2,1)S(1)} collective-permute-done((bf16[16,1024]{1,0:T(8,128)(2,1)S(1)}, bf16[16,1024]{1,0:T(8,128)(2,1)S(1)}, u32[]{:S(2)}, u32[]{:S(2)}) %collective-permute-start.1) | collective-permute-done | bytes 32800 | tf_op jit(solution)/shard_map/ppermute | solution.py:26
  38.4 8.1 %all-to-all-done = bf16[8,16,1024]{2,1,0:T(8,128)(2,1)S(1)} async-done(((bf16[8,16,1024]{2,1,0:T(8,128)(2,1)}), bf16[8,16,1024]{2,1,0:T(8,128)(2,1)S(1)}, u32[]{:S(2)}, u32[]{:S(2)}) %all-to-all-start) | async-done | bytes 262176 | tf_op jit(solution)/shard_map/all_to_all | solution.py:607
  46.5 0.1 collective-permute-start.4
  46.5 0.1 broadcast_select_fusion
  46.6 0.8 collective-permute-start.8
  47.4 0.7 collective-permute-start.11
  48.1 1.3 %collective-permute-start.12 = (bf16[4,512,128]{2,1,0:T(8,128)(2,1)}, bf16[4,512,128]{2,1,0:T(8,128)(2,1)S(1)}, u32[]{:S(2)}, u32[]{:S(2)}) collective-permute-start(bf16[4,512,128]{2,1,0:T(8,128)(2,1)} %collective-permute-done.10.refs_9_.refs_10_), channel_id=1, source_target_pairs={{0,16},{1,17},{2,18},{3,19},{4,20},{5,21},{6,22},{7,23},{8,9},{9,8... | collective-permute-start | bytes 1572872 | tf_op jit(solution)/shard_map/ppermute | solution.py:599
  49.5 0.8 collective-permute-start.18
  50.2 11.2 %collective-permute-done.8.refs_13_.refs_8_ = bf16[4,512,128]{2,1,0:T(8,128)(2,1)S(1)} collective-permute-done((bf16[4,512,128]{2,1,0:T(8,128)(2,1)S(1)}, bf16[4,512,128]{2,1,0:T(8,128)(2,1)S(1)}, u32[]{:S(2)}, u32[]{:S(2)}) %collective-permute-start.8) | collective-permute-done | bytes 524320 | tf_op jit(solution)/shard_map/ppermute | solution.py:599
  61.5 8.9 %shard_map.105 = (bf16[512,256]{1,0:T(8,128)(2,1)S(1)}, bf16[512,256]{1,0:T(8,128)(2,1)S(1)}, bf16[1024,256]{1,0:T(8,128)(2,1)}) custom-call(s32[17]{0:T(128)S(1)} %stack.63.scalars, s32[1]{0:T(128)} %collective-permute-done.other_length, bf16[512,1024]{1,0:T(8,128)(2,1)S(1)} %get-tuple-element.15.refs_0_, ...), custom_call_target="tpu_custom_call" | custom-call | flops 1610612736 | bytes 4194304 | tf_op jit(solution)/shard_map/pallas_call | solution.py:262
  70.4 0.0 copy-start.4
  70.4 0.1 collective-permute-start.15
  70.5 2.2 %collective-permute-done.12.refs_12_.refs_13_ = bf16[4,512,128]{2,1,0:T(8,128)(2,1)S(1)} collective-permute-done((bf16[4,512,128]{2,1,0:T(8,128)(2,1)}, bf16[4,512,128]{2,1,0:T(8,128)(2,1)S(1)}, u32[]{:S(2)}, u32[]{:S(2)}) %collective-permute-start.12) | collective-permute-done | bytes 524320 | tf_op jit(solution)/shard_map/ppermute | solution.py:599
  72.7 9.0 %shard_map.106 = (bf16[512,256]{1,0:T(8,128)(2,1)S(1)}, bf16[512,256]{1,0:T(8,128)(2,1)}, bf16[1024,256]{1,0:T(8,128)(2,1)}) custom-call(s32[17]{0:T(128)S(1)} %stack.63.scalars, s32[1]{0:T(128)} %collective-permute-done.other_length, bf16[512,1024]{1,0:T(8,128)(2,1)S(1)} %get-tuple-element.15.refs_0_, bf16[16,1024]{1,0:T(8,128)(2,1)S(1)} %collective-permute-done.1.refs_1_, ...), custom_call_target="tpu_custom_call" | custom-call | flops 1610612736 | bytes 4194304 | tf_op jit(solution)/shard_map/pallas_call | solution.py:262
  81.8 0.7 copy-done.6
  82.4 0.5 collective-permute-start.13
  83.0 6.2 %collective-permute-done.18.refs_3_ = bf16[1024,512]{1,0:T(8,128)(2,1)} collective-permute-done((bf16[1024,512]{1,0:T(8,128)(2,1)}, bf16[1024,512]{1,0:T(8,128)(2,1)}, u32[]{:S(2)}, u32[]{:S(2)}) %collective-permute-start.18) | collective-permute-done | bytes 1048608 | tf_op jit(solution)/shard_map/ppermute | solution.py:599
  89.2 0.5 collective-permute-start.19
  89.7 0.1 copy.11.owners_col
  89.8 0.7 copy-done.14
  90.5 0.9 shard_map.108
  91.4 0.0 copy-done.5
  91.4 0.1 copy-done.7
  91.5 4.3 %shard_map.109 = bf16[256,1024]{1,0:T(8,128)(2,1)} custom-call(s32[17]{0:T(128)S(1)} %stack.63.scalars, f32[128,1024]{1,0:T(8,128)S(1)} %get-tuple-element.24.base, bf16[128,512]{1,0:T(8,128)(2,1)S(1)} %get-tuple-element.25.member, f32[128,128]{1,0:T(8,128)S(1)} %get-tuple-element.26.inverse, bf16[256,128]{1,0:T(8,128)(2,1)S(1)} %get-tuple-element.27.route, ...), custom_call_target="tpu_custom_call" | custom-call | flops 536870912 | bytes 3145728 | tf_op jit(solution)/shard_map/pallas_call | solution.py:262
  95.8 3.7 %all-to-all-start.1 = ((bf16[8,32,1024]{2,1,0:T(8,128)(2,1)}), bf16[8,32,1024]{2,1,0:T(8,128)(2,1)S(1)}, u32[]{:S(2)}, u32[]{:S(2)}) async-start(bf16[8,32,1024]{2,1,0:T(8,128)(2,1)} %bitcast.24), calls=%async_computation.1 | async-start | bytes 1048576 | tf_op jit(solution)/shard_map/all_to_all | solution.py:607
  99.6 0.9 copy-done.9
  100.5 4.1 %shard_map.107 = bf16[512,1024]{1,0:T(8,128)(2,1)} custom-call(s32[17]{0:T(128)S(1)} %stack.63.scalars, bf16[512,256]{1,0:T(8,128)(2,1)S(1)} %copy-done.5, bf16[512,256]{1,0:T(8,128)(2,1)S(1)} %copy-done.7, bf16[512,256]{1,0:T(8,128)(2,1)S(1)} %collective-permute-done.13.refs_2_, bf16[512,256]{1,0:T(8,128)(2,1)S(1)} %copy-done.9, ...), custom_call_target="tpu_custom_call" | custom-call | flops 1073741824 | bytes 3145728 | tf_op jit(solution)/shard_map/pallas_call | solution.py:262
  104.6 9.6 %all-to-all-done.1 = bf16[8,32,1024]{2,1,0:T(8,128)(2,1)S(1)} async-done(((bf16[8,32,1024]{2,1,0:T(8,128)(2,1)}), bf16[8,32,1024]{2,1,0:T(8,128)(2,1)S(1)}, u32[]{:S(2)}, u32[]{:S(2)}) %all-to-all-start.1) | async-done | bytes 524320 | tf_op jit(solution)/shard_map/all_to_all | solution.py:607
  114.2 4.3 %shard_map.110 = bf16[256,2048]{1,0:T(8,128)(2,1)} custom-call(s32[17]{0:T(128)S(1)} %stack.63.scalars, bf16[256,1024]{1,0:T(8,128)(2,1)S(1)} %bitcast.33, bf16[1024,512]{1,0:T(8,128)(2,1)} %refs_1_.1, bf16[1024,512]{1,0:T(8,128)(2,1)} %collective-permute-done.17.refs_2_, bf16[1024,512]{1,0:T(8,128)(2,1)} %collective-permute-done.18.refs_3_, ...), custom_call_target="tpu_custom_call" | custom-call | flops 1073741824 | bytes 4194304 | tf_op jit(solution)/shard_map/pallas_call | solution.py:262
  (37 shorter events, 0.1 us)
Async XLA Ops:
  0.7 15.7 %copy-start = (bf16[1,512,1024]{2,1,0:T(8,128)(2,1)S(1)}, bf16[1,512,1024]{2,1,0:T(8,128)(2,1)}, u32[]{:S(2)}) copy-start(bf16[1,512,1024]{2,1,0:T(8,128)(2,1)} %param.9) | copy-start | bytes 3145732
  3.3 10.2 %collective-permute-start.5 = (bf16[4,512,128]{2,1,0:T(8,128)(2,1)S(1)}, bf16[4,512,128]{2,1,0:T(8,128)(2,1)}, u32[]{:S(2)}, u32[]{:S(2)}) collective-permute-start(bf16[4,512,128]{2,1,0:T(8,128)(2,1)S(1)} %get-tuple-element.30.refs_6_), channel_id=1, source_target_pairs={{0,1},{1,0},{2,3},{3,2},{4,5},{5,4},{6,7},{7,6},{8,10},{9,11},{10,... | collective-permute-start | bytes 1572872 | tf_op jit(solution)/shard_map/ppermute | solution.py:599
  6.2 0.8 copy-start.2
  7.1 20.1 %collective-permute-start.6 = (bf16[4,512,128]{2,1,0:T(8,128)(2,1)}, bf16[4,512,128]{2,1,0:T(8,128)(2,1)S(1)}, u32[]{:S(2)}, u32[]{:S(2)}) collective-permute-start(bf16[4,512,128]{2,1,0:T(8,128)(2,1)} %get-tuple-element.28), channel_id=1, source_target_pairs={{0,6},{1,7},{2,0},{3,1},{4,2},{5,3},{6,4},{7,5},{8,10},{9,11},{10,... | collective-permute-start | bytes 1572872 | tf_op jit(solution)/shard_map/ppermute | solution.py:599
  13.5 32.9 %collective-permute-start.7 = (bf16[4,512,128]{2,1,0:T(8,128)(2,1)}, bf16[4,512,128]{2,1,0:T(8,128)(2,1)S(1)}, u32[]{:S(2)}, u32[]{:S(2)}) collective-permute-start(bf16[4,512,128]{2,1,0:T(8,128)(2,1)} %collective-permute-done.5.refs_7_.refs_10_), channel_id=1, source_target_pairs={{0,16},{1,17},{2,18},{3,19},{4,20},{5,21},{6,22},{7,23},{8,9},{9,8... | collective-permute-start | bytes 1572872 | tf_op jit(solution)/shard_map/ppermute | solution.py:599
  16.2 0.7 copy-start.12
  16.3 0.7 copy-start.11
  18.5 0.7 copy-start.10
  19.2 27.2 %all-to-all-start = ((bf16[8,16,1024]{2,1,0:T(8,128)(2,1)}), bf16[8,16,1024]{2,1,0:T(8,128)(2,1)S(1)}, u32[]{:S(2)}, u32[]{:S(2)}) async-start(bf16[8,16,1024]{2,1,0:T(8,128)(2,1)} %copy-done.10), calls=%async_computation | async-start | bytes 524288 | tf_op jit(solution)/shard_map/all_to_all | solution.py:607
  25.0 25.2 %collective-permute-start.2 = (bf16[512,1024]{1,0:T(8,128)(2,1)S(1)}, bf16[512,1024]{1,0:T(8,128)(2,1)}, u32[]{:S(2)}, u32[]{:S(2)}) collective-permute-start(bf16[512,1024]{1,0:T(8,128)(2,1)S(1)} %get-tuple-element.15.refs_0_), channel_id=1, source_target_pairs={{0,8},{1,9},{2,10},{3,11},{4,12},{5,13},{6,14},{7,15},{8,0},{9,1},... | collective-permute-start | bytes 3145736 | tf_op jit(solution)/shard_map/ppermute | solution.py:599
  25.7 21.7 %collective-permute-start.9 = (bf16[4,512,128]{2,1,0:T(8,128)(2,1)}, bf16[4,512,128]{2,1,0:T(8,128)(2,1)}, u32[]{:S(2)}, u32[]{:S(2)}) collective-permute-start(bf16[4,512,128]{2,1,0:T(8,128)(2,1)} %collective-permute-done.5.refs_7_.refs_10_), channel_id=1, source_target_pairs={{8,10},{9,11},{10,12},{11,13},{12,14},{13,15},{14,8},{15,9},{24,26... | collective-permute-start | bytes 1572872 | tf_op jit(solution)/shard_map/ppermute | solution.py:599
  27.1 21.0 %collective-permute-start.10 = (bf16[4,512,128]{2,1,0:T(8,128)(2,1)S(1)}, bf16[4,512,128]{2,1,0:T(8,128)(2,1)}, u32[]{:S(2)}, u32[]{:S(2)}) collective-permute-start(bf16[4,512,128]{2,1,0:T(8,128)(2,1)S(1)} %collective-permute-done.6.refs_9_.refs_6_), channel_id=1, source_target_pairs={{0,1},{1,0},{2,3},{3,2},{4,5},{5,4},{6,7},{7,6},{8,10},{9,11},{10,... | collective-permute-start | bytes 1572872 | tf_op jit(solution)/shard_map/ppermute | solution.py:599
  28.7 2.8 %collective-permute-start = (s32[1]{0:T(128)}, s32[1]{0:T(128)}, u32[]{:S(2)}, u32[]{:S(2)}) collective-permute-start(s32[1]{0:T(128)} %param.10), channel_id=1, source_target_pairs={{0,8},{1,9},{2,10},{3,11},{4,12},{5,13},{6,14},{7,15},{8,0},{9,1},... | collective-permute-start | bytes 20 | tf_op jit(solution)/shard_map/ppermute | solution.py:599
  31.5 6.8 %collective-permute-start.1 = (bf16[16,1024]{1,0:T(8,128)(2,1)S(1)}, bf16[16,1024]{1,0:T(8,128)(2,1)S(1)}, u32[]{:S(2)}, u32[]{:S(2)}) collective-permute-start(bf16[16,1024]{1,0:T(8,128)(2,1)S(1)} %get-tuple-element.16), channel_id=1, source_target_pairs={{1,0},{2,1},{3,2},{4,3},{5,4},{6,5},{7,6},{9,8},{10,9},{11,10},{12... | collective-permute-start | bytes 98312 | tf_op jit(solution)/shard_map/ppermute | solution.py:26
  38.4 8.2 %collective-permute-start.3 = (bf16[16,1024]{1,0:T(8,128)(2,1)S(1)}, bf16[16,1024]{1,0:T(8,128)(2,1)S(1)}, u32[]{:S(2)}, u32[]{:S(2)}) collective-permute-start(bf16[16,1024]{1,0:T(8,128)(2,1)S(1)} %collective-permute-done.1.refs_1_), channel_id=1, source_target_pairs={{0,8},{1,9},{2,10},{3,11},{4,12},{5,13},{6,14},{7,15},{8,0},{9,1},... | collective-permute-start | bytes 98312 | tf_op jit(solution)/shard_map/ppermute | solution.py:599
  46.5 15.0 %copy-start.1 = (bf16[4,512,128]{2,1,0:T(8,128)(2,1)S(1)}, bf16[4,512,128]{2,1,0:T(8,128)(2,1)}, u32[]{:S(2)}) copy-start(bf16[4,512,128]{2,1,0:T(8,128)(2,1)} %get-tuple-element.29.refs_8_) | copy-start | bytes 1572868
  46.5 15.0 %copy-start.3 = (bf16[4,512,128]{2,1,0:T(8,128)(2,1)S(1)}, bf16[4,512,128]{2,1,0:T(8,128)(2,1)}, u32[]{:S(2)}) copy-start(bf16[4,512,128]{2,1,0:T(8,128)(2,1)} %copy-done.2) | copy-start | bytes 1572868
  46.5 3.0 %collective-permute-start.4 = (bf16[128,1024]{1,0:T(8,128)(2,1)S(1)}, bf16[128,1024]{1,0:T(8,128)(2,1)S(1)}, u32[]{:S(2)}, u32[]{:S(2)}) collective-permute-start(bf16[128,1024]{1,0:T(8,128)(2,1)S(1)} %bitcast.30), channel_id=1, source_target_pairs={{0,8},{1,9},{2,10},{3,11},{4,12},{5,13},{6,14},{7,15},{8,0},{9,1},... | collective-permute-start | bytes 786440 | tf_op jit(solution)/shard_map/ppermute | solution.py:599
  46.6 14.9 %collective-permute-start.8 = (bf16[4,512,128]{2,1,0:T(8,128)(2,1)S(1)}, bf16[4,512,128]{2,1,0:T(8,128)(2,1)S(1)}, u32[]{:S(2)}, u32[]{:S(2)}) collective-permute-start(bf16[4,512,128]{2,1,0:T(8,128)(2,1)S(1)} %broadcast_select_fusion), channel_id=1, source_target_pairs={{0,16},{1,17},{2,18},{3,19},{4,20},{5,21},{6,22},{7,23},{8,24},{9,... | collective-permute-start | bytes 1572872 | tf_op jit(solution)/shard_map/ppermute | solution.py:599
  47.4 23.1 %collective-permute-start.11 = (bf16[4,512,128]{2,1,0:T(8,128)(2,1)}, bf16[4,512,128]{2,1,0:T(8,128)(2,1)S(1)}, u32[]{:S(2)}, u32[]{:S(2)}) collective-permute-start(bf16[4,512,128]{2,1,0:T(8,128)(2,1)} %collective-permute-done.9.refs_7_), channel_id=1, source_target_pairs={{8,9},{9,8},{10,11},{11,10},{12,13},{13,12},{14,15},{15,14},{24,25... | collective-permute-start | bytes 1572872 | tf_op jit(solution)/shard_map/ppermute | solution.py:599
  48.1 24.6 %collective-permute-start.12 = (bf16[4,512,128]{2,1,0:T(8,128)(2,1)}, bf16[4,512,128]{2,1,0:T(8,128)(2,1)S(1)}, u32[]{:S(2)}, u32[]{:S(2)}) collective-permute-start(bf16[4,512,128]{2,1,0:T(8,128)(2,1)} %collective-permute-done.10.refs_9_.refs_10_), channel_id=1, source_target_pairs={{0,16},{1,17},{2,18},{3,19},{4,20},{5,21},{6,22},{7,23},{8,9},{9,8... | collective-permute-start | bytes 1572872 | tf_op jit(solution)/shard_map/ppermute | solution.py:599
  49.5 39.7 %collective-permute-start.18 = (bf16[1024,512]{1,0:T(8,128)(2,1)}, bf16[1024,512]{1,0:T(8,128)(2,1)}, u32[]{:S(2)}, u32[]{:S(2)}) collective-permute-start(bf16[1024,512]{1,0:T(8,128)(2,1)} %refs_1_.1), channel_id=1, source_target_pairs={{0,16},{1,17},{2,18},{3,19},{4,20},{5,21},{6,22},{7,23},{8,24},{9,... | collective-permute-start | bytes 3145736 | tf_op jit(solution)/shard_map/ppermute | solution.py:599
  70.4 11.3 %copy-start.4 = (bf16[512,256]{1,0:T(8,128)(2,1)}, bf16[512,256]{1,0:T(8,128)(2,1)S(1)}, u32[]{:S(2)}) copy-start(bf16[512,256]{1,0:T(8,128)(2,1)S(1)} %get-tuple-element.18.refs_0_) | copy-start | bytes 786436
  70.4 21.0 %collective-permute-start.15 = (bf16[1024,256]{1,0:T(8,128)(2,1)}, bf16[1024,256]{1,0:T(8,128)(2,1)S(1)}, u32[]{:S(2)}, u32[]{:S(2)}) collective-permute-start(bf16[1024,256]{1,0:T(8,128)(2,1)} %get-tuple-element.22.refs_4_), channel_id=1, source_target_pairs={{0,8},{1,9},{2,10},{3,11},{4,12},{5,13},{6,14},{7,15},{8,0},{9,1},... | collective-permute-start | bytes 1572872 | tf_op jit(solution)/shard_map/ppermute | solution.py:599
  81.8 0.7 copy-start.6
  82.4 9.0 %collective-permute-start.16 = (bf16[1024,256]{1,0:T(8,128)(2,1)}, bf16[1024,256]{1,0:T(8,128)(2,1)S(1)}, u32[]{:S(2)}, u32[]{:S(2)}) collective-permute-start(bf16[1024,256]{1,0:T(8,128)(2,1)} %get-tuple-element.23.refs_5_), channel_id=1, source_target_pairs={{0,8},{1,9},{2,10},{3,11},{4,12},{5,13},{6,14},{7,15},{8,0},{9,1},... | collective-permute-start | bytes 1572872 | tf_op jit(solution)/shard_map/ppermute | solution.py:599
  82.4 6.7 %collective-permute-start.13 = (bf16[512,256]{1,0:T(8,128)(2,1)S(1)}, bf16[512,256]{1,0:T(8,128)(2,1)S(1)}, u32[]{:S(2)}, u32[]{:S(2)}) collective-permute-start(bf16[512,256]{1,0:T(8,128)(2,1)S(1)} %get-tuple-element.20), channel_id=1, source_target_pairs={{0,8},{1,9},{2,10},{3,11},{4,12},{5,13},{6,14},{7,15},{8,0},{9,1},... | collective-permute-start | bytes 786440 | tf_op jit(solution)/shard_map/ppermute | solution.py:599
  83.0 6.7 %copy-start.13 = (s32[1,1,128,1]{2,3,1,0:T(1,128)S(1)}, s32[1,1,128,1]{2,3,1,0:T(1,128)}, u32[]{:S(2)}) copy-start(s32[1,1,128,1]{2,3,1,0:T(1,128)} %param.16) | copy-start | bytes 1540
  83.0 8.4 %collective-permute-start.14 = (bf16[512,256]{1,0:T(8,128)(2,1)}, bf16[512,256]{1,0:T(8,128)(2,1)S(1)}, u32[]{:S(2)}, u32[]{:S(2)}) collective-permute-start(bf16[512,256]{1,0:T(8,128)(2,1)} %get-tuple-element.21), channel_id=1, source_target_pairs={{0,8},{1,9},{2,10},{3,11},{4,12},{5,13},{6,14},{7,15},{8,0},{9,1},... | collective-permute-start | bytes 786440 | tf_op jit(solution)/shard_map/ppermute | solution.py:599
  89.2 15.4 %collective-permute-start.17 = (bf16[1024,512]{1,0:T(8,128)(2,1)}, bf16[1024,512]{1,0:T(8,128)(2,1)}, u32[]{:S(2)}, u32[]{:S(2)}) collective-permute-start(bf16[1024,512]{1,0:T(8,128)(2,1)} %refs_1_.1), channel_id=1, source_target_pairs={{0,8},{1,9},{2,10},{3,11},{4,12},{5,13},{6,14},{7,15},{8,0},{9,1},... | collective-permute-start | bytes 3145736 | tf_op jit(solution)/shard_map/ppermute | solution.py:599
  89.2 15.4 %collective-permute-start.19 = (bf16[1024,512]{1,0:T(8,128)(2,1)}, bf16[1024,512]{1,0:T(8,128)(2,1)}, u32[]{:S(2)}, u32[]{:S(2)}) collective-permute-start(bf16[1024,512]{1,0:T(8,128)(2,1)} %collective-permute-done.18.refs_3_), channel_id=1, source_target_pairs={{0,8},{1,9},{2,10},{3,11},{4,12},{5,13},{6,14},{7,15},{8,0},{9,1},... | collective-permute-start | bytes 3145736 | tf_op jit(solution)/shard_map/ppermute | solution.py:599
  89.8 0.7 copy-start.14
  90.5 0.9 copy-start.5
  90.5 1.0 copy-start.7
  91.4 4.4 %copy-start.8 = (bf16[512,256]{1,0:T(8,128)(2,1)}, bf16[512,256]{1,0:T(8,128)(2,1)S(1)}, u32[]{:S(2)}) copy-start(bf16[512,256]{1,0:T(8,128)(2,1)S(1)} %collective-permute-done.14.refs_3_) | copy-start | bytes 786436
  95.8 18.4 %all-to-all-start.1 = ((bf16[8,32,1024]{2,1,0:T(8,128)(2,1)}), bf16[8,32,1024]{2,1,0:T(8,128)(2,1)S(1)}, u32[]{:S(2)}, u32[]{:S(2)}) async-start(bf16[8,32,1024]{2,1,0:T(8,128)(2,1)} %bitcast.24), calls=%async_computation.1 | async-start | bytes 1048576 | tf_op jit(solution)/shard_map/all_to_all | solution.py:607
  99.6 0.9 copy-start.9

commit v3 on v2

--- a/solution.py
+++ b/solution.py
@@ -329,9 +329,9 @@
 
 
 def attend_kernel(span_len, right_len, head_size, scalars, other_length, *refs):
-    sources, pieces = refs[:6], refs[6:14]
-    outs, projection = refs[14:16], refs[16]
-    rows_in, weight, query, key, value, bias, scores, peaks, weights, sems = refs[17:]
+    members, sources, pieces = refs[:2], refs[2:8], refs[8:16]
+    outs, sums_out, projection = refs[16:18], refs[18:20], refs[20]
+    rows_in, weight, query, key, value, bias, scores, peaks, weights, sems = refs[21:]
     first_frame, core, y_half = scalars[0], scalars[2], scalars[3]
     frame_count, model_width = sources[0].shape
     half = model_width // 2
@@ -460,6 +460,10 @@
             weigh_block(step - 1)
         if step < count:
             score_block(step)
+    for rec in range(2):
+        sums_out[rec][...] = jnp.dot(
+            members[rec][...], outs[rec][...], preferred_element_type=jnp.float32
+        )
     for copy in piece_copies(0, True):
         copy.wait()
 
@@ -476,39 +480,22 @@
     return offsets, shard
 
 
-def pool_kernel(offsets_at, scalars, base, member, inverse, route, *refs):
-    attended, projections = refs[:4], refs[4:8]
-    sent_out, gathered, weight, pooled, sems = refs[8:]
-    shard = attended[0].shape[1] // 2
+def pool_kernel(offsets_at, scalars, base, inverse, route, *refs):
+    sums, projections = refs[:4], refs[4:8]
+    sent_out, means, pooled = refs[8:]
+    shard = sums[0].shape[1] // 2
     offsets = [
         [pl.multiple_of(scalars[offsets_at + 2 * i + s], LANES) for s in range(2)]
         for i in range(4)
     ]
-    row_copies, weight_copies = [], []
     for i in range(4):
         for s in range(2):
-            row_copies.append(
-                pltpu.make_async_copy(
-                    attended[i].at[:, pl.ds(s * shard, shard)],
-                    gathered.at[:, pl.ds(offsets[i][s], shard)],
-                    sems.at[2 * i + s],
-                )
-            )
-        weight_copies.append(
-            pltpu.make_async_copy(projections[i], weight.at[i], sems.at[8 + i])
-        )
-    for copy in row_copies + weight_copies:
-        copy.start()
-    for copy in row_copies:
-        copy.wait()
-    means = jnp.dot(member[...], gathered[...], preferred_element_type=jnp.float32)
-    model_width = means.shape[1]
-    means = (means * jnp.concatenate([inverse[...]] * (model_width // LANES), axis=1)).astype(
-        jnp.bfloat16
-    )
+            for lane in range(0, shard, LANES):
+                means[:, pl.ds(offsets[i][s] + lane, LANES)] = (
+                    sums[i][:, s * shard + lane : s * shard + lane + LANES] * inverse[...]
+                ).astype(jnp.bfloat16)
     for i in range(4):
-        weight_copies[i].wait()
-        mixed = jnp.dot(means, weight[i], preferred_element_type=jnp.float32)
+        mixed = jnp.dot(means[...], projections[i][...], preferred_element_type=jnp.float32)
         for s in range(2):
             columns = pl.ds(offsets[i][s], shard)
             pooled[:, columns] = (
@@ -540,23 +527,20 @@
             ).astype(jnp.bfloat16)
 
 
-def language_kernel(places_at, scalars, *refs):
-    received, pieces, out = refs[0], refs[1:-6], refs[-6]
-    rows, weights, product, sems, out_sems = refs[-5:]
+def language_kernel(places_at, scalars, received, *refs):
+    pieces, out = refs[:-5], refs[-5]
+    weights, product, sems, out_sems = refs[-4:]
     count, width = len(pieces), pieces[0].shape[1]
-    row_copy = pltpu.make_async_copy(received, rows, sems.at[count])
-    row_copy.start()
     copies = [
         pltpu.make_async_copy(piece, weights.at[i], sems.at[i]) for i, piece in enumerate(pieces)
     ]
     for copy in copies:
         copy.start()
-    row_copy.wait()
     out_copies = []
     for i in range(count):
         copies[i].wait()
         product[i] = jnp.dot(
-            rows[...], weights[i], preferred_element_type=jnp.float32
+            received[...], weights[i], preferred_element_type=jnp.float32
         ).astype(jnp.bfloat16)
         place = pl.multiple_of(scalars[places_at + i], LANES)
         out_copies.append(
@@ -635,7 +619,9 @@
 
     own = jnp.concatenate([qkv_weight, out_weight[None]], axis=0)
     own_a = lax.dynamic_slice_in_dim(own, y_half * half, half, 1)
-    own_b = lax.dynamic_slice_in_dim(own, (1 - y_half) * half, half, 1)
+    later_qkv, later_out, own_a = lax.optimization_barrier((qkv_weight, out_weight, own_a))
+    later = jnp.concatenate([later_qkv, later_out[None]], axis=0)
+    own_b = lax.dynamic_slice_in_dim(later, (1 - y_half) * half, half, 1)
 
     def pick(for_core_0, for_core_1):
         return jnp.where(core == 0, for_core_0, for_core_1)
@@ -680,7 +666,7 @@
     ahead = shifted(start_rows, "tm", -1)
     memories = exchange_blocks(memory).reshape(-1, model_width)
     owners_col = owners[0, 0]
-    prepared = local_call(
+    base, member, inverse, route = local_call(
         prepare_kernel,
         (
             shape_of(token_count, model_width, dtype=jnp.float32),
@@ -693,6 +679,7 @@
         flops=2 * token_count * frame_count * model_width,
         moved=2 * frame_count * model_width,
     )
+    other_member = swap_cores(member)
     other_ahead = swap_cores(ahead)
     other_memories = swap_cores(memories)
 
@@ -713,18 +700,20 @@
     keys_seen = block + pad + memories.shape[0]
     lanes = width // head_size * block
     block_count = 2 * (frame_count // block)
-    attended, outs = [], []
+    attended, sums, outs = [], [], []
     for pieces in slot_pieces:
         flat = [p for pair in pieces for p in pair]
-        *pair, out_piece = local_call(
+        *results, out_piece = local_call(
             functools.partial(attend_kernel, C, RC, head_size),
             (
                 shape_of(frame_count, width),
                 shape_of(frame_count, width),
+                shape_of(token_count, width, dtype=jnp.float32),
+                shape_of(token_count, width, dtype=jnp.float32),
                 shape_of(model_width, width),
             ),
             (scalars, other_length),
-            (normed, ahead, memories, other_normed, other_ahead, other_memories, *flat),
+            (member, other_member, normed, ahead, memories, other_normed, other_ahead, other_memories, *flat),
             in_place=6 + len(flat),
             scratch=(
                 pltpu.VMEM((2 * row_count, model_width), bf16),
@@ -742,23 +731,23 @@
             flops=12 * frame_count * model_width * width,
             moved=8 * frame_count * model_width,
         )
-        attended.append(pair)
+        attended.append(results[:2])
+        sums.append(results[2:])
         outs.append(out_piece)
     other_outs = [swap_cores(w) for w in outs]
     other_attended = [swap_cores(for_other) for _, for_other in attended]
 
-    features = (attended[0][0], attended[1][0], *other_attended, *outs, *other_outs)
+    other_sums = [swap_cores(for_other) for _, for_other in sums]
+    projections = (*outs, *other_outs)
+    features = (attended[0][0], attended[1][0], *other_attended, *projections)
     sent_rows = local_call(
         functools.partial(pool_kernel, offsets_at),
         shape_of(slot_count, model_width),
         (scalars,),
-        (*prepared, *features),
-        in_place=len(features),
+        (base, inverse, route, sums[0][0], sums[1][0], *other_sums, *projections),
         scratch=(
-            pltpu.VMEM((frame_count, model_width), bf16),
-            pltpu.VMEM((4, model_width, width), bf16),
             pltpu.VMEM((token_count, model_width), bf16),
-            pltpu.SemaphoreType.DMA((12,)),
+            pltpu.VMEM((token_count, model_width), bf16),
         ),
         flops=4 * token_count * model_width * model_width,
         moved=6 * frame_count * model_width,
@@ -781,13 +770,12 @@
         shape_of(slot_count, rec_count * language_shard),
         (scalars,),
         (received, *language_pieces),
-        in_place=1 + rec_count,
+        in_place=rec_count,
         out_in_place=True,
         scratch=(
-            pltpu.VMEM((slot_count, model_width), bf16),
             pltpu.VMEM((rec_count, model_width, language_shard), bf16),
             pltpu.VMEM((rec_count, slot_count, language_shard), bf16),
-            pltpu.SemaphoreType.DMA((rec_count + 1,)),
+            pltpu.SemaphoreType.DMA((rec_count,)),
             pltpu.SemaphoreType.DMA((rec_count,)),
         ),
         flops=2 * slot_count * model_width * rec_count * language_shard,

time: 119 us -> 120 us (level)
  waiting for transfers between devices: 46.9 us -> 36.2 us
  starting transfers between devices: 29.6 us -> 37.8 us
  local copies, waits for them, and re-layouts: 4.84 us -> 10.2 us
  Pallas kernels: 33 us -> 30 us
    all_to_all x2, waiting for transfers between devices: 17.7 us -> 8.74 us  [exchange_blocks(): return lax.all_to_all(blocks, 'tm', split_axis=0, concat_axis=0, tiled=True)]
    all_to_all x2, starting transfers between devices: 9.53 us -> 15.7 us  [exchange_blocks(): return lax.all_to_all(blocks, 'tm', split_axis=0, concat_axis=0, tiled=True)]
    unnamed x30 -> x56, local copies, waits for them, and re-layouts: 4.63 us -> 9.32 us
    pallas_call x7, Pallas kernels: 33 us -> 30 us  [local_call(): pl.pallas_call(kernel, out_shape=out_shapes, in_specs=[smem_spec()] * len...]
    ppermute x19 -> x22, starting transfers between devices: 18.8 us -> 20.7 us  [relocate(): return lax.ppermute(value, ('rec', 'tm'), pairs)]
    ppermute x19 -> x22, waiting for transfers between devices: 23.6 us -> 22.4 us  [relocate(): return lax.ppermute(value, ('rec', 'tm'), pairs)]
  transfers between devices with their start and end apart: 22 -> 25, of which waited for: 8 -> 10; matrix products, arithmetic and copies ran while one was open for 0% -> 2% of each run, Pallas kernels for 24% -> 22%
where the time goes in v3:
time: 120 us; the launch traced here: 119 us
  starting transfers between devices  37.8 us (31%)
  waiting for transfers between devices  36.2 us (30%)
  Pallas kernels  30 us (25%)
  local copies, waits for them, and re-layouts  10.2 us (8%)
  other arithmetic  3.24 us (3%)
  between operations  1.81 us (2%)
    pallas_call x7, Pallas kernels, local_call(): pl.pallas_call(kernel, out_shape=out_shapes, in_specs=[smem_spec()] * len...  30 us
    ppermute x22, waiting for transfers between devices, relocate(): return lax.ppermute(value, ('rec', 'tm'), pairs)  22.4 us
    ppermute x22, starting transfers between devices, relocate(): return lax.ppermute(value, ('rec', 'tm'), pairs)  20.7 us
    all_to_all x2, starting transfers between devices, exchange_blocks(): return lax.all_to_all(blocks, 'tm', split_axis=0, concat_axis=0, tiled=True)  15.7 us
    unnamed x56, local copies, waits for them, and re-layouts  9.32 us
    all_to_all x2, waiting for transfers between devices, exchange_blocks(): return lax.all_to_all(blocks, 'tm', split_axis=0, concat_axis=0, tiled=True)  8.74 us
    ppermute x1, waiting for transfers between devices, shifted(): return lax.ppermute(block, axis, route)  5.07 us
  transfers between devices with their start and end apart: 25, of which 10 were waited for; matrix products, arithmetic and copies ran while one was open for 2% of the time, Pallas kernels for 22%

profile of v3, /device:TPU:0, one launch (start us, length us, event | category | flops | bytes accessed | tf_op | source)
XLA Modules:
  0.0 119.2 jit_solution(275503127272819254)
XLA Ops:
  0.7 1.1 fusion.1.refs_8_
  1.8 3.0 %collective-permute-start.6 = (bf16[4,512,128]{2,1,0:T(8,128)(2,1)S(1)}, bf16[4,512,128]{2,1,0:T(8,128)(2,1)}, u32[]{:S(2)}, u32[]{:S(2)}) collective-permute-start(bf16[4,512,128]{2,1,0:T(8,128)(2,1)S(1)} %fusion.1.refs_8_), channel_id=1, source_target_pairs={{0,1},{1,0},{2,3},{3,2},{4,5},{5,4},{6,7},{7,6},{8,10},{9,11},{10,... | collective-permute-start | bytes 1572872 | tf_op jit(solution)/shard_map/ppermute | solution.py:583
  4.8 2.1 %broadcast_select_fusion.1 = (bf16[4,512,128]{2,1,0:T(8,128)(2,1)}, bf16[4,512,128]{2,1,0:T(8,128)(2,1)S(1)}) fusion(bf16[4,512,128]{2,1,0:T(8,128)(2,1)S(1)} %fusion.1.refs_8_, pred[]{:T(512)S(6)} %eq.18, s32[]{:T(128)S(6)} %select_n.82, bf16[1,1024,128]{2,1,0:T(8,128)(2,1)S(1)} %bitcast.41, bf16[3,1024,128]{2,1,0:T(8,128)(2,1)} %param.13), kind=kLoop, calls=%fused_computation.7 | loop fusion | flops 1310720 | bytes 2621445 | tf_op jit(solution)/shard_map/jit(_where)/select_n | solution.py:627
  6.9 3.6 %collective-permute-start.7 = (bf16[4,512,128]{2,1,0:T(8,128)(2,1)}, bf16[4,512,128]{2,1,0:T(8,128)(2,1)S(1)}, u32[]{:S(2)}, u32[]{:S(2)}) collective-permute-start(bf16[4,512,128]{2,1,0:T(8,128)(2,1)} %get-tuple-element.42), channel_id=1, source_target_pairs={{0,6},{1,7},{2,0},{3,1},{4,2},{5,3},{6,4},{7,5},{8,10},{9,11},{10,... | collective-permute-start | bytes 1572872 | tf_op jit(solution)/shard_map/ppermute | solution.py:583
  10.5 1.6 %collective-permute-done.6.refs_9_.refs_12_ = bf16[4,512,128]{2,1,0:T(8,128)(2,1)} collective-permute-done((bf16[4,512,128]{2,1,0:T(8,128)(2,1)S(1)}, bf16[4,512,128]{2,1,0:T(8,128)(2,1)}, u32[]{:S(2)}, u32[]{:S(2)}) %collective-permute-start.6) | collective-permute-done | bytes 524320 | tf_op jit(solution)/shard_map/ppermute | solution.py:583
  12.1 2.0 %collective-permute-start.8 = (bf16[4,512,128]{2,1,0:T(8,128)(2,1)}, bf16[4,512,128]{2,1,0:T(8,128)(2,1)S(1)}, u32[]{:S(2)}, u32[]{:S(2)}) collective-permute-start(bf16[4,512,128]{2,1,0:T(8,128)(2,1)} %collective-permute-done.6.refs_9_.refs_12_), channel_id=1, source_target_pairs={{0,16},{1,17},{2,18},{3,19},{4,20},{5,21},{6,22},{7,23},{8,9},{9,8... | collective-permute-start | bytes 1572872 | tf_op jit(solution)/shard_map/ppermute | solution.py:583
  14.9 0.6 copy-done.22
  15.6 1.5 %shard_map.105 = (bf16[512,1024]{1,0:T(8,128)(2,1)S(1)}, bf16[16,1024]{1,0:T(8,128)(2,1)S(1)}, bf16[8,16,1024]{2,1,0:T(8,128)(2,1)S(1)}) custom-call(s32[17]{0:T(128)S(1)} %stack.63.scalars, bf16[512,1024]{1,0:T(8,128)(2,1)S(1)} %bitcast.28, f32[1,1024]{1,0:T(1,128)S(1)} %bitcast.35, f32[1,1024]{1,0:T(1,128)S(1)} %bitcast.36), custom_call_target="tpu_custom_call" | custom-call | flops 5242880 | bytes 2097152 | tf_op jit(solution)/shard_map/pallas_call | solution.py:262
  17.1 1.0 copy-done.1
  18.1 0.7 copy-done.12
  18.8 5.8 %all-to-all-start = ((bf16[8,16,1024]{2,1,0:T(8,128)(2,1)}), bf16[8,16,1024]{2,1,0:T(8,128)(2,1)S(1)}, u32[]{:S(2)}, u32[]{:S(2)}) async-start(bf16[8,16,1024]{2,1,0:T(8,128)(2,1)} %copy-done.12), calls=%async_computation | async-start | bytes 524288 | tf_op jit(solution)/shard_map/all_to_all | solution.py:591
  24.6 1.5 %collective-permute-start.10 = (bf16[4,512,128]{2,1,0:T(8,128)(2,1)}, bf16[4,512,128]{2,1,0:T(8,128)(2,1)}, u32[]{:S(2)}, u32[]{:S(2)}) collective-permute-start(bf16[4,512,128]{2,1,0:T(8,128)(2,1)} %collective-permute-done.6.refs_9_.refs_12_), channel_id=1, source_target_pairs={{8,10},{9,11},{10,12},{11,13},{12,14},{13,15},{14,8},{15,9},{24,26... | collective-permute-start | bytes 1572872 | tf_op jit(solution)/shard_map/ppermute | solution.py:583
  26.0 2.0 %collective-permute-start.11 = (bf16[4,512,128]{2,1,0:T(8,128)(2,1)S(1)}, bf16[4,512,128]{2,1,0:T(8,128)(2,1)}, u32[]{:S(2)}, u32[]{:S(2)}) collective-permute-start(bf16[4,512,128]{2,1,0:T(8,128)(2,1)S(1)} %collective-permute-done.7.refs_11_.refs_8_), channel_id=1, source_target_pairs={{0,1},{1,0},{2,3},{3,2},{4,5},{5,4},{6,7},{7,6},{8,10},{9,11},{10,... | collective-permute-start | bytes 1572872 | tf_op jit(solution)/shard_map/ppermute | solution.py:583
  28.0 1.9 %collective-permute-start = (s32[1]{0:T(128)}, s32[1]{0:T(128)}, u32[]{:S(2)}, u32[]{:S(2)}) collective-permute-start(s32[1]{0:T(128)} %param.10), channel_id=1, source_target_pairs={{0,8},{1,9},{2,10},{3,11},{4,12},{5,13},{6,14},{7,15},{8,0},{9,1},... | collective-permute-start | bytes 20 | tf_op jit(solution)/shard_map/ppermute | solution.py:583
  30.0 1.0 collective-permute-done.other_length
  30.9 1.4 %collective-permute-start.2 = (bf16[16,1024]{1,0:T(8,128)(2,1)S(1)}, bf16[16,1024]{1,0:T(8,128)(2,1)}, u32[]{:S(2)}, u32[]{:S(2)}) collective-permute-start(bf16[16,1024]{1,0:T(8,128)(2,1)S(1)} %get-tuple-element.24), channel_id=1, source_target_pairs={{1,0},{2,1},{3,2},{4,3},{5,4},{6,5},{7,6},{9,8},{10,9},{11,10},{12... | collective-permute-start | bytes 98312 | tf_op jit(solution)/shard_map/ppermute | solution.py:26
  32.3 5.1 %collective-permute-done.2.refs_3_ = bf16[16,1024]{1,0:T(8,128)(2,1)} collective-permute-done((bf16[16,1024]{1,0:T(8,128)(2,1)S(1)}, bf16[16,1024]{1,0:T(8,128)(2,1)}, u32[]{:S(2)}, u32[]{:S(2)}) %collective-permute-start.2) | collective-permute-done | bytes 32800 | tf_op jit(solution)/shard_map/ppermute | solution.py:26
  37.4 0.7 copy.11.owners_col
  38.2 0.7 copy-done.24
  38.8 0.8 copy-done.11
  39.7 0.9 shard_map.104
  40.6 0.8 copy-done.9
  41.4 0.6 copy-done.17
  42.0 0.6 copy-done.19
  42.6 0.5 collective-permute-start.1
  43.1 1.6 %all-to-all-done = bf16[8,16,1024]{2,1,0:T(8,128)(2,1)S(1)} async-done(((bf16[8,16,1024]{2,1,0:T(8,128)(2,1)}), bf16[8,16,1024]{2,1,0:T(8,128)(2,1)S(1)}, u32[]{:S(2)}, u32[]{:S(2)}) %all-to-all-start) | async-done | bytes 262176 | tf_op jit(solution)/shard_map/all_to_all | solution.py:591
  44.8 1.6 %collective-permute-start.9 = (bf16[4,512,128]{2,1,0:T(8,128)(2,1)S(1)}, bf16[4,512,128]{2,1,0:T(8,128)(2,1)S(1)}, u32[]{:S(2)}, u32[]{:S(2)}) collective-permute-start(bf16[4,512,128]{2,1,0:T(8,128)(2,1)S(1)} %broadcast_select_fusion), channel_id=1, source_target_pairs={{0,16},{1,17},{2,18},{3,19},{4,20},{5,21},{6,22},{7,23},{8,24},{9,... | collective-permute-start | bytes 1572872 | tf_op jit(solution)/shard_map/ppermute | solution.py:583
  46.4 0.7 collective-permute-start.12
  47.1 0.6 collective-permute-start.13
  47.7 1.5 %collective-permute-start.21 = (bf16[1024,512]{1,0:T(8,128)(2,1)}, bf16[1024,512]{1,0:T(8,128)(2,1)}, u32[]{:S(2)}, u32[]{:S(2)}) collective-permute-start(bf16[1024,512]{1,0:T(8,128)(2,1)} %refs_0_.1), channel_id=1, source_target_pairs={{0,16},{1,17},{2,18},{3,19},{4,20},{5,21},{6,22},{7,23},{8,24},{9,... | collective-permute-start | bytes 3145736 | tf_op jit(solution)/shard_map/ppermute | solution.py:583
  49.2 10.0 %collective-permute-done.9.refs_15_.refs_10_ = bf16[4,512,128]{2,1,0:T(8,128)(2,1)S(1)} collective-permute-done((bf16[4,512,128]{2,1,0:T(8,128)(2,1)S(1)}, bf16[4,512,128]{2,1,0:T(8,128)(2,1)S(1)}, u32[]{:S(2)}, u32[]{:S(2)}) %collective-permute-start.9) | collective-permute-done | bytes 524320 | tf_op jit(solution)/shard_map/ppermute | solution.py:583
  59.2 8.9 %shard_map.106 = (bf16[512,256]{1,0:T(8,128)(2,1)S(1)}, bf16[512,256]{1,0:T(8,128)(2,1)S(1)}, f32[128,256]{1,0:T(8,128)S(1)}, f32[128,256]{1,0:T(8,128)S(1)}, bf16[1024,256]{1,0:T(8,128)(2,1)S(1)}) custom-call(s32[17]{0:T(128)S(1)} %stack.63.scalars, s32[1]{0:T(128)} %collective-permute-done.other_length, bf16[128,512]{1,0:T(8,128)(2,1)S(1)} %get-tuple-element.22.refs_0_, ...), custom_call_target="tpu_custom_call" | custom-call | flops 1610612736 | bytes 4194304 | tf_op jit(solution)/shard_map/pallas_call | solution.py:262
  68.1 0.7 copy-done.13
  68.8 0.7 copy-done.25
  69.6 0.5 collective-permute-done.13.refs_14_.refs_15_
  70.0 8.9 %shard_map.107 = (bf16[512,256]{1,0:T(8,128)(2,1)S(1)}, bf16[512,256]{1,0:T(8,128)(2,1)S(1)}, f32[128,256]{1,0:T(8,128)S(1)}, f32[128,256]{1,0:T(8,128)S(1)}, bf16[1024,256]{1,0:T(8,128)(2,1)S(1)}) custom-call(s32[17]{0:T(128)S(1)} %stack.63.scalars, s32[1]{0:T(128)} %collective-permute-done.other_length, bf16[128,512]{1,0:T(8,128)(2,1)S(1)} %get-tuple-element.22.refs_0_, ...), custom_call_target="tpu_custom_call" | custom-call | flops 1610612736 | bytes 4194304 | tf_op jit(solution)/shard_map/pallas_call | solution.py:262
  79.7 7.7 %collective-permute-done.21.refs_2_ = bf16[1024,512]{1,0:T(8,128)(2,1)} collective-permute-done((bf16[1024,512]{1,0:T(8,128)(2,1)}, bf16[1024,512]{1,0:T(8,128)(2,1)}, u32[]{:S(2)}, u32[]{:S(2)}) %collective-permute-start.21) | collective-permute-done | bytes 1048608 | tf_op jit(solution)/shard_map/ppermute | solution.py:583
  87.4 0.5 collective-permute-start.22
  88.0 2.2 %shard_map.109 = bf16[256,1024]{1,0:T(8,128)(2,1)} custom-call(s32[17]{0:T(128)S(1)} %stack.63.scalars, f32[128,1024]{1,0:T(8,128)S(1)} %copy-done.10, f32[128,128]{1,0:T(8,128)S(1)} %copy-done.18, bf16[256,128]{1,0:T(8,128)(2,1)S(1)} %copy-done.20, f32[128,256]{1,0:T(8,128)S(1)} %get-tuple-element.38.refs_0_, f32[128,256]{1,0:T(8,128)S(1)} %get-tuple-element.39.refs_1_, ...), custom_call_target="tpu_custom_call" | custom-call | flops 536870912 | bytes 3145728 | tf_op jit(solution)/shard_map/pallas_call | solution.py:262
  90.2 9.9 %all-to-all-start.1 = ((bf16[8,32,1024]{2,1,0:T(8,128)(2,1)}), bf16[8,32,1024]{2,1,0:T(8,128)(2,1)S(1)}, u32[]{:S(2)}, u32[]{:S(2)}) async-start(bf16[8,32,1024]{2,1,0:T(8,128)(2,1)} %bitcast.25), calls=%async_computation.1 | async-start | bytes 1048576 | tf_op jit(solution)/shard_map/all_to_all | solution.py:591
  100.1 0.5 collective-permute-start.15
  100.6 1.2 %collective-permute-done.14.refs_2_ = bf16[512,256]{1,0:T(8,128)(2,1)S(1)} collective-permute-done((bf16[512,256]{1,0:T(8,128)(2,1)}, bf16[512,256]{1,0:T(8,128)(2,1)S(1)}, u32[]{:S(2)}, u32[]{:S(2)}) %collective-permute-start.14) | collective-permute-done | bytes 262176 | tf_op jit(solution)/shard_map/ppermute | solution.py:583
  101.8 0.4 collective-permute-done.15.refs_3_
  102.2 1.0 copy-done.8
  103.2 0.9 copy-done.16
  104.2 3.4 %shard_map.108 = bf16[512,1024]{1,0:T(8,128)(2,1)} custom-call(s32[17]{0:T(128)S(1)} %stack.63.scalars, bf16[512,256]{1,0:T(8,128)(2,1)S(1)} %copy-done.14, bf16[512,256]{1,0:T(8,128)(2,1)S(1)} %copy-done.16, bf16[512,256]{1,0:T(8,128)(2,1)S(1)} %collective-permute-done.14.refs_2_, bf16[512,256]{1,0:T(8,128)(2,1)S(1)} %collective-permute-done.15.refs_3_, ...), custom_call_target="tpu_custom_call" | custom-call | flops 1073741824 | bytes 3145728 | tf_op jit(solution)/shard_map/pallas_call | solution.py:262
  107.6 7.1 %all-to-all-done.1 = bf16[8,32,1024]{2,1,0:T(8,128)(2,1)S(1)} async-done(((bf16[8,32,1024]{2,1,0:T(8,128)(2,1)}), bf16[8,32,1024]{2,1,0:T(8,128)(2,1)S(1)}, u32[]{:S(2)}, u32[]{:S(2)}) %all-to-all-start.1) | async-done | bytes 524320 | tf_op jit(solution)/shard_map/all_to_all | solution.py:591
  114.7 4.3 %shard_map.110 = bf16[256,2048]{1,0:T(8,128)(2,1)} custom-call(s32[17]{0:T(128)S(1)} %stack.63.scalars, bf16[256,1024]{1,0:T(8,128)(2,1)S(1)} %bitcast.34, bf16[1024,512]{1,0:T(8,128)(2,1)} %refs_0_.1, bf16[1024,512]{1,0:T(8,128)(2,1)} %collective-permute-done.20.refs_1_, bf16[1024,512]{1,0:T(8,128)(2,1)} %collective-permute-done.21.refs_2_, ...), custom_call_target="tpu_custom_call" | custom-call | flops 1073741824 | bytes 4194304 | tf_op jit(solution)/shard_map/pallas_call | solution.py:262
  (70 shorter events, 1.2 us)
Async XLA Ops:
  0.7 4.1 %copy-start.27 = (bf16[1024,128]{1,0:T(8,128)(2,1)S(1)}, bf16[1024,128]{1,0:T(8,128)(2,1)}, u32[]{:S(2)}) copy-start(bf16[1024,128]{1,0:T(8,128)(2,1)} %param.14) | copy-start | bytes 786436
  1.8 10.3 %collective-permute-start.6 = (bf16[4,512,128]{2,1,0:T(8,128)(2,1)S(1)}, bf16[4,512,128]{2,1,0:T(8,128)(2,1)}, u32[]{:S(2)}, u32[]{:S(2)}) collective-permute-start(bf16[4,512,128]{2,1,0:T(8,128)(2,1)S(1)} %fusion.1.refs_8_), channel_id=1, source_target_pairs={{0,1},{1,0},{2,3},{3,2},{4,5},{5,4},{6,7},{7,6},{8,10},{9,11},{10,... | collective-permute-start | bytes 1572872 | tf_op jit(solution)/shard_map/ppermute | solution.py:583
  4.8 10.1 %copy-start = (bf16[1,512,1024]{2,1,0:T(8,128)(2,1)S(1)}, bf16[1,512,1024]{2,1,0:T(8,128)(2,1)}, u32[]{:S(2)}) copy-start(bf16[1,512,1024]{2,1,0:T(8,128)(2,1)} %param.9) | copy-start | bytes 3145732
  6.9 19.2 %collective-permute-start.7 = (bf16[4,512,128]{2,1,0:T(8,128)(2,1)}, bf16[4,512,128]{2,1,0:T(8,128)(2,1)S(1)}, u32[]{:S(2)}, u32[]{:S(2)}) collective-permute-start(bf16[4,512,128]{2,1,0:T(8,128)(2,1)} %get-tuple-element.42), channel_id=1, source_target_pairs={{0,6},{1,7},{2,0},{3,1},{4,2},{5,3},{6,4},{7,5},{8,10},{9,11},{10,... | collective-permute-start | bytes 1572872 | tf_op jit(solution)/shard_map/ppermute | solution.py:583
  12.1 32.7 %collective-permute-start.8 = (bf16[4,512,128]{2,1,0:T(8,128)(2,1)}, bf16[4,512,128]{2,1,0:T(8,128)(2,1)S(1)}, u32[]{:S(2)}, u32[]{:S(2)}) collective-permute-start(bf16[4,512,128]{2,1,0:T(8,128)(2,1)} %collective-permute-done.6.refs_9_.refs_12_), channel_id=1, source_target_pairs={{0,16},{1,17},{2,18},{3,19},{4,20},{5,21},{6,22},{7,23},{8,9},{9,8... | collective-permute-start | bytes 1572872 | tf_op jit(solution)/shard_map/ppermute | solution.py:583
  17.1 1.0 copy-start.1
  18.1 0.7 copy-start.12
  18.8 26.0 %all-to-all-start = ((bf16[8,16,1024]{2,1,0:T(8,128)(2,1)}), bf16[8,16,1024]{2,1,0:T(8,128)(2,1)S(1)}, u32[]{:S(2)}, u32[]{:S(2)}) async-start(bf16[8,16,1024]{2,1,0:T(8,128)(2,1)} %copy-done.12), calls=%async_computation | async-start | bytes 524288 | tf_op jit(solution)/shard_map/all_to_all | solution.py:591
  24.6 24.6 %collective-permute-start.3 = (bf16[512,1024]{1,0:T(8,128)(2,1)}, bf16[512,1024]{1,0:T(8,128)(2,1)}, u32[]{:S(2)}, u32[]{:S(2)}) collective-permute-start(bf16[512,1024]{1,0:T(8,128)(2,1)} %copy-done.1), channel_id=1, source_target_pairs={{0,8},{1,9},{2,10},{3,11},{4,12},{5,13},{6,14},{7,15},{8,0},{9,1},... | collective-permute-start | bytes 3145736 | tf_op jit(solution)/shard_map/ppermute | solution.py:583
  24.6 21.8 %collective-permute-start.10 = (bf16[4,512,128]{2,1,0:T(8,128)(2,1)}, bf16[4,512,128]{2,1,0:T(8,128)(2,1)}, u32[]{:S(2)}, u32[]{:S(2)}) collective-permute-start(bf16[4,512,128]{2,1,0:T(8,128)(2,1)} %collective-permute-done.6.refs_9_.refs_12_), channel_id=1, source_target_pairs={{8,10},{9,11},{10,12},{11,13},{12,14},{13,15},{14,8},{15,9},{24,26... | collective-permute-start | bytes 1572872 | tf_op jit(solution)/shard_map/ppermute | solution.py:583
  26.0 21.1 %collective-permute-start.11 = (bf16[4,512,128]{2,1,0:T(8,128)(2,1)S(1)}, bf16[4,512,128]{2,1,0:T(8,128)(2,1)}, u32[]{:S(2)}, u32[]{:S(2)}) collective-permute-start(bf16[4,512,128]{2,1,0:T(8,128)(2,1)S(1)} %collective-permute-done.7.refs_11_.refs_8_), channel_id=1, source_target_pairs={{0,1},{1,0},{2,3},{3,2},{4,5},{5,4},{6,7},{7,6},{8,10},{9,11},{10,... | collective-permute-start | bytes 1572872 | tf_op jit(solution)/shard_map/ppermute | solution.py:583
  28.0 2.9 %collective-permute-start = (s32[1]{0:T(128)}, s32[1]{0:T(128)}, u32[]{:S(2)}, u32[]{:S(2)}) collective-permute-start(s32[1]{0:T(128)} %param.10), channel_id=1, source_target_pairs={{0,8},{1,9},{2,10},{3,11},{4,12},{5,13},{6,14},{7,15},{8,0},{9,1},... | collective-permute-start | bytes 20 | tf_op jit(solution)/shard_map/ppermute | solution.py:583
  30.9 6.5 %copy-start.23 = (s32[1,1,128,1]{2,3,1,0:T(1,128)S(1)}, s32[1,1,128,1]{2,3,1,0:T(1,128)}, u32[]{:S(2)}) copy-start(s32[1,1,128,1]{2,3,1,0:T(1,128)} %param.16) | copy-start | bytes 1540
  30.9 6.5 %collective-permute-start.2 = (bf16[16,1024]{1,0:T(8,128)(2,1)S(1)}, bf16[16,1024]{1,0:T(8,128)(2,1)}, u32[]{:S(2)}, u32[]{:S(2)}) collective-permute-start(bf16[16,1024]{1,0:T(8,128)(2,1)S(1)} %get-tuple-element.24), channel_id=1, source_target_pairs={{1,0},{2,1},{3,2},{4,3},{5,4},{6,5},{7,6},{9,8},{10,9},{11,10},{12... | collective-permute-start | bytes 98312 | tf_op jit(solution)/shard_map/ppermute | solution.py:26
  37.4 5.2 %collective-permute-start.4 = (bf16[16,1024]{1,0:T(8,128)(2,1)}, bf16[16,1024]{1,0:T(8,128)(2,1)}, u32[]{:S(2)}, u32[]{:S(2)}) collective-permute-start(bf16[16,1024]{1,0:T(8,128)(2,1)} %collective-permute-done.2.refs_3_), channel_id=1, source_target_pairs={{0,8},{1,9},{2,10},{3,11},{4,12},{5,13},{6,14},{7,15},{8,0},{9,1},... | collective-permute-start | bytes 98312 | tf_op jit(solution)/shard_map/ppermute | solution.py:583
  38.8 0.8 copy-start.11
  40.6 0.8 copy-start.9
  42.6 2.2 %collective-permute-start.1 = (bf16[128,512]{1,0:T(8,128)(2,1)S(1)}, bf16[128,512]{1,0:T(8,128)(2,1)}, u32[]{:S(2)}, u32[]{:S(2)}) collective-permute-start(bf16[128,512]{1,0:T(8,128)(2,1)S(1)} %get-tuple-element.22.refs_0_), channel_id=1, source_target_pairs={{0,8},{1,9},{2,10},{3,11},{4,12},{5,13},{6,14},{7,15},{8,0},{9,1},... | collective-permute-start | bytes 393224 | tf_op jit(solution)/shard_map/ppermute | solution.py:583
  44.7 14.5 %copy-start.2 = (bf16[512,1024]{1,0:T(8,128)(2,1)S(1)}, bf16[512,1024]{1,0:T(8,128)(2,1)}, u32[]{:S(2)}) copy-start(bf16[512,1024]{1,0:T(8,128)(2,1)} %copy-done.1) | copy-start | bytes 3145732
  44.7 2.9 %collective-permute-start.5 = (bf16[128,1024]{1,0:T(8,128)(2,1)S(1)}, bf16[128,1024]{1,0:T(8,128)(2,1)S(1)}, u32[]{:S(2)}, u32[]{:S(2)}) collective-permute-start(bf16[128,1024]{1,0:T(8,128)(2,1)S(1)} %bitcast.31), channel_id=1, source_target_pairs={{0,8},{1,9},{2,10},{3,11},{4,12},{5,13},{6,14},{7,15},{8,0},{9,1},... | collective-permute-start | bytes 786440 | tf_op jit(solution)/shard_map/ppermute | solution.py:583
  44.8 14.4 %collective-permute-start.9 = (bf16[4,512,128]{2,1,0:T(8,128)(2,1)S(1)}, bf16[4,512,128]{2,1,0:T(8,128)(2,1)S(1)}, u32[]{:S(2)}, u32[]{:S(2)}) collective-permute-start(bf16[4,512,128]{2,1,0:T(8,128)(2,1)S(1)} %broadcast_select_fusion), channel_id=1, source_target_pairs={{0,16},{1,17},{2,18},{3,19},{4,20},{5,21},{6,22},{7,23},{8,24},{9,... | collective-permute-start | bytes 1572872 | tf_op jit(solution)/shard_map/ppermute | solution.py:583
  46.4 23.2 %collective-permute-start.12 = (bf16[4,512,128]{2,1,0:T(8,128)(2,1)}, bf16[4,512,128]{2,1,0:T(8,128)(2,1)S(1)}, u32[]{:S(2)}, u32[]{:S(2)}) collective-permute-start(bf16[4,512,128]{2,1,0:T(8,128)(2,1)} %collective-permute-done.10.refs_9_), channel_id=1, source_target_pairs={{8,9},{9,8},{10,11},{11,10},{12,13},{13,12},{14,15},{15,14},{24,25... | collective-permute-start | bytes 1572872 | tf_op jit(solution)/shard_map/ppermute | solution.py:583
  47.1 22.9 %collective-permute-start.13 = (bf16[4,512,128]{2,1,0:T(8,128)(2,1)}, bf16[4,512,128]{2,1,0:T(8,128)(2,1)S(1)}, u32[]{:S(2)}, u32[]{:S(2)}) collective-permute-start(bf16[4,512,128]{2,1,0:T(8,128)(2,1)} %collective-permute-done.11.refs_11_.refs_12_), channel_id=1, source_target_pairs={{0,16},{1,17},{2,18},{3,19},{4,20},{5,21},{6,22},{7,23},{8,9},{9,8... | collective-permute-start | bytes 1572872 | tf_op jit(solution)/shard_map/ppermute | solution.py:583
  47.7 39.7 %collective-permute-start.21 = (bf16[1024,512]{1,0:T(8,128)(2,1)}, bf16[1024,512]{1,0:T(8,128)(2,1)}, u32[]{:S(2)}, u32[]{:S(2)}) collective-permute-start(bf16[1024,512]{1,0:T(8,128)(2,1)} %refs_0_.1), channel_id=1, source_target_pairs={{0,16},{1,17},{2,18},{3,19},{4,20},{5,21},{6,22},{7,23},{8,24},{9,... | collective-permute-start | bytes 3145736 | tf_op jit(solution)/shard_map/ppermute | solution.py:583
  68.1 0.7 copy-start.13
  68.8 0.7 copy-start.25
  69.5 18.5 %copy-start.3 = (bf16[1024,256]{1,0:T(8,128)(2,1)}, bf16[1024,256]{1,0:T(8,128)(2,1)S(1)}, u32[]{:S(2)}) copy-start(bf16[1024,256]{1,0:T(8,128)(2,1)S(1)} %get-tuple-element.33.refs_4_) | copy-start | bytes 1572868
  69.5 18.5 %copy-start.10 = (f32[128,1024]{1,0:T(8,128)S(1)}, f32[128,1024]{1,0:T(8,128)}, u32[]{:S(2)}) copy-start(f32[128,1024]{1,0:T(8,128)} %copy-done.9) | copy-start | bytes 1572868
  69.5 18.5 %copy-start.18 = (f32[128,128]{1,0:T(8,128)S(1)}, f32[128,128]{1,0:T(8,128)}, u32[]{:S(2)}) copy-start(f32[128,128]{1,0:T(8,128)} %copy-done.17) | copy-start | bytes 196612
  69.5 18.5 %copy-start.20 = (bf16[256,128]{1,0:T(8,128)(2,1)S(1)}, bf16[256,128]{1,0:T(8,128)(2,1)}, u32[]{:S(2)}) copy-start(bf16[256,128]{1,0:T(8,128)(2,1)} %copy-done.19) | copy-start | bytes 196612
  69.5 18.4 %collective-permute-start.16 = (bf16[1024,256]{1,0:T(8,128)(2,1)S(1)}, bf16[1024,256]{1,0:T(8,128)(2,1)S(1)}, u32[]{:S(2)}, u32[]{:S(2)}) collective-permute-start(bf16[1024,256]{1,0:T(8,128)(2,1)S(1)} %get-tuple-element.33.refs_4_), channel_id=1, source_target_pairs={{0,8},{1,9},{2,10},{3,11},{4,12},{5,13},{6,14},{7,15},{8,0},{9,1},... | collective-permute-start | bytes 1572872 | tf_op jit(solution)/shard_map/ppermute | solution.py:583
  78.9 11.2 %copy-start.5 = (bf16[1024,256]{1,0:T(8,128)(2,1)}, bf16[1024,256]{1,0:T(8,128)(2,1)S(1)}, u32[]{:S(2)}) copy-start(bf16[1024,256]{1,0:T(8,128)(2,1)S(1)} %get-tuple-element.34.refs_5_) | copy-start | bytes 1572868
  78.9 11.2 %copy-start.15 = (bf16[512,256]{1,0:T(8,128)(2,1)}, bf16[512,256]{1,0:T(8,128)(2,1)S(1)}, u32[]{:S(2)}) copy-start(bf16[512,256]{1,0:T(8,128)(2,1)S(1)} %get-tuple-element.30.refs_1_) | copy-start | bytes 786436
  78.9 11.2 %copy-start.26 = (bf16[512,256]{1,0:T(8,128)(2,1)}, bf16[512,256]{1,0:T(8,128)(2,1)S(1)}, u32[]{:S(2)}) copy-start(bf16[512,256]{1,0:T(8,128)(2,1)S(1)} %get-tuple-element.32) | copy-start | bytes 786436
  78.9 9.0 %collective-permute-start.17 = (bf16[1024,256]{1,0:T(8,128)(2,1)S(1)}, bf16[1024,256]{1,0:T(8,128)(2,1)S(1)}, u32[]{:S(2)}, u32[]{:S(2)}) collective-permute-start(bf16[1024,256]{1,0:T(8,128)(2,1)S(1)} %get-tuple-element.34.refs_5_), channel_id=1, source_target_pairs={{0,8},{1,9},{2,10},{3,11},{4,12},{5,13},{6,14},{7,15},{8,0},{9,1},... | collective-permute-start | bytes 1572872 | tf_op jit(solution)/shard_map/ppermute | solution.py:583
  79.1 8.3 %collective-permute-start.18 = (f32[128,256]{1,0:T(8,128)S(1)}, f32[128,256]{1,0:T(8,128)S(1)}, u32[]{:S(2)}, u32[]{:S(2)}) collective-permute-start(f32[128,256]{1,0:T(8,128)S(1)} %get-tuple-element.40), channel_id=1, source_target_pairs={{0,8},{1,9},{2,10},{3,11},{4,12},{5,13},{6,14},{7,15},{8,0},{9,1},... | collective-permute-start | bytes 393224 | tf_op jit(solution)/shard_map/ppermute | solution.py:583
  79.5 8.4 %collective-permute-start.19 = (f32[128,256]{1,0:T(8,128)S(1)}, f32[128,256]{1,0:T(8,128)S(1)}, u32[]{:S(2)}, u32[]{:S(2)}) collective-permute-start(f32[128,256]{1,0:T(8,128)S(1)} %get-tuple-element.41), channel_id=1, source_target_pairs={{0,8},{1,9},{2,10},{3,11},{4,12},{5,13},{6,14},{7,15},{8,0},{9,1},... | collective-permute-start | bytes 393224 | tf_op jit(solution)/shard_map/ppermute | solution.py:583
  87.4 20.2 %collective-permute-start.20 = (bf16[1024,512]{1,0:T(8,128)(2,1)}, bf16[1024,512]{1,0:T(8,128)(2,1)}, u32[]{:S(2)}, u32[]{:S(2)}) collective-permute-start(bf16[1024,512]{1,0:T(8,128)(2,1)} %refs_0_.1), channel_id=1, source_target_pairs={{0,8},{1,9},{2,10},{3,11},{4,12},{5,13},{6,14},{7,15},{8,0},{9,1},... | collective-permute-start | bytes 3145736 | tf_op jit(solution)/shard_map/ppermute | solution.py:583
  87.4 20.2 %collective-permute-start.22 = (bf16[1024,512]{1,0:T(8,128)(2,1)}, bf16[1024,512]{1,0:T(8,128)(2,1)}, u32[]{:S(2)}, u32[]{:S(2)}) collective-permute-start(bf16[1024,512]{1,0:T(8,128)(2,1)} %collective-permute-done.21.refs_2_), channel_id=1, source_target_pairs={{0,8},{1,9},{2,10},{3,11},{4,12},{5,13},{6,14},{7,15},{8,0},{9,1},... | collective-permute-start | bytes 3145736 | tf_op jit(solution)/shard_map/ppermute | solution.py:583
  87.9 2.2 %copy-start.7 = (bf16[1024,256]{1,0:T(8,128)(2,1)}, bf16[1024,256]{1,0:T(8,128)(2,1)S(1)}, u32[]{:S(2)}) copy-start(bf16[1024,256]{1,0:T(8,128)(2,1)S(1)} %collective-permute-done.17.refs_7_) | copy-start | bytes 1572868
  88.0 14.2 %copy-start.14 = (bf16[512,256]{1,0:T(8,128)(2,1)S(1)}, bf16[512,256]{1,0:T(8,128)(2,1)}, u32[]{:S(2)}) copy-start(bf16[512,256]{1,0:T(8,128)(2,1)} %copy-done.13) | copy-start | bytes 786436
  90.2 12.0 %copy-start.4 = (bf16[1024,256]{1,0:T(8,128)(2,1)S(1)}, bf16[1024,256]{1,0:T(8,128)(2,1)}, u32[]{:S(2)}) copy-start(bf16[1024,256]{1,0:T(8,128)(2,1)} %copy-done.3) | copy-start | bytes 1572868
  90.2 12.0 %copy-start.6 = (bf16[1024,256]{1,0:T(8,128)(2,1)S(1)}, bf16[1024,256]{1,0:T(8,128)(2,1)}, u32[]{:S(2)}) copy-start(bf16[1024,256]{1,0:T(8,128)(2,1)} %copy-done.5) | copy-start | bytes 1572868
  90.2 24.5 %all-to-all-start.1 = ((bf16[8,32,1024]{2,1,0:T(8,128)(2,1)}), bf16[8,32,1024]{2,1,0:T(8,128)(2,1)S(1)}, u32[]{:S(2)}, u32[]{:S(2)}) async-start(bf16[8,32,1024]{2,1,0:T(8,128)(2,1)} %bitcast.25), calls=%async_computation.1 | async-start | bytes 1048576 | tf_op jit(solution)/shard_map/all_to_all | solution.py:591
  100.0 1.7 %collective-permute-start.14 = (bf16[512,256]{1,0:T(8,128)(2,1)}, bf16[512,256]{1,0:T(8,128)(2,1)S(1)}, u32[]{:S(2)}, u32[]{:S(2)}) collective-permute-start(bf16[512,256]{1,0:T(8,128)(2,1)} %copy-done.25), channel_id=1, source_target_pairs={{0,8},{1,9},{2,10},{3,11},{4,12},{5,13},{6,14},{7,15},{8,0},{9,1},... | collective-permute-start | bytes 786440 | tf_op jit(solution)/shard_map/ppermute | solution.py:583
  100.1 2.1 %collective-permute-start.15 = (bf16[512,256]{1,0:T(8,128)(2,1)}, bf16[512,256]{1,0:T(8,128)(2,1)S(1)}, u32[]{:S(2)}, u32[]{:S(2)}) collective-permute-start(bf16[512,256]{1,0:T(8,128)(2,1)} %copy-done.26), channel_id=1, source_target_pairs={{0,8},{1,9},{2,10},{3,11},{4,12},{5,13},{6,14},{7,15},{8,0},{9,1},... | collective-permute-start | bytes 786440 | tf_op jit(solution)/shard_map/ppermute | solution.py:583
  102.2 1.0 copy-start.8
  103.2 0.9 copy-start.16
  (5 other events, 3.3 us)

commit v4 on v3

--- a/solution.py
+++ b/solution.py
@@ -17,6 +17,7 @@
 EPS_MEMORY = 1e-06
 NEG_BIG = -1e30
 LANES = 128
+RING = 4
 LOG2_E = 1.4426950408889634
 
 
@@ -264,7 +265,7 @@
         out_shape=out_shapes,
         in_specs=[smem_spec()] * len(scalars)
         + [vmem_spec()] * whole
-        + [pl.BlockSpec(memory_space=pl.ANY)] * in_place,
+        + [pl.BlockSpec(memory_space=pltpu.HBM if out_in_place else pl.ANY)] * in_place,
         out_specs=jax.tree.map(
             lambda _: pl.BlockSpec(memory_space=pl.ANY) if out_in_place else vmem_spec(), out_shapes
         ),
@@ -420,14 +421,16 @@
         live_spans = (length + span_len - 1) // span_len
         span_limit = jnp.minimum(first_frame // span_len + 2 * b + lane_spans, live_spans)
         memory = jnp.where(memory_rows < span_limit, raw[near:], NEG_BIG)
-        scores[i, 0:near, :] = local
-        scores[i, near:, :] = memory
-        peaks[i] = jnp.maximum(
+        slot = i % scores.shape[0]
+        scores[slot, 0:near, :] = local
+        scores[slot, near:, :] = memory
+        peaks[slot] = jnp.maximum(
             jnp.max(local, axis=0, keepdims=True), jnp.max(memory, axis=0, keepdims=True)
         )
 
     def weigh_block(i):
-        weights[i] = jnp.exp2(scores[i] - peaks[i]).astype(jnp.bfloat16)
+        slot = i % scores.shape[0]
+        weights[slot] = jnp.exp2(scores[slot] - peaks[slot]).astype(jnp.bfloat16)
 
     ones = jnp.ones((near + memory_count, LANES), jnp.bfloat16)
     first_of_pair = lax.broadcasted_iota(jnp.int32, (1, 2 * LANES), 1) % LANES < head_size
@@ -442,7 +445,7 @@
             columns = slice(pair * LANES, (pair + 1) * LANES)
             pair_rows = slice(pair * 2 * block, (pair + 1) * 2 * block)
             sums = lax.dot_general(
-                weights[i, :, pair_rows],
+                weights[i % weights.shape[0], :, pair_rows],
                 jnp.concatenate([values[:, columns], ones], axis=1),
                 (((0,), (0,)), ((), ())),
                 preferred_element_type=jnp.float32,
@@ -686,20 +689,19 @@
     m3 = relocate(m1, along_y, along_x)
     m4 = relocate(m1, None, z_up)
     m5 = relocate(m2, along_x, z_up)
-    m6 = relocate(pick(m2, m3), along_y, along_y)
-    m7 = relocate(m4, None, along_x)
+    m6 = relocate(m3, None, along_y)
+    m7 = relocate(pick(m2, m4), along_y, along_x)
     m8 = relocate(m5, along_y, along_x)
 
     slot_pieces = (
         ((own_a, m1), (own_b, m2), (m1, m3), (m3, m6)),
-        ((m2, m4), (m6, m5), (m5, m7), (m8, m8)),
+        ((m2, m4), (m7, m5), (m5, m7), (m8, m8)),
     )
     block = 2 * C
     width = 2 * shard
     row_count = frame_count + pad + memories.shape[0]
     keys_seen = block + pad + memories.shape[0]
     lanes = width // head_size * block
-    block_count = 2 * (frame_count // block)
     attended, sums, outs = [], [], []
     for pieces in slot_pieces:
         flat = [p for pair in pieces for p in pair]
@@ -722,12 +724,12 @@
                 pltpu.VMEM((2 * row_count, width), bf16),
                 pltpu.VMEM((2 * row_count, width), bf16),
                 pltpu.VMEM((block + pad, lanes), jnp.float32),
-                pltpu.VMEM((block_count, keys_seen, lanes), jnp.float32),
-                pltpu.VMEM((block_count, 1, lanes), jnp.float32),
-                pltpu.VMEM((block_count, keys_seen, lanes), bf16),
+                pltpu.VMEM((RING, keys_seen, lanes), jnp.float32),
+                pltpu.VMEM((RING, 1, lanes), jnp.float32),
+                pltpu.VMEM((RING, keys_seen, lanes), bf16),
                 pltpu.SemaphoreType.DMA((22,)),
             ),
-            vmem_mib=32,
+            vmem_mib=20,
             flops=12 * frame_count * model_width * width,
             moved=8 * frame_count * model_width,
         )

time: 120 us -> 118 us (0.983)
  waiting for transfers between devices: 36.2 us -> 27.5 us
  starting transfers between devices: 37.8 us -> 45.8 us
    ppermute x22, starting transfers between devices: 20.7 us -> 32.8 us  [relocate(): return lax.ppermute(value, ('rec', 'tm'), pairs)]
    ppermute x22, waiting for transfers between devices: 22.4 us -> 12.8 us  [relocate(): return lax.ppermute(value, ('rec', 'tm'), pairs)]
    all_to_all x2, starting transfers between devices: 15.7 us -> 11.6 us  [exchange_blocks(): return lax.all_to_all(blocks, 'tm', split_axis=0, concat_axis=0, tiled=True)]
    ppermute x1, waiting for transfers between devices: 5.07 us -> 7.66 us  [shifted(): return lax.ppermute(block, axis, route)]
    all_to_all x2, waiting for transfers between devices: 8.74 us -> 7.12 us  [exchange_blocks(): return lax.all_to_all(blocks, 'tm', split_axis=0, concat_axis=0, tiled=True)]
  transfers between devices with their start and end apart: 25 -> 25, of which waited for: 10 -> 8; matrix products, arithmetic and copies ran while one was open for 2% -> 2% of each run, Pallas kernels for 22% -> 22%
where the time goes in v4:
time: 118 us; the launch traced here: 117 us
  starting transfers between devices  45.8 us (39%)
  Pallas kernels  30.1 us (26%)
  waiting for transfers between devices  27.5 us (23%)
  local copies, waits for them, and re-layouts  9.19 us (8%)
  other arithmetic  2.32 us (2%)
  between operations  1.78 us (2%)
    ppermute x22, starting transfers between devices, relocate(): return lax.ppermute(value, ('rec', 'tm'), pairs)  32.8 us
    pallas_call x7, Pallas kernels, local_call(): pl.pallas_call(kernel, out_shape=out_shapes, in_specs=[smem_spec()] * len...  30.1 us
    ppermute x22, waiting for transfers between devices, relocate(): return lax.ppermute(value, ('rec', 'tm'), pairs)  12.8 us
    all_to_all x2, starting transfers between devices, exchange_blocks(): return lax.all_to_all(blocks, 'tm', split_axis=0, concat_axis=0, tiled=True)  11.6 us
    unnamed x56, local copies, waits for them, and re-layouts  8.36 us
    ppermute x1, waiting for transfers between devices, shifted(): return lax.ppermute(block, axis, route)  7.66 us
    all_to_all x2, waiting for transfers between devices, exchange_blocks(): return lax.all_to_all(blocks, 'tm', split_axis=0, concat_axis=0, tiled=True)  7.12 us
  transfers between devices with their start and end apart: 25, of which 8 were waited for; matrix products, arithmetic and copies ran while one was open for 2% of the time, Pallas kernels for 22%

profile of v4, /device:TPU:0, one launch (start us, length us, event | category | flops | bytes accessed | tf_op | source)
XLA Modules:
  0.0 116.7 jit_solution(12941875723051078692)
XLA Ops:
  0.7 1.2 fusion.1.refs_8_
  1.8 3.0 %collective-permute-start.6 = (bf16[4,512,128]{2,1,0:T(8,128)(2,1)S(1)}, bf16[4,512,128]{2,1,0:T(8,128)(2,1)}, u32[]{:S(2)}, u32[]{:S(2)}) collective-permute-start(bf16[4,512,128]{2,1,0:T(8,128)(2,1)S(1)} %fusion.1.refs_8_), channel_id=1, source_target_pairs={{0,1},{1,0},{2,3},{3,2},{4,5},{5,4},{6,7},{7,6},{8,10},{9,11},{10,... | collective-permute-start | bytes 1572872 | tf_op jit(solution)/shard_map/ppermute | solution.py:586
  4.9 1.1 broadcast_select_fusion.1
  6.0 3.6 %collective-permute-start.7 = (bf16[4,512,128]{2,1,0:T(8,128)(2,1)}, bf16[4,512,128]{2,1,0:T(8,128)(2,1)S(1)}, u32[]{:S(2)}, u32[]{:S(2)}) collective-permute-start(bf16[4,512,128]{2,1,0:T(8,128)(2,1)} %get-tuple-element.42), channel_id=1, source_target_pairs={{0,6},{1,7},{2,0},{3,1},{4,2},{5,3},{6,4},{7,5},{8,10},{9,11},{10,... | collective-permute-start | bytes 1572872 | tf_op jit(solution)/shard_map/ppermute | solution.py:586
  9.6 2.6 %collective-permute-done.6.refs_9_.refs_12_ = bf16[4,512,128]{2,1,0:T(8,128)(2,1)} collective-permute-done((bf16[4,512,128]{2,1,0:T(8,128)(2,1)S(1)}, bf16[4,512,128]{2,1,0:T(8,128)(2,1)}, u32[]{:S(2)}, u32[]{:S(2)}) %collective-permute-start.6) | collective-permute-done | bytes 524320 | tf_op jit(solution)/shard_map/ppermute | solution.py:586
  12.1 2.0 %collective-permute-start.8 = (bf16[4,512,128]{2,1,0:T(8,128)(2,1)}, bf16[4,512,128]{2,1,0:T(8,128)(2,1)}, u32[]{:S(2)}, u32[]{:S(2)}) collective-permute-start(bf16[4,512,128]{2,1,0:T(8,128)(2,1)} %collective-permute-done.6.refs_9_.refs_12_), channel_id=1, source_target_pairs={{0,16},{1,17},{2,18},{3,19},{4,20},{5,21},{6,22},{7,23},{8,9},{9,8... | collective-permute-start | bytes 1572872 | tf_op jit(solution)/shard_map/ppermute | solution.py:586
  14.2 1.5 %collective-permute-start.10 = (bf16[4,512,128]{2,1,0:T(8,128)(2,1)}, bf16[4,512,128]{2,1,0:T(8,128)(2,1)}, u32[]{:S(2)}, u32[]{:S(2)}) collective-permute-start(bf16[4,512,128]{2,1,0:T(8,128)(2,1)} %collective-permute-done.6.refs_9_.refs_12_), channel_id=1, source_target_pairs={{8,10},{9,11},{10,12},{11,13},{12,14},{13,15},{14,8},{15,9},{24,26... | collective-permute-start | bytes 1572872 | tf_op jit(solution)/shard_map/ppermute | solution.py:586
  16.4 0.6 copy-done.21
  17.1 1.5 %shard_map.105 = (bf16[512,1024]{1,0:T(8,128)(2,1)S(1)}, bf16[16,1024]{1,0:T(8,128)(2,1)S(1)}, bf16[8,16,1024]{2,1,0:T(8,128)(2,1)S(1)}) custom-call(s32[17]{0:T(128)S(1)} %stack.63.scalars, bf16[512,1024]{1,0:T(8,128)(2,1)S(1)} %bitcast.28, f32[1,1024]{1,0:T(1,128)S(1)} %bitcast.35, f32[1,1024]{1,0:T(1,128)S(1)} %bitcast.36), custom_call_target="tpu_custom_call" | custom-call | flops 5242880 | bytes 2097152 | tf_op jit(solution)/shard_map/pallas_call | solution.py:263
  18.6 0.7 copy-done.11
  19.3 5.8 %all-to-all-start = ((bf16[8,16,1024]{2,1,0:T(8,128)(2,1)}), bf16[8,16,1024]{2,1,0:T(8,128)(2,1)S(1)}, u32[]{:S(2)}, u32[]{:S(2)}) async-start(bf16[8,16,1024]{2,1,0:T(8,128)(2,1)} %copy-done.11), calls=%async_computation | async-start | bytes 524288 | tf_op jit(solution)/shard_map/all_to_all | solution.py:594
  25.1 2.0 %collective-permute-start.3 = (bf16[512,1024]{1,0:T(8,128)(2,1)S(1)}, bf16[512,1024]{1,0:T(8,128)(2,1)}, u32[]{:S(2)}, u32[]{:S(2)}) collective-permute-start(bf16[512,1024]{1,0:T(8,128)(2,1)S(1)} %get-tuple-element.23.refs_2_), channel_id=1, source_target_pairs={{0,8},{1,9},{2,10},{3,11},{4,12},{5,13},{6,14},{7,15},{8,0},{9,1},... | collective-permute-start | bytes 3145736 | tf_op jit(solution)/shard_map/ppermute | solution.py:586
  27.1 1.7 %collective-permute-start.12 = (bf16[4,512,128]{2,1,0:T(8,128)(2,1)S(1)}, bf16[4,512,128]{2,1,0:T(8,128)(2,1)}, u32[]{:S(2)}, u32[]{:S(2)}) collective-permute-start(bf16[4,512,128]{2,1,0:T(8,128)(2,1)S(1)} %collective-permute-done.7.refs_11_.refs_8_), channel_id=1, source_target_pairs={{0,1},{1,0},{2,3},{3,2},{4,5},{5,4},{6,7},{7,6},{8,10},{9,11},{10,... | collective-permute-start | bytes 1572872 | tf_op jit(solution)/shard_map/ppermute | solution.py:586
  28.8 1.3 %collective-permute-done.other_length = s32[1]{0:T(128)} collective-permute-done((s32[1]{0:T(128)}, s32[1]{0:T(128)}, u32[]{:S(2)}, u32[]{:S(2)}) %collective-permute-start) | collective-permute-done | bytes 36 | tf_op jit(solution)/shard_map/ppermute | solution.py:586
  30.1 1.4 %collective-permute-start.2 = (bf16[16,1024]{1,0:T(8,128)(2,1)S(1)}, bf16[16,1024]{1,0:T(8,128)(2,1)}, u32[]{:S(2)}, u32[]{:S(2)}) collective-permute-start(bf16[16,1024]{1,0:T(8,128)(2,1)S(1)} %get-tuple-element.24), channel_id=1, source_target_pairs={{1,0},{2,1},{3,2},{4,3},{5,4},{6,5},{7,6},{9,8},{10,9},{11,10},{12... | collective-permute-start | bytes 98312 | tf_op jit(solution)/shard_map/ppermute | solution.py:27
  31.5 7.7 %collective-permute-done.2.refs_3_ = bf16[16,1024]{1,0:T(8,128)(2,1)} collective-permute-done((bf16[16,1024]{1,0:T(8,128)(2,1)S(1)}, bf16[16,1024]{1,0:T(8,128)(2,1)}, u32[]{:S(2)}, u32[]{:S(2)}) %collective-permute-start.2) | collective-permute-done | bytes 32800 | tf_op jit(solution)/shard_map/ppermute | solution.py:27
  39.2 0.7 copy.11.owners_col
  39.9 0.7 copy-done.23
  40.6 0.8 copy-done.10
  41.4 0.9 shard_map.104
  42.3 0.8 copy-done.8
  43.1 0.6 copy-done.16
  43.7 0.6 copy-done.18
  44.4 0.5 collective-permute-start.1
  45.0 0.8 collective-permute-start.9
  46.0 1.5 %collective-permute-start.11 = (bf16[4,512,128]{2,1,0:T(8,128)(2,1)S(1)}, bf16[4,512,128]{2,1,0:T(8,128)(2,1)S(1)}, u32[]{:S(2)}, u32[]{:S(2)}) collective-permute-start(bf16[4,512,128]{2,1,0:T(8,128)(2,1)S(1)} %broadcast_select_fusion), channel_id=1, source_target_pairs={{0,16},{1,17},{2,18},{3,19},{4,20},{5,21},{6,22},{7,23},{8,9},{9,8... | collective-permute-start | bytes 1572872 | tf_op jit(solution)/shard_map/ppermute | solution.py:586
  47.5 0.5 collective-permute-start.13
  48.0 1.5 %collective-permute-start.21 = (bf16[1024,512]{1,0:T(8,128)(2,1)}, bf16[1024,512]{1,0:T(8,128)(2,1)}, u32[]{:S(2)}, u32[]{:S(2)}) collective-permute-start(bf16[1024,512]{1,0:T(8,128)(2,1)} %refs_0_.1), channel_id=1, source_target_pairs={{0,16},{1,17},{2,18},{3,19},{4,20},{5,21},{6,22},{7,23},{8,24},{9,... | collective-permute-start | bytes 3145736 | tf_op jit(solution)/shard_map/ppermute | solution.py:586
  49.6 9.0 %shard_map.106 = (bf16[512,256]{1,0:T(8,128)(2,1)S(1)}, bf16[512,256]{1,0:T(8,128)(2,1)S(1)}, f32[128,256]{1,0:T(8,128)S(1)}, f32[128,256]{1,0:T(8,128)S(1)}, bf16[1024,256]{1,0:T(8,128)(2,1)S(1)}) custom-call(s32[17]{0:T(128)S(1)} %stack.63.scalars, s32[1]{0:T(128)} %collective-permute-done.other_length, bf16[128,512]{1,0:T(8,128)(2,1)S(1)} %get-tuple-element.22.refs_0_, ...), custom_call_target="tpu_custom_call" | custom-call | flops 1610612736 | bytes 4194304 | tf_op jit(solution)/shard_map/pallas_call | solution.py:263
  58.6 0.7 copy-done.12
  59.3 0.7 copy-done.24
  60.0 12.0 %collective-permute-start.16 = (bf16[1024,256]{1,0:T(8,128)(2,1)S(1)}, bf16[1024,256]{1,0:T(8,128)(2,1)S(1)}, u32[]{:S(2)}, u32[]{:S(2)}) collective-permute-start(bf16[1024,256]{1,0:T(8,128)(2,1)S(1)} %get-tuple-element.33.refs_4_), channel_id=1, source_target_pairs={{0,8},{1,9},{2,10},{3,11},{4,12},{5,13},{6,14},{7,15},{8,0},{9,1},... | collective-permute-start | bytes 1572872 | tf_op jit(solution)/shard_map/ppermute | solution.py:586
  72.0 8.9 %shard_map.107 = (bf16[512,256]{1,0:T(8,128)(2,1)S(1)}, bf16[512,256]{1,0:T(8,128)(2,1)S(1)}, f32[128,256]{1,0:T(8,128)S(1)}, f32[128,256]{1,0:T(8,128)S(1)}, bf16[1024,256]{1,0:T(8,128)(2,1)S(1)}) custom-call(s32[17]{0:T(128)S(1)} %stack.63.scalars, s32[1]{0:T(128)} %collective-permute-done.other_length, bf16[128,512]{1,0:T(8,128)(2,1)S(1)} %get-tuple-element.22.refs_0_, ...), custom_call_target="tpu_custom_call" | custom-call | flops 1610612736 | bytes 4194304 | tf_op jit(solution)/shard_map/pallas_call | solution.py:263
  80.9 0.4 collective-permute-start.17
  81.3 0.1 collective-permute-start.18
  81.4 0.4 collective-permute-start.19
  81.8 7.2 %collective-permute-done.21.refs_2_ = bf16[1024,512]{1,0:T(8,128)(2,1)} collective-permute-done((bf16[1024,512]{1,0:T(8,128)(2,1)}, bf16[1024,512]{1,0:T(8,128)(2,1)}, u32[]{:S(2)}, u32[]{:S(2)}) %collective-permute-start.21) | collective-permute-done | bytes 1048608 | tf_op jit(solution)/shard_map/ppermute | solution.py:586
  89.0 0.5 collective-permute-start.22
  89.6 2.2 %shard_map.109 = bf16[256,1024]{1,0:T(8,128)(2,1)} custom-call(s32[17]{0:T(128)S(1)} %stack.63.scalars, f32[128,1024]{1,0:T(8,128)S(1)} %copy-done.9, f32[128,128]{1,0:T(8,128)S(1)} %copy-done.17, bf16[256,128]{1,0:T(8,128)(2,1)S(1)} %copy-done.19, f32[128,256]{1,0:T(8,128)S(1)} %get-tuple-element.38.refs_0_, f32[128,256]{1,0:T(8,128)S(1)} %get-tuple-element.39.refs_1_, ...), custom_call_target="tpu_custom_call" | custom-call | flops 536870912 | bytes 3145728 | tf_op jit(solution)/shard_map/pallas_call | solution.py:263
  91.8 5.8 %all-to-all-start.1 = ((bf16[8,32,1024]{2,1,0:T(8,128)(2,1)}), bf16[8,32,1024]{2,1,0:T(8,128)(2,1)S(1)}, u32[]{:S(2)}, u32[]{:S(2)}) async-start(bf16[8,32,1024]{2,1,0:T(8,128)(2,1)} %bitcast.25), calls=%async_computation.1 | async-start | bytes 1048576 | tf_op jit(solution)/shard_map/all_to_all | solution.py:594
  97.6 0.5 collective-permute-start.15
  98.1 1.2 %collective-permute-done.14.refs_2_ = bf16[512,256]{1,0:T(8,128)(2,1)S(1)} collective-permute-done((bf16[512,256]{1,0:T(8,128)(2,1)}, bf16[512,256]{1,0:T(8,128)(2,1)S(1)}, u32[]{:S(2)}, u32[]{:S(2)}) %collective-permute-start.14) | collective-permute-done | bytes 262176 | tf_op jit(solution)/shard_map/ppermute | solution.py:586
  99.4 0.4 collective-permute-done.15.refs_3_
  99.8 1.0 copy-done.7
  100.8 0.9 copy-done.15
  101.8 3.4 %shard_map.108 = bf16[512,1024]{1,0:T(8,128)(2,1)} custom-call(s32[17]{0:T(128)S(1)} %stack.63.scalars, bf16[512,256]{1,0:T(8,128)(2,1)S(1)} %copy-done.13, bf16[512,256]{1,0:T(8,128)(2,1)S(1)} %copy-done.15, bf16[512,256]{1,0:T(8,128)(2,1)S(1)} %collective-permute-done.14.refs_2_, bf16[512,256]{1,0:T(8,128)(2,1)S(1)} %collective-permute-done.15.refs_3_, ...), custom_call_target="tpu_custom_call" | custom-call | flops 1073741824 | bytes 3145728 | tf_op jit(solution)/shard_map/pallas_call | solution.py:263
  105.2 7.1 %all-to-all-done.1 = bf16[8,32,1024]{2,1,0:T(8,128)(2,1)S(1)} async-done(((bf16[8,32,1024]{2,1,0:T(8,128)(2,1)}), bf16[8,32,1024]{2,1,0:T(8,128)(2,1)S(1)}, u32[]{:S(2)}, u32[]{:S(2)}) %all-to-all-start.1) | async-done | bytes 524320 | tf_op jit(solution)/shard_map/all_to_all | solution.py:594
  112.3 4.3 %shard_map.110 = bf16[256,2048]{1,0:T(8,128)(2,1)} custom-call(s32[17]{0:T(128)S(1)} %stack.63.scalars, bf16[256,1024]{1,0:T(8,128)(2,1)S(1)} %bitcast.34, bf16[1024,512]{1,0:T(8,128)(2,1)} %refs_0_.1, bf16[1024,512]{1,0:T(8,128)(2,1)} %collective-permute-done.20.refs_1_, bf16[1024,512]{1,0:T(8,128)(2,1)} %collective-permute-done.21.refs_2_, ...), custom_call_target="tpu_custom_call" | custom-call | flops 1073741824 | bytes 4194304 | tf_op jit(solution)/shard_map/pallas_call | solution.py:263
  (70 shorter events, 0.6 us)
Async XLA Ops:
  0.7 4.2 %copy-start.26 = (bf16[3,1024,128]{2,1,0:T(8,128)(2,1)S(1)}, bf16[3,1024,128]{2,1,0:T(8,128)(2,1)}, u32[]{:S(2)}) copy-start(bf16[3,1024,128]{2,1,0:T(8,128)(2,1)} %param.13) | copy-start | bytes 2359300
  0.7 4.2 %copy-start.27 = (bf16[1024,128]{1,0:T(8,128)(2,1)S(1)}, bf16[1024,128]{1,0:T(8,128)(2,1)}, u32[]{:S(2)}) copy-start(bf16[1024,128]{1,0:T(8,128)(2,1)} %param.14) | copy-start | bytes 786436
  1.8 10.3 %collective-permute-start.6 = (bf16[4,512,128]{2,1,0:T(8,128)(2,1)S(1)}, bf16[4,512,128]{2,1,0:T(8,128)(2,1)}, u32[]{:S(2)}, u32[]{:S(2)}) collective-permute-start(bf16[4,512,128]{2,1,0:T(8,128)(2,1)S(1)} %fusion.1.refs_8_), channel_id=1, source_target_pairs={{0,1},{1,0},{2,3},{3,2},{4,5},{5,4},{6,7},{7,6},{8,10},{9,11},{10,... | collective-permute-start | bytes 1572872 | tf_op jit(solution)/shard_map/ppermute | solution.py:586
  4.9 11.6 %copy-start = (bf16[1,512,1024]{2,1,0:T(8,128)(2,1)S(1)}, bf16[1,512,1024]{2,1,0:T(8,128)(2,1)}, u32[]{:S(2)}) copy-start(bf16[1,512,1024]{2,1,0:T(8,128)(2,1)} %param.9) | copy-start | bytes 3145732
  6.0 21.1 %collective-permute-start.7 = (bf16[4,512,128]{2,1,0:T(8,128)(2,1)}, bf16[4,512,128]{2,1,0:T(8,128)(2,1)S(1)}, u32[]{:S(2)}, u32[]{:S(2)}) collective-permute-start(bf16[4,512,128]{2,1,0:T(8,128)(2,1)} %get-tuple-element.42), channel_id=1, source_target_pairs={{0,6},{1,7},{2,0},{3,1},{4,2},{5,3},{6,4},{7,5},{8,10},{9,11},{10,... | collective-permute-start | bytes 1572872 | tf_op jit(solution)/shard_map/ppermute | solution.py:586
  12.1 32.8 %collective-permute-start.8 = (bf16[4,512,128]{2,1,0:T(8,128)(2,1)}, bf16[4,512,128]{2,1,0:T(8,128)(2,1)}, u32[]{:S(2)}, u32[]{:S(2)}) collective-permute-start(bf16[4,512,128]{2,1,0:T(8,128)(2,1)} %collective-permute-done.6.refs_9_.refs_12_), channel_id=1, source_target_pairs={{0,16},{1,17},{2,18},{3,19},{4,20},{5,21},{6,22},{7,23},{8,9},{9,8... | collective-permute-start | bytes 1572872 | tf_op jit(solution)/shard_map/ppermute | solution.py:586
  14.2 30.8 %collective-permute-start.10 = (bf16[4,512,128]{2,1,0:T(8,128)(2,1)}, bf16[4,512,128]{2,1,0:T(8,128)(2,1)}, u32[]{:S(2)}, u32[]{:S(2)}) collective-permute-start(bf16[4,512,128]{2,1,0:T(8,128)(2,1)} %collective-permute-done.6.refs_9_.refs_12_), channel_id=1, source_target_pairs={{8,10},{9,11},{10,12},{11,13},{12,14},{13,15},{14,8},{15,9},{24,26... | collective-permute-start | bytes 1572872 | tf_op jit(solution)/shard_map/ppermute | solution.py:586
  18.6 0.7 copy-start.11
  19.3 25.6 %all-to-all-start = ((bf16[8,16,1024]{2,1,0:T(8,128)(2,1)}), bf16[8,16,1024]{2,1,0:T(8,128)(2,1)S(1)}, u32[]{:S(2)}, u32[]{:S(2)}) async-start(bf16[8,16,1024]{2,1,0:T(8,128)(2,1)} %copy-done.11), calls=%async_computation | async-start | bytes 524288 | tf_op jit(solution)/shard_map/all_to_all | solution.py:594
  25.1 24.5 %collective-permute-start.3 = (bf16[512,1024]{1,0:T(8,128)(2,1)S(1)}, bf16[512,1024]{1,0:T(8,128)(2,1)}, u32[]{:S(2)}, u32[]{:S(2)}) collective-permute-start(bf16[512,1024]{1,0:T(8,128)(2,1)S(1)} %get-tuple-element.23.refs_2_), channel_id=1, source_target_pairs={{0,8},{1,9},{2,10},{3,11},{4,12},{5,13},{6,14},{7,15},{8,0},{9,1},... | collective-permute-start | bytes 3145736 | tf_op jit(solution)/shard_map/ppermute | solution.py:586
  27.1 20.5 %collective-permute-start.12 = (bf16[4,512,128]{2,1,0:T(8,128)(2,1)S(1)}, bf16[4,512,128]{2,1,0:T(8,128)(2,1)}, u32[]{:S(2)}, u32[]{:S(2)}) collective-permute-start(bf16[4,512,128]{2,1,0:T(8,128)(2,1)S(1)} %collective-permute-done.7.refs_11_.refs_8_), channel_id=1, source_target_pairs={{0,1},{1,0},{2,3},{3,2},{4,5},{5,4},{6,7},{7,6},{8,10},{9,11},{10,... | collective-permute-start | bytes 1572872 | tf_op jit(solution)/shard_map/ppermute | solution.py:586
  28.8 1.3 %collective-permute-start = (s32[1]{0:T(128)}, s32[1]{0:T(128)}, u32[]{:S(2)}, u32[]{:S(2)}) collective-permute-start(s32[1]{0:T(128)} %param.10), channel_id=1, source_target_pairs={{0,8},{1,9},{2,10},{3,11},{4,12},{5,13},{6,14},{7,15},{8,0},{9,1},... | collective-permute-start | bytes 20 | tf_op jit(solution)/shard_map/ppermute | solution.py:586
  30.1 9.1 %copy-start.22 = (s32[1,1,128,1]{2,3,1,0:T(1,128)S(1)}, s32[1,1,128,1]{2,3,1,0:T(1,128)}, u32[]{:S(2)}) copy-start(s32[1,1,128,1]{2,3,1,0:T(1,128)} %param.16) | copy-start | bytes 1540
  30.1 9.1 %collective-permute-start.2 = (bf16[16,1024]{1,0:T(8,128)(2,1)S(1)}, bf16[16,1024]{1,0:T(8,128)(2,1)}, u32[]{:S(2)}, u32[]{:S(2)}) collective-permute-start(bf16[16,1024]{1,0:T(8,128)(2,1)S(1)} %get-tuple-element.24), channel_id=1, source_target_pairs={{1,0},{2,1},{3,2},{4,3},{5,4},{6,5},{7,6},{9,8},{10,9},{11,10},{12... | collective-permute-start | bytes 98312 | tf_op jit(solution)/shard_map/ppermute | solution.py:27
  39.2 5.2 %collective-permute-start.4 = (bf16[16,1024]{1,0:T(8,128)(2,1)}, bf16[16,1024]{1,0:T(8,128)(2,1)}, u32[]{:S(2)}, u32[]{:S(2)}) collective-permute-start(bf16[16,1024]{1,0:T(8,128)(2,1)} %collective-permute-done.2.refs_3_), channel_id=1, source_target_pairs={{0,8},{1,9},{2,10},{3,11},{4,12},{5,13},{6,14},{7,15},{8,0},{9,1},... | collective-permute-start | bytes 98312 | tf_op jit(solution)/shard_map/ppermute | solution.py:586
  40.6 0.8 copy-start.10
  42.3 0.8 copy-start.8
  44.4 1.6 %collective-permute-start.1 = (bf16[128,512]{1,0:T(8,128)(2,1)S(1)}, bf16[128,512]{1,0:T(8,128)(2,1)}, u32[]{:S(2)}, u32[]{:S(2)}) collective-permute-start(bf16[128,512]{1,0:T(8,128)(2,1)S(1)} %get-tuple-element.22.refs_0_), channel_id=1, source_target_pairs={{0,8},{1,9},{2,10},{3,11},{4,12},{5,13},{6,14},{7,15},{8,0},{9,1},... | collective-permute-start | bytes 393224 | tf_op jit(solution)/shard_map/ppermute | solution.py:586
  44.9 4.7 %copy-start.1 = (bf16[4,512,128]{2,1,0:T(8,128)(2,1)S(1)}, bf16[4,512,128]{2,1,0:T(8,128)(2,1)}, u32[]{:S(2)}) copy-start(bf16[4,512,128]{2,1,0:T(8,128)(2,1)} %get-tuple-element.43.refs_10_) | copy-start | bytes 1572868
  44.9 3.1 %collective-permute-start.5 = (bf16[128,1024]{1,0:T(8,128)(2,1)S(1)}, bf16[128,1024]{1,0:T(8,128)(2,1)S(1)}, u32[]{:S(2)}, u32[]{:S(2)}) collective-permute-start(bf16[128,1024]{1,0:T(8,128)(2,1)S(1)} %bitcast.31), channel_id=1, source_target_pairs={{0,8},{1,9},{2,10},{3,11},{4,12},{5,13},{6,14},{7,15},{8,0},{9,1},... | collective-permute-start | bytes 786440 | tf_op jit(solution)/shard_map/ppermute | solution.py:586
  45.0 4.6 %collective-permute-start.9 = (bf16[4,512,128]{2,1,0:T(8,128)(2,1)}, bf16[4,512,128]{2,1,0:T(8,128)(2,1)S(1)}, u32[]{:S(2)}, u32[]{:S(2)}) collective-permute-start(bf16[4,512,128]{2,1,0:T(8,128)(2,1)} %collective-permute-done.8.refs_13_.refs_14_), channel_id=1, source_target_pairs={{8,24},{9,25},{10,26},{11,27},{12,28},{13,29},{14,30},{15,31},{24,... | collective-permute-start | bytes 1572872 | tf_op jit(solution)/shard_map/ppermute | solution.py:586
  46.0 26.0 %collective-permute-start.11 = (bf16[4,512,128]{2,1,0:T(8,128)(2,1)S(1)}, bf16[4,512,128]{2,1,0:T(8,128)(2,1)S(1)}, u32[]{:S(2)}, u32[]{:S(2)}) collective-permute-start(bf16[4,512,128]{2,1,0:T(8,128)(2,1)S(1)} %broadcast_select_fusion), channel_id=1, source_target_pairs={{0,16},{1,17},{2,18},{3,19},{4,20},{5,21},{6,22},{7,23},{8,9},{9,8... | collective-permute-start | bytes 1572872 | tf_op jit(solution)/shard_map/ppermute | solution.py:586
  47.5 24.4 %collective-permute-start.13 = (bf16[4,512,128]{2,1,0:T(8,128)(2,1)}, bf16[4,512,128]{2,1,0:T(8,128)(2,1)S(1)}, u32[]{:S(2)}, u32[]{:S(2)}) collective-permute-start(bf16[4,512,128]{2,1,0:T(8,128)(2,1)} %collective-permute-done.12.refs_11_.refs_12_), channel_id=1, source_target_pairs={{0,16},{1,17},{2,18},{3,19},{4,20},{5,21},{6,22},{7,23},{8,9},{9,8... | collective-permute-start | bytes 1572872 | tf_op jit(solution)/shard_map/ppermute | solution.py:586
  48.0 41.0 %collective-permute-start.21 = (bf16[1024,512]{1,0:T(8,128)(2,1)}, bf16[1024,512]{1,0:T(8,128)(2,1)}, u32[]{:S(2)}, u32[]{:S(2)}) collective-permute-start(bf16[1024,512]{1,0:T(8,128)(2,1)} %refs_0_.1), channel_id=1, source_target_pairs={{0,16},{1,17},{2,18},{3,19},{4,20},{5,21},{6,22},{7,23},{8,24},{9,... | collective-permute-start | bytes 3145736 | tf_op jit(solution)/shard_map/ppermute | solution.py:586
  58.6 0.7 copy-start.12
  59.3 0.7 copy-start.24
  60.0 29.6 %copy-start.2 = (bf16[1024,256]{1,0:T(8,128)(2,1)}, bf16[1024,256]{1,0:T(8,128)(2,1)S(1)}, u32[]{:S(2)}) copy-start(bf16[1024,256]{1,0:T(8,128)(2,1)S(1)} %get-tuple-element.33.refs_4_) | copy-start | bytes 1572868
  60.0 29.6 %copy-start.9 = (f32[128,1024]{1,0:T(8,128)S(1)}, f32[128,1024]{1,0:T(8,128)}, u32[]{:S(2)}) copy-start(f32[128,1024]{1,0:T(8,128)} %copy-done.8) | copy-start | bytes 1572868
  60.0 29.6 %copy-start.17 = (f32[128,128]{1,0:T(8,128)S(1)}, f32[128,128]{1,0:T(8,128)}, u32[]{:S(2)}) copy-start(f32[128,128]{1,0:T(8,128)} %copy-done.16) | copy-start | bytes 196612
  60.0 29.6 %copy-start.19 = (bf16[256,128]{1,0:T(8,128)(2,1)S(1)}, bf16[256,128]{1,0:T(8,128)(2,1)}, u32[]{:S(2)}) copy-start(bf16[256,128]{1,0:T(8,128)(2,1)} %copy-done.18) | copy-start | bytes 196612
  60.0 29.6 %collective-permute-start.16 = (bf16[1024,256]{1,0:T(8,128)(2,1)S(1)}, bf16[1024,256]{1,0:T(8,128)(2,1)S(1)}, u32[]{:S(2)}, u32[]{:S(2)}) collective-permute-start(bf16[1024,256]{1,0:T(8,128)(2,1)S(1)} %get-tuple-element.33.refs_4_), channel_id=1, source_target_pairs={{0,8},{1,9},{2,10},{3,11},{4,12},{5,13},{6,14},{7,15},{8,0},{9,1},... | collective-permute-start | bytes 1572872 | tf_op jit(solution)/shard_map/ppermute | solution.py:586
  80.8 10.9 %copy-start.6 = (bf16[1024,256]{1,0:T(8,128)(2,1)}, bf16[1024,256]{1,0:T(8,128)(2,1)S(1)}, u32[]{:S(2)}) copy-start(bf16[1024,256]{1,0:T(8,128)(2,1)S(1)} %get-tuple-element.34.refs_5_) | copy-start | bytes 1572868
  80.8 10.9 %copy-start.14 = (bf16[512,256]{1,0:T(8,128)(2,1)}, bf16[512,256]{1,0:T(8,128)(2,1)S(1)}, u32[]{:S(2)}) copy-start(bf16[512,256]{1,0:T(8,128)(2,1)S(1)} %get-tuple-element.30.refs_1_) | copy-start | bytes 786436
  80.9 10.9 %copy-start.25 = (bf16[512,256]{1,0:T(8,128)(2,1)}, bf16[512,256]{1,0:T(8,128)(2,1)S(1)}, u32[]{:S(2)}) copy-start(bf16[512,256]{1,0:T(8,128)(2,1)S(1)} %get-tuple-element.32) | copy-start | bytes 786436
  80.9 8.7 %collective-permute-start.17 = (bf16[1024,256]{1,0:T(8,128)(2,1)S(1)}, bf16[1024,256]{1,0:T(8,128)(2,1)S(1)}, u32[]{:S(2)}, u32[]{:S(2)}) collective-permute-start(bf16[1024,256]{1,0:T(8,128)(2,1)S(1)} %get-tuple-element.34.refs_5_), channel_id=1, source_target_pairs={{0,8},{1,9},{2,10},{3,11},{4,12},{5,13},{6,14},{7,15},{8,0},{9,1},... | collective-permute-start | bytes 1572872 | tf_op jit(solution)/shard_map/ppermute | solution.py:586
  81.3 7.7 %collective-permute-start.18 = (f32[128,256]{1,0:T(8,128)S(1)}, f32[128,256]{1,0:T(8,128)S(1)}, u32[]{:S(2)}, u32[]{:S(2)}) collective-permute-start(f32[128,256]{1,0:T(8,128)S(1)} %get-tuple-element.40), channel_id=1, source_target_pairs={{0,8},{1,9},{2,10},{3,11},{4,12},{5,13},{6,14},{7,15},{8,0},{9,1},... | collective-permute-start | bytes 393224 | tf_op jit(solution)/shard_map/ppermute | solution.py:586
  81.4 8.1 %collective-permute-start.19 = (f32[128,256]{1,0:T(8,128)S(1)}, f32[128,256]{1,0:T(8,128)S(1)}, u32[]{:S(2)}, u32[]{:S(2)}) collective-permute-start(f32[128,256]{1,0:T(8,128)S(1)} %get-tuple-element.41), channel_id=1, source_target_pairs={{0,8},{1,9},{2,10},{3,11},{4,12},{5,13},{6,14},{7,15},{8,0},{9,1},... | collective-permute-start | bytes 393224 | tf_op jit(solution)/shard_map/ppermute | solution.py:586
  89.0 16.2 %collective-permute-start.20 = (bf16[1024,512]{1,0:T(8,128)(2,1)}, bf16[1024,512]{1,0:T(8,128)(2,1)}, u32[]{:S(2)}, u32[]{:S(2)}) collective-permute-start(bf16[1024,512]{1,0:T(8,128)(2,1)} %refs_0_.1), channel_id=1, source_target_pairs={{0,8},{1,9},{2,10},{3,11},{4,12},{5,13},{6,14},{7,15},{8,0},{9,1},... | collective-permute-start | bytes 3145736 | tf_op jit(solution)/shard_map/ppermute | solution.py:586
  89.0 16.2 %collective-permute-start.22 = (bf16[1024,512]{1,0:T(8,128)(2,1)}, bf16[1024,512]{1,0:T(8,128)(2,1)}, u32[]{:S(2)}, u32[]{:S(2)}) collective-permute-start(bf16[1024,512]{1,0:T(8,128)(2,1)} %collective-permute-done.21.refs_2_), channel_id=1, source_target_pairs={{0,8},{1,9},{2,10},{3,11},{4,12},{5,13},{6,14},{7,15},{8,0},{9,1},... | collective-permute-start | bytes 3145736 | tf_op jit(solution)/shard_map/ppermute | solution.py:586
  89.5 2.2 %copy-start.4 = (bf16[1024,256]{1,0:T(8,128)(2,1)}, bf16[1024,256]{1,0:T(8,128)(2,1)S(1)}, u32[]{:S(2)}) copy-start(bf16[1024,256]{1,0:T(8,128)(2,1)S(1)} %collective-permute-done.16.refs_6_) | copy-start | bytes 1572868
  89.6 10.2 %copy-start.13 = (bf16[512,256]{1,0:T(8,128)(2,1)S(1)}, bf16[512,256]{1,0:T(8,128)(2,1)}, u32[]{:S(2)}) copy-start(bf16[512,256]{1,0:T(8,128)(2,1)} %copy-done.12) | copy-start | bytes 786436
  91.8 8.0 %copy-start.3 = (bf16[1024,256]{1,0:T(8,128)(2,1)S(1)}, bf16[1024,256]{1,0:T(8,128)(2,1)}, u32[]{:S(2)}) copy-start(bf16[1024,256]{1,0:T(8,128)(2,1)} %copy-done.2) | copy-start | bytes 1572868
  91.8 8.0 %copy-start.5 = (bf16[1024,256]{1,0:T(8,128)(2,1)S(1)}, bf16[1024,256]{1,0:T(8,128)(2,1)}, u32[]{:S(2)}) copy-start(bf16[1024,256]{1,0:T(8,128)(2,1)} %copy-done.4) | copy-start | bytes 1572868
  91.8 20.5 %all-to-all-start.1 = ((bf16[8,32,1024]{2,1,0:T(8,128)(2,1)}), bf16[8,32,1024]{2,1,0:T(8,128)(2,1)S(1)}, u32[]{:S(2)}, u32[]{:S(2)}) async-start(bf16[8,32,1024]{2,1,0:T(8,128)(2,1)} %bitcast.25), calls=%async_computation.1 | async-start | bytes 1048576 | tf_op jit(solution)/shard_map/all_to_all | solution.py:594
  97.6 1.7 %collective-permute-start.14 = (bf16[512,256]{1,0:T(8,128)(2,1)}, bf16[512,256]{1,0:T(8,128)(2,1)S(1)}, u32[]{:S(2)}, u32[]{:S(2)}) collective-permute-start(bf16[512,256]{1,0:T(8,128)(2,1)} %copy-done.24), channel_id=1, source_target_pairs={{0,8},{1,9},{2,10},{3,11},{4,12},{5,13},{6,14},{7,15},{8,0},{9,1},... | collective-permute-start | bytes 786440 | tf_op jit(solution)/shard_map/ppermute | solution.py:586
  97.6 2.1 %collective-permute-start.15 = (bf16[512,256]{1,0:T(8,128)(2,1)}, bf16[512,256]{1,0:T(8,128)(2,1)S(1)}, u32[]{:S(2)}, u32[]{:S(2)}) collective-permute-start(bf16[512,256]{1,0:T(8,128)(2,1)} %copy-done.25), channel_id=1, source_target_pairs={{0,8},{1,9},{2,10},{3,11},{4,12},{5,13},{6,14},{7,15},{8,0},{9,1},... | collective-permute-start | bytes 786440 | tf_op jit(solution)/shard_map/ppermute | solution.py:586
  99.8 1.0 copy-start.7
  100.8 0.9 copy-start.15
  (5 other events, 3.3 us)

commit v5 on v4

--- a/solution.py
+++ b/solution.py
@@ -17,7 +17,7 @@
 EPS_MEMORY = 1e-06
 NEG_BIG = -1e30
 LANES = 128
-RING = 4
+RING = 16
 LOG2_E = 1.4426950408889634
 
 
@@ -260,15 +260,17 @@
 
 def local_call(kernel, out_shapes, scalars, operands, scratch=(), in_place=0, out_in_place=False, vmem_mib=16, flops=0, moved=0):
     whole = len(operands) - in_place
+    anywhere = pl.BlockSpec(memory_space=pl.ANY)
+    if isinstance(out_shapes, tuple):
+        stays = out_in_place or (False,) * len(out_shapes)
+        out_specs = tuple(anywhere if stay else vmem_spec() for stay in stays)
+    else:
+        out_specs = anywhere if out_in_place else vmem_spec()
     return pl.pallas_call(
         kernel,
         out_shape=out_shapes,
-        in_specs=[smem_spec()] * len(scalars)
-        + [vmem_spec()] * whole
-        + [pl.BlockSpec(memory_space=pltpu.HBM if out_in_place else pl.ANY)] * in_place,
-        out_specs=jax.tree.map(
-            lambda _: pl.BlockSpec(memory_space=pl.ANY) if out_in_place else vmem_spec(), out_shapes
-        ),
+        in_specs=[smem_spec()] * len(scalars) + [vmem_spec()] * whole + [anywhere] * in_place,
+        out_specs=out_specs,
         compiler_params=pltpu.CompilerParams(vmem_limit_bytes=vmem_mib << 20),
         scratch_shapes=list(scratch),
         cost_estimate=pl.CostEstimate(flops=flops, bytes_accessed=moved, transcendentals=0),
@@ -329,14 +331,17 @@
     )
 
 
-def attend_kernel(span_len, right_len, head_size, scalars, other_length, *refs):
+def attend_kernel(span_len, right_len, head_size, starts_here, scalars, other_length, *refs):
     members, sources, pieces = refs[:2], refs[2:8], refs[8:16]
-    outs, sums_out, projection = refs[16:18], refs[18:20], refs[20]
-    rows_in, weight, query, key, value, bias, scores, peaks, weights, sems = refs[21:]
+    out_refs, sums_out, projection = refs[16:18], refs[18:20], refs[20]
+    outs, rows_in, weight, query, key, value, bias, scores, peaks, weights, sems = refs[21:]
     first_frame, core, y_half = scalars[0], scalars[2], scalars[3]
     frame_count, model_width = sources[0].shape
     half = model_width // 2
-    width = outs[0].shape[1]
+    width = out_refs[0].shape[1]
+    out_copies = [
+        pltpu.make_async_copy(outs.at[rec], out_refs[rec], sems.at[22 + rec]) for rec in range(2)
+    ]
     heads = width // head_size
     block = 2 * span_len
     blocks = frame_count // block
@@ -353,14 +358,20 @@
             place = pl.ds(pl.multiple_of(places[side], half), half)
             for shard in range(2):
                 piece = pieces[4 * shard + 2 * side + of_core]
+                raw = starts_here and of_core == 0 and shard == 0
+                shard_width = pieces[-1].shape[2]
                 index = 2 * side + shard
                 for part in (3,) if projected else (0, 1, 2):
                     target = projection if projected else weight
-                    start = shard * piece.shape[2] + (0 if projected else part * width)
+                    start = shard * shard_width + (0 if projected else part * width)
+                    if raw:
+                        source = pieces[2].at[place] if projected else pieces[0].at[part, place]
+                    else:
+                        source = piece.at[part]
                     copies.append(
                         pltpu.make_async_copy(
-                            piece.at[part],
-                            target.at[place, pl.ds(start, piece.shape[2])],
+                            source,
+                            target.at[place, pl.ds(start, shard_width)],
                             sems.at[4 * part + index],
                         )
                     )
@@ -397,7 +408,7 @@
     head_masks = [(feature_head == h).astype(jnp.bfloat16) for h in range(heads)]
     scale = head_size ** (-0.5) * LOG2_E
 
-    for copy in row_copies + piece_copies(0, False):
+    for copy in row_copies + piece_copies(1, False):
         copy.wait()
     mixed = jnp.dot(rows_in[...], weight[...], preferred_element_type=jnp.float32)
     query[...] = (mixed[:, :width] * scale).astype(jnp.bfloat16)
@@ -451,23 +462,24 @@
                 preferred_element_type=jnp.float32,
             )
             picked = jnp.where(first_of_pair, sums[:block], sums[block:])
-            outs[rec][start : start + block, columns] = (
+            outs[rec, start : start + block, columns] = (
                 picked[:, :LANES] / picked[:, LANES:]
             ).astype(jnp.bfloat16)
 
     count = 2 * blocks
-    for step in range(count + 2):
-        if step >= 2:
-            mix_block(step - 2)
-        if 1 <= step <= count:
-            weigh_block(step - 1)
-        if step < count:
-            score_block(step)
+    ring = scores.shape[0]
+    for first in range(0, count, ring):
+        for stage in (score_block, weigh_block, mix_block):
+            for i in range(first, min(first + ring, count)):
+                stage(i)
+        for rec in range(2):
+            if first < (rec + 1) * blocks <= first + ring:
+                out_copies[rec].start()
     for rec in range(2):
         sums_out[rec][...] = jnp.dot(
-            members[rec][...], outs[rec][...], preferred_element_type=jnp.float32
+            members[rec][...], outs[rec], preferred_element_type=jnp.float32
         )
-    for copy in piece_copies(0, True):
+    for copy in piece_copies(1, True) + out_copies:
         copy.wait()
 
 
@@ -622,9 +634,6 @@
 
     own = jnp.concatenate([qkv_weight, out_weight[None]], axis=0)
     own_a = lax.dynamic_slice_in_dim(own, y_half * half, half, 1)
-    later_qkv, later_out, own_a = lax.optimization_barrier((qkv_weight, out_weight, own_a))
-    later = jnp.concatenate([later_qkv, later_out[None]], axis=0)
-    own_b = lax.dynamic_slice_in_dim(later, (1 - y_half) * half, half, 1)
 
     def pick(for_core_0, for_core_1):
         return jnp.where(core == 0, for_core_0, for_core_1)
@@ -648,7 +657,7 @@
     scalars = jnp.stack(numbers).astype(jnp.int32)
 
     m1 = relocate(own_a, along_x, z_up)
-    m2 = relocate(pick(own_a, own_b), z_down, z_up)
+    m2 = relocate(own_a, z_down, None)
     l1 = relocate(language_weight, along_y, along_y)
 
     pad = 2 * RC
@@ -688,14 +697,15 @@
 
     m3 = relocate(m1, along_y, along_x)
     m4 = relocate(m1, None, z_up)
-    m5 = relocate(m2, along_x, z_up)
+    m5 = relocate(pick(m2, m1), along_x, along_y)
     m6 = relocate(m3, None, along_y)
-    m7 = relocate(pick(m2, m4), along_y, along_x)
-    m8 = relocate(m5, along_y, along_x)
+    m7 = relocate(pick(m2, m5), along_y, z_up)
+    m8 = relocate(pick(m5, m4), along_y, along_x)
+    m9 = relocate(m7, None, along_x)
 
     slot_pieces = (
-        ((own_a, m1), (own_b, m2), (m1, m3), (m3, m6)),
-        ((m2, m4), (m7, m5), (m5, m7), (m8, m8)),
+        ((qkv_weight, m1), (out_weight, m5), (m1, m3), (m3, m6)),
+        ((m2, m4), (m7, m7), (m5, m8), (m8, m9)),
     )
     block = 2 * C
     width = 2 * shard
@@ -703,10 +713,10 @@
     keys_seen = block + pad + memories.shape[0]
     lanes = width // head_size * block
     attended, sums, outs = [], [], []
-    for pieces in slot_pieces:
+    for slot, pieces in enumerate(slot_pieces):
         flat = [p for pair in pieces for p in pair]
         *results, out_piece = local_call(
-            functools.partial(attend_kernel, C, RC, head_size),
+            functools.partial(attend_kernel, C, RC, head_size, slot == 0),
             (
                 shape_of(frame_count, width),
                 shape_of(frame_count, width),
@@ -717,7 +727,9 @@
             (scalars, other_length),
             (member, other_member, normed, ahead, memories, other_normed, other_ahead, other_memories, *flat),
             in_place=6 + len(flat),
+            out_in_place=(True, True, False, False, False),
             scratch=(
+                pltpu.VMEM((2, frame_count, width), bf16),
                 pltpu.VMEM((2 * row_count, model_width), bf16),
                 pltpu.VMEM((model_width, 3 * width), bf16),
                 pltpu.VMEM((2 * row_count, width), bf16),
@@ -727,9 +739,9 @@
                 pltpu.VMEM((RING, keys_seen, lanes), jnp.float32),
                 pltpu.VMEM((RING, 1, lanes), jnp.float32),
                 pltpu.VMEM((RING, keys_seen, lanes), bf16),
-                pltpu.SemaphoreType.DMA((22,)),
+                pltpu.SemaphoreType.DMA((24,)),
             ),
-            vmem_mib=20,
+            vmem_mib=24,
             flops=12 * frame_count * model_width * width,
             moved=8 * frame_count * model_width,
         )
@@ -774,6 +786,7 @@
         (received, *language_pieces),
         in_place=rec_count,
         out_in_place=True,
+        vmem_mib=63,
         scratch=(
             pltpu.VMEM((rec_count, model_width, language_shard), bf16),
             pltpu.VMEM((rec_count, slot_count, language_shard), bf16),

time: 118 us -> 113 us (0.958)
  waiting for transfers between devices: 27.5 us -> 38.5 us
  starting transfers between devices: 45.8 us -> 36.8 us
  local copies, waits for them, and re-layouts: 9.19 us -> 3.38 us
  Pallas kernels: 30.1 us -> 28.4 us
    all_to_all x2, waiting for transfers between devices: 7.12 us -> 16.8 us  [exchange_blocks(): return lax.all_to_all(blocks, 'tm', split_axis=0, concat_axis=0, tiled=True)]
    ppermute x22 -> x23, waiting for transfers between devices: 12.8 us -> 21.8 us  [relocate(): return lax.ppermute(value, ('rec', 'tm'), pairs)]
    ppermute x1, waiting for transfers between devices: 7.66 us -> 0.01 us  [shifted(): return lax.ppermute(block, axis, route)]
    ppermute x22 -> x23, starting transfers between devices: 32.8 us -> 26.1 us  [relocate(): return lax.ppermute(value, ('rec', 'tm'), pairs)]
    unnamed x56 -> x36, local copies, waits for them, and re-layouts: 8.36 us -> 3.17 us
    all_to_all x2, starting transfers between devices: 11.6 us -> 9.43 us  [exchange_blocks(): return lax.all_to_all(blocks, 'tm', split_axis=0, concat_axis=0, tiled=True)]
    pallas_call x7, Pallas kernels: 30.1 us -> 28.4 us  [local_call(): pl.pallas_call(kernel, out_shape=out_shapes, in_specs=[smem_spec()] * len...]
  transfers between devices with their start and end apart: 25 -> 26, of which waited for: 8 -> 9; matrix products, arithmetic and copies ran while one was open for 2% -> 1% of each run, Pallas kernels for 22% -> 21%
where the time goes in v5:
time: 113 us; the launch traced here: 112 us
  waiting for transfers between devices  38.5 us (34%)
  starting transfers between devices  36.8 us (33%)
  Pallas kernels  28.4 us (25%)
  local copies, waits for them, and re-layouts  3.38 us (3%)
  other arithmetic  3 us (3%)
  between operations  1.86 us (2%)
    pallas_call x7, Pallas kernels, local_call(): pl.pallas_call(kernel, out_shape=out_shapes, in_specs=[smem_spec()] * len...  28.4 us
    ppermute x23, starting transfers between devices, relocate(): return lax.ppermute(value, ('rec', 'tm'), pairs)  26.1 us
    ppermute x23, waiting for transfers between devices, relocate(): return lax.ppermute(value, ('rec', 'tm'), pairs)  21.8 us
    all_to_all x2, waiting for transfers between devices, exchange_blocks(): return lax.all_to_all(blocks, 'tm', split_axis=0, concat_axis=0, tiled=True)  16.8 us
    all_to_all x2, starting transfers between devices, exchange_blocks(): return lax.all_to_all(blocks, 'tm', split_axis=0, concat_axis=0, tiled=True)  9.43 us
    unnamed x36, local copies, waits for them, and re-layouts  3.17 us
  transfers between devices with their start and end apart: 26, of which 9 were waited for; matrix products, arithmetic and copies ran while one was open for 1% of the time, Pallas kernels for 21%

profile of v5, /device:TPU:0, one launch (start us, length us, event | category | flops | bytes accessed | tf_op | source)
XLA Modules:
  0.0 112.0 jit_solution(6543370049251280256)
XLA Ops:
  0.7 1.1 fusion
  1.8 3.0 %collective-permute-start.6 = (bf16[4,512,128]{2,1,0:T(8,128)(2,1)S(1)}, bf16[4,512,128]{2,1,0:T(8,128)(2,1)S(1)}, u32[]{:S(2)}, u32[]{:S(2)}) collective-permute-start(bf16[4,512,128]{2,1,0:T(8,128)(2,1)S(1)} %fusion), channel_id=1, source_target_pairs={{0,1},{1,0},{2,3},{3,2},{4,5},{5,4},{6,7},{7,6},{8,10},{9,11},{10,... | collective-permute-start | bytes 1572872 | tf_op jit(solution)/shard_map/ppermute | solution.py:598
  4.8 5.5 %collective-permute-start.7 = (bf16[4,512,128]{2,1,0:T(8,128)(2,1)S(1)}, bf16[4,512,128]{2,1,0:T(8,128)(2,1)S(1)}, u32[]{:S(2)}, u32[]{:S(2)}) collective-permute-start(bf16[4,512,128]{2,1,0:T(8,128)(2,1)S(1)} %fusion), channel_id=1, source_target_pairs={{0,6},{1,7},{2,0},{3,1},{4,2},{5,3},{6,4},{7,5},{16,22},{17,23},{1... | collective-permute-start | bytes 1572872 | tf_op jit(solution)/shard_map/ppermute | solution.py:598
  10.3 1.6 %collective-permute-done.6.refs_9_.refs_12_ = bf16[4,512,128]{2,1,0:T(8,128)(2,1)S(1)} collective-permute-done((bf16[4,512,128]{2,1,0:T(8,128)(2,1)S(1)}, bf16[4,512,128]{2,1,0:T(8,128)(2,1)S(1)}, u32[]{:S(2)}, u32[]{:S(2)}) %collective-permute-start.6) | collective-permute-done | bytes 524320 | tf_op jit(solution)/shard_map/ppermute | solution.py:598
  11.9 6.9 %collective-permute-done.7.refs_8_ = bf16[4,512,128]{2,1,0:T(8,128)(2,1)S(1)} collective-permute-done((bf16[4,512,128]{2,1,0:T(8,128)(2,1)S(1)}, bf16[4,512,128]{2,1,0:T(8,128)(2,1)S(1)}, u32[]{:S(2)}, u32[]{:S(2)}) %collective-permute-start.7) | collective-permute-done | bytes 524320 | tf_op jit(solution)/shard_map/ppermute | solution.py:598
  18.8 0.8 broadcast_select_fusion.2
  19.7 1.5 %collective-permute-start.8 = (bf16[4,512,128]{2,1,0:T(8,128)(2,1)}, bf16[4,512,128]{2,1,0:T(8,128)(2,1)S(1)}, u32[]{:S(2)}, u32[]{:S(2)}) collective-permute-start(bf16[4,512,128]{2,1,0:T(8,128)(2,1)} %broadcast_select_fusion.2), channel_id=1, source_target_pairs={{0,1},{1,0},{2,3},{3,2},{4,5},{5,4},{6,7},{7,6},{8,24},{9,25},{10,... | collective-permute-start | bytes 1572872 | tf_op jit(solution)/shard_map/ppermute | solution.py:598
  21.1 0.7 collective-permute-start.11
  22.6 0.1 stack.63.scalars
  22.7 0.5 copy-done.13
  23.3 0.1 copy-done.12
  23.4 2.3 %shard_map.105 = (bf16[512,1024]{1,0:T(8,128)(2,1)}, bf16[16,1024]{1,0:T(8,128)(2,1)S(1)}, bf16[8,16,1024]{2,1,0:T(8,128)(2,1)}) custom-call(s32[17]{0:T(128)S(1)} %stack.63.scalars, bf16[512,1024]{1,0:T(8,128)(2,1)S(1)} %bitcast.27, f32[1,1024]{1,0:T(1,128)S(1)} %bitcast.31, f32[1,1024]{1,0:T(1,128)S(1)} %bitcast.32), custom_call_target="tpu_custom_call" | custom-call | flops 5242880 | bytes 2097152 | tf_op jit(solution)/shard_map/pallas_call | solution.py:269
  25.7 5.1 %all-to-all-start = ((bf16[8,16,1024]{2,1,0:T(8,128)(2,1)}), bf16[8,16,1024]{2,1,0:T(8,128)(2,1)}, u32[]{:S(2)}, u32[]{:S(2)}) async-start(bf16[8,16,1024]{2,1,0:T(8,128)(2,1)} %get-tuple-element.22), calls=%async_computation | async-start | bytes 524288 | tf_op jit(solution)/shard_map/all_to_all | solution.py:606
  30.9 0.5 collective-permute-start.9
  31.4 1.1 broadcast_select_fusion
  32.5 0.8 copy-done.2
  33.3 1.5 %collective-permute-start.12 = (bf16[4,512,128]{2,1,0:T(8,128)(2,1)}, bf16[4,512,128]{2,1,0:T(8,128)(2,1)}, u32[]{:S(2)}, u32[]{:S(2)}) collective-permute-start(bf16[4,512,128]{2,1,0:T(8,128)(2,1)} %get-tuple-element.37), channel_id=1, source_target_pairs={{0,16},{1,17},{2,18},{3,19},{4,20},{5,21},{6,22},{7,23},{8,10},{9,... | collective-permute-start | bytes 1572872 | tf_op jit(solution)/shard_map/ppermute | solution.py:598
  34.8 1.3 %collective-permute-start.2 = (bf16[16,1024]{1,0:T(8,128)(2,1)S(1)}, bf16[16,1024]{1,0:T(8,128)(2,1)S(1)}, u32[]{:S(2)}, u32[]{:S(2)}) collective-permute-start(bf16[16,1024]{1,0:T(8,128)(2,1)S(1)} %get-tuple-element.21), channel_id=1, source_target_pairs={{1,0},{2,1},{3,2},{4,3},{5,4},{6,5},{7,6},{9,8},{10,9},{11,10},{12... | collective-permute-start | bytes 98312 | tf_op jit(solution)/shard_map/ppermute | solution.py:27
  36.1 0.4 collective-permute-start
  36.5 1.1 collective-permute-done.other_length
  37.6 8.4 %all-to-all-done = bf16[8,16,1024]{2,1,0:T(8,128)(2,1)} async-done(((bf16[8,16,1024]{2,1,0:T(8,128)(2,1)}), bf16[8,16,1024]{2,1,0:T(8,128)(2,1)}, u32[]{:S(2)}, u32[]{:S(2)}) %all-to-all-start) | async-done | bytes 262176 | tf_op jit(solution)/shard_map/all_to_all | solution.py:606
  46.0 0.5 collective-permute-start.4
  46.5 1.5 %collective-permute-start.10 = (bf16[4,512,128]{2,1,0:T(8,128)(2,1)}, bf16[4,512,128]{2,1,0:T(8,128)(2,1)}, u32[]{:S(2)}, u32[]{:S(2)}) collective-permute-start(bf16[4,512,128]{2,1,0:T(8,128)(2,1)} %collective-permute-done.9.refs_13_.refs_14_), channel_id=1, source_target_pairs={{8,24},{9,25},{10,26},{11,27},{12,28},{13,29},{14,30},{15,31},{24,... | collective-permute-start | bytes 1572872 | tf_op jit(solution)/shard_map/ppermute | solution.py:598
  48.0 0.1 copy.11.owners_col
  48.1 0.9 shard_map.104
  49.0 1.4 %collective-permute-start.1 = (bf16[128,512]{1,0:T(8,128)(2,1)S(1)}, bf16[128,512]{1,0:T(8,128)(2,1)S(1)}, u32[]{:S(2)}, u32[]{:S(2)}) collective-permute-start(bf16[128,512]{1,0:T(8,128)(2,1)S(1)} %get-tuple-element.19.refs_0_), channel_id=1, source_target_pairs={{0,8},{1,9},{2,10},{3,11},{4,12},{5,13},{6,14},{7,15},{8,0},{9,1},... | collective-permute-start | bytes 393224 | tf_op jit(solution)/shard_map/ppermute | solution.py:598
  50.4 1.0 collective-permute-done.1.refs_1_
  51.4 0.9 collective-permute-start.13
  52.3 0.7 collective-permute-start.14
  53.0 1.2 %collective-permute-start.22 = (bf16[1024,512]{1,0:T(8,128)(2,1)}, bf16[1024,512]{1,0:T(8,128)(2,1)}, u32[]{:S(2)}, u32[]{:S(2)}) collective-permute-start(bf16[1024,512]{1,0:T(8,128)(2,1)} %refs_0_.1), channel_id=1, source_target_pairs={{0,16},{1,17},{2,18},{3,19},{4,20},{5,21},{6,22},{7,23},{8,24},{9,... | collective-permute-start | bytes 3145736 | tf_op jit(solution)/shard_map/ppermute | solution.py:598
  54.2 7.4 %shard_map.106 = (bf16[512,256]{1,0:T(8,128)(2,1)S(1)}, bf16[512,256]{1,0:T(8,128)(2,1)S(1)}, f32[128,256]{1,0:T(8,128)S(1)}, f32[128,256]{1,0:T(8,128)S(1)}, bf16[1024,256]{1,0:T(8,128)(2,1)S(1)}) custom-call(s32[17]{0:T(128)S(1)} %stack.63.scalars, s32[1]{0:T(128)} %collective-permute-done.other_length, bf16[128,512]{1,0:T(8,128)(2,1)S(1)} %get-tuple-element.19.refs_0_, ...), custom_call_target="tpu_custom_call" | custom-call | flops 1610612736 | bytes 4194304 | tf_op jit(solution)/shard_map/pallas_call | solution.py:269
  61.6 0.7 copy-done.7
  62.3 4.4 %collective-permute-start.17 = (bf16[1024,256]{1,0:T(8,128)(2,1)S(1)}, bf16[1024,256]{1,0:T(8,128)(2,1)S(1)}, u32[]{:S(2)}, u32[]{:S(2)}) collective-permute-start(bf16[1024,256]{1,0:T(8,128)(2,1)S(1)} %get-tuple-element.27.refs_4_), channel_id=1, source_target_pairs={{0,8},{1,9},{2,10},{3,11},{4,12},{5,13},{6,14},{7,15},{8,0},{9,1},... | collective-permute-start | bytes 1572872 | tf_op jit(solution)/shard_map/ppermute | solution.py:598
  66.8 7.4 %shard_map.107 = (bf16[512,256]{1,0:T(8,128)(2,1)S(1)}, bf16[512,256]{1,0:T(8,128)(2,1)S(1)}, f32[128,256]{1,0:T(8,128)S(1)}, f32[128,256]{1,0:T(8,128)S(1)}, bf16[1024,256]{1,0:T(8,128)(2,1)S(1)}) custom-call(s32[17]{0:T(128)S(1)} %stack.63.scalars, s32[1]{0:T(128)} %collective-permute-done.other_length, bf16[128,512]{1,0:T(8,128)(2,1)S(1)} %get-tuple-element.19.refs_0_, ...), custom_call_target="tpu_custom_call" | custom-call | flops 1610612736 | bytes 4194304 | tf_op jit(solution)/shard_map/pallas_call | solution.py:269
  74.2 0.8 collective-permute-start.18
  75.0 0.1 collective-permute-start.19
  75.1 0.4 collective-permute-start.20
  75.5 9.5 %collective-permute-done.22.refs_2_ = bf16[1024,512]{1,0:T(8,128)(2,1)} collective-permute-done((bf16[1024,512]{1,0:T(8,128)(2,1)}, bf16[1024,512]{1,0:T(8,128)(2,1)}, u32[]{:S(2)}, u32[]{:S(2)}) %collective-permute-start.22) | collective-permute-done | bytes 1048608 | tf_op jit(solution)/shard_map/ppermute | solution.py:598
  85.0 0.5 collective-permute-start.23
  85.5 2.2 %shard_map.109 = bf16[256,1024]{1,0:T(8,128)(2,1)} custom-call(s32[17]{0:T(128)S(1)} %stack.63.scalars, f32[128,1024]{1,0:T(8,128)S(1)} %get-tuple-element.29.base, f32[128,128]{1,0:T(8,128)S(1)} %get-tuple-element.30.inverse, bf16[256,128]{1,0:T(8,128)(2,1)S(1)} %get-tuple-element.31.route, f32[128,256]{1,0:T(8,128)S(1)} %get-tuple-element.32.refs_0_, ...), custom_call_target="tpu_custom_call" | custom-call | flops 536870912 | bytes 3145728 | tf_op jit(solution)/shard_map/pallas_call | solution.py:269
  87.7 4.3 %all-to-all-start.1 = ((bf16[8,32,1024]{2,1,0:T(8,128)(2,1)}), bf16[8,32,1024]{2,1,0:T(8,128)(2,1)}, u32[]{:S(2)}, u32[]{:S(2)}) async-start(bf16[8,32,1024]{2,1,0:T(8,128)(2,1)} %bitcast.24), calls=%async_computation.1 | async-start | bytes 1048576 | tf_op jit(solution)/shard_map/all_to_all | solution.py:606
  92.1 0.5 collective-permute-start.16
  92.6 1.2 %collective-permute-done.15.refs_2_ = bf16[512,256]{1,0:T(8,128)(2,1)S(1)} collective-permute-done((bf16[512,256]{1,0:T(8,128)(2,1)}, bf16[512,256]{1,0:T(8,128)(2,1)S(1)}, u32[]{:S(2)}, u32[]{:S(2)}) %collective-permute-start.15) | collective-permute-done | bytes 262176 | tf_op jit(solution)/shard_map/ppermute | solution.py:598
  93.9 0.4 collective-permute-done.16.refs_3_
  94.3 0.9 copy-done.10
  95.2 3.4 %shard_map.108 = bf16[512,1024]{1,0:T(8,128)(2,1)} custom-call(s32[17]{0:T(128)S(1)} %stack.63.scalars, bf16[512,256]{1,0:T(8,128)(2,1)S(1)} %copy-done.8, bf16[512,256]{1,0:T(8,128)(2,1)S(1)} %copy-done.10, bf16[512,256]{1,0:T(8,128)(2,1)S(1)} %collective-permute-done.15.refs_2_, bf16[512,256]{1,0:T(8,128)(2,1)S(1)} %collective-permute-done.16.refs_3_, ...), custom_call_target="tpu_custom_call" | custom-call | flops 1073741824 | bytes 3145728 | tf_op jit(solution)/shard_map/pallas_call | solution.py:269
  98.6 8.4 %all-to-all-done.1 = bf16[8,32,1024]{2,1,0:T(8,128)(2,1)} async-done(((bf16[8,32,1024]{2,1,0:T(8,128)(2,1)}), bf16[8,32,1024]{2,1,0:T(8,128)(2,1)}, u32[]{:S(2)}, u32[]{:S(2)}) %all-to-all-start.1) | async-done | bytes 524320 | tf_op jit(solution)/shard_map/all_to_all | solution.py:606
  107.0 4.8 %shard_map.110 = bf16[256,2048]{1,0:T(8,128)(2,1)} custom-call(s32[17]{0:T(128)} %copy-done.11, bf16[256,1024]{1,0:T(8,128)(2,1)} %bitcast.25.received, bf16[1024,512]{1,0:T(8,128)(2,1)} %refs_0_.1, bf16[1024,512]{1,0:T(8,128)(2,1)} %collective-permute-done.21.refs_1_, bf16[1024,512]{1,0:T(8,128)(2,1)} %collective-permute-done.22.refs_2_, ...), custom_call_target="tpu_custom_call" | custom-call | flops 1073741824 | bytes 4194304 | tf_op jit(solution)/shard_map/pallas_call | solution.py:269
  (52 shorter events, 0.2 us)
Async XLA Ops:
  1.7 21.0 %copy-start = (bf16[1,512,1024]{2,1,0:T(8,128)(2,1)S(1)}, bf16[1,512,1024]{2,1,0:T(8,128)(2,1)}, u32[]{:S(2)}) copy-start(bf16[1,512,1024]{2,1,0:T(8,128)(2,1)} %param.9) | copy-start | bytes 3145732
  1.8 10.2 %collective-permute-start.6 = (bf16[4,512,128]{2,1,0:T(8,128)(2,1)S(1)}, bf16[4,512,128]{2,1,0:T(8,128)(2,1)S(1)}, u32[]{:S(2)}, u32[]{:S(2)}) collective-permute-start(bf16[4,512,128]{2,1,0:T(8,128)(2,1)S(1)} %fusion), channel_id=1, source_target_pairs={{0,1},{1,0},{2,3},{3,2},{4,5},{5,4},{6,7},{7,6},{8,10},{9,11},{10,... | collective-permute-start | bytes 1572872 | tf_op jit(solution)/shard_map/ppermute | solution.py:598
  4.8 14.0 %collective-permute-start.7 = (bf16[4,512,128]{2,1,0:T(8,128)(2,1)S(1)}, bf16[4,512,128]{2,1,0:T(8,128)(2,1)S(1)}, u32[]{:S(2)}, u32[]{:S(2)}) collective-permute-start(bf16[4,512,128]{2,1,0:T(8,128)(2,1)S(1)} %fusion), channel_id=1, source_target_pairs={{0,6},{1,7},{2,0},{3,1},{4,2},{5,3},{6,4},{7,5},{16,22},{17,23},{1... | collective-permute-start | bytes 1572872 | tf_op jit(solution)/shard_map/ppermute | solution.py:598
  19.7 11.8 %collective-permute-start.8 = (bf16[4,512,128]{2,1,0:T(8,128)(2,1)}, bf16[4,512,128]{2,1,0:T(8,128)(2,1)S(1)}, u32[]{:S(2)}, u32[]{:S(2)}) collective-permute-start(bf16[4,512,128]{2,1,0:T(8,128)(2,1)} %broadcast_select_fusion.2), channel_id=1, source_target_pairs={{0,1},{1,0},{2,3},{3,2},{4,5},{5,4},{6,7},{7,6},{8,24},{9,25},{10,... | collective-permute-start | bytes 1572872 | tf_op jit(solution)/shard_map/ppermute | solution.py:598
  21.1 10.3 %collective-permute-start.11 = (bf16[4,512,128]{2,1,0:T(8,128)(2,1)S(1)}, bf16[4,512,128]{2,1,0:T(8,128)(2,1)S(1)}, u32[]{:S(2)}, u32[]{:S(2)}) collective-permute-start(bf16[4,512,128]{2,1,0:T(8,128)(2,1)S(1)} %collective-permute-done.6.refs_9_.refs_12_), channel_id=1, source_target_pairs={{8,10},{9,11},{10,12},{11,13},{12,14},{13,15},{14,8},{15,9},{24,26... | collective-permute-start | bytes 1572872 | tf_op jit(solution)/shard_map/ppermute | solution.py:598
  22.6 0.7 copy-start.13
  22.7 71.5 %copy-start.11 = (s32[17]{0:T(128)}, s32[17]{0:T(128)S(1)}, u32[]{:S(2)}) copy-start(s32[17]{0:T(128)S(1)} %stack.63.scalars) | copy-start | bytes 208
  22.7 0.7 copy-start.12
  25.7 28.5 %collective-permute-start.3 = (bf16[512,1024]{1,0:T(8,128)(2,1)}, bf16[512,1024]{1,0:T(8,128)(2,1)}, u32[]{:S(2)}, u32[]{:S(2)}) collective-permute-start(bf16[512,1024]{1,0:T(8,128)(2,1)} %get-tuple-element.20.refs_2_), channel_id=1, source_target_pairs={{0,8},{1,9},{2,10},{3,11},{4,12},{5,13},{6,14},{7,15},{8,0},{9,1},... | collective-permute-start | bytes 3145736 | tf_op jit(solution)/shard_map/ppermute | solution.py:598
  25.7 20.2 %all-to-all-start = ((bf16[8,16,1024]{2,1,0:T(8,128)(2,1)}), bf16[8,16,1024]{2,1,0:T(8,128)(2,1)}, u32[]{:S(2)}, u32[]{:S(2)}) async-start(bf16[8,16,1024]{2,1,0:T(8,128)(2,1)} %get-tuple-element.22), calls=%async_computation | async-start | bytes 524288 | tf_op jit(solution)/shard_map/all_to_all | solution.py:606
  30.9 15.6 %collective-permute-start.9 = (bf16[4,512,128]{2,1,0:T(8,128)(2,1)S(1)}, bf16[4,512,128]{2,1,0:T(8,128)(2,1)}, u32[]{:S(2)}, u32[]{:S(2)}) collective-permute-start(bf16[4,512,128]{2,1,0:T(8,128)(2,1)S(1)} %collective-permute-done.6.refs_9_.refs_12_), channel_id=1, source_target_pairs={{0,16},{1,17},{2,18},{3,19},{4,20},{5,21},{6,22},{7,23},{8,9},{9,8... | collective-permute-start | bytes 1572872 | tf_op jit(solution)/shard_map/ppermute | solution.py:598
  31.4 16.5 %copy-start.14 = (s32[1,1,128,1]{2,3,1,0:T(1,128)S(1)}, s32[1,1,128,1]{2,3,1,0:T(1,128)}, u32[]{:S(2)}) copy-start(s32[1,1,128,1]{2,3,1,0:T(1,128)} %param.16) | copy-start | bytes 1540
  31.4 16.7 %copy-start.15 = (s32[1,1,512]{2,1,0:T(1,128)S(1)}, s32[1,1,512]{2,1,0:T(1,128)}, u32[]{:S(2)}) copy-start(s32[1,1,512]{2,1,0:T(1,128)} %param.15) | copy-start | bytes 6148
  32.5 0.8 copy-start.2
  33.3 20.9 %copy-start.1 = (bf16[3,1024,128]{2,1,0:T(8,128)(2,1)S(1)}, bf16[3,1024,128]{2,1,0:T(8,128)(2,1)}, u32[]{:S(2)}) copy-start(bf16[3,1024,128]{2,1,0:T(8,128)(2,1)} %refs_8_.1) | copy-start | bytes 2359300
  33.3 19.0 %collective-permute-start.12 = (bf16[4,512,128]{2,1,0:T(8,128)(2,1)}, bf16[4,512,128]{2,1,0:T(8,128)(2,1)}, u32[]{:S(2)}, u32[]{:S(2)}) collective-permute-start(bf16[4,512,128]{2,1,0:T(8,128)(2,1)} %get-tuple-element.37), channel_id=1, source_target_pairs={{0,16},{1,17},{2,18},{3,19},{4,20},{5,21},{6,22},{7,23},{8,10},{9,... | collective-permute-start | bytes 1572872 | tf_op jit(solution)/shard_map/ppermute | solution.py:598
  34.8 11.2 %collective-permute-start.2 = (bf16[16,1024]{1,0:T(8,128)(2,1)S(1)}, bf16[16,1024]{1,0:T(8,128)(2,1)S(1)}, u32[]{:S(2)}, u32[]{:S(2)}) collective-permute-start(bf16[16,1024]{1,0:T(8,128)(2,1)S(1)} %get-tuple-element.21), channel_id=1, source_target_pairs={{1,0},{2,1},{3,2},{4,3},{5,4},{6,5},{7,6},{9,8},{10,9},{11,10},{12... | collective-permute-start | bytes 98312 | tf_op jit(solution)/shard_map/ppermute | solution.py:27
  36.1 1.5 %collective-permute-start = (s32[1]{0:T(128)}, s32[1]{0:T(128)}, u32[]{:S(2)}, u32[]{:S(2)}) collective-permute-start(s32[1]{0:T(128)} %param.10), channel_id=1, source_target_pairs={{0,8},{1,9},{2,10},{3,11},{4,12},{5,13},{6,14},{7,15},{8,0},{9,1},... | collective-permute-start | bytes 20 | tf_op jit(solution)/shard_map/ppermute | solution.py:598
  46.0 7.0 %collective-permute-start.5 = (bf16[128,1024]{1,0:T(8,128)(2,1)}, bf16[128,1024]{1,0:T(8,128)(2,1)}, u32[]{:S(2)}, u32[]{:S(2)}) collective-permute-start(bf16[128,1024]{1,0:T(8,128)(2,1)} %bitcast.21.refs_4_), channel_id=1, source_target_pairs={{0,8},{1,9},{2,10},{3,11},{4,12},{5,13},{6,14},{7,15},{8,0},{9,1},... | collective-permute-start | bytes 786440 | tf_op jit(solution)/shard_map/ppermute | solution.py:598
  46.0 3.0 %collective-permute-start.4 = (bf16[16,1024]{1,0:T(8,128)(2,1)S(1)}, bf16[16,1024]{1,0:T(8,128)(2,1)S(1)}, u32[]{:S(2)}, u32[]{:S(2)}) collective-permute-start(bf16[16,1024]{1,0:T(8,128)(2,1)S(1)} %collective-permute-done.2.refs_3_), channel_id=1, source_target_pairs={{0,8},{1,9},{2,10},{3,11},{4,12},{5,13},{6,14},{7,15},{8,0},{9,1},... | collective-permute-start | bytes 98312 | tf_op jit(solution)/shard_map/ppermute | solution.py:598
  46.5 7.7 %collective-permute-start.10 = (bf16[4,512,128]{2,1,0:T(8,128)(2,1)}, bf16[4,512,128]{2,1,0:T(8,128)(2,1)}, u32[]{:S(2)}, u32[]{:S(2)}) collective-permute-start(bf16[4,512,128]{2,1,0:T(8,128)(2,1)} %collective-permute-done.9.refs_13_.refs_14_), channel_id=1, source_target_pairs={{8,24},{9,25},{10,26},{11,27},{12,28},{13,29},{14,30},{15,31},{24,... | collective-permute-start | bytes 1572872 | tf_op jit(solution)/shard_map/ppermute | solution.py:598
  48.1 6.1 %copy-start.6 = (bf16[1024,128]{1,0:T(8,128)(2,1)S(1)}, bf16[1024,128]{1,0:T(8,128)(2,1)}, u32[]{:S(2)}) copy-start(bf16[1024,128]{1,0:T(8,128)(2,1)} %refs_10_.1) | copy-start | bytes 786436
  49.0 2.4 %collective-permute-start.1 = (bf16[128,512]{1,0:T(8,128)(2,1)S(1)}, bf16[128,512]{1,0:T(8,128)(2,1)S(1)}, u32[]{:S(2)}, u32[]{:S(2)}) collective-permute-start(bf16[128,512]{1,0:T(8,128)(2,1)S(1)} %get-tuple-element.19.refs_0_), channel_id=1, source_target_pairs={{0,8},{1,9},{2,10},{3,11},{4,12},{5,13},{6,14},{7,15},{8,0},{9,1},... | collective-permute-start | bytes 393224 | tf_op jit(solution)/shard_map/ppermute | solution.py:598
  51.4 15.4 %copy-start.3 = (bf16[4,512,128]{2,1,0:T(8,128)(2,1)S(1)}, bf16[4,512,128]{2,1,0:T(8,128)(2,1)}, u32[]{:S(2)}) copy-start(bf16[4,512,128]{2,1,0:T(8,128)(2,1)} %copy-done.2) | copy-start | bytes 1572868
  51.4 15.4 %collective-permute-start.13 = (bf16[4,512,128]{2,1,0:T(8,128)(2,1)}, bf16[4,512,128]{2,1,0:T(8,128)(2,1)S(1)}, u32[]{:S(2)}, u32[]{:S(2)}) collective-permute-start(bf16[4,512,128]{2,1,0:T(8,128)(2,1)} %get-tuple-element.36), channel_id=1, source_target_pairs={{0,16},{1,17},{2,18},{3,19},{4,20},{5,21},{6,22},{7,23},{8,9},{9,8... | collective-permute-start | bytes 1572872 | tf_op jit(solution)/shard_map/ppermute | solution.py:598
  52.3 14.5 %collective-permute-start.14 = (bf16[4,512,128]{2,1,0:T(8,128)(2,1)}, bf16[4,512,128]{2,1,0:T(8,128)(2,1)S(1)}, u32[]{:S(2)}, u32[]{:S(2)}) collective-permute-start(bf16[4,512,128]{2,1,0:T(8,128)(2,1)} %collective-permute-done.12.refs_10_.refs_11_), channel_id=1, source_target_pairs={{8,9},{9,8},{10,11},{11,10},{12,13},{13,12},{14,15},{15,14},{24,25... | collective-permute-start | bytes 1572872 | tf_op jit(solution)/shard_map/ppermute | solution.py:598
  53.0 32.0 %collective-permute-start.22 = (bf16[1024,512]{1,0:T(8,128)(2,1)}, bf16[1024,512]{1,0:T(8,128)(2,1)}, u32[]{:S(2)}, u32[]{:S(2)}) collective-permute-start(bf16[1024,512]{1,0:T(8,128)(2,1)} %refs_0_.1), channel_id=1, source_target_pairs={{0,16},{1,17},{2,18},{3,19},{4,20},{5,21},{6,22},{7,23},{8,24},{9,... | collective-permute-start | bytes 3145736 | tf_op jit(solution)/shard_map/ppermute | solution.py:598
  61.6 0.7 copy-start.7
  62.3 4.5 %copy-start.16 = (bf16[512,256]{1,0:T(8,128)(2,1)}, bf16[512,256]{1,0:T(8,128)(2,1)S(1)}, u32[]{:S(2)}) copy-start(bf16[512,256]{1,0:T(8,128)(2,1)S(1)} %get-tuple-element.25) | copy-start | bytes 786436
  62.3 23.2 %copy-start.4 = (bf16[1024,256]{1,0:T(8,128)(2,1)}, bf16[1024,256]{1,0:T(8,128)(2,1)S(1)}, u32[]{:S(2)}) copy-start(bf16[1024,256]{1,0:T(8,128)(2,1)S(1)} %get-tuple-element.27.refs_4_) | copy-start | bytes 1572868
  62.3 23.2 %collective-permute-start.17 = (bf16[1024,256]{1,0:T(8,128)(2,1)S(1)}, bf16[1024,256]{1,0:T(8,128)(2,1)S(1)}, u32[]{:S(2)}, u32[]{:S(2)}) collective-permute-start(bf16[1024,256]{1,0:T(8,128)(2,1)S(1)} %get-tuple-element.27.refs_4_), channel_id=1, source_target_pairs={{0,8},{1,9},{2,10},{3,11},{4,12},{5,13},{6,14},{7,15},{8,0},{9,1},... | collective-permute-start | bytes 1572872 | tf_op jit(solution)/shard_map/ppermute | solution.py:598
  74.2 13.5 %copy-start.9 = (bf16[512,256]{1,0:T(8,128)(2,1)}, bf16[512,256]{1,0:T(8,128)(2,1)S(1)}, u32[]{:S(2)}) copy-start(bf16[512,256]{1,0:T(8,128)(2,1)S(1)} %get-tuple-element.24.refs_1_) | copy-start | bytes 786436
  74.2 13.5 %copy-start.17 = (bf16[512,256]{1,0:T(8,128)(2,1)}, bf16[512,256]{1,0:T(8,128)(2,1)S(1)}, u32[]{:S(2)}) copy-start(bf16[512,256]{1,0:T(8,128)(2,1)S(1)} %get-tuple-element.26) | copy-start | bytes 786436
  74.2 11.3 %collective-permute-start.18 = (bf16[1024,256]{1,0:T(8,128)(2,1)S(1)}, bf16[1024,256]{1,0:T(8,128)(2,1)S(1)}, u32[]{:S(2)}, u32[]{:S(2)}) collective-permute-start(bf16[1024,256]{1,0:T(8,128)(2,1)S(1)} %get-tuple-element.28.refs_5_), channel_id=1, source_target_pairs={{0,8},{1,9},{2,10},{3,11},{4,12},{5,13},{6,14},{7,15},{8,0},{9,1},... | collective-permute-start | bytes 1572872 | tf_op jit(solution)/shard_map/ppermute | solution.py:598
  75.0 10.0 %collective-permute-start.19 = (f32[128,256]{1,0:T(8,128)S(1)}, f32[128,256]{1,0:T(8,128)S(1)}, u32[]{:S(2)}, u32[]{:S(2)}) collective-permute-start(f32[128,256]{1,0:T(8,128)S(1)} %get-tuple-element.34), channel_id=1, source_target_pairs={{0,8},{1,9},{2,10},{3,11},{4,12},{5,13},{6,14},{7,15},{8,0},{9,1},... | collective-permute-start | bytes 393224 | tf_op jit(solution)/shard_map/ppermute | solution.py:598
  75.1 10.5 %collective-permute-start.20 = (f32[128,256]{1,0:T(8,128)S(1)}, f32[128,256]{1,0:T(8,128)S(1)}, u32[]{:S(2)}, u32[]{:S(2)}) collective-permute-start(f32[128,256]{1,0:T(8,128)S(1)} %get-tuple-element.35), channel_id=1, source_target_pairs={{0,8},{1,9},{2,10},{3,11},{4,12},{5,13},{6,14},{7,15},{8,0},{9,1},... | collective-permute-start | bytes 393224 | tf_op jit(solution)/shard_map/ppermute | solution.py:598
  85.0 13.6 %collective-permute-start.21 = (bf16[1024,512]{1,0:T(8,128)(2,1)}, bf16[1024,512]{1,0:T(8,128)(2,1)}, u32[]{:S(2)}, u32[]{:S(2)}) collective-permute-start(bf16[1024,512]{1,0:T(8,128)(2,1)} %refs_0_.1), channel_id=1, source_target_pairs={{0,8},{1,9},{2,10},{3,11},{4,12},{5,13},{6,14},{7,15},{8,0},{9,1},... | collective-permute-start | bytes 3145736 | tf_op jit(solution)/shard_map/ppermute | solution.py:598
  85.0 13.6 %collective-permute-start.23 = (bf16[1024,512]{1,0:T(8,128)(2,1)}, bf16[1024,512]{1,0:T(8,128)(2,1)}, u32[]{:S(2)}, u32[]{:S(2)}) collective-permute-start(bf16[1024,512]{1,0:T(8,128)(2,1)} %collective-permute-done.22.refs_2_), channel_id=1, source_target_pairs={{0,8},{1,9},{2,10},{3,11},{4,12},{5,13},{6,14},{7,15},{8,0},{9,1},... | collective-permute-start | bytes 3145736 | tf_op jit(solution)/shard_map/ppermute | solution.py:598
  87.7 6.5 %copy-start.5 = (bf16[1024,256]{1,0:T(8,128)(2,1)S(1)}, bf16[1024,256]{1,0:T(8,128)(2,1)}, u32[]{:S(2)}) copy-start(bf16[1024,256]{1,0:T(8,128)(2,1)} %copy-done.4) | copy-start | bytes 1572868
  87.7 6.5 %copy-start.8 = (bf16[512,256]{1,0:T(8,128)(2,1)S(1)}, bf16[512,256]{1,0:T(8,128)(2,1)}, u32[]{:S(2)}) copy-start(bf16[512,256]{1,0:T(8,128)(2,1)} %copy-done.7) | copy-start | bytes 786436
  87.7 19.3 %all-to-all-start.1 = ((bf16[8,32,1024]{2,1,0:T(8,128)(2,1)}), bf16[8,32,1024]{2,1,0:T(8,128)(2,1)}, u32[]{:S(2)}, u32[]{:S(2)}) async-start(bf16[8,32,1024]{2,1,0:T(8,128)(2,1)} %bitcast.24), calls=%async_computation.1 | async-start | bytes 1048576 | tf_op jit(solution)/shard_map/all_to_all | solution.py:606
  92.1 1.8 %collective-permute-start.15 = (bf16[512,256]{1,0:T(8,128)(2,1)}, bf16[512,256]{1,0:T(8,128)(2,1)S(1)}, u32[]{:S(2)}, u32[]{:S(2)}) collective-permute-start(bf16[512,256]{1,0:T(8,128)(2,1)} %copy-done.16), channel_id=1, source_target_pairs={{0,8},{1,9},{2,10},{3,11},{4,12},{5,13},{6,14},{7,15},{8,0},{9,1},... | collective-permute-start | bytes 786440 | tf_op jit(solution)/shard_map/ppermute | solution.py:598
  92.1 2.1 %collective-permute-start.16 = (bf16[512,256]{1,0:T(8,128)(2,1)}, bf16[512,256]{1,0:T(8,128)(2,1)S(1)}, u32[]{:S(2)}, u32[]{:S(2)}) collective-permute-start(bf16[512,256]{1,0:T(8,128)(2,1)} %copy-done.17), channel_id=1, source_target_pairs={{0,8},{1,9},{2,10},{3,11},{4,12},{5,13},{6,14},{7,15},{8,0},{9,1},... | collective-permute-start | bytes 786440 | tf_op jit(solution)/shard_map/ppermute | solution.py:598
  94.3 1.0 copy-start.10

commit v6 on v5

--- a/solution.py
+++ b/solution.py
@@ -634,6 +634,9 @@
 
     own = jnp.concatenate([qkv_weight, out_weight[None]], axis=0)
     own_a = lax.dynamic_slice_in_dim(own, y_half * half, half, 1)
+    later_qkv, later_out, own_a = lax.optimization_barrier((qkv_weight, out_weight, own_a))
+    later = jnp.concatenate([later_qkv, later_out[None]], axis=0)
+    own_b = lax.dynamic_slice_in_dim(later, (1 - y_half) * half, half, 1)
 
     def pick(for_core_0, for_core_1):
         return jnp.where(core == 0, for_core_0, for_core_1)
@@ -657,7 +660,7 @@
     scalars = jnp.stack(numbers).astype(jnp.int32)
 
     m1 = relocate(own_a, along_x, z_up)
-    m2 = relocate(own_a, z_down, None)
+    m2 = relocate(pick(own_a, own_b), z_down, z_up)
     l1 = relocate(language_weight, along_y, along_y)
 
     pad = 2 * RC
@@ -697,15 +700,14 @@
 
     m3 = relocate(m1, along_y, along_x)
     m4 = relocate(m1, None, z_up)
-    m5 = relocate(pick(m2, m1), along_x, along_y)
+    m5 = relocate(m2, along_x, z_up)
     m6 = relocate(m3, None, along_y)
-    m7 = relocate(pick(m2, m5), along_y, z_up)
-    m8 = relocate(pick(m5, m4), along_y, along_x)
-    m9 = relocate(m7, None, along_x)
+    m7 = relocate(pick(m2, m4), along_y, along_x)
+    m8 = relocate(m5, along_y, along_x)
 
     slot_pieces = (
-        ((qkv_weight, m1), (out_weight, m5), (m1, m3), (m3, m6)),
-        ((m2, m4), (m7, m7), (m5, m8), (m8, m9)),
+        ((qkv_weight, m1), (out_weight, m2), (m1, m3), (m3, m6)),
+        ((m2, m4), (m7, m5), (m5, m7), (m8, m8)),
     )
     block = 2 * C
     width = 2 * shard
@@ -786,7 +788,6 @@
         (received, *language_pieces),
         in_place=rec_count,
         out_in_place=True,
-        vmem_mib=63,
         scratch=(
             pltpu.VMEM((rec_count, model_width, language_shard), bf16),
             pltpu.VMEM((rec_count, slot_count, language_shard), bf16),

time: 113 us -> 121 us (1.071)
  local copies, waits for them, and re-layouts: 3.38 us -> 10.2 us
  waiting for transfers between devices: 38.5 us -> 45.2 us
  starting transfers between devices: 36.8 us -> 33.3 us
    ppermute x1, waiting for transfers between devices: 0.01 us -> 11.1 us  [shifted(): return lax.ppermute(block, axis, route)]
    all_to_all x2, waiting for transfers between devices: 16.8 us -> 6.42 us  [exchange_blocks(): return lax.all_to_all(blocks, 'tm', split_axis=0, concat_axis=0, tiled=True)]
    unnamed x36 -> x58, local copies, waits for them, and re-layouts: 3.17 us -> 9.32 us
    ppermute x23 -> x22, waiting for transfers between devices: 21.8 us -> 27.6 us  [relocate(): return lax.ppermute(value, ('rec', 'tm'), pairs)]
    ppermute x23 -> x22, starting transfers between devices: 26.1 us -> 21.8 us  [relocate(): return lax.ppermute(value, ('rec', 'tm'), pairs)]
  transfers between devices with their start and end apart: 26 -> 25, of which waited for: 9 -> 10; matrix products, arithmetic and copies ran while one was open for 1% -> 2% of each run, Pallas kernels for 21% -> 19%
where the time goes in v6:
time: 121 us; the launch traced here: 120 us
  waiting for transfers between devices  45.2 us (37%)
  starting transfers between devices  33.3 us (28%)
  Pallas kernels  27.4 us (23%)
  local copies, waits for them, and re-layouts  10.2 us (8%)
  other arithmetic  2.14 us (2%)
  between operations  1.8 us (1%)
    ppermute x22, waiting for transfers between devices, relocate(): return lax.ppermute(value, ('rec', 'tm'), pairs)  27.6 us
    pallas_call x7, Pallas kernels, local_call(): pl.pallas_call(kernel, out_shape=out_shapes, in_specs=[smem_spec()] * len...  27.4 us
    ppermute x22, starting transfers between devices, relocate(): return lax.ppermute(value, ('rec', 'tm'), pairs)  21.8 us
    ppermute x1, waiting for transfers between devices, shifted(): return lax.ppermute(block, axis, route)  11.1 us
    all_to_all x2, starting transfers between devices, exchange_blocks(): return lax.all_to_all(blocks, 'tm', split_axis=0, concat_axis=0, tiled=True)  10.1 us
    unnamed x58, local copies, waits for them, and re-layouts  9.32 us
    all_to_all x2, waiting for transfers between devices, exchange_blocks(): return lax.all_to_all(blocks, 'tm', split_axis=0, concat_axis=0, tiled=True)  6.42 us
  transfers between devices with their start and end apart: 25, of which 10 were waited for; matrix products, arithmetic and copies ran while one was open for 2% of the time, Pallas kernels for 19%

profile of v6, /device:TPU:0, one launch (start us, length us, event | category | flops | bytes accessed | tf_op | source)
XLA Modules:
  0.0 119.9 jit_solution(9934737567076955824)
XLA Ops:
  0.7 1.2 fusion.2
  1.8 3.0 %collective-permute-start.6 = (bf16[4,512,128]{2,1,0:T(8,128)(2,1)S(1)}, bf16[4,512,128]{2,1,0:T(8,128)(2,1)}, u32[]{:S(2)}, u32[]{:S(2)}) collective-permute-start(bf16[4,512,128]{2,1,0:T(8,128)(2,1)S(1)} %fusion.2), channel_id=1, source_target_pairs={{0,1},{1,0},{2,3},{3,2},{4,5},{5,4},{6,7},{7,6},{8,10},{9,11},{10,... | collective-permute-start | bytes 1572872 | tf_op jit(solution)/shard_map/ppermute | solution.py:598
  4.9 0.9 fusion.1
  5.8 3.6 %collective-permute-start.7 = (bf16[4,512,128]{2,1,0:T(8,128)(2,1)}, bf16[4,512,128]{2,1,0:T(8,128)(2,1)S(1)}, u32[]{:S(2)}, u32[]{:S(2)}) collective-permute-start(bf16[4,512,128]{2,1,0:T(8,128)(2,1)} %fusion.1), channel_id=1, source_target_pairs={{0,6},{1,7},{2,0},{3,1},{4,2},{5,3},{6,4},{7,5},{8,10},{9,11},{10,... | collective-permute-start | bytes 1572872 | tf_op jit(solution)/shard_map/ppermute | solution.py:598
  9.4 2.7 %collective-permute-done.6.refs_9_.refs_12_ = bf16[4,512,128]{2,1,0:T(8,128)(2,1)} collective-permute-done((bf16[4,512,128]{2,1,0:T(8,128)(2,1)S(1)}, bf16[4,512,128]{2,1,0:T(8,128)(2,1)}, u32[]{:S(2)}, u32[]{:S(2)}) %collective-permute-start.6) | collective-permute-done | bytes 524320 | tf_op jit(solution)/shard_map/ppermute | solution.py:598
  12.1 1.5 %collective-permute-start.10 = (bf16[4,512,128]{2,1,0:T(8,128)(2,1)}, bf16[4,512,128]{2,1,0:T(8,128)(2,1)}, u32[]{:S(2)}, u32[]{:S(2)}) collective-permute-start(bf16[4,512,128]{2,1,0:T(8,128)(2,1)} %collective-permute-done.6.refs_9_.refs_12_), channel_id=1, source_target_pairs={{8,10},{9,11},{10,12},{11,13},{12,14},{13,15},{14,8},{15,9},{24,26... | collective-permute-start | bytes 1572872 | tf_op jit(solution)/shard_map/ppermute | solution.py:598
  14.4 0.6 copy-done.23
  15.0 1.5 %shard_map.105 = (bf16[512,1024]{1,0:T(8,128)(2,1)S(1)}, bf16[16,1024]{1,0:T(8,128)(2,1)S(1)}, bf16[8,16,1024]{2,1,0:T(8,128)(2,1)S(1)}) custom-call(s32[17]{0:T(128)S(1)} %stack.63.scalars, bf16[512,1024]{1,0:T(8,128)(2,1)S(1)} %bitcast.28, f32[1,1024]{1,0:T(1,128)S(1)} %bitcast.34, f32[1,1024]{1,0:T(1,128)S(1)} %bitcast.35), custom_call_target="tpu_custom_call" | custom-call | flops 5242880 | bytes 2097152 | tf_op jit(solution)/shard_map/pallas_call | solution.py:269
  16.6 0.7 copy-done.13
  17.2 6.3 %all-to-all-start = ((bf16[8,16,1024]{2,1,0:T(8,128)(2,1)}), bf16[8,16,1024]{2,1,0:T(8,128)(2,1)}, u32[]{:S(2)}, u32[]{:S(2)}) async-start(bf16[8,16,1024]{2,1,0:T(8,128)(2,1)} %copy-done.13), calls=%async_computation | async-start | bytes 524288 | tf_op jit(solution)/shard_map/all_to_all | solution.py:606
  23.6 3.4 %collective-permute-start.3 = (bf16[512,1024]{1,0:T(8,128)(2,1)S(1)}, bf16[512,1024]{1,0:T(8,128)(2,1)}, u32[]{:S(2)}, u32[]{:S(2)}) collective-permute-start(bf16[512,1024]{1,0:T(8,128)(2,1)S(1)} %get-tuple-element.23.refs_2_), channel_id=1, source_target_pairs={{0,8},{1,9},{2,10},{3,11},{4,12},{5,13},{6,14},{7,15},{8,0},{9,1},... | collective-permute-start | bytes 3145736 | tf_op jit(solution)/shard_map/ppermute | solution.py:598
  27.0 1.7 %collective-permute-start.12 = (bf16[4,512,128]{2,1,0:T(8,128)(2,1)S(1)}, bf16[4,512,128]{2,1,0:T(8,128)(2,1)}, u32[]{:S(2)}, u32[]{:S(2)}) collective-permute-start(bf16[4,512,128]{2,1,0:T(8,128)(2,1)S(1)} %collective-permute-done.7.refs_11_.refs_8_), channel_id=1, source_target_pairs={{0,1},{1,0},{2,3},{3,2},{4,5},{5,4},{6,7},{7,6},{8,10},{9,11},{10,... | collective-permute-start | bytes 1572872 | tf_op jit(solution)/shard_map/ppermute | solution.py:598
  28.7 1.5 %collective-permute-start.8 = (bf16[4,512,128]{2,1,0:T(8,128)(2,1)}, bf16[4,512,128]{2,1,0:T(8,128)(2,1)}, u32[]{:S(2)}, u32[]{:S(2)}) collective-permute-start(bf16[4,512,128]{2,1,0:T(8,128)(2,1)} %collective-permute-done.6.refs_9_.refs_12_), channel_id=1, source_target_pairs={{0,16},{1,17},{2,18},{3,19},{4,20},{5,21},{6,22},{7,23},{8,9},{9,8... | collective-permute-start | bytes 1572872 | tf_op jit(solution)/shard_map/ppermute | solution.py:598
  30.3 1.4 %collective-permute-done.other_length = s32[1]{0:T(128)} collective-permute-done((s32[1]{0:T(128)}, s32[1]{0:T(128)}, u32[]{:S(2)}, u32[]{:S(2)}) %collective-permute-start) | collective-permute-done | bytes 36 | tf_op jit(solution)/shard_map/ppermute | solution.py:598
  31.7 1.4 %collective-permute-start.2 = (bf16[16,1024]{1,0:T(8,128)(2,1)S(1)}, bf16[16,1024]{1,0:T(8,128)(2,1)}, u32[]{:S(2)}, u32[]{:S(2)}) collective-permute-start(bf16[16,1024]{1,0:T(8,128)(2,1)S(1)} %get-tuple-element.24), channel_id=1, source_target_pairs={{1,0},{2,1},{3,2},{4,3},{5,4},{6,5},{7,6},{9,8},{10,9},{11,10},{12... | collective-permute-start | bytes 98312 | tf_op jit(solution)/shard_map/ppermute | solution.py:27
  33.1 11.1 %collective-permute-done.2.refs_3_ = bf16[16,1024]{1,0:T(8,128)(2,1)} collective-permute-done((bf16[16,1024]{1,0:T(8,128)(2,1)S(1)}, bf16[16,1024]{1,0:T(8,128)(2,1)}, u32[]{:S(2)}, u32[]{:S(2)}) %collective-permute-start.2) | collective-permute-done | bytes 32800 | tf_op jit(solution)/shard_map/ppermute | solution.py:27
  44.5 0.7 copy.11.owners_col
  45.3 0.7 copy-done.25
  46.0 0.8 copy-done.12
  46.8 0.9 shard_map.104
  47.7 0.8 copy-done.10
  48.5 0.6 copy-done.18
  49.1 0.6 copy-done.20
  49.9 0.3 collective-permute-start.5
  50.3 0.9 collective-permute-done.1.refs_1_
  51.2 1.5 %collective-permute-start.11 = (bf16[4,512,128]{2,1,0:T(8,128)(2,1)S(1)}, bf16[4,512,128]{2,1,0:T(8,128)(2,1)S(1)}, u32[]{:S(2)}, u32[]{:S(2)}) collective-permute-start(bf16[4,512,128]{2,1,0:T(8,128)(2,1)S(1)} %broadcast_select_fusion), channel_id=1, source_target_pairs={{0,16},{1,17},{2,18},{3,19},{4,20},{5,21},{6,22},{7,23},{8,9},{9,8... | collective-permute-start | bytes 1572872 | tf_op jit(solution)/shard_map/ppermute | solution.py:598
  52.7 0.5 collective-permute-start.13
  53.2 0.7 collective-permute-start.9
  53.9 1.6 %collective-permute-start.21 = (bf16[1024,512]{1,0:T(8,128)(2,1)}, bf16[1024,512]{1,0:T(8,128)(2,1)}, u32[]{:S(2)}, u32[]{:S(2)}) collective-permute-start(bf16[1024,512]{1,0:T(8,128)(2,1)} %refs_0_.1), channel_id=1, source_target_pairs={{0,16},{1,17},{2,18},{3,19},{4,20},{5,21},{6,22},{7,23},{8,24},{9,... | collective-permute-start | bytes 3145736 | tf_op jit(solution)/shard_map/ppermute | solution.py:598
  55.5 7.4 %collective-permute-done.11.refs_10_.refs_13_ = bf16[4,512,128]{2,1,0:T(8,128)(2,1)S(1)} collective-permute-done((bf16[4,512,128]{2,1,0:T(8,128)(2,1)S(1)}, bf16[4,512,128]{2,1,0:T(8,128)(2,1)S(1)}, u32[]{:S(2)}, u32[]{:S(2)}) %collective-permute-start.11) | collective-permute-done | bytes 524320 | tf_op jit(solution)/shard_map/ppermute | solution.py:598
  62.9 11.2 %collective-permute-done.13.refs_14_.refs_15_ = bf16[4,512,128]{2,1,0:T(8,128)(2,1)S(1)} collective-permute-done((bf16[4,512,128]{2,1,0:T(8,128)(2,1)}, bf16[4,512,128]{2,1,0:T(8,128)(2,1)S(1)}, u32[]{:S(2)}, u32[]{:S(2)}) %collective-permute-start.13) | collective-permute-done | bytes 524320 | tf_op jit(solution)/shard_map/ppermute | solution.py:598
  74.2 7.4 %shard_map.107 = (bf16[512,256]{1,0:T(8,128)(2,1)S(1)}, bf16[512,256]{1,0:T(8,128)(2,1)S(1)}, f32[128,256]{1,0:T(8,128)S(1)}, f32[128,256]{1,0:T(8,128)S(1)}, bf16[1024,256]{1,0:T(8,128)(2,1)S(1)}) custom-call(s32[17]{0:T(128)S(1)} %stack.63.scalars, s32[1]{0:T(128)} %collective-permute-done.other_length, bf16[128,512]{1,0:T(8,128)(2,1)S(1)} %get-tuple-element.22.refs_0_, ...), custom_call_target="tpu_custom_call" | custom-call | flops 1610612736 | bytes 4194304 | tf_op jit(solution)/shard_map/pallas_call | solution.py:269
  81.6 0.7 copy-done.14
  82.3 0.7 copy-done.26
  83.1 7.7 %shard_map.106 = (bf16[512,256]{1,0:T(8,128)(2,1)S(1)}, bf16[512,256]{1,0:T(8,128)(2,1)S(1)}, f32[128,256]{1,0:T(8,128)S(1)}, f32[128,256]{1,0:T(8,128)S(1)}, bf16[1024,256]{1,0:T(8,128)(2,1)S(1)}) custom-call(s32[17]{0:T(128)S(1)} %stack.63.scalars, s32[1]{0:T(128)} %collective-permute-done.other_length, bf16[128,512]{1,0:T(8,128)(2,1)S(1)} %get-tuple-element.22.refs_0_, ...), custom_call_target="tpu_custom_call" | custom-call | flops 1610612736 | bytes 4194304 | tf_op jit(solution)/shard_map/pallas_call | solution.py:269
  91.7 2.5 %collective-permute-done.21.refs_2_ = bf16[1024,512]{1,0:T(8,128)(2,1)} collective-permute-done((bf16[1024,512]{1,0:T(8,128)(2,1)}, bf16[1024,512]{1,0:T(8,128)(2,1)}, u32[]{:S(2)}, u32[]{:S(2)}) %collective-permute-start.21) | collective-permute-done | bytes 1048608 | tf_op jit(solution)/shard_map/ppermute | solution.py:598
  94.2 0.5 collective-permute-start.22
  94.8 2.2 %shard_map.109 = bf16[256,1024]{1,0:T(8,128)(2,1)} custom-call(s32[17]{0:T(128)S(1)} %stack.63.scalars, f32[128,1024]{1,0:T(8,128)S(1)} %copy-done.11, f32[128,128]{1,0:T(8,128)S(1)} %copy-done.19, bf16[256,128]{1,0:T(8,128)(2,1)S(1)} %copy-done.21, f32[128,256]{1,0:T(8,128)S(1)} %get-tuple-element.38.refs_0_, f32[128,256]{1,0:T(8,128)S(1)} %get-tuple-element.39.refs_1_, ...), custom_call_target="tpu_custom_call" | custom-call | flops 536870912 | bytes 3145728 | tf_op jit(solution)/shard_map/pallas_call | solution.py:269
  97.0 3.7 %all-to-all-start.1 = ((bf16[8,32,1024]{2,1,0:T(8,128)(2,1)}), bf16[8,32,1024]{2,1,0:T(8,128)(2,1)S(1)}, u32[]{:S(2)}, u32[]{:S(2)}) async-start(bf16[8,32,1024]{2,1,0:T(8,128)(2,1)} %bitcast.25), calls=%async_computation.1 | async-start | bytes 1048576 | tf_op jit(solution)/shard_map/all_to_all | solution.py:606
  100.8 0.5 collective-permute-start.14
  101.3 1.0 collective-permute-done.15.refs_3_
  102.3 0.4 collective-permute-done.14.refs_2_
  102.7 1.0 copy-done.9
  103.7 0.9 copy-done.15
  104.7 0.9 copy-done.17
  105.6 3.4 %shard_map.108 = bf16[512,1024]{1,0:T(8,128)(2,1)} custom-call(s32[17]{0:T(128)S(1)} %stack.63.scalars, bf16[512,256]{1,0:T(8,128)(2,1)S(1)} %copy-done.17, bf16[512,256]{1,0:T(8,128)(2,1)S(1)} %copy-done.15, bf16[512,256]{1,0:T(8,128)(2,1)S(1)} %collective-permute-done.14.refs_2_, bf16[512,256]{1,0:T(8,128)(2,1)S(1)} %collective-permute-done.15.refs_3_, ...), custom_call_target="tpu_custom_call" | custom-call | flops 1073741824 | bytes 3145728 | tf_op jit(solution)/shard_map/pallas_call | solution.py:269
  109.1 6.4 %all-to-all-done.1 = bf16[8,32,1024]{2,1,0:T(8,128)(2,1)S(1)} async-done(((bf16[8,32,1024]{2,1,0:T(8,128)(2,1)}), bf16[8,32,1024]{2,1,0:T(8,128)(2,1)S(1)}, u32[]{:S(2)}, u32[]{:S(2)}) %all-to-all-start.1) | async-done | bytes 524320 | tf_op jit(solution)/shard_map/all_to_all | solution.py:606
  115.5 4.3 %shard_map.110 = bf16[256,2048]{1,0:T(8,128)(2,1)} custom-call(s32[17]{0:T(128)S(1)} %stack.63.scalars, bf16[256,1024]{1,0:T(8,128)(2,1)S(1)} %bitcast.33, bf16[1024,512]{1,0:T(8,128)(2,1)} %refs_0_.1, bf16[1024,512]{1,0:T(8,128)(2,1)} %collective-permute-done.20.refs_1_, bf16[1024,512]{1,0:T(8,128)(2,1)} %collective-permute-done.21.refs_2_, ...), custom_call_target="tpu_custom_call" | custom-call | flops 1073741824 | bytes 4194304 | tf_op jit(solution)/shard_map/pallas_call | solution.py:269
  (72 shorter events, 1.9 us)
Async XLA Ops:
  0.7 4.2 %copy-start.1 = (bf16[3,1024,128]{2,1,0:T(8,128)(2,1)S(1)}, bf16[3,1024,128]{2,1,0:T(8,128)(2,1)}, u32[]{:S(2)}) copy-start(bf16[3,1024,128]{2,1,0:T(8,128)(2,1)} %refs_8_.1) | copy-start | bytes 2359300
  0.7 4.2 %copy-start.2 = (bf16[1024,128]{1,0:T(8,128)(2,1)S(1)}, bf16[1024,128]{1,0:T(8,128)(2,1)}, u32[]{:S(2)}) copy-start(bf16[1024,128]{1,0:T(8,128)(2,1)} %refs_10_.1) | copy-start | bytes 786436
  1.8 10.3 %collective-permute-start.6 = (bf16[4,512,128]{2,1,0:T(8,128)(2,1)S(1)}, bf16[4,512,128]{2,1,0:T(8,128)(2,1)}, u32[]{:S(2)}, u32[]{:S(2)}) collective-permute-start(bf16[4,512,128]{2,1,0:T(8,128)(2,1)S(1)} %fusion.2), channel_id=1, source_target_pairs={{0,1},{1,0},{2,3},{3,2},{4,5},{5,4},{6,7},{7,6},{8,10},{9,11},{10,... | collective-permute-start | bytes 1572872 | tf_op jit(solution)/shard_map/ppermute | solution.py:598
  4.9 9.5 %copy-start = (bf16[1,512,1024]{2,1,0:T(8,128)(2,1)S(1)}, bf16[1,512,1024]{2,1,0:T(8,128)(2,1)}, u32[]{:S(2)}) copy-start(bf16[1,512,1024]{2,1,0:T(8,128)(2,1)} %param.9) | copy-start | bytes 3145732
  5.8 21.2 %collective-permute-start.7 = (bf16[4,512,128]{2,1,0:T(8,128)(2,1)}, bf16[4,512,128]{2,1,0:T(8,128)(2,1)S(1)}, u32[]{:S(2)}, u32[]{:S(2)}) collective-permute-start(bf16[4,512,128]{2,1,0:T(8,128)(2,1)} %fusion.1), channel_id=1, source_target_pairs={{0,6},{1,7},{2,0},{3,1},{4,2},{5,3},{6,4},{7,5},{8,10},{9,11},{10,... | collective-permute-start | bytes 1572872 | tf_op jit(solution)/shard_map/ppermute | solution.py:598
  12.1 37.8 %collective-permute-start.10 = (bf16[4,512,128]{2,1,0:T(8,128)(2,1)}, bf16[4,512,128]{2,1,0:T(8,128)(2,1)}, u32[]{:S(2)}, u32[]{:S(2)}) collective-permute-start(bf16[4,512,128]{2,1,0:T(8,128)(2,1)} %collective-permute-done.6.refs_9_.refs_12_), channel_id=1, source_target_pairs={{8,10},{9,11},{10,12},{11,13},{12,14},{13,15},{14,8},{15,9},{24,26... | collective-permute-start | bytes 1572872 | tf_op jit(solution)/shard_map/ppermute | solution.py:598
  16.5 0.7 copy-start.13
  17.2 32.7 %all-to-all-start = ((bf16[8,16,1024]{2,1,0:T(8,128)(2,1)}), bf16[8,16,1024]{2,1,0:T(8,128)(2,1)}, u32[]{:S(2)}, u32[]{:S(2)}) async-start(bf16[8,16,1024]{2,1,0:T(8,128)(2,1)} %copy-done.13), calls=%async_computation | async-start | bytes 524288 | tf_op jit(solution)/shard_map/all_to_all | solution.py:606
  23.6 31.9 %collective-permute-start.3 = (bf16[512,1024]{1,0:T(8,128)(2,1)S(1)}, bf16[512,1024]{1,0:T(8,128)(2,1)}, u32[]{:S(2)}, u32[]{:S(2)}) collective-permute-start(bf16[512,1024]{1,0:T(8,128)(2,1)S(1)} %get-tuple-element.23.refs_2_), channel_id=1, source_target_pairs={{0,8},{1,9},{2,10},{3,11},{4,12},{5,13},{6,14},{7,15},{8,0},{9,1},... | collective-permute-start | bytes 3145736 | tf_op jit(solution)/shard_map/ppermute | solution.py:598
  27.0 25.7 %collective-permute-start.12 = (bf16[4,512,128]{2,1,0:T(8,128)(2,1)S(1)}, bf16[4,512,128]{2,1,0:T(8,128)(2,1)}, u32[]{:S(2)}, u32[]{:S(2)}) collective-permute-start(bf16[4,512,128]{2,1,0:T(8,128)(2,1)S(1)} %collective-permute-done.7.refs_11_.refs_8_), channel_id=1, source_target_pairs={{0,1},{1,0},{2,3},{3,2},{4,5},{5,4},{6,7},{7,6},{8,10},{9,11},{10,... | collective-permute-start | bytes 1572872 | tf_op jit(solution)/shard_map/ppermute | solution.py:598
  28.7 24.5 %collective-permute-start.8 = (bf16[4,512,128]{2,1,0:T(8,128)(2,1)}, bf16[4,512,128]{2,1,0:T(8,128)(2,1)}, u32[]{:S(2)}, u32[]{:S(2)}) collective-permute-start(bf16[4,512,128]{2,1,0:T(8,128)(2,1)} %collective-permute-done.6.refs_9_.refs_12_), channel_id=1, source_target_pairs={{0,16},{1,17},{2,18},{3,19},{4,20},{5,21},{6,22},{7,23},{8,9},{9,8... | collective-permute-start | bytes 1572872 | tf_op jit(solution)/shard_map/ppermute | solution.py:598
  30.2 1.4 %collective-permute-start = (s32[1]{0:T(128)}, s32[1]{0:T(128)}, u32[]{:S(2)}, u32[]{:S(2)}) collective-permute-start(s32[1]{0:T(128)} %param.10), channel_id=1, source_target_pairs={{0,8},{1,9},{2,10},{3,11},{4,12},{5,13},{6,14},{7,15},{8,0},{9,1},... | collective-permute-start | bytes 20 | tf_op jit(solution)/shard_map/ppermute | solution.py:598
  31.7 12.8 %copy-start.24 = (s32[1,1,128,1]{2,3,1,0:T(1,128)S(1)}, s32[1,1,128,1]{2,3,1,0:T(1,128)}, u32[]{:S(2)}) copy-start(s32[1,1,128,1]{2,3,1,0:T(1,128)} %param.16) | copy-start | bytes 1540
  31.7 12.5 %collective-permute-start.2 = (bf16[16,1024]{1,0:T(8,128)(2,1)S(1)}, bf16[16,1024]{1,0:T(8,128)(2,1)}, u32[]{:S(2)}, u32[]{:S(2)}) collective-permute-start(bf16[16,1024]{1,0:T(8,128)(2,1)S(1)} %get-tuple-element.24), channel_id=1, source_target_pairs={{1,0},{2,1},{3,2},{4,3},{5,4},{6,5},{7,6},{9,8},{10,9},{11,10},{12... | collective-permute-start | bytes 98312 | tf_op jit(solution)/shard_map/ppermute | solution.py:27
  44.2 5.5 %collective-permute-start.4 = (bf16[16,1024]{1,0:T(8,128)(2,1)}, bf16[16,1024]{1,0:T(8,128)(2,1)}, u32[]{:S(2)}, u32[]{:S(2)}) collective-permute-start(bf16[16,1024]{1,0:T(8,128)(2,1)} %collective-permute-done.2.refs_3_), channel_id=1, source_target_pairs={{0,8},{1,9},{2,10},{3,11},{4,12},{5,13},{6,14},{7,15},{8,0},{9,1},... | collective-permute-start | bytes 98312 | tf_op jit(solution)/shard_map/ppermute | solution.py:598
  45.9 0.8 copy-start.12
  47.7 0.8 copy-start.10
  49.7 1.5 %collective-permute-start.1 = (bf16[128,512]{1,0:T(8,128)(2,1)S(1)}, bf16[128,512]{1,0:T(8,128)(2,1)}, u32[]{:S(2)}, u32[]{:S(2)}) collective-permute-start(bf16[128,512]{1,0:T(8,128)(2,1)S(1)} %get-tuple-element.22.refs_0_), channel_id=1, source_target_pairs={{0,8},{1,9},{2,10},{3,11},{4,12},{5,13},{6,14},{7,15},{8,0},{9,1},... | collective-permute-start | bytes 393224 | tf_op jit(solution)/shard_map/ppermute | solution.py:598
  49.9 4.0 %collective-permute-start.5 = (bf16[128,1024]{1,0:T(8,128)(2,1)}, bf16[128,1024]{1,0:T(8,128)(2,1)S(1)}, u32[]{:S(2)}, u32[]{:S(2)}) collective-permute-start(bf16[128,1024]{1,0:T(8,128)(2,1)} %bitcast.21.refs_4_), channel_id=1, source_target_pairs={{0,8},{1,9},{2,10},{3,11},{4,12},{5,13},{6,14},{7,15},{8,0},{9,1},... | collective-permute-start | bytes 786440 | tf_op jit(solution)/shard_map/ppermute | solution.py:598
  50.3 32.8 %copy-start.3 = (bf16[1024,128]{1,0:T(8,128)(2,1)S(1)}, bf16[1024,128]{1,0:T(8,128)(2,1)}, u32[]{:S(2)}) copy-start(bf16[1024,128]{1,0:T(8,128)(2,1)} %refs_10_.1) | copy-start | bytes 786436
  51.2 11.8 %collective-permute-start.11 = (bf16[4,512,128]{2,1,0:T(8,128)(2,1)S(1)}, bf16[4,512,128]{2,1,0:T(8,128)(2,1)S(1)}, u32[]{:S(2)}, u32[]{:S(2)}) collective-permute-start(bf16[4,512,128]{2,1,0:T(8,128)(2,1)S(1)} %broadcast_select_fusion), channel_id=1, source_target_pairs={{0,16},{1,17},{2,18},{3,19},{4,20},{5,21},{6,22},{7,23},{8,9},{9,8... | collective-permute-start | bytes 1572872 | tf_op jit(solution)/shard_map/ppermute | solution.py:598
  52.7 21.5 %collective-permute-start.13 = (bf16[4,512,128]{2,1,0:T(8,128)(2,1)}, bf16[4,512,128]{2,1,0:T(8,128)(2,1)S(1)}, u32[]{:S(2)}, u32[]{:S(2)}) collective-permute-start(bf16[4,512,128]{2,1,0:T(8,128)(2,1)} %collective-permute-done.12.refs_11_.refs_12_), channel_id=1, source_target_pairs={{0,16},{1,17},{2,18},{3,19},{4,20},{5,21},{6,22},{7,23},{8,9},{9,8... | collective-permute-start | bytes 1572872 | tf_op jit(solution)/shard_map/ppermute | solution.py:598
  53.2 29.9 %collective-permute-start.9 = (bf16[4,512,128]{2,1,0:T(8,128)(2,1)}, bf16[4,512,128]{2,1,0:T(8,128)(2,1)S(1)}, u32[]{:S(2)}, u32[]{:S(2)}) collective-permute-start(bf16[4,512,128]{2,1,0:T(8,128)(2,1)} %collective-permute-done.8.refs_13_.refs_14_), channel_id=1, source_target_pairs={{8,24},{9,25},{10,26},{11,27},{12,28},{13,29},{14,30},{15,31},{24,... | collective-permute-start | bytes 1572872 | tf_op jit(solution)/shard_map/ppermute | solution.py:598
  53.9 40.3 %collective-permute-start.21 = (bf16[1024,512]{1,0:T(8,128)(2,1)}, bf16[1024,512]{1,0:T(8,128)(2,1)}, u32[]{:S(2)}, u32[]{:S(2)}) collective-permute-start(bf16[1024,512]{1,0:T(8,128)(2,1)} %refs_0_.1), channel_id=1, source_target_pairs={{0,16},{1,17},{2,18},{3,19},{4,20},{5,21},{6,22},{7,23},{8,24},{9,... | collective-permute-start | bytes 3145736 | tf_op jit(solution)/shard_map/ppermute | solution.py:598
  82.3 0.7 copy-start.26
  83.0 11.7 %copy-start.4 = (bf16[1024,256]{1,0:T(8,128)(2,1)}, bf16[1024,256]{1,0:T(8,128)(2,1)S(1)}, u32[]{:S(2)}) copy-start(bf16[1024,256]{1,0:T(8,128)(2,1)S(1)} %get-tuple-element.34.refs_5_) | copy-start | bytes 1572868
  83.0 11.7 %copy-start.11 = (f32[128,1024]{1,0:T(8,128)S(1)}, f32[128,1024]{1,0:T(8,128)}, u32[]{:S(2)}) copy-start(f32[128,1024]{1,0:T(8,128)} %copy-done.10) | copy-start | bytes 1572868
  83.0 11.7 %copy-start.19 = (f32[128,128]{1,0:T(8,128)S(1)}, f32[128,128]{1,0:T(8,128)}, u32[]{:S(2)}) copy-start(f32[128,128]{1,0:T(8,128)} %copy-done.18) | copy-start | bytes 196612
  83.0 11.8 %copy-start.21 = (bf16[256,128]{1,0:T(8,128)(2,1)S(1)}, bf16[256,128]{1,0:T(8,128)(2,1)}, u32[]{:S(2)}) copy-start(bf16[256,128]{1,0:T(8,128)(2,1)} %copy-done.20) | copy-start | bytes 196612
  83.0 11.7 %collective-permute-start.17 = (bf16[1024,256]{1,0:T(8,128)(2,1)S(1)}, bf16[1024,256]{1,0:T(8,128)(2,1)S(1)}, u32[]{:S(2)}, u32[]{:S(2)}) collective-permute-start(bf16[1024,256]{1,0:T(8,128)(2,1)S(1)} %get-tuple-element.34.refs_5_), channel_id=1, source_target_pairs={{0,8},{1,9},{2,10},{3,11},{4,12},{5,13},{6,14},{7,15},{8,0},{9,1},... | collective-permute-start | bytes 1572872 | tf_op jit(solution)/shard_map/ppermute | solution.py:598
  90.8 6.1 %copy-start.8 = (bf16[1024,256]{1,0:T(8,128)(2,1)}, bf16[1024,256]{1,0:T(8,128)(2,1)S(1)}, u32[]{:S(2)}) copy-start(bf16[1024,256]{1,0:T(8,128)(2,1)S(1)} %get-tuple-element.33.refs_4_) | copy-start | bytes 1572868
  90.9 6.1 %copy-start.16 = (bf16[512,256]{1,0:T(8,128)(2,1)}, bf16[512,256]{1,0:T(8,128)(2,1)S(1)}, u32[]{:S(2)}) copy-start(bf16[512,256]{1,0:T(8,128)(2,1)S(1)} %get-tuple-element.29.refs_0_) | copy-start | bytes 786436
  90.9 6.1 %copy-start.28 = (bf16[512,256]{1,0:T(8,128)(2,1)}, bf16[512,256]{1,0:T(8,128)(2,1)S(1)}, u32[]{:S(2)}) copy-start(bf16[512,256]{1,0:T(8,128)(2,1)S(1)} %get-tuple-element.31) | copy-start | bytes 786436
  90.9 3.8 %collective-permute-start.16 = (bf16[1024,256]{1,0:T(8,128)(2,1)S(1)}, bf16[1024,256]{1,0:T(8,128)(2,1)S(1)}, u32[]{:S(2)}, u32[]{:S(2)}) collective-permute-start(bf16[1024,256]{1,0:T(8,128)(2,1)S(1)} %get-tuple-element.33.refs_4_), channel_id=1, source_target_pairs={{0,8},{1,9},{2,10},{3,11},{4,12},{5,13},{6,14},{7,15},{8,0},{9,1},... | collective-permute-start | bytes 1572872 | tf_op jit(solution)/shard_map/ppermute | solution.py:598
  91.2 3.0 %collective-permute-start.19 = (f32[128,256]{1,0:T(8,128)S(1)}, f32[128,256]{1,0:T(8,128)S(1)}, u32[]{:S(2)}, u32[]{:S(2)}) collective-permute-start(f32[128,256]{1,0:T(8,128)S(1)} %get-tuple-element.41), channel_id=1, source_target_pairs={{0,8},{1,9},{2,10},{3,11},{4,12},{5,13},{6,14},{7,15},{8,0},{9,1},... | collective-permute-start | bytes 393224 | tf_op jit(solution)/shard_map/ppermute | solution.py:598
  91.5 3.2 %collective-permute-start.18 = (f32[128,256]{1,0:T(8,128)S(1)}, f32[128,256]{1,0:T(8,128)S(1)}, u32[]{:S(2)}, u32[]{:S(2)}) collective-permute-start(f32[128,256]{1,0:T(8,128)S(1)} %get-tuple-element.40), channel_id=1, source_target_pairs={{0,8},{1,9},{2,10},{3,11},{4,12},{5,13},{6,14},{7,15},{8,0},{9,1},... | collective-permute-start | bytes 393224 | tf_op jit(solution)/shard_map/ppermute | solution.py:598
  94.2 14.9 %collective-permute-start.20 = (bf16[1024,512]{1,0:T(8,128)(2,1)}, bf16[1024,512]{1,0:T(8,128)(2,1)}, u32[]{:S(2)}, u32[]{:S(2)}) collective-permute-start(bf16[1024,512]{1,0:T(8,128)(2,1)} %refs_0_.1), channel_id=1, source_target_pairs={{0,8},{1,9},{2,10},{3,11},{4,12},{5,13},{6,14},{7,15},{8,0},{9,1},... | collective-permute-start | bytes 3145736 | tf_op jit(solution)/shard_map/ppermute | solution.py:598
  94.2 14.9 %collective-permute-start.22 = (bf16[1024,512]{1,0:T(8,128)(2,1)}, bf16[1024,512]{1,0:T(8,128)(2,1)}, u32[]{:S(2)}, u32[]{:S(2)}) collective-permute-start(bf16[1024,512]{1,0:T(8,128)(2,1)} %collective-permute-done.21.refs_2_), channel_id=1, source_target_pairs={{0,8},{1,9},{2,10},{3,11},{4,12},{5,13},{6,14},{7,15},{8,0},{9,1},... | collective-permute-start | bytes 3145736 | tf_op jit(solution)/shard_map/ppermute | solution.py:598
  94.7 2.2 %copy-start.6 = (bf16[1024,256]{1,0:T(8,128)(2,1)}, bf16[1024,256]{1,0:T(8,128)(2,1)S(1)}, u32[]{:S(2)}) copy-start(bf16[1024,256]{1,0:T(8,128)(2,1)S(1)} %collective-permute-done.17.refs_7_) | copy-start | bytes 1572868
  94.8 5.9 %copy-start.27 = (bf16[512,256]{1,0:T(8,128)(2,1)S(1)}, bf16[512,256]{1,0:T(8,128)(2,1)}, u32[]{:S(2)}) copy-start(bf16[512,256]{1,0:T(8,128)(2,1)} %copy-done.26) | copy-start | bytes 786436
  96.9 5.7 %copy-start.5 = (bf16[1024,256]{1,0:T(8,128)(2,1)S(1)}, bf16[1024,256]{1,0:T(8,128)(2,1)}, u32[]{:S(2)}) copy-start(bf16[1024,256]{1,0:T(8,128)(2,1)} %copy-done.4) | copy-start | bytes 1572868
  97.0 5.7 %copy-start.7 = (bf16[1024,256]{1,0:T(8,128)(2,1)S(1)}, bf16[1024,256]{1,0:T(8,128)(2,1)}, u32[]{:S(2)}) copy-start(bf16[1024,256]{1,0:T(8,128)(2,1)} %copy-done.6) | copy-start | bytes 1572868
  97.0 18.5 %all-to-all-start.1 = ((bf16[8,32,1024]{2,1,0:T(8,128)(2,1)}), bf16[8,32,1024]{2,1,0:T(8,128)(2,1)S(1)}, u32[]{:S(2)}, u32[]{:S(2)}) async-start(bf16[8,32,1024]{2,1,0:T(8,128)(2,1)} %bitcast.25), calls=%async_computation.1 | async-start | bytes 1048576 | tf_op jit(solution)/shard_map/all_to_all | solution.py:606
  100.7 1.6 %collective-permute-start.15 = (bf16[512,256]{1,0:T(8,128)(2,1)S(1)}, bf16[512,256]{1,0:T(8,128)(2,1)S(1)}, u32[]{:S(2)}, u32[]{:S(2)}) collective-permute-start(bf16[512,256]{1,0:T(8,128)(2,1)S(1)} %copy-done.27), channel_id=1, source_target_pairs={{0,8},{1,9},{2,10},{3,11},{4,12},{5,13},{6,14},{7,15},{8,0},{9,1},... | collective-permute-start | bytes 786440 | tf_op jit(solution)/shard_map/ppermute | solution.py:598
  100.8 1.9 %collective-permute-start.14 = (bf16[512,256]{1,0:T(8,128)(2,1)}, bf16[512,256]{1,0:T(8,128)(2,1)S(1)}, u32[]{:S(2)}, u32[]{:S(2)}) collective-permute-start(bf16[512,256]{1,0:T(8,128)(2,1)} %copy-done.28), channel_id=1, source_target_pairs={{0,8},{1,9},{2,10},{3,11},{4,12},{5,13},{6,14},{7,15},{8,0},{9,1},... | collective-permute-start | bytes 786440 | tf_op jit(solution)/shard_map/ppermute | solution.py:598
  102.7 1.0 copy-start.9
  103.7 0.9 copy-start.15
  104.7 0.9 copy-start.17
  (6 other events, 4.0 us)

commit v7 on v6

--- a/solution.py
+++ b/solution.py
@@ -634,9 +634,6 @@
 
     own = jnp.concatenate([qkv_weight, out_weight[None]], axis=0)
     own_a = lax.dynamic_slice_in_dim(own, y_half * half, half, 1)
-    later_qkv, later_out, own_a = lax.optimization_barrier((qkv_weight, out_weight, own_a))
-    later = jnp.concatenate([later_qkv, later_out[None]], axis=0)
-    own_b = lax.dynamic_slice_in_dim(later, (1 - y_half) * half, half, 1)
 
     def pick(for_core_0, for_core_1):
         return jnp.where(core == 0, for_core_0, for_core_1)
@@ -660,7 +657,7 @@
     scalars = jnp.stack(numbers).astype(jnp.int32)
 
     m1 = relocate(own_a, along_x, z_up)
-    m2 = relocate(pick(own_a, own_b), z_down, z_up)
+    m2 = relocate(own_a, z_down, None)
     l1 = relocate(language_weight, along_y, along_y)
 
     pad = 2 * RC
@@ -698,15 +695,16 @@
     other_ahead = swap_cores(ahead)
     other_memories = swap_cores(memories)
 
-    m3 = relocate(m1, along_y, along_x)
+    m3 = relocate(m1, along_y, along_y)
+    m3x = relocate(m1, None, along_x)
     m4 = relocate(m1, None, z_up)
-    m5 = relocate(m2, along_x, z_up)
-    m6 = relocate(m3, None, along_y)
+    m5 = relocate(pick(m2, m3), along_x, z_up)
+    m6 = relocate(m3x, None, along_y)
     m7 = relocate(pick(m2, m4), along_y, along_x)
     m8 = relocate(m5, along_y, along_x)
 
     slot_pieces = (
-        ((qkv_weight, m1), (out_weight, m2), (m1, m3), (m3, m6)),
+        ((qkv_weight, m1), (out_weight, m3), (m1, m3x), (m3, m6)),
         ((m2, m4), (m7, m5), (m5, m7), (m8, m8)),
     )
     block = 2 * C

time: 121 us -> 120 us (level)
  starting transfers between devices: 33.3 us -> 46.8 us
  waiting for transfers between devices: 45.2 us -> 36.4 us
  local copies, waits for them, and re-layouts: 10.2 us -> 4.44 us
    ppermute x22 -> x23, starting transfers between devices: 21.8 us -> 32.5 us  [relocate(): return lax.ppermute(value, ('rec', 'tm'), pairs)]
    ppermute x22 -> x23, waiting for transfers between devices: 27.6 us -> 21.2 us  [relocate(): return lax.ppermute(value, ('rec', 'tm'), pairs)]
    unnamed x58 -> x42, local copies, waits for them, and re-layouts: 9.32 us -> 4.23 us
    all_to_all x2, starting transfers between devices: 10.1 us -> 13 us  [exchange_blocks(): return lax.all_to_all(blocks, 'tm', split_axis=0, concat_axis=0, tiled=True)]
    ppermute x1, waiting for transfers between devices: 11.1 us -> 8.14 us  [shifted(): return lax.ppermute(block, axis, route)]
  transfers between devices with their start and end apart: 25 -> 26, of which waited for: 10 -> 9; matrix products, arithmetic and copies ran while one was open for 2% -> 1% of each run, Pallas kernels for 19% -> 19%
where the time goes in v7:
time: 120 us
  starting transfers between devices  46.8 us (39%)
  waiting for transfers between devices  36.4 us (30%)
  Pallas kernels  27.2 us (23%)
  local copies, waits for them, and re-layouts  4.44 us (4%)
  other arithmetic  3.01 us (3%)
  between operations  1.75 us (1%)
    ppermute x23, starting transfers between devices, relocate(): return lax.ppermute(value, ('rec', 'tm'), pairs)  32.5 us
    pallas_call x7, Pallas kernels, local_call(): pl.pallas_call(kernel, out_shape=out_shapes, in_specs=[smem_spec()] * len...  27.2 us
    ppermute x23, waiting for transfers between devices, relocate(): return lax.ppermute(value, ('rec', 'tm'), pairs)  21.2 us
    all_to_all x2, starting transfers between devices, exchange_blocks(): return lax.all_to_all(blocks, 'tm', split_axis=0, concat_axis=0, tiled=True)  13 us
    ppermute x1, waiting for transfers between devices, shifted(): return lax.ppermute(block, axis, route)  8.14 us
    all_to_all x2, waiting for transfers between devices, exchange_blocks(): return lax.all_to_all(blocks, 'tm', split_axis=0, concat_axis=0, tiled=True)  7.12 us
    unnamed x42, local copies, waits for them, and re-layouts  4.23 us
  transfers between devices with their start and end apart: 26, of which 9 were waited for; matrix products, arithmetic and copies ran while one was open for 1% of the time, Pallas kernels for 19%

profile of v7, /device:TPU:0, one launch (start us, length us, event | category | flops | bytes accessed | tf_op | source)
XLA Modules:
  0.0 119.7 jit_solution(18277065603830520194)
XLA Ops:
  0.7 1.9 %fusion = bf16[4,512,128]{2,1,0:T(8,128)(2,1)} fusion(s32[]{:T(128)S(6)} %select_n.78, bf16[3,1024,128]{2,1,0:T(8,128)(2,1)} %refs_8_.1, bf16[1,1024,128]{2,1,0:T(8,128)(2,1)} %bitcast.31), kind=kLoop, calls=%fused_computation.2 | loop fusion | flops 1048576 | bytes 1572868 | tf_op jit(solution)/shard_map/concatenate | solution.py:635
  2.6 3.0 %collective-permute-start.6 = (bf16[4,512,128]{2,1,0:T(8,128)(2,1)}, bf16[4,512,128]{2,1,0:T(8,128)(2,1)}, u32[]{:S(2)}, u32[]{:S(2)}) collective-permute-start(bf16[4,512,128]{2,1,0:T(8,128)(2,1)} %fusion), channel_id=1, source_target_pairs={{0,1},{1,0},{2,3},{3,2},{4,5},{5,4},{6,7},{7,6},{8,10},{9,11},{10,... | collective-permute-start | bytes 1572872 | tf_op jit(solution)/shard_map/ppermute | solution.py:598
  5.6 5.5 %collective-permute-start.10 = (bf16[4,512,128]{2,1,0:T(8,128)(2,1)}, bf16[4,512,128]{2,1,0:T(8,128)(2,1)S(1)}, u32[]{:S(2)}, u32[]{:S(2)}) collective-permute-start(bf16[4,512,128]{2,1,0:T(8,128)(2,1)} %fusion), channel_id=1, source_target_pairs={{0,6},{1,7},{2,0},{3,1},{4,2},{5,3},{6,4},{7,5},{16,22},{17,23},{1... | collective-permute-start | bytes 1572872 | tf_op jit(solution)/shard_map/ppermute | solution.py:598
  11.1 2.0 %collective-permute-done.6.refs_9_.refs_12_ = bf16[4,512,128]{2,1,0:T(8,128)(2,1)} collective-permute-done((bf16[4,512,128]{2,1,0:T(8,128)(2,1)}, bf16[4,512,128]{2,1,0:T(8,128)(2,1)}, u32[]{:S(2)}, u32[]{:S(2)}) %collective-permute-start.6) | collective-permute-done | bytes 524320 | tf_op jit(solution)/shard_map/ppermute | solution.py:598
  13.1 1.5 %collective-permute-start.11 = (bf16[4,512,128]{2,1,0:T(8,128)(2,1)}, bf16[4,512,128]{2,1,0:T(8,128)(2,1)}, u32[]{:S(2)}, u32[]{:S(2)}) collective-permute-start(bf16[4,512,128]{2,1,0:T(8,128)(2,1)} %collective-permute-done.6.refs_9_.refs_12_), channel_id=1, source_target_pairs={{8,10},{9,11},{10,12},{11,13},{12,14},{13,15},{14,8},{15,9},{24,26... | collective-permute-start | bytes 1572872 | tf_op jit(solution)/shard_map/ppermute | solution.py:598
  14.5 2.1 %collective-permute-start.7 = (bf16[4,512,128]{2,1,0:T(8,128)(2,1)}, bf16[4,512,128]{2,1,0:T(8,128)(2,1)S(1)}, u32[]{:S(2)}, u32[]{:S(2)}) collective-permute-start(bf16[4,512,128]{2,1,0:T(8,128)(2,1)} %collective-permute-done.6.refs_9_.refs_12_), channel_id=1, source_target_pairs={{0,16},{1,17},{2,18},{3,19},{4,20},{5,21},{6,22},{7,23},{8,24},{9,... | collective-permute-start | bytes 1572872 | tf_op jit(solution)/shard_map/ppermute | solution.py:598
  17.2 0.1 stack.63.scalars
  17.3 0.6 copy-done.16
  17.9 0.1 copy-done.15
  18.0 2.2 %shard_map.105 = (bf16[512,1024]{1,0:T(8,128)(2,1)S(1)}, bf16[16,1024]{1,0:T(8,128)(2,1)S(1)}, bf16[8,16,1024]{2,1,0:T(8,128)(2,1)}) custom-call(s32[17]{0:T(128)S(1)} %stack.63.scalars, bf16[512,1024]{1,0:T(8,128)(2,1)S(1)} %bitcast.27, f32[1,1024]{1,0:T(1,128)S(1)} %bitcast.32, f32[1,1024]{1,0:T(1,128)S(1)} %bitcast.33), custom_call_target="tpu_custom_call" | custom-call | flops 5242880 | bytes 2097152 | tf_op jit(solution)/shard_map/pallas_call | solution.py:269
  20.2 1.7 %collective-permute-start.3 = (bf16[512,1024]{1,0:T(8,128)(2,1)S(1)}, bf16[512,1024]{1,0:T(8,128)(2,1)}, u32[]{:S(2)}, u32[]{:S(2)}) collective-permute-start(bf16[512,1024]{1,0:T(8,128)(2,1)S(1)} %get-tuple-element.20.refs_2_), channel_id=1, source_target_pairs={{0,8},{1,9},{2,10},{3,11},{4,12},{5,13},{6,14},{7,15},{8,0},{9,1},... | collective-permute-start | bytes 3145736 | tf_op jit(solution)/shard_map/ppermute | solution.py:598
  21.9 8.9 %all-to-all-start = ((bf16[8,16,1024]{2,1,0:T(8,128)(2,1)}), bf16[8,16,1024]{2,1,0:T(8,128)(2,1)}, u32[]{:S(2)}, u32[]{:S(2)}) async-start(bf16[8,16,1024]{2,1,0:T(8,128)(2,1)} %get-tuple-element.22), calls=%async_computation | async-start | bytes 524288 | tf_op jit(solution)/shard_map/all_to_all | solution.py:606
  30.9 1.4 %collective-permute-start.8 = (bf16[4,512,128]{2,1,0:T(8,128)(2,1)}, bf16[4,512,128]{2,1,0:T(8,128)(2,1)}, u32[]{:S(2)}, u32[]{:S(2)}) collective-permute-start(bf16[4,512,128]{2,1,0:T(8,128)(2,1)} %collective-permute-done.6.refs_9_.refs_12_), channel_id=1, source_target_pairs={{8,9},{9,8},{10,11},{11,10},{12,13},{13,12},{14,15},{15,14},{24,25... | collective-permute-start | bytes 1572872 | tf_op jit(solution)/shard_map/ppermute | solution.py:598
  32.3 1.1 broadcast_select_fusion
  33.4 0.8 copy-done.2
  34.2 2.0 %collective-permute-start.13 = (bf16[4,512,128]{2,1,0:T(8,128)(2,1)}, bf16[4,512,128]{2,1,0:T(8,128)(2,1)}, u32[]{:S(2)}, u32[]{:S(2)}) collective-permute-start(bf16[4,512,128]{2,1,0:T(8,128)(2,1)} %get-tuple-element.36), channel_id=1, source_target_pairs={{0,1},{1,0},{2,3},{3,2},{4,5},{5,4},{6,7},{7,6},{8,10},{9,11},{10,... | collective-permute-start | bytes 1572872 | tf_op jit(solution)/shard_map/ppermute | solution.py:598
  36.2 1.3 %collective-permute-start.2 = (bf16[16,1024]{1,0:T(8,128)(2,1)S(1)}, bf16[16,1024]{1,0:T(8,128)(2,1)S(1)}, u32[]{:S(2)}, u32[]{:S(2)}) collective-permute-start(bf16[16,1024]{1,0:T(8,128)(2,1)S(1)} %get-tuple-element.21), channel_id=1, source_target_pairs={{1,0},{2,1},{3,2},{4,3},{5,4},{6,5},{7,6},{9,8},{10,9},{11,10},{12... | collective-permute-start | bytes 98312 | tf_op jit(solution)/shard_map/ppermute | solution.py:27
  37.5 1.9 %collective-permute-start = (s32[1]{0:T(128)}, s32[1]{0:T(128)}, u32[]{:S(2)}, u32[]{:S(2)}) collective-permute-start(s32[1]{0:T(128)} %param.10), channel_id=1, source_target_pairs={{0,8},{1,9},{2,10},{3,11},{4,12},{5,13},{6,14},{7,15},{8,0},{9,1},... | collective-permute-start | bytes 20 | tf_op jit(solution)/shard_map/ppermute | solution.py:598
  39.4 1.1 collective-permute-done.other_length
  40.5 0.3 collective-permute-start.5
  40.9 8.1 %collective-permute-done.2.refs_3_ = bf16[16,1024]{1,0:T(8,128)(2,1)S(1)} collective-permute-done((bf16[16,1024]{1,0:T(8,128)(2,1)S(1)}, bf16[16,1024]{1,0:T(8,128)(2,1)S(1)}, u32[]{:S(2)}, u32[]{:S(2)}) %collective-permute-start.2) | collective-permute-done | bytes 32800 | tf_op jit(solution)/shard_map/ppermute | solution.py:27
  49.0 1.5 %collective-permute-start.9 = (bf16[4,512,128]{2,1,0:T(8,128)(2,1)}, bf16[4,512,128]{2,1,0:T(8,128)(2,1)}, u32[]{:S(2)}, u32[]{:S(2)}) collective-permute-start(bf16[4,512,128]{2,1,0:T(8,128)(2,1)} %collective-permute-done.8.refs_13_), channel_id=1, source_target_pairs={{8,24},{9,25},{10,26},{11,27},{12,28},{13,29},{14,30},{15,31},{24,... | collective-permute-start | bytes 1572872 | tf_op jit(solution)/shard_map/ppermute | solution.py:598
  50.5 0.1 copy.11.owners_col
  50.6 0.9 shard_map.104
  51.5 1.2 %collective-permute-start.1 = (bf16[128,512]{1,0:T(8,128)(2,1)S(1)}, bf16[128,512]{1,0:T(8,128)(2,1)S(1)}, u32[]{:S(2)}, u32[]{:S(2)}) collective-permute-start(bf16[128,512]{1,0:T(8,128)(2,1)S(1)} %get-tuple-element.19.refs_0_), channel_id=1, source_target_pairs={{0,8},{1,9},{2,10},{3,11},{4,12},{5,13},{6,14},{7,15},{8,0},{9,1},... | collective-permute-start | bytes 393224 | tf_op jit(solution)/shard_map/ppermute | solution.py:598
  52.8 1.0 collective-permute-done.1.refs_1_
  53.8 1.5 %collective-permute-start.12 = (bf16[4,512,128]{2,1,0:T(8,128)(2,1)}, bf16[4,512,128]{2,1,0:T(8,128)(2,1)S(1)}, u32[]{:S(2)}, u32[]{:S(2)}) collective-permute-start(bf16[4,512,128]{2,1,0:T(8,128)(2,1)} %get-tuple-element.37), channel_id=1, source_target_pairs={{0,16},{1,17},{2,18},{3,19},{4,20},{5,21},{6,22},{7,23},{8,9},{9,8... | collective-permute-start | bytes 1572872 | tf_op jit(solution)/shard_map/ppermute | solution.py:598
  55.3 0.5 collective-permute-start.14
  55.8 1.5 %collective-permute-start.22 = (bf16[1024,512]{1,0:T(8,128)(2,1)}, bf16[1024,512]{1,0:T(8,128)(2,1)}, u32[]{:S(2)}, u32[]{:S(2)}) collective-permute-start(bf16[1024,512]{1,0:T(8,128)(2,1)} %refs_0_.1), channel_id=1, source_target_pairs={{0,16},{1,17},{2,18},{3,19},{4,20},{5,21},{6,22},{7,23},{8,24},{9,... | collective-permute-start | bytes 3145736 | tf_op jit(solution)/shard_map/ppermute | solution.py:598
  57.3 7.1 %shard_map.106 = (bf16[512,256]{1,0:T(8,128)(2,1)S(1)}, bf16[512,256]{1,0:T(8,128)(2,1)S(1)}, f32[128,256]{1,0:T(8,128)S(1)}, f32[128,256]{1,0:T(8,128)S(1)}, bf16[1024,256]{1,0:T(8,128)(2,1)S(1)}) custom-call(s32[17]{0:T(128)S(1)} %stack.63.scalars, s32[1]{0:T(128)} %collective-permute-done.other_length, bf16[128,512]{1,0:T(8,128)(2,1)S(1)} %get-tuple-element.19.refs_0_, ...), custom_call_target="tpu_custom_call" | custom-call | flops 1610612736 | bytes 4194304 | tf_op jit(solution)/shard_map/pallas_call | solution.py:269
  64.5 0.7 copy-done.11
  65.2 5.2 %collective-permute-start.17 = (bf16[1024,256]{1,0:T(8,128)(2,1)S(1)}, bf16[1024,256]{1,0:T(8,128)(2,1)S(1)}, u32[]{:S(2)}, u32[]{:S(2)}) collective-permute-start(bf16[1024,256]{1,0:T(8,128)(2,1)S(1)} %get-tuple-element.27.refs_4_), channel_id=1, source_target_pairs={{0,8},{1,9},{2,10},{3,11},{4,12},{5,13},{6,14},{7,15},{8,0},{9,1},... | collective-permute-start | bytes 1572872 | tf_op jit(solution)/shard_map/ppermute | solution.py:598
  70.3 9.7 %collective-permute-done.14.refs_14_.refs_15_ = bf16[4,512,128]{2,1,0:T(8,128)(2,1)S(1)} collective-permute-done((bf16[4,512,128]{2,1,0:T(8,128)(2,1)}, bf16[4,512,128]{2,1,0:T(8,128)(2,1)S(1)}, u32[]{:S(2)}, u32[]{:S(2)}) %collective-permute-start.14) | collective-permute-done | bytes 524320 | tf_op jit(solution)/shard_map/ppermute | solution.py:598
  80.0 7.1 %shard_map.107 = (bf16[512,256]{1,0:T(8,128)(2,1)S(1)}, bf16[512,256]{1,0:T(8,128)(2,1)S(1)}, f32[128,256]{1,0:T(8,128)S(1)}, f32[128,256]{1,0:T(8,128)S(1)}, bf16[1024,256]{1,0:T(8,128)(2,1)S(1)}) custom-call(s32[17]{0:T(128)S(1)} %stack.63.scalars, s32[1]{0:T(128)} %collective-permute-done.other_length, bf16[128,512]{1,0:T(8,128)(2,1)S(1)} %get-tuple-element.19.refs_0_, ...), custom_call_target="tpu_custom_call" | custom-call | flops 1610612736 | bytes 4194304 | tf_op jit(solution)/shard_map/pallas_call | solution.py:269
  87.3 0.5 collective-permute-start.19
  87.7 0.1 collective-permute-start.20
  87.8 5.8 %collective-permute-done.22.refs_2_ = bf16[1024,512]{1,0:T(8,128)(2,1)} collective-permute-done((bf16[1024,512]{1,0:T(8,128)(2,1)}, bf16[1024,512]{1,0:T(8,128)(2,1)}, u32[]{:S(2)}, u32[]{:S(2)}) %collective-permute-start.22) | collective-permute-done | bytes 1048608 | tf_op jit(solution)/shard_map/ppermute | solution.py:598
  93.7 0.5 collective-permute-start.23
  94.2 2.2 %shard_map.109 = bf16[256,1024]{1,0:T(8,128)(2,1)} custom-call(s32[17]{0:T(128)S(1)} %stack.63.scalars, f32[128,1024]{1,0:T(8,128)S(1)} %get-tuple-element.29.base, f32[128,128]{1,0:T(8,128)S(1)} %get-tuple-element.30.inverse, bf16[256,128]{1,0:T(8,128)(2,1)S(1)} %get-tuple-element.31.route, f32[128,256]{1,0:T(8,128)S(1)} %get-tuple-element.32.refs_0_, ...), custom_call_target="tpu_custom_call" | custom-call | flops 536870912 | bytes 3145728 | tf_op jit(solution)/shard_map/pallas_call | solution.py:269
  96.4 4.1 %all-to-all-start.1 = ((bf16[8,32,1024]{2,1,0:T(8,128)(2,1)}), bf16[8,32,1024]{2,1,0:T(8,128)(2,1)S(1)}, u32[]{:S(2)}, u32[]{:S(2)}) async-start(bf16[8,32,1024]{2,1,0:T(8,128)(2,1)} %bitcast.24), calls=%async_computation.1 | async-start | bytes 1048576 | tf_op jit(solution)/shard_map/all_to_all | solution.py:606
  100.6 0.5 collective-permute-start.16
  101.1 1.2 %collective-permute-done.15.refs_2_ = bf16[512,256]{1,0:T(8,128)(2,1)S(1)} collective-permute-done((bf16[512,256]{1,0:T(8,128)(2,1)}, bf16[512,256]{1,0:T(8,128)(2,1)S(1)}, u32[]{:S(2)}, u32[]{:S(2)}) %collective-permute-start.15) | collective-permute-done | bytes 262176 | tf_op jit(solution)/shard_map/ppermute | solution.py:598
  102.3 0.4 collective-permute-done.16.refs_3_
  102.7 1.0 copy-done.9
  103.7 0.9 copy-done.14
  104.7 3.4 %shard_map.108 = bf16[512,1024]{1,0:T(8,128)(2,1)} custom-call(s32[17]{0:T(128)S(1)} %stack.63.scalars, bf16[512,256]{1,0:T(8,128)(2,1)S(1)} %copy-done.12, bf16[512,256]{1,0:T(8,128)(2,1)S(1)} %copy-done.14, bf16[512,256]{1,0:T(8,128)(2,1)S(1)} %collective-permute-done.15.refs_2_, bf16[512,256]{1,0:T(8,128)(2,1)S(1)} %collective-permute-done.16.refs_3_, ...), custom_call_target="tpu_custom_call" | custom-call | flops 1073741824 | bytes 3145728 | tf_op jit(solution)/shard_map/pallas_call | solution.py:269
  108.1 7.1 %all-to-all-done.1 = bf16[8,32,1024]{2,1,0:T(8,128)(2,1)S(1)} async-done(((bf16[8,32,1024]{2,1,0:T(8,128)(2,1)}), bf16[8,32,1024]{2,1,0:T(8,128)(2,1)S(1)}, u32[]{:S(2)}, u32[]{:S(2)}) %all-to-all-start.1) | async-done | bytes 524320 | tf_op jit(solution)/shard_map/all_to_all | solution.py:606
  115.2 4.3 %shard_map.110 = bf16[256,2048]{1,0:T(8,128)(2,1)} custom-call(s32[17]{0:T(128)S(1)} %stack.63.scalars, bf16[256,1024]{1,0:T(8,128)(2,1)S(1)} %bitcast.30, bf16[1024,512]{1,0:T(8,128)(2,1)} %refs_0_.1, bf16[1024,512]{1,0:T(8,128)(2,1)} %collective-permute-done.21.refs_1_, bf16[1024,512]{1,0:T(8,128)(2,1)} %collective-permute-done.22.refs_2_, ...), custom_call_target="tpu_custom_call" | custom-call | flops 1073741824 | bytes 4194304 | tf_op jit(solution)/shard_map/pallas_call | solution.py:269
  (57 shorter events, 0.2 us)
Async XLA Ops:
  0.6 16.7 %copy-start = (bf16[1,512,1024]{2,1,0:T(8,128)(2,1)S(1)}, bf16[1,512,1024]{2,1,0:T(8,128)(2,1)}, u32[]{:S(2)}) copy-start(bf16[1,512,1024]{2,1,0:T(8,128)(2,1)} %param.9) | copy-start | bytes 3145732
  2.6 10.4 %collective-permute-start.6 = (bf16[4,512,128]{2,1,0:T(8,128)(2,1)}, bf16[4,512,128]{2,1,0:T(8,128)(2,1)}, u32[]{:S(2)}, u32[]{:S(2)}) collective-permute-start(bf16[4,512,128]{2,1,0:T(8,128)(2,1)} %fusion), channel_id=1, source_target_pairs={{0,1},{1,0},{2,3},{3,2},{4,5},{5,4},{6,7},{7,6},{8,10},{9,11},{10,... | collective-permute-start | bytes 1572872 | tf_op jit(solution)/shard_map/ppermute | solution.py:598
  5.6 26.7 %collective-permute-start.10 = (bf16[4,512,128]{2,1,0:T(8,128)(2,1)}, bf16[4,512,128]{2,1,0:T(8,128)(2,1)S(1)}, u32[]{:S(2)}, u32[]{:S(2)}) collective-permute-start(bf16[4,512,128]{2,1,0:T(8,128)(2,1)} %fusion), channel_id=1, source_target_pairs={{0,6},{1,7},{2,0},{3,1},{4,2},{5,3},{6,4},{7,5},{16,22},{17,23},{1... | collective-permute-start | bytes 1572872 | tf_op jit(solution)/shard_map/ppermute | solution.py:598
  13.1 19.2 %collective-permute-start.11 = (bf16[4,512,128]{2,1,0:T(8,128)(2,1)}, bf16[4,512,128]{2,1,0:T(8,128)(2,1)}, u32[]{:S(2)}, u32[]{:S(2)}) collective-permute-start(bf16[4,512,128]{2,1,0:T(8,128)(2,1)} %collective-permute-done.6.refs_9_.refs_12_), channel_id=1, source_target_pairs={{8,10},{9,11},{10,12},{11,13},{12,14},{13,15},{14,8},{15,9},{24,26... | collective-permute-start | bytes 1572872 | tf_op jit(solution)/shard_map/ppermute | solution.py:598
  14.5 17.8 %collective-permute-start.7 = (bf16[4,512,128]{2,1,0:T(8,128)(2,1)}, bf16[4,512,128]{2,1,0:T(8,128)(2,1)S(1)}, u32[]{:S(2)}, u32[]{:S(2)}) collective-permute-start(bf16[4,512,128]{2,1,0:T(8,128)(2,1)} %collective-permute-done.6.refs_9_.refs_12_), channel_id=1, source_target_pairs={{0,16},{1,17},{2,18},{3,19},{4,20},{5,21},{6,22},{7,23},{8,24},{9,... | collective-permute-start | bytes 1572872 | tf_op jit(solution)/shard_map/ppermute | solution.py:598
  17.2 0.7 copy-start.16
  17.3 0.7 copy-start.15
  20.2 37.1 %collective-permute-start.3 = (bf16[512,1024]{1,0:T(8,128)(2,1)S(1)}, bf16[512,1024]{1,0:T(8,128)(2,1)}, u32[]{:S(2)}, u32[]{:S(2)}) collective-permute-start(bf16[512,1024]{1,0:T(8,128)(2,1)S(1)} %get-tuple-element.20.refs_2_), channel_id=1, source_target_pairs={{0,8},{1,9},{2,10},{3,11},{4,12},{5,13},{6,14},{7,15},{8,0},{9,1},... | collective-permute-start | bytes 3145736 | tf_op jit(solution)/shard_map/ppermute | solution.py:598
  21.9 18.6 %all-to-all-start = ((bf16[8,16,1024]{2,1,0:T(8,128)(2,1)}), bf16[8,16,1024]{2,1,0:T(8,128)(2,1)}, u32[]{:S(2)}, u32[]{:S(2)}) async-start(bf16[8,16,1024]{2,1,0:T(8,128)(2,1)} %get-tuple-element.22), calls=%async_computation | async-start | bytes 524288 | tf_op jit(solution)/shard_map/all_to_all | solution.py:606
  30.9 18.2 %collective-permute-start.8 = (bf16[4,512,128]{2,1,0:T(8,128)(2,1)}, bf16[4,512,128]{2,1,0:T(8,128)(2,1)}, u32[]{:S(2)}, u32[]{:S(2)}) collective-permute-start(bf16[4,512,128]{2,1,0:T(8,128)(2,1)} %collective-permute-done.6.refs_9_.refs_12_), channel_id=1, source_target_pairs={{8,9},{9,8},{10,11},{11,10},{12,13},{13,12},{14,15},{15,14},{24,25... | collective-permute-start | bytes 1572872 | tf_op jit(solution)/shard_map/ppermute | solution.py:598
  32.3 18.2 %copy-start.17 = (s32[1,1,128,1]{2,3,1,0:T(1,128)S(1)}, s32[1,1,128,1]{2,3,1,0:T(1,128)}, u32[]{:S(2)}) copy-start(s32[1,1,128,1]{2,3,1,0:T(1,128)} %param.16) | copy-start | bytes 1540
  32.3 18.3 %copy-start.18 = (s32[1,1,512]{2,1,0:T(1,128)S(1)}, s32[1,1,512]{2,1,0:T(1,128)}, u32[]{:S(2)}) copy-start(s32[1,1,512]{2,1,0:T(1,128)} %param.15) | copy-start | bytes 6148
  33.4 0.8 copy-start.2
  34.2 23.1 %copy-start.1 = (bf16[3,1024,128]{2,1,0:T(8,128)(2,1)S(1)}, bf16[3,1024,128]{2,1,0:T(8,128)(2,1)}, u32[]{:S(2)}) copy-start(bf16[3,1024,128]{2,1,0:T(8,128)(2,1)} %refs_8_.1) | copy-start | bytes 2359300
  34.2 21.1 %collective-permute-start.13 = (bf16[4,512,128]{2,1,0:T(8,128)(2,1)}, bf16[4,512,128]{2,1,0:T(8,128)(2,1)}, u32[]{:S(2)}, u32[]{:S(2)}) collective-permute-start(bf16[4,512,128]{2,1,0:T(8,128)(2,1)} %get-tuple-element.36), channel_id=1, source_target_pairs={{0,1},{1,0},{2,3},{3,2},{4,5},{5,4},{6,7},{7,6},{8,10},{9,11},{10,... | collective-permute-start | bytes 1572872 | tf_op jit(solution)/shard_map/ppermute | solution.py:598
  36.2 12.8 %collective-permute-start.2 = (bf16[16,1024]{1,0:T(8,128)(2,1)S(1)}, bf16[16,1024]{1,0:T(8,128)(2,1)S(1)}, u32[]{:S(2)}, u32[]{:S(2)}) collective-permute-start(bf16[16,1024]{1,0:T(8,128)(2,1)S(1)} %get-tuple-element.21), channel_id=1, source_target_pairs={{1,0},{2,1},{3,2},{4,3},{5,4},{6,5},{7,6},{9,8},{10,9},{11,10},{12... | collective-permute-start | bytes 98312 | tf_op jit(solution)/shard_map/ppermute | solution.py:27
  37.5 3.0 %collective-permute-start = (s32[1]{0:T(128)}, s32[1]{0:T(128)}, u32[]{:S(2)}, u32[]{:S(2)}) collective-permute-start(s32[1]{0:T(128)} %param.10), channel_id=1, source_target_pairs={{0,8},{1,9},{2,10},{3,11},{4,12},{5,13},{6,14},{7,15},{8,0},{9,1},... | collective-permute-start | bytes 20 | tf_op jit(solution)/shard_map/ppermute | solution.py:598
  40.5 15.3 %collective-permute-start.5 = (bf16[128,1024]{1,0:T(8,128)(2,1)}, bf16[128,1024]{1,0:T(8,128)(2,1)}, u32[]{:S(2)}, u32[]{:S(2)}) collective-permute-start(bf16[128,1024]{1,0:T(8,128)(2,1)} %bitcast.21.refs_4_), channel_id=1, source_target_pairs={{0,8},{1,9},{2,10},{3,11},{4,12},{5,13},{6,14},{7,15},{8,0},{9,1},... | collective-permute-start | bytes 786440 | tf_op jit(solution)/shard_map/ppermute | solution.py:598
  49.0 2.5 %collective-permute-start.4 = (bf16[16,1024]{1,0:T(8,128)(2,1)S(1)}, bf16[16,1024]{1,0:T(8,128)(2,1)S(1)}, u32[]{:S(2)}, u32[]{:S(2)}) collective-permute-start(bf16[16,1024]{1,0:T(8,128)(2,1)S(1)} %collective-permute-done.2.refs_3_), channel_id=1, source_target_pairs={{0,8},{1,9},{2,10},{3,11},{4,12},{5,13},{6,14},{7,15},{8,0},{9,1},... | collective-permute-start | bytes 98312 | tf_op jit(solution)/shard_map/ppermute | solution.py:598
  49.0 8.3 %collective-permute-start.9 = (bf16[4,512,128]{2,1,0:T(8,128)(2,1)}, bf16[4,512,128]{2,1,0:T(8,128)(2,1)}, u32[]{:S(2)}, u32[]{:S(2)}) collective-permute-start(bf16[4,512,128]{2,1,0:T(8,128)(2,1)} %collective-permute-done.8.refs_13_), channel_id=1, source_target_pairs={{8,24},{9,25},{10,26},{11,27},{12,28},{13,29},{14,30},{15,31},{24,... | collective-permute-start | bytes 1572872 | tf_op jit(solution)/shard_map/ppermute | solution.py:598
  50.6 6.7 %copy-start.10 = (bf16[1024,128]{1,0:T(8,128)(2,1)S(1)}, bf16[1024,128]{1,0:T(8,128)(2,1)}, u32[]{:S(2)}) copy-start(bf16[1024,128]{1,0:T(8,128)(2,1)} %refs_10_.1) | copy-start | bytes 786436
  51.5 2.2 %collective-permute-start.1 = (bf16[128,512]{1,0:T(8,128)(2,1)S(1)}, bf16[128,512]{1,0:T(8,128)(2,1)S(1)}, u32[]{:S(2)}, u32[]{:S(2)}) collective-permute-start(bf16[128,512]{1,0:T(8,128)(2,1)S(1)} %get-tuple-element.19.refs_0_), channel_id=1, source_target_pairs={{0,8},{1,9},{2,10},{3,11},{4,12},{5,13},{6,14},{7,15},{8,0},{9,1},... | collective-permute-start | bytes 393224 | tf_op jit(solution)/shard_map/ppermute | solution.py:598
  53.8 26.2 %copy-start.3 = (bf16[4,512,128]{2,1,0:T(8,128)(2,1)S(1)}, bf16[4,512,128]{2,1,0:T(8,128)(2,1)}, u32[]{:S(2)}) copy-start(bf16[4,512,128]{2,1,0:T(8,128)(2,1)} %copy-done.2) | copy-start | bytes 1572868
  53.8 16.6 %collective-permute-start.12 = (bf16[4,512,128]{2,1,0:T(8,128)(2,1)}, bf16[4,512,128]{2,1,0:T(8,128)(2,1)S(1)}, u32[]{:S(2)}, u32[]{:S(2)}) collective-permute-start(bf16[4,512,128]{2,1,0:T(8,128)(2,1)} %get-tuple-element.37), channel_id=1, source_target_pairs={{0,16},{1,17},{2,18},{3,19},{4,20},{5,21},{6,22},{7,23},{8,9},{9,8... | collective-permute-start | bytes 1572872 | tf_op jit(solution)/shard_map/ppermute | solution.py:598
  55.3 24.7 %collective-permute-start.14 = (bf16[4,512,128]{2,1,0:T(8,128)(2,1)}, bf16[4,512,128]{2,1,0:T(8,128)(2,1)S(1)}, u32[]{:S(2)}, u32[]{:S(2)}) collective-permute-start(bf16[4,512,128]{2,1,0:T(8,128)(2,1)} %collective-permute-done.13.refs_11_.refs_12_), channel_id=1, source_target_pairs={{0,16},{1,17},{2,18},{3,19},{4,20},{5,21},{6,22},{7,23},{8,9},{9,8... | collective-permute-start | bytes 1572872 | tf_op jit(solution)/shard_map/ppermute | solution.py:598
  55.8 37.9 %collective-permute-start.22 = (bf16[1024,512]{1,0:T(8,128)(2,1)}, bf16[1024,512]{1,0:T(8,128)(2,1)}, u32[]{:S(2)}, u32[]{:S(2)}) collective-permute-start(bf16[1024,512]{1,0:T(8,128)(2,1)} %refs_0_.1), channel_id=1, source_target_pairs={{0,16},{1,17},{2,18},{3,19},{4,20},{5,21},{6,22},{7,23},{8,24},{9,... | collective-permute-start | bytes 3145736 | tf_op jit(solution)/shard_map/ppermute | solution.py:598
  64.4 0.7 copy-start.11
  65.2 22.0 %copy-start.19 = (bf16[512,256]{1,0:T(8,128)(2,1)}, bf16[512,256]{1,0:T(8,128)(2,1)S(1)}, u32[]{:S(2)}) copy-start(bf16[512,256]{1,0:T(8,128)(2,1)S(1)} %get-tuple-element.25) | copy-start | bytes 786436
  65.2 29.0 %copy-start.4 = (bf16[1024,256]{1,0:T(8,128)(2,1)}, bf16[1024,256]{1,0:T(8,128)(2,1)S(1)}, u32[]{:S(2)}) copy-start(bf16[1024,256]{1,0:T(8,128)(2,1)S(1)} %get-tuple-element.27.refs_4_) | copy-start | bytes 1572868
  65.2 29.0 %collective-permute-start.17 = (bf16[1024,256]{1,0:T(8,128)(2,1)S(1)}, bf16[1024,256]{1,0:T(8,128)(2,1)S(1)}, u32[]{:S(2)}, u32[]{:S(2)}) collective-permute-start(bf16[1024,256]{1,0:T(8,128)(2,1)S(1)} %get-tuple-element.27.refs_4_), channel_id=1, source_target_pairs={{0,8},{1,9},{2,10},{3,11},{4,12},{5,13},{6,14},{7,15},{8,0},{9,1},... | collective-permute-start | bytes 1572872 | tf_op jit(solution)/shard_map/ppermute | solution.py:598
  87.1 7.0 %copy-start.20 = (bf16[512,256]{1,0:T(8,128)(2,1)}, bf16[512,256]{1,0:T(8,128)(2,1)S(1)}, u32[]{:S(2)}) copy-start(bf16[512,256]{1,0:T(8,128)(2,1)S(1)} %get-tuple-element.26) | copy-start | bytes 786436
  87.2 9.2 %copy-start.6 = (bf16[1024,256]{1,0:T(8,128)(2,1)}, bf16[1024,256]{1,0:T(8,128)(2,1)S(1)}, u32[]{:S(2)}) copy-start(bf16[1024,256]{1,0:T(8,128)(2,1)S(1)} %get-tuple-element.28.refs_5_) | copy-start | bytes 1572868
  87.2 9.2 %copy-start.13 = (bf16[512,256]{1,0:T(8,128)(2,1)}, bf16[512,256]{1,0:T(8,128)(2,1)S(1)}, u32[]{:S(2)}) copy-start(bf16[512,256]{1,0:T(8,128)(2,1)S(1)} %get-tuple-element.24.refs_1_) | copy-start | bytes 786436
  87.2 7.0 %collective-permute-start.18 = (bf16[1024,256]{1,0:T(8,128)(2,1)S(1)}, bf16[1024,256]{1,0:T(8,128)(2,1)S(1)}, u32[]{:S(2)}, u32[]{:S(2)}) collective-permute-start(bf16[1024,256]{1,0:T(8,128)(2,1)S(1)} %get-tuple-element.28.refs_5_), channel_id=1, source_target_pairs={{0,8},{1,9},{2,10},{3,11},{4,12},{5,13},{6,14},{7,15},{8,0},{9,1},... | collective-permute-start | bytes 1572872 | tf_op jit(solution)/shard_map/ppermute | solution.py:598
  87.3 6.4 %collective-permute-start.19 = (f32[128,256]{1,0:T(8,128)S(1)}, f32[128,256]{1,0:T(8,128)S(1)}, u32[]{:S(2)}, u32[]{:S(2)}) collective-permute-start(f32[128,256]{1,0:T(8,128)S(1)} %get-tuple-element.34), channel_id=1, source_target_pairs={{0,8},{1,9},{2,10},{3,11},{4,12},{5,13},{6,14},{7,15},{8,0},{9,1},... | collective-permute-start | bytes 393224 | tf_op jit(solution)/shard_map/ppermute | solution.py:598
  87.7 6.4 %collective-permute-start.20 = (f32[128,256]{1,0:T(8,128)S(1)}, f32[128,256]{1,0:T(8,128)S(1)}, u32[]{:S(2)}, u32[]{:S(2)}) collective-permute-start(f32[128,256]{1,0:T(8,128)S(1)} %get-tuple-element.35), channel_id=1, source_target_pairs={{0,8},{1,9},{2,10},{3,11},{4,12},{5,13},{6,14},{7,15},{8,0},{9,1},... | collective-permute-start | bytes 393224 | tf_op jit(solution)/shard_map/ppermute | solution.py:598
  93.6 14.5 %collective-permute-start.21 = (bf16[1024,512]{1,0:T(8,128)(2,1)}, bf16[1024,512]{1,0:T(8,128)(2,1)}, u32[]{:S(2)}, u32[]{:S(2)}) collective-permute-start(bf16[1024,512]{1,0:T(8,128)(2,1)} %refs_0_.1), channel_id=1, source_target_pairs={{0,8},{1,9},{2,10},{3,11},{4,12},{5,13},{6,14},{7,15},{8,0},{9,1},... | collective-permute-start | bytes 3145736 | tf_op jit(solution)/shard_map/ppermute | solution.py:598
  93.7 14.5 %collective-permute-start.23 = (bf16[1024,512]{1,0:T(8,128)(2,1)}, bf16[1024,512]{1,0:T(8,128)(2,1)}, u32[]{:S(2)}, u32[]{:S(2)}) collective-permute-start(bf16[1024,512]{1,0:T(8,128)(2,1)} %collective-permute-done.22.refs_2_), channel_id=1, source_target_pairs={{0,8},{1,9},{2,10},{3,11},{4,12},{5,13},{6,14},{7,15},{8,0},{9,1},... | collective-permute-start | bytes 3145736 | tf_op jit(solution)/shard_map/ppermute | solution.py:598
  94.2 2.2 %copy-start.8 = (bf16[1024,256]{1,0:T(8,128)(2,1)}, bf16[1024,256]{1,0:T(8,128)(2,1)S(1)}, u32[]{:S(2)}) copy-start(bf16[1024,256]{1,0:T(8,128)(2,1)S(1)} %collective-permute-done.18.refs_7_) | copy-start | bytes 1572868
  94.2 8.5 %copy-start.12 = (bf16[512,256]{1,0:T(8,128)(2,1)S(1)}, bf16[512,256]{1,0:T(8,128)(2,1)}, u32[]{:S(2)}) copy-start(bf16[512,256]{1,0:T(8,128)(2,1)} %copy-done.11) | copy-start | bytes 786436
  96.4 6.3 %copy-start.5 = (bf16[1024,256]{1,0:T(8,128)(2,1)S(1)}, bf16[1024,256]{1,0:T(8,128)(2,1)}, u32[]{:S(2)}) copy-start(bf16[1024,256]{1,0:T(8,128)(2,1)} %copy-done.4) | copy-start | bytes 1572868
  96.4 6.3 %copy-start.7 = (bf16[1024,256]{1,0:T(8,128)(2,1)S(1)}, bf16[1024,256]{1,0:T(8,128)(2,1)}, u32[]{:S(2)}) copy-start(bf16[1024,256]{1,0:T(8,128)(2,1)} %copy-done.6) | copy-start | bytes 1572868
  96.4 18.8 %all-to-all-start.1 = ((bf16[8,32,1024]{2,1,0:T(8,128)(2,1)}), bf16[8,32,1024]{2,1,0:T(8,128)(2,1)S(1)}, u32[]{:S(2)}, u32[]{:S(2)}) async-start(bf16[8,32,1024]{2,1,0:T(8,128)(2,1)} %bitcast.24), calls=%async_computation.1 | async-start | bytes 1048576 | tf_op jit(solution)/shard_map/all_to_all | solution.py:606
  100.6 1.7 %collective-permute-start.15 = (bf16[512,256]{1,0:T(8,128)(2,1)}, bf16[512,256]{1,0:T(8,128)(2,1)S(1)}, u32[]{:S(2)}, u32[]{:S(2)}) collective-permute-start(bf16[512,256]{1,0:T(8,128)(2,1)} %copy-done.19), channel_id=1, source_target_pairs={{0,8},{1,9},{2,10},{3,11},{4,12},{5,13},{6,14},{7,15},{8,0},{9,1},... | collective-permute-start | bytes 786440 | tf_op jit(solution)/shard_map/ppermute | solution.py:598
  100.6 2.1 %collective-permute-start.16 = (bf16[512,256]{1,0:T(8,128)(2,1)}, bf16[512,256]{1,0:T(8,128)(2,1)S(1)}, u32[]{:S(2)}, u32[]{:S(2)}) collective-permute-start(bf16[512,256]{1,0:T(8,128)(2,1)} %copy-done.20), channel_id=1, source_target_pairs={{0,8},{1,9},{2,10},{3,11},{4,12},{5,13},{6,14},{7,15},{8,0},{9,1},... | collective-permute-start | bytes 786440 | tf_op jit(solution)/shard_map/ppermute | solution.py:598
  102.7 1.0 copy-start.9
  103.7 0.9 copy-start.14

commit v8 on v6

--- a/solution.py
+++ b/solution.py
@@ -543,19 +543,22 @@
 
 
 def language_kernel(places_at, scalars, received, *refs):
-    pieces, out = refs[:-5], refs[-5]
-    weights, product, sems, out_sems = refs[-4:]
+    pieces, out = refs[:-6], refs[-6]
+    rows, weights, product, sems, out_sems = refs[-5:]
     count, width = len(pieces), pieces[0].shape[1]
+    row_copy = pltpu.make_async_copy(received, rows, sems.at[count])
+    row_copy.start()
     copies = [
         pltpu.make_async_copy(piece, weights.at[i], sems.at[i]) for i, piece in enumerate(pieces)
     ]
     for copy in copies:
         copy.start()
+    row_copy.wait()
     out_copies = []
     for i in range(count):
         copies[i].wait()
         product[i] = jnp.dot(
-            received[...], weights[i], preferred_element_type=jnp.float32
+            rows[...], weights[i], preferred_element_type=jnp.float32
         ).astype(jnp.bfloat16)
         place = pl.multiple_of(scalars[places_at + i], LANES)
         out_copies.append(
@@ -786,12 +789,14 @@
         shape_of(slot_count, rec_count * language_shard),
         (scalars,),
         (received, *language_pieces),
-        in_place=rec_count,
+        in_place=1 + rec_count,
         out_in_place=True,
+        vmem_mib=62,
         scratch=(
+            pltpu.VMEM((slot_count, model_width), bf16),
             pltpu.VMEM((rec_count, model_width, language_shard), bf16),
             pltpu.VMEM((rec_count, slot_count, language_shard), bf16),
-            pltpu.SemaphoreType.DMA((rec_count,)),
+            pltpu.SemaphoreType.DMA((rec_count + 1,)),
             pltpu.SemaphoreType.DMA((rec_count,)),
         ),
         flops=2 * slot_count * model_width * rec_count * language_shard,

time: 121 us -> 122 us (level)
  local copies, waits for them, and re-layouts: 10.2 us -> 8.53 us
  waiting for transfers between devices: 45.2 us -> 46.8 us
    unnamed x58 -> x60, local copies, waits for them, and re-layouts: 9.32 us -> 7.7 us
where the time goes in v8:
time: 122 us; the launch traced here: 121 us
  waiting for transfers between devices  46.8 us (38%)
  starting transfers between devices  33.7 us (28%)
  Pallas kernels  28 us (23%)
  local copies, waits for them, and re-layouts  8.53 us (7%)
  other arithmetic  2.14 us (2%)
  between operations  1.85 us (2%)
    ppermute x22, waiting for transfers between devices, relocate(): return lax.ppermute(value, ('rec', 'tm'), pairs)  28.2 us
    pallas_call x7, Pallas kernels, local_call(): pl.pallas_call(kernel, out_shape=out_shapes, in_specs=[smem_spec()] * len...  28 us
    ppermute x22, starting transfers between devices, relocate(): return lax.ppermute(value, ('rec', 'tm'), pairs)  21.7 us
    ppermute x1, waiting for transfers between devices, shifted(): return lax.ppermute(block, axis, route)  11.1 us
    all_to_all x2, starting transfers between devices, exchange_blocks(): return lax.all_to_all(blocks, 'tm', split_axis=0, concat_axis=0, tiled=True)  10.6 us
    unnamed x60, local copies, waits for them, and re-layouts  7.7 us
    all_to_all x2, waiting for transfers between devices, exchange_blocks(): return lax.all_to_all(blocks, 'tm', split_axis=0, concat_axis=0, tiled=True)  7.51 us
  transfers between devices with their start and end apart: 25, of which 10 were waited for; matrix products, arithmetic and copies ran while one was open for 2% of the time, Pallas kernels for 19%

profile of v8, /device:TPU:0, one launch (start us, length us, event | category | flops | bytes accessed | tf_op | source)
XLA Modules:
  0.0 121.0 jit_solution(16781698850317318287)
XLA Ops:
  0.7 1.2 fusion.2
  1.8 3.0 %collective-permute-start.6 = (bf16[4,512,128]{2,1,0:T(8,128)(2,1)S(1)}, bf16[4,512,128]{2,1,0:T(8,128)(2,1)}, u32[]{:S(2)}, u32[]{:S(2)}) collective-permute-start(bf16[4,512,128]{2,1,0:T(8,128)(2,1)S(1)} %fusion.2), channel_id=1, source_target_pairs={{0,1},{1,0},{2,3},{3,2},{4,5},{5,4},{6,7},{7,6},{8,10},{9,11},{10,... | collective-permute-start | bytes 1572872 | tf_op jit(solution)/shard_map/ppermute | solution.py:601
  4.9 0.9 fusion.1
  5.8 3.6 %collective-permute-start.7 = (bf16[4,512,128]{2,1,0:T(8,128)(2,1)}, bf16[4,512,128]{2,1,0:T(8,128)(2,1)S(1)}, u32[]{:S(2)}, u32[]{:S(2)}) collective-permute-start(bf16[4,512,128]{2,1,0:T(8,128)(2,1)} %fusion.1), channel_id=1, source_target_pairs={{0,6},{1,7},{2,0},{3,1},{4,2},{5,3},{6,4},{7,5},{8,10},{9,11},{10,... | collective-permute-start | bytes 1572872 | tf_op jit(solution)/shard_map/ppermute | solution.py:601
  9.4 2.7 %collective-permute-done.6.refs_9_.refs_12_ = bf16[4,512,128]{2,1,0:T(8,128)(2,1)} collective-permute-done((bf16[4,512,128]{2,1,0:T(8,128)(2,1)S(1)}, bf16[4,512,128]{2,1,0:T(8,128)(2,1)}, u32[]{:S(2)}, u32[]{:S(2)}) %collective-permute-start.6) | collective-permute-done | bytes 524320 | tf_op jit(solution)/shard_map/ppermute | solution.py:601
  12.1 1.5 %collective-permute-start.10 = (bf16[4,512,128]{2,1,0:T(8,128)(2,1)}, bf16[4,512,128]{2,1,0:T(8,128)(2,1)}, u32[]{:S(2)}, u32[]{:S(2)}) collective-permute-start(bf16[4,512,128]{2,1,0:T(8,128)(2,1)} %collective-permute-done.6.refs_9_.refs_12_), channel_id=1, source_target_pairs={{8,10},{9,11},{10,12},{11,13},{12,14},{13,15},{14,8},{15,9},{24,26... | collective-permute-start | bytes 1572872 | tf_op jit(solution)/shard_map/ppermute | solution.py:601
  14.4 0.5 copy-done.24
  15.1 1.5 %shard_map.105 = (bf16[512,1024]{1,0:T(8,128)(2,1)S(1)}, bf16[16,1024]{1,0:T(8,128)(2,1)S(1)}, bf16[8,16,1024]{2,1,0:T(8,128)(2,1)S(1)}) custom-call(s32[17]{0:T(128)S(1)} %stack.63.scalars, bf16[512,1024]{1,0:T(8,128)(2,1)S(1)} %bitcast.28, f32[1,1024]{1,0:T(1,128)S(1)} %bitcast.33, f32[1,1024]{1,0:T(1,128)S(1)} %bitcast.34), custom_call_target="tpu_custom_call" | custom-call | flops 5242880 | bytes 2097152 | tf_op jit(solution)/shard_map/pallas_call | solution.py:269
  16.6 0.7 copy-done.13
  17.3 6.3 %all-to-all-start = ((bf16[8,16,1024]{2,1,0:T(8,128)(2,1)}), bf16[8,16,1024]{2,1,0:T(8,128)(2,1)}, u32[]{:S(2)}, u32[]{:S(2)}) async-start(bf16[8,16,1024]{2,1,0:T(8,128)(2,1)} %copy-done.13), calls=%async_computation | async-start | bytes 524288 | tf_op jit(solution)/shard_map/all_to_all | solution.py:609
  23.6 3.4 %collective-permute-start.3 = (bf16[512,1024]{1,0:T(8,128)(2,1)S(1)}, bf16[512,1024]{1,0:T(8,128)(2,1)}, u32[]{:S(2)}, u32[]{:S(2)}) collective-permute-start(bf16[512,1024]{1,0:T(8,128)(2,1)S(1)} %get-tuple-element.23.refs_2_), channel_id=1, source_target_pairs={{0,8},{1,9},{2,10},{3,11},{4,12},{5,13},{6,14},{7,15},{8,0},{9,1},... | collective-permute-start | bytes 3145736 | tf_op jit(solution)/shard_map/ppermute | solution.py:601
  27.0 1.7 %collective-permute-start.12 = (bf16[4,512,128]{2,1,0:T(8,128)(2,1)S(1)}, bf16[4,512,128]{2,1,0:T(8,128)(2,1)}, u32[]{:S(2)}, u32[]{:S(2)}) collective-permute-start(bf16[4,512,128]{2,1,0:T(8,128)(2,1)S(1)} %collective-permute-done.7.refs_11_.refs_8_), channel_id=1, source_target_pairs={{0,1},{1,0},{2,3},{3,2},{4,5},{5,4},{6,7},{7,6},{8,10},{9,11},{10,... | collective-permute-start | bytes 1572872 | tf_op jit(solution)/shard_map/ppermute | solution.py:601
  28.7 1.5 %collective-permute-start.8 = (bf16[4,512,128]{2,1,0:T(8,128)(2,1)}, bf16[4,512,128]{2,1,0:T(8,128)(2,1)}, u32[]{:S(2)}, u32[]{:S(2)}) collective-permute-start(bf16[4,512,128]{2,1,0:T(8,128)(2,1)} %collective-permute-done.6.refs_9_.refs_12_), channel_id=1, source_target_pairs={{0,16},{1,17},{2,18},{3,19},{4,20},{5,21},{6,22},{7,23},{8,9},{9,8... | collective-permute-start | bytes 1572872 | tf_op jit(solution)/shard_map/ppermute | solution.py:601
  30.3 1.4 %collective-permute-done.other_length = s32[1]{0:T(128)} collective-permute-done((s32[1]{0:T(128)}, s32[1]{0:T(128)}, u32[]{:S(2)}, u32[]{:S(2)}) %collective-permute-start) | collective-permute-done | bytes 36 | tf_op jit(solution)/shard_map/ppermute | solution.py:601
  31.7 1.4 %collective-permute-start.2 = (bf16[16,1024]{1,0:T(8,128)(2,1)S(1)}, bf16[16,1024]{1,0:T(8,128)(2,1)}, u32[]{:S(2)}, u32[]{:S(2)}) collective-permute-start(bf16[16,1024]{1,0:T(8,128)(2,1)S(1)} %get-tuple-element.24), channel_id=1, source_target_pairs={{1,0},{2,1},{3,2},{4,3},{5,4},{6,5},{7,6},{9,8},{10,9},{11,10},{12... | collective-permute-start | bytes 98312 | tf_op jit(solution)/shard_map/ppermute | solution.py:27
  33.1 11.1 %collective-permute-done.2.refs_3_ = bf16[16,1024]{1,0:T(8,128)(2,1)} collective-permute-done((bf16[16,1024]{1,0:T(8,128)(2,1)S(1)}, bf16[16,1024]{1,0:T(8,128)(2,1)}, u32[]{:S(2)}, u32[]{:S(2)}) %collective-permute-start.2) | collective-permute-done | bytes 32800 | tf_op jit(solution)/shard_map/ppermute | solution.py:27
  44.2 0.3 collective-permute-start.4
  44.5 0.7 copy.11.owners_col
  45.3 0.7 copy-done.26
  46.0 0.8 copy-done.12
  46.8 0.9 shard_map.104
  47.7 0.8 copy-done.10
  48.5 0.6 copy-done.18
  49.1 0.6 copy-done.20
  49.9 0.3 collective-permute-start.5
  50.3 0.9 collective-permute-done.1.refs_1_
  51.2 1.5 %collective-permute-start.11 = (bf16[4,512,128]{2,1,0:T(8,128)(2,1)S(1)}, bf16[4,512,128]{2,1,0:T(8,128)(2,1)S(1)}, u32[]{:S(2)}, u32[]{:S(2)}) collective-permute-start(bf16[4,512,128]{2,1,0:T(8,128)(2,1)S(1)} %broadcast_select_fusion), channel_id=1, source_target_pairs={{0,16},{1,17},{2,18},{3,19},{4,20},{5,21},{6,22},{7,23},{8,9},{9,8... | collective-permute-start | bytes 1572872 | tf_op jit(solution)/shard_map/ppermute | solution.py:601
  52.7 0.5 collective-permute-start.13
  53.2 0.7 collective-permute-start.9
  53.9 1.6 %collective-permute-start.21 = (bf16[1024,512]{1,0:T(8,128)(2,1)}, bf16[1024,512]{1,0:T(8,128)(2,1)}, u32[]{:S(2)}, u32[]{:S(2)}) collective-permute-start(bf16[1024,512]{1,0:T(8,128)(2,1)} %refs_0_.1), channel_id=1, source_target_pairs={{0,16},{1,17},{2,18},{3,19},{4,20},{5,21},{6,22},{7,23},{8,24},{9,... | collective-permute-start | bytes 3145736 | tf_op jit(solution)/shard_map/ppermute | solution.py:601
  55.5 7.5 %collective-permute-done.11.refs_10_.refs_13_ = bf16[4,512,128]{2,1,0:T(8,128)(2,1)S(1)} collective-permute-done((bf16[4,512,128]{2,1,0:T(8,128)(2,1)S(1)}, bf16[4,512,128]{2,1,0:T(8,128)(2,1)S(1)}, u32[]{:S(2)}, u32[]{:S(2)}) %collective-permute-start.11) | collective-permute-done | bytes 524320 | tf_op jit(solution)/shard_map/ppermute | solution.py:601
  63.0 11.2 %collective-permute-done.13.refs_14_.refs_15_ = bf16[4,512,128]{2,1,0:T(8,128)(2,1)S(1)} collective-permute-done((bf16[4,512,128]{2,1,0:T(8,128)(2,1)}, bf16[4,512,128]{2,1,0:T(8,128)(2,1)S(1)}, u32[]{:S(2)}, u32[]{:S(2)}) %collective-permute-start.13) | collective-permute-done | bytes 524320 | tf_op jit(solution)/shard_map/ppermute | solution.py:601
  74.2 7.5 %shard_map.107 = (bf16[512,256]{1,0:T(8,128)(2,1)S(1)}, bf16[512,256]{1,0:T(8,128)(2,1)S(1)}, f32[128,256]{1,0:T(8,128)S(1)}, f32[128,256]{1,0:T(8,128)S(1)}, bf16[1024,256]{1,0:T(8,128)(2,1)S(1)}) custom-call(s32[17]{0:T(128)S(1)} %stack.63.scalars, s32[1]{0:T(128)} %collective-permute-done.other_length, bf16[128,512]{1,0:T(8,128)(2,1)S(1)} %get-tuple-element.22.refs_0_, ...), custom_call_target="tpu_custom_call" | custom-call | flops 1610612736 | bytes 4194304 | tf_op jit(solution)/shard_map/pallas_call | solution.py:269
  81.7 0.7 copy-done.27
  82.5 7.9 %shard_map.106 = (bf16[512,256]{1,0:T(8,128)(2,1)S(1)}, bf16[512,256]{1,0:T(8,128)(2,1)S(1)}, f32[128,256]{1,0:T(8,128)S(1)}, f32[128,256]{1,0:T(8,128)S(1)}, bf16[1024,256]{1,0:T(8,128)(2,1)S(1)}) custom-call(s32[17]{0:T(128)S(1)} %stack.63.scalars, s32[1]{0:T(128)} %collective-permute-done.other_length, bf16[128,512]{1,0:T(8,128)(2,1)S(1)} %get-tuple-element.22.refs_0_, ...), custom_call_target="tpu_custom_call" | custom-call | flops 1610612736 | bytes 4194304 | tf_op jit(solution)/shard_map/pallas_call | solution.py:269
  90.7 0.4 collective-permute-start.19
  91.2 3.0 %collective-permute-done.21.refs_2_ = bf16[1024,512]{1,0:T(8,128)(2,1)} collective-permute-done((bf16[1024,512]{1,0:T(8,128)(2,1)}, bf16[1024,512]{1,0:T(8,128)(2,1)}, u32[]{:S(2)}, u32[]{:S(2)}) %collective-permute-start.21) | collective-permute-done | bytes 1048608 | tf_op jit(solution)/shard_map/ppermute | solution.py:601
  94.2 0.5 collective-permute-start.22
  94.8 2.2 %shard_map.109 = bf16[256,1024]{1,0:T(8,128)(2,1)} custom-call(s32[17]{0:T(128)S(1)} %stack.63.scalars, f32[128,1024]{1,0:T(8,128)S(1)} %copy-done.11, f32[128,128]{1,0:T(8,128)S(1)} %copy-done.19, bf16[256,128]{1,0:T(8,128)(2,1)S(1)} %copy-done.21, f32[128,256]{1,0:T(8,128)S(1)} %get-tuple-element.38.refs_0_, f32[128,256]{1,0:T(8,128)S(1)} %get-tuple-element.39.refs_1_, ...), custom_call_target="tpu_custom_call" | custom-call | flops 536870912 | bytes 3145728 | tf_op jit(solution)/shard_map/pallas_call | solution.py:269
  97.0 4.3 %all-to-all-start.1 = ((bf16[8,32,1024]{2,1,0:T(8,128)(2,1)}), bf16[8,32,1024]{2,1,0:T(8,128)(2,1)}, u32[]{:S(2)}, u32[]{:S(2)}) async-start(bf16[8,32,1024]{2,1,0:T(8,128)(2,1)} %bitcast.25), calls=%async_computation.1 | async-start | bytes 1048576 | tf_op jit(solution)/shard_map/all_to_all | solution.py:609
  101.4 0.5 collective-permute-start.14
  101.9 1.0 collective-permute-done.15.refs_3_
  102.9 0.4 collective-permute-done.14.refs_2_
  103.3 1.0 copy-done.9
  104.4 0.9 copy-done.17
  105.3 3.4 %shard_map.108 = bf16[512,1024]{1,0:T(8,128)(2,1)} custom-call(s32[17]{0:T(128)S(1)} %stack.63.scalars, bf16[512,256]{1,0:T(8,128)(2,1)S(1)} %copy-done.17, bf16[512,256]{1,0:T(8,128)(2,1)S(1)} %copy-done.15, bf16[512,256]{1,0:T(8,128)(2,1)S(1)} %collective-permute-done.14.refs_2_, bf16[512,256]{1,0:T(8,128)(2,1)S(1)} %collective-permute-done.15.refs_3_, ...), custom_call_target="tpu_custom_call" | custom-call | flops 1073741824 | bytes 3145728 | tf_op jit(solution)/shard_map/pallas_call | solution.py:269
  108.8 7.5 %all-to-all-done.1 = bf16[8,32,1024]{2,1,0:T(8,128)(2,1)} async-done(((bf16[8,32,1024]{2,1,0:T(8,128)(2,1)}), bf16[8,32,1024]{2,1,0:T(8,128)(2,1)}, u32[]{:S(2)}, u32[]{:S(2)}) %all-to-all-start.1) | async-done | bytes 524320 | tf_op jit(solution)/shard_map/all_to_all | solution.py:609
  116.3 4.6 %shard_map.110 = bf16[256,2048]{1,0:T(8,128)(2,1)} custom-call(s32[17]{0:T(128)} %copy-done.22, bf16[256,1024]{1,0:T(8,128)(2,1)} %bitcast.26.received, bf16[1024,512]{1,0:T(8,128)(2,1)} %refs_0_.1, bf16[1024,512]{1,0:T(8,128)(2,1)} %collective-permute-done.20.refs_1_, bf16[1024,512]{1,0:T(8,128)(2,1)} %collective-permute-done.21.refs_2_, ...), custom_call_target="tpu_custom_call" | custom-call | flops 1073741824 | bytes 4194304 | tf_op jit(solution)/shard_map/pallas_call | solution.py:269
  (74 shorter events, 1.1 us)
Async XLA Ops:
  0.7 4.2 %copy-start.1 = (bf16[3,1024,128]{2,1,0:T(8,128)(2,1)S(1)}, bf16[3,1024,128]{2,1,0:T(8,128)(2,1)}, u32[]{:S(2)}) copy-start(bf16[3,1024,128]{2,1,0:T(8,128)(2,1)} %refs_8_.1) | copy-start | bytes 2359300
  0.7 4.2 %copy-start.2 = (bf16[1024,128]{1,0:T(8,128)(2,1)S(1)}, bf16[1024,128]{1,0:T(8,128)(2,1)}, u32[]{:S(2)}) copy-start(bf16[1024,128]{1,0:T(8,128)(2,1)} %refs_10_.1) | copy-start | bytes 786436
  1.8 10.3 %collective-permute-start.6 = (bf16[4,512,128]{2,1,0:T(8,128)(2,1)S(1)}, bf16[4,512,128]{2,1,0:T(8,128)(2,1)}, u32[]{:S(2)}, u32[]{:S(2)}) collective-permute-start(bf16[4,512,128]{2,1,0:T(8,128)(2,1)S(1)} %fusion.2), channel_id=1, source_target_pairs={{0,1},{1,0},{2,3},{3,2},{4,5},{5,4},{6,7},{7,6},{8,10},{9,11},{10,... | collective-permute-start | bytes 1572872 | tf_op jit(solution)/shard_map/ppermute | solution.py:601
  4.9 9.5 %copy-start = (bf16[1,512,1024]{2,1,0:T(8,128)(2,1)S(1)}, bf16[1,512,1024]{2,1,0:T(8,128)(2,1)}, u32[]{:S(2)}) copy-start(bf16[1,512,1024]{2,1,0:T(8,128)(2,1)} %param.9) | copy-start | bytes 3145732
  5.8 21.2 %collective-permute-start.7 = (bf16[4,512,128]{2,1,0:T(8,128)(2,1)}, bf16[4,512,128]{2,1,0:T(8,128)(2,1)S(1)}, u32[]{:S(2)}, u32[]{:S(2)}) collective-permute-start(bf16[4,512,128]{2,1,0:T(8,128)(2,1)} %fusion.1), channel_id=1, source_target_pairs={{0,6},{1,7},{2,0},{3,1},{4,2},{5,3},{6,4},{7,5},{8,10},{9,11},{10,... | collective-permute-start | bytes 1572872 | tf_op jit(solution)/shard_map/ppermute | solution.py:601
  12.1 37.8 %collective-permute-start.10 = (bf16[4,512,128]{2,1,0:T(8,128)(2,1)}, bf16[4,512,128]{2,1,0:T(8,128)(2,1)}, u32[]{:S(2)}, u32[]{:S(2)}) collective-permute-start(bf16[4,512,128]{2,1,0:T(8,128)(2,1)} %collective-permute-done.6.refs_9_.refs_12_), channel_id=1, source_target_pairs={{8,10},{9,11},{10,12},{11,13},{12,14},{13,15},{14,8},{15,9},{24,26... | collective-permute-start | bytes 1572872 | tf_op jit(solution)/shard_map/ppermute | solution.py:601
  14.4 89.0 %copy-start.22 = (s32[17]{0:T(128)}, s32[17]{0:T(128)S(1)}, u32[]{:S(2)}) copy-start(s32[17]{0:T(128)S(1)} %stack.63.scalars) | copy-start | bytes 208
  17.3 32.7 %all-to-all-start = ((bf16[8,16,1024]{2,1,0:T(8,128)(2,1)}), bf16[8,16,1024]{2,1,0:T(8,128)(2,1)}, u32[]{:S(2)}, u32[]{:S(2)}) async-start(bf16[8,16,1024]{2,1,0:T(8,128)(2,1)} %copy-done.13), calls=%async_computation | async-start | bytes 524288 | tf_op jit(solution)/shard_map/all_to_all | solution.py:609
  23.6 31.9 %collective-permute-start.3 = (bf16[512,1024]{1,0:T(8,128)(2,1)S(1)}, bf16[512,1024]{1,0:T(8,128)(2,1)}, u32[]{:S(2)}, u32[]{:S(2)}) collective-permute-start(bf16[512,1024]{1,0:T(8,128)(2,1)S(1)} %get-tuple-element.23.refs_2_), channel_id=1, source_target_pairs={{0,8},{1,9},{2,10},{3,11},{4,12},{5,13},{6,14},{7,15},{8,0},{9,1},... | collective-permute-start | bytes 3145736 | tf_op jit(solution)/shard_map/ppermute | solution.py:601
  27.0 25.7 %collective-permute-start.12 = (bf16[4,512,128]{2,1,0:T(8,128)(2,1)S(1)}, bf16[4,512,128]{2,1,0:T(8,128)(2,1)}, u32[]{:S(2)}, u32[]{:S(2)}) collective-permute-start(bf16[4,512,128]{2,1,0:T(8,128)(2,1)S(1)} %collective-permute-done.7.refs_11_.refs_8_), channel_id=1, source_target_pairs={{0,1},{1,0},{2,3},{3,2},{4,5},{5,4},{6,7},{7,6},{8,10},{9,11},{10,... | collective-permute-start | bytes 1572872 | tf_op jit(solution)/shard_map/ppermute | solution.py:601
  28.7 24.5 %collective-permute-start.8 = (bf16[4,512,128]{2,1,0:T(8,128)(2,1)}, bf16[4,512,128]{2,1,0:T(8,128)(2,1)}, u32[]{:S(2)}, u32[]{:S(2)}) collective-permute-start(bf16[4,512,128]{2,1,0:T(8,128)(2,1)} %collective-permute-done.6.refs_9_.refs_12_), channel_id=1, source_target_pairs={{0,16},{1,17},{2,18},{3,19},{4,20},{5,21},{6,22},{7,23},{8,9},{9,8... | collective-permute-start | bytes 1572872 | tf_op jit(solution)/shard_map/ppermute | solution.py:601
  30.3 1.4 %collective-permute-start = (s32[1]{0:T(128)}, s32[1]{0:T(128)}, u32[]{:S(2)}, u32[]{:S(2)}) collective-permute-start(s32[1]{0:T(128)} %param.10), channel_id=1, source_target_pairs={{0,8},{1,9},{2,10},{3,11},{4,12},{5,13},{6,14},{7,15},{8,0},{9,1},... | collective-permute-start | bytes 20 | tf_op jit(solution)/shard_map/ppermute | solution.py:601
  31.7 12.8 %copy-start.25 = (s32[1,1,128,1]{2,3,1,0:T(1,128)S(1)}, s32[1,1,128,1]{2,3,1,0:T(1,128)}, u32[]{:S(2)}) copy-start(s32[1,1,128,1]{2,3,1,0:T(1,128)} %param.16) | copy-start | bytes 1540
  31.7 12.5 %collective-permute-start.2 = (bf16[16,1024]{1,0:T(8,128)(2,1)S(1)}, bf16[16,1024]{1,0:T(8,128)(2,1)}, u32[]{:S(2)}, u32[]{:S(2)}) collective-permute-start(bf16[16,1024]{1,0:T(8,128)(2,1)S(1)} %get-tuple-element.24), channel_id=1, source_target_pairs={{1,0},{2,1},{3,2},{4,3},{5,4},{6,5},{7,6},{9,8},{10,9},{11,10},{12... | collective-permute-start | bytes 98312 | tf_op jit(solution)/shard_map/ppermute | solution.py:27
  44.2 5.5 %collective-permute-start.4 = (bf16[16,1024]{1,0:T(8,128)(2,1)}, bf16[16,1024]{1,0:T(8,128)(2,1)}, u32[]{:S(2)}, u32[]{:S(2)}) collective-permute-start(bf16[16,1024]{1,0:T(8,128)(2,1)} %collective-permute-done.2.refs_3_), channel_id=1, source_target_pairs={{0,8},{1,9},{2,10},{3,11},{4,12},{5,13},{6,14},{7,15},{8,0},{9,1},... | collective-permute-start | bytes 98312 | tf_op jit(solution)/shard_map/ppermute | solution.py:601
  46.0 0.8 copy-start.12
  47.7 0.8 copy-start.10
  49.7 1.5 %collective-permute-start.1 = (bf16[128,512]{1,0:T(8,128)(2,1)S(1)}, bf16[128,512]{1,0:T(8,128)(2,1)}, u32[]{:S(2)}, u32[]{:S(2)}) collective-permute-start(bf16[128,512]{1,0:T(8,128)(2,1)S(1)} %get-tuple-element.22.refs_0_), channel_id=1, source_target_pairs={{0,8},{1,9},{2,10},{3,11},{4,12},{5,13},{6,14},{7,15},{8,0},{9,1},... | collective-permute-start | bytes 393224 | tf_op jit(solution)/shard_map/ppermute | solution.py:601
  49.9 4.0 %collective-permute-start.5 = (bf16[128,1024]{1,0:T(8,128)(2,1)}, bf16[128,1024]{1,0:T(8,128)(2,1)S(1)}, u32[]{:S(2)}, u32[]{:S(2)}) collective-permute-start(bf16[128,1024]{1,0:T(8,128)(2,1)} %bitcast.21.refs_4_), channel_id=1, source_target_pairs={{0,8},{1,9},{2,10},{3,11},{4,12},{5,13},{6,14},{7,15},{8,0},{9,1},... | collective-permute-start | bytes 786440 | tf_op jit(solution)/shard_map/ppermute | solution.py:601
  50.3 32.2 %copy-start.3 = (bf16[1024,128]{1,0:T(8,128)(2,1)S(1)}, bf16[1024,128]{1,0:T(8,128)(2,1)}, u32[]{:S(2)}) copy-start(bf16[1024,128]{1,0:T(8,128)(2,1)} %refs_10_.1) | copy-start | bytes 786436
  51.2 11.8 %collective-permute-start.11 = (bf16[4,512,128]{2,1,0:T(8,128)(2,1)S(1)}, bf16[4,512,128]{2,1,0:T(8,128)(2,1)S(1)}, u32[]{:S(2)}, u32[]{:S(2)}) collective-permute-start(bf16[4,512,128]{2,1,0:T(8,128)(2,1)S(1)} %broadcast_select_fusion), channel_id=1, source_target_pairs={{0,16},{1,17},{2,18},{3,19},{4,20},{5,21},{6,22},{7,23},{8,9},{9,8... | collective-permute-start | bytes 1572872 | tf_op jit(solution)/shard_map/ppermute | solution.py:601
  52.7 21.5 %collective-permute-start.13 = (bf16[4,512,128]{2,1,0:T(8,128)(2,1)}, bf16[4,512,128]{2,1,0:T(8,128)(2,1)S(1)}, u32[]{:S(2)}, u32[]{:S(2)}) collective-permute-start(bf16[4,512,128]{2,1,0:T(8,128)(2,1)} %collective-permute-done.12.refs_11_.refs_12_), channel_id=1, source_target_pairs={{0,16},{1,17},{2,18},{3,19},{4,20},{5,21},{6,22},{7,23},{8,9},{9,8... | collective-permute-start | bytes 1572872 | tf_op jit(solution)/shard_map/ppermute | solution.py:601
  53.2 29.3 %collective-permute-start.9 = (bf16[4,512,128]{2,1,0:T(8,128)(2,1)}, bf16[4,512,128]{2,1,0:T(8,128)(2,1)S(1)}, u32[]{:S(2)}, u32[]{:S(2)}) collective-permute-start(bf16[4,512,128]{2,1,0:T(8,128)(2,1)} %collective-permute-done.8.refs_13_.refs_14_), channel_id=1, source_target_pairs={{8,24},{9,25},{10,26},{11,27},{12,28},{13,29},{14,30},{15,31},{24,... | collective-permute-start | bytes 1572872 | tf_op jit(solution)/shard_map/ppermute | solution.py:601
  53.9 40.3 %collective-permute-start.21 = (bf16[1024,512]{1,0:T(8,128)(2,1)}, bf16[1024,512]{1,0:T(8,128)(2,1)}, u32[]{:S(2)}, u32[]{:S(2)}) collective-permute-start(bf16[1024,512]{1,0:T(8,128)(2,1)} %refs_0_.1), channel_id=1, source_target_pairs={{0,16},{1,17},{2,18},{3,19},{4,20},{5,21},{6,22},{7,23},{8,24},{9,... | collective-permute-start | bytes 3145736 | tf_op jit(solution)/shard_map/ppermute | solution.py:601
  82.4 8.1 %copy-start.14 = (bf16[512,256]{1,0:T(8,128)(2,1)}, bf16[512,256]{1,0:T(8,128)(2,1)S(1)}, u32[]{:S(2)}) copy-start(bf16[512,256]{1,0:T(8,128)(2,1)S(1)} %get-tuple-element.30.refs_1_) | copy-start | bytes 786436
  82.4 12.3 %copy-start.4 = (bf16[1024,256]{1,0:T(8,128)(2,1)}, bf16[1024,256]{1,0:T(8,128)(2,1)S(1)}, u32[]{:S(2)}) copy-start(bf16[1024,256]{1,0:T(8,128)(2,1)S(1)} %get-tuple-element.34.refs_5_) | copy-start | bytes 1572868
  82.4 12.3 %copy-start.11 = (f32[128,1024]{1,0:T(8,128)S(1)}, f32[128,1024]{1,0:T(8,128)}, u32[]{:S(2)}) copy-start(f32[128,1024]{1,0:T(8,128)} %copy-done.10) | copy-start | bytes 1572868
  82.4 12.4 %copy-start.19 = (f32[128,128]{1,0:T(8,128)S(1)}, f32[128,128]{1,0:T(8,128)}, u32[]{:S(2)}) copy-start(f32[128,128]{1,0:T(8,128)} %copy-done.18) | copy-start | bytes 196612
  82.4 12.4 %copy-start.21 = (bf16[256,128]{1,0:T(8,128)(2,1)S(1)}, bf16[256,128]{1,0:T(8,128)(2,1)}, u32[]{:S(2)}) copy-start(bf16[256,128]{1,0:T(8,128)(2,1)} %copy-done.20) | copy-start | bytes 196612
  82.4 12.3 %collective-permute-start.17 = (bf16[1024,256]{1,0:T(8,128)(2,1)S(1)}, bf16[1024,256]{1,0:T(8,128)(2,1)S(1)}, u32[]{:S(2)}, u32[]{:S(2)}) collective-permute-start(bf16[1024,256]{1,0:T(8,128)(2,1)S(1)} %get-tuple-element.34.refs_5_), channel_id=1, source_target_pairs={{0,8},{1,9},{2,10},{3,11},{4,12},{5,13},{6,14},{7,15},{8,0},{9,1},... | collective-permute-start | bytes 1572872 | tf_op jit(solution)/shard_map/ppermute | solution.py:601
  90.5 6.5 %copy-start.8 = (bf16[1024,256]{1,0:T(8,128)(2,1)}, bf16[1024,256]{1,0:T(8,128)(2,1)S(1)}, u32[]{:S(2)}) copy-start(bf16[1024,256]{1,0:T(8,128)(2,1)S(1)} %get-tuple-element.33.refs_4_) | copy-start | bytes 1572868
  90.5 6.5 %copy-start.16 = (bf16[512,256]{1,0:T(8,128)(2,1)}, bf16[512,256]{1,0:T(8,128)(2,1)S(1)}, u32[]{:S(2)}) copy-start(bf16[512,256]{1,0:T(8,128)(2,1)S(1)} %get-tuple-element.29.refs_0_) | copy-start | bytes 786436
  90.5 6.5 %copy-start.29 = (bf16[512,256]{1,0:T(8,128)(2,1)}, bf16[512,256]{1,0:T(8,128)(2,1)S(1)}, u32[]{:S(2)}) copy-start(bf16[512,256]{1,0:T(8,128)(2,1)S(1)} %get-tuple-element.31) | copy-start | bytes 786436
  90.5 4.2 %collective-permute-start.16 = (bf16[1024,256]{1,0:T(8,128)(2,1)S(1)}, bf16[1024,256]{1,0:T(8,128)(2,1)S(1)}, u32[]{:S(2)}, u32[]{:S(2)}) collective-permute-start(bf16[1024,256]{1,0:T(8,128)(2,1)S(1)} %get-tuple-element.33.refs_4_), channel_id=1, source_target_pairs={{0,8},{1,9},{2,10},{3,11},{4,12},{5,13},{6,14},{7,15},{8,0},{9,1},... | collective-permute-start | bytes 1572872 | tf_op jit(solution)/shard_map/ppermute | solution.py:601
  90.7 3.5 %collective-permute-start.19 = (f32[128,256]{1,0:T(8,128)S(1)}, f32[128,256]{1,0:T(8,128)S(1)}, u32[]{:S(2)}, u32[]{:S(2)}) collective-permute-start(f32[128,256]{1,0:T(8,128)S(1)} %get-tuple-element.41), channel_id=1, source_target_pairs={{0,8},{1,9},{2,10},{3,11},{4,12},{5,13},{6,14},{7,15},{8,0},{9,1},... | collective-permute-start | bytes 393224 | tf_op jit(solution)/shard_map/ppermute | solution.py:601
  91.1 3.6 %collective-permute-start.18 = (f32[128,256]{1,0:T(8,128)S(1)}, f32[128,256]{1,0:T(8,128)S(1)}, u32[]{:S(2)}, u32[]{:S(2)}) collective-permute-start(f32[128,256]{1,0:T(8,128)S(1)} %get-tuple-element.40), channel_id=1, source_target_pairs={{0,8},{1,9},{2,10},{3,11},{4,12},{5,13},{6,14},{7,15},{8,0},{9,1},... | collective-permute-start | bytes 393224 | tf_op jit(solution)/shard_map/ppermute | solution.py:601
  94.2 14.6 %collective-permute-start.20 = (bf16[1024,512]{1,0:T(8,128)(2,1)}, bf16[1024,512]{1,0:T(8,128)(2,1)}, u32[]{:S(2)}, u32[]{:S(2)}) collective-permute-start(bf16[1024,512]{1,0:T(8,128)(2,1)} %refs_0_.1), channel_id=1, source_target_pairs={{0,8},{1,9},{2,10},{3,11},{4,12},{5,13},{6,14},{7,15},{8,0},{9,1},... | collective-permute-start | bytes 3145736 | tf_op jit(solution)/shard_map/ppermute | solution.py:601
  94.2 14.5 %collective-permute-start.22 = (bf16[1024,512]{1,0:T(8,128)(2,1)}, bf16[1024,512]{1,0:T(8,128)(2,1)}, u32[]{:S(2)}, u32[]{:S(2)}) collective-permute-start(bf16[1024,512]{1,0:T(8,128)(2,1)} %collective-permute-done.21.refs_2_), channel_id=1, source_target_pairs={{0,8},{1,9},{2,10},{3,11},{4,12},{5,13},{6,14},{7,15},{8,0},{9,1},... | collective-permute-start | bytes 3145736 | tf_op jit(solution)/shard_map/ppermute | solution.py:601
  94.7 2.3 %copy-start.6 = (bf16[1024,256]{1,0:T(8,128)(2,1)}, bf16[1024,256]{1,0:T(8,128)(2,1)S(1)}, u32[]{:S(2)}) copy-start(bf16[1024,256]{1,0:T(8,128)(2,1)S(1)} %collective-permute-done.17.refs_7_) | copy-start | bytes 1572868
  94.8 6.6 %copy-start.28 = (bf16[512,256]{1,0:T(8,128)(2,1)S(1)}, bf16[512,256]{1,0:T(8,128)(2,1)}, u32[]{:S(2)}) copy-start(bf16[512,256]{1,0:T(8,128)(2,1)} %copy-done.27) | copy-start | bytes 786436
  94.8 8.5 %copy-start.15 = (bf16[512,256]{1,0:T(8,128)(2,1)S(1)}, bf16[512,256]{1,0:T(8,128)(2,1)}, u32[]{:S(2)}) copy-start(bf16[512,256]{1,0:T(8,128)(2,1)} %copy-done.14) | copy-start | bytes 786436
  97.0 6.3 %copy-start.5 = (bf16[1024,256]{1,0:T(8,128)(2,1)S(1)}, bf16[1024,256]{1,0:T(8,128)(2,1)}, u32[]{:S(2)}) copy-start(bf16[1024,256]{1,0:T(8,128)(2,1)} %copy-done.4) | copy-start | bytes 1572868
  97.0 6.3 %copy-start.7 = (bf16[1024,256]{1,0:T(8,128)(2,1)S(1)}, bf16[1024,256]{1,0:T(8,128)(2,1)}, u32[]{:S(2)}) copy-start(bf16[1024,256]{1,0:T(8,128)(2,1)} %copy-done.6) | copy-start | bytes 1572868
  97.0 19.2 %all-to-all-start.1 = ((bf16[8,32,1024]{2,1,0:T(8,128)(2,1)}), bf16[8,32,1024]{2,1,0:T(8,128)(2,1)}, u32[]{:S(2)}, u32[]{:S(2)}) async-start(bf16[8,32,1024]{2,1,0:T(8,128)(2,1)} %bitcast.25), calls=%async_computation.1 | async-start | bytes 1048576 | tf_op jit(solution)/shard_map/all_to_all | solution.py:609
  101.3 1.6 %collective-permute-start.15 = (bf16[512,256]{1,0:T(8,128)(2,1)S(1)}, bf16[512,256]{1,0:T(8,128)(2,1)S(1)}, u32[]{:S(2)}, u32[]{:S(2)}) collective-permute-start(bf16[512,256]{1,0:T(8,128)(2,1)S(1)} %copy-done.28), channel_id=1, source_target_pairs={{0,8},{1,9},{2,10},{3,11},{4,12},{5,13},{6,14},{7,15},{8,0},{9,1},... | collective-permute-start | bytes 786440 | tf_op jit(solution)/shard_map/ppermute | solution.py:601
  101.4 1.9 %collective-permute-start.14 = (bf16[512,256]{1,0:T(8,128)(2,1)}, bf16[512,256]{1,0:T(8,128)(2,1)S(1)}, u32[]{:S(2)}, u32[]{:S(2)}) collective-permute-start(bf16[512,256]{1,0:T(8,128)(2,1)} %copy-done.29), channel_id=1, source_target_pairs={{0,8},{1,9},{2,10},{3,11},{4,12},{5,13},{6,14},{7,15},{8,0},{9,1},... | collective-permute-start | bytes 786440 | tf_op jit(solution)/shard_map/ppermute | solution.py:601
  103.3 1.0 copy-start.9
  104.4 0.9 copy-start.17
  (7 other events, 4.7 us)

commit v9 on v8

--- a/solution.py
+++ b/solution.py
@@ -410,10 +410,13 @@
 
     for copy in row_copies + piece_copies(1, False):
         copy.wait()
-    mixed = jnp.dot(rows_in[...], weight[...], preferred_element_type=jnp.float32)
-    query[...] = (mixed[:, :width] * scale).astype(jnp.bfloat16)
-    key[...] = mixed[:, width : 2 * width].astype(jnp.bfloat16)
-    value[...] = mixed[:, 2 * width :].astype(jnp.bfloat16)
+    for part, target in enumerate((query, key, value)):
+        mixed = jnp.dot(
+            rows_in[...],
+            weight[:, part * width : (part + 1) * width],
+            preferred_element_type=jnp.float32,
+        )
+        target[...] = (mixed * scale if part == 0 else mixed).astype(jnp.bfloat16)
 
     def score_block(i):
         rec, b = divmod(i, blocks)
@@ -709,7 +712,7 @@
     m8 = relocate(m5, along_y, along_x)
 
     slot_pieces = (
-        ((qkv_weight, m1), (out_weight, m2), (m1, m3), (m3, m6)),
+        ((own_a, m1), (own_b, m2), (m1, m3), (m3, m6)),
         ((m2, m4), (m7, m5), (m5, m7), (m8, m8)),
     )
     block = 2 * C
@@ -718,10 +721,10 @@
     keys_seen = block + pad + memories.shape[0]
     lanes = width // head_size * block
     attended, sums, outs = [], [], []
-    for slot, pieces in enumerate(slot_pieces):
+    for pieces in slot_pieces:
         flat = [p for pair in pieces for p in pair]
         *results, out_piece = local_call(
-            functools.partial(attend_kernel, C, RC, head_size, slot == 0),
+            functools.partial(attend_kernel, C, RC, head_size, False),
             (
                 shape_of(frame_count, width),
                 shape_of(frame_count, width),
@@ -746,7 +749,7 @@
                 pltpu.VMEM((RING, keys_seen, lanes), bf16),
                 pltpu.SemaphoreType.DMA((24,)),
             ),
-            vmem_mib=24,
+            vmem_mib=20,
             flops=12 * frame_count * model_width * width,
             moved=8 * frame_count * model_width,
         )
@@ -791,7 +794,6 @@
         (received, *language_pieces),
         in_place=1 + rec_count,
         out_in_place=True,
-        vmem_mib=62,
         scratch=(
             pltpu.VMEM((slot_count, model_width), bf16),
             pltpu.VMEM((rec_count, model_width, language_shard), bf16),

time: 122 us -> 118 us (0.967)
  waiting for transfers between devices: 46.8 us -> 30.6 us
  starting transfers between devices: 33.7 us -> 45.5 us
    ppermute x22, waiting for transfers between devices: 28.2 us -> 15.8 us  [relocate(): return lax.ppermute(value, ('rec', 'tm'), pairs)]
    ppermute x22, starting transfers between devices: 21.7 us -> 32.5 us  [relocate(): return lax.ppermute(value, ('rec', 'tm'), pairs)]
    ppermute x1, waiting for transfers between devices: 11.1 us -> 7.66 us  [shifted(): return lax.ppermute(block, axis, route)]
    unnamed x60 -> x56, local copies, waits for them, and re-layouts: 7.7 us -> 8.36 us
  transfers between devices with their start and end apart: 25 -> 25, of which waited for: 10 -> 9; matrix products, arithmetic and copies ran while one was open for 2% -> 2% of each run, Pallas kernels for 19% -> 20%
where the time goes in v9:
time: 118 us; the launch traced here: 117 us
  starting transfers between devices  45.5 us (39%)
  waiting for transfers between devices  30.6 us (26%)
  Pallas kernels  27.4 us (23%)
  local copies, waits for them, and re-layouts  9.19 us (8%)
  other arithmetic  2.32 us (2%)
  between operations  1.79 us (2%)
    ppermute x22, starting transfers between devices, relocate(): return lax.ppermute(value, ('rec', 'tm'), pairs)  32.5 us
    pallas_call x7, Pallas kernels, local_call(): pl.pallas_call(kernel, out_shape=out_shapes, in_specs=[smem_spec()] * len...  27.4 us
    ppermute x22, waiting for transfers between devices, relocate(): return lax.ppermute(value, ('rec', 'tm'), pairs)  15.8 us
    all_to_all x2, starting transfers between devices, exchange_blocks(): return lax.all_to_all(blocks, 'tm', split_axis=0, concat_axis=0, tiled=True)  11.6 us
    unnamed x56, local copies, waits for them, and re-layouts  8.36 us
    ppermute x1, waiting for transfers between devices, shifted(): return lax.ppermute(block, axis, route)  7.66 us
    all_to_all x2, waiting for transfers between devices, exchange_blocks(): return lax.all_to_all(blocks, 'tm', split_axis=0, concat_axis=0, tiled=True)  7.12 us
  transfers between devices with their start and end apart: 25, of which 9 were waited for; matrix products, arithmetic and copies ran while one was open for 2% of the time, Pallas kernels for 20%

profile of v9, /device:TPU:0, one launch (start us, length us, event | category | flops | bytes accessed | tf_op | source)
XLA Modules:
  0.0 116.8 jit_solution(14355790095477613474)
XLA Ops:
  0.7 1.2 fusion.1.refs_8_
  1.8 3.0 %collective-permute-start.6 = (bf16[4,512,128]{2,1,0:T(8,128)(2,1)S(1)}, bf16[4,512,128]{2,1,0:T(8,128)(2,1)}, u32[]{:S(2)}, u32[]{:S(2)}) collective-permute-start(bf16[4,512,128]{2,1,0:T(8,128)(2,1)S(1)} %fusion.1.refs_8_), channel_id=1, source_target_pairs={{0,1},{1,0},{2,3},{3,2},{4,5},{5,4},{6,7},{7,6},{8,10},{9,11},{10,... | collective-permute-start | bytes 1572872 | tf_op jit(solution)/shard_map/ppermute | solution.py:604
  4.9 1.1 broadcast_select_fusion.1
  6.0 3.6 %collective-permute-start.7 = (bf16[4,512,128]{2,1,0:T(8,128)(2,1)}, bf16[4,512,128]{2,1,0:T(8,128)(2,1)S(1)}, u32[]{:S(2)}, u32[]{:S(2)}) collective-permute-start(bf16[4,512,128]{2,1,0:T(8,128)(2,1)} %get-tuple-element.42), channel_id=1, source_target_pairs={{0,6},{1,7},{2,0},{3,1},{4,2},{5,3},{6,4},{7,5},{8,10},{9,11},{10,... | collective-permute-start | bytes 1572872 | tf_op jit(solution)/shard_map/ppermute | solution.py:604
  9.6 2.6 %collective-permute-done.6.refs_9_.refs_12_ = bf16[4,512,128]{2,1,0:T(8,128)(2,1)} collective-permute-done((bf16[4,512,128]{2,1,0:T(8,128)(2,1)S(1)}, bf16[4,512,128]{2,1,0:T(8,128)(2,1)}, u32[]{:S(2)}, u32[]{:S(2)}) %collective-permute-start.6) | collective-permute-done | bytes 524320 | tf_op jit(solution)/shard_map/ppermute | solution.py:604
  12.1 2.0 %collective-permute-start.8 = (bf16[4,512,128]{2,1,0:T(8,128)(2,1)}, bf16[4,512,128]{2,1,0:T(8,128)(2,1)}, u32[]{:S(2)}, u32[]{:S(2)}) collective-permute-start(bf16[4,512,128]{2,1,0:T(8,128)(2,1)} %collective-permute-done.6.refs_9_.refs_12_), channel_id=1, source_target_pairs={{0,16},{1,17},{2,18},{3,19},{4,20},{5,21},{6,22},{7,23},{8,9},{9,8... | collective-permute-start | bytes 1572872 | tf_op jit(solution)/shard_map/ppermute | solution.py:604
  14.2 1.5 %collective-permute-start.10 = (bf16[4,512,128]{2,1,0:T(8,128)(2,1)}, bf16[4,512,128]{2,1,0:T(8,128)(2,1)}, u32[]{:S(2)}, u32[]{:S(2)}) collective-permute-start(bf16[4,512,128]{2,1,0:T(8,128)(2,1)} %collective-permute-done.6.refs_9_.refs_12_), channel_id=1, source_target_pairs={{8,10},{9,11},{10,12},{11,13},{12,14},{13,15},{14,8},{15,9},{24,26... | collective-permute-start | bytes 1572872 | tf_op jit(solution)/shard_map/ppermute | solution.py:604
  16.4 0.6 copy-done.21
  17.0 0.1 copy-done.20
  17.1 1.5 %shard_map.105 = (bf16[512,1024]{1,0:T(8,128)(2,1)S(1)}, bf16[16,1024]{1,0:T(8,128)(2,1)S(1)}, bf16[8,16,1024]{2,1,0:T(8,128)(2,1)S(1)}) custom-call(s32[17]{0:T(128)S(1)} %stack.63.scalars, bf16[512,1024]{1,0:T(8,128)(2,1)S(1)} %bitcast.28, f32[1,1024]{1,0:T(1,128)S(1)} %bitcast.35, f32[1,1024]{1,0:T(1,128)S(1)} %bitcast.36), custom_call_target="tpu_custom_call" | custom-call | flops 5242880 | bytes 2097152 | tf_op jit(solution)/shard_map/pallas_call | solution.py:269
  18.6 0.7 copy-done.11
  19.3 5.8 %all-to-all-start = ((bf16[8,16,1024]{2,1,0:T(8,128)(2,1)}), bf16[8,16,1024]{2,1,0:T(8,128)(2,1)S(1)}, u32[]{:S(2)}, u32[]{:S(2)}) async-start(bf16[8,16,1024]{2,1,0:T(8,128)(2,1)} %copy-done.11), calls=%async_computation | async-start | bytes 524288 | tf_op jit(solution)/shard_map/all_to_all | solution.py:612
  25.1 2.0 %collective-permute-start.3 = (bf16[512,1024]{1,0:T(8,128)(2,1)S(1)}, bf16[512,1024]{1,0:T(8,128)(2,1)}, u32[]{:S(2)}, u32[]{:S(2)}) collective-permute-start(bf16[512,1024]{1,0:T(8,128)(2,1)S(1)} %get-tuple-element.23.refs_2_), channel_id=1, source_target_pairs={{0,8},{1,9},{2,10},{3,11},{4,12},{5,13},{6,14},{7,15},{8,0},{9,1},... | collective-permute-start | bytes 3145736 | tf_op jit(solution)/shard_map/ppermute | solution.py:604
  27.1 1.7 %collective-permute-start.12 = (bf16[4,512,128]{2,1,0:T(8,128)(2,1)S(1)}, bf16[4,512,128]{2,1,0:T(8,128)(2,1)}, u32[]{:S(2)}, u32[]{:S(2)}) collective-permute-start(bf16[4,512,128]{2,1,0:T(8,128)(2,1)S(1)} %collective-permute-done.7.refs_11_.refs_8_), channel_id=1, source_target_pairs={{0,1},{1,0},{2,3},{3,2},{4,5},{5,4},{6,7},{7,6},{8,10},{9,11},{10,... | collective-permute-start | bytes 1572872 | tf_op jit(solution)/shard_map/ppermute | solution.py:604
  28.8 1.3 %collective-permute-done.other_length = s32[1]{0:T(128)} collective-permute-done((s32[1]{0:T(128)}, s32[1]{0:T(128)}, u32[]{:S(2)}, u32[]{:S(2)}) %collective-permute-start) | collective-permute-done | bytes 36 | tf_op jit(solution)/shard_map/ppermute | solution.py:604
  30.1 1.4 %collective-permute-start.2 = (bf16[16,1024]{1,0:T(8,128)(2,1)S(1)}, bf16[16,1024]{1,0:T(8,128)(2,1)}, u32[]{:S(2)}, u32[]{:S(2)}) collective-permute-start(bf16[16,1024]{1,0:T(8,128)(2,1)S(1)} %get-tuple-element.24), channel_id=1, source_target_pairs={{1,0},{2,1},{3,2},{4,3},{5,4},{6,5},{7,6},{9,8},{10,9},{11,10},{12... | collective-permute-start | bytes 98312 | tf_op jit(solution)/shard_map/ppermute | solution.py:27
  31.5 7.7 %collective-permute-done.2.refs_3_ = bf16[16,1024]{1,0:T(8,128)(2,1)} collective-permute-done((bf16[16,1024]{1,0:T(8,128)(2,1)S(1)}, bf16[16,1024]{1,0:T(8,128)(2,1)}, u32[]{:S(2)}, u32[]{:S(2)}) %collective-permute-start.2) | collective-permute-done | bytes 32800 | tf_op jit(solution)/shard_map/ppermute | solution.py:27
  39.2 0.7 copy.11.owners_col
  39.9 0.7 copy-done.23
  40.6 0.8 copy-done.10
  41.4 0.9 shard_map.104
  42.3 0.8 copy-done.8
  43.1 0.6 copy-done.16
  43.7 0.6 copy-done.18
  44.4 0.5 collective-permute-start.1
  45.0 0.8 collective-permute-start.9
  46.0 1.5 %collective-permute-start.11 = (bf16[4,512,128]{2,1,0:T(8,128)(2,1)S(1)}, bf16[4,512,128]{2,1,0:T(8,128)(2,1)S(1)}, u32[]{:S(2)}, u32[]{:S(2)}) collective-permute-start(bf16[4,512,128]{2,1,0:T(8,128)(2,1)S(1)} %broadcast_select_fusion), channel_id=1, source_target_pairs={{0,16},{1,17},{2,18},{3,19},{4,20},{5,21},{6,22},{7,23},{8,9},{9,8... | collective-permute-start | bytes 1572872 | tf_op jit(solution)/shard_map/ppermute | solution.py:604
  47.5 0.5 collective-permute-start.13
  48.0 1.5 %collective-permute-start.21 = (bf16[1024,512]{1,0:T(8,128)(2,1)}, bf16[1024,512]{1,0:T(8,128)(2,1)}, u32[]{:S(2)}, u32[]{:S(2)}) collective-permute-start(bf16[1024,512]{1,0:T(8,128)(2,1)} %refs_0_.1), channel_id=1, source_target_pairs={{0,16},{1,17},{2,18},{3,19},{4,20},{5,21},{6,22},{7,23},{8,24},{9,... | collective-permute-start | bytes 3145736 | tf_op jit(solution)/shard_map/ppermute | solution.py:604
  49.6 7.6 %shard_map.106 = (bf16[512,256]{1,0:T(8,128)(2,1)S(1)}, bf16[512,256]{1,0:T(8,128)(2,1)S(1)}, f32[128,256]{1,0:T(8,128)S(1)}, f32[128,256]{1,0:T(8,128)S(1)}, bf16[1024,256]{1,0:T(8,128)(2,1)S(1)}) custom-call(s32[17]{0:T(128)S(1)} %stack.63.scalars, s32[1]{0:T(128)} %collective-permute-done.other_length, bf16[128,512]{1,0:T(8,128)(2,1)S(1)} %get-tuple-element.22.refs_0_, ...), custom_call_target="tpu_custom_call" | custom-call | flops 1610612736 | bytes 4194304 | tf_op jit(solution)/shard_map/pallas_call | solution.py:269
  57.2 0.7 copy-done.12
  57.9 0.7 copy-done.24
  58.6 12.0 %collective-permute-start.16 = (bf16[1024,256]{1,0:T(8,128)(2,1)S(1)}, bf16[1024,256]{1,0:T(8,128)(2,1)S(1)}, u32[]{:S(2)}, u32[]{:S(2)}) collective-permute-start(bf16[1024,256]{1,0:T(8,128)(2,1)S(1)} %get-tuple-element.33.refs_4_), channel_id=1, source_target_pairs={{0,8},{1,9},{2,10},{3,11},{4,12},{5,13},{6,14},{7,15},{8,0},{9,1},... | collective-permute-start | bytes 1572872 | tf_op jit(solution)/shard_map/ppermute | solution.py:604
  70.6 0.9 collective-permute-done.13.refs_14_.refs_15_
  71.4 7.5 %shard_map.107 = (bf16[512,256]{1,0:T(8,128)(2,1)S(1)}, bf16[512,256]{1,0:T(8,128)(2,1)S(1)}, f32[128,256]{1,0:T(8,128)S(1)}, f32[128,256]{1,0:T(8,128)S(1)}, bf16[1024,256]{1,0:T(8,128)(2,1)S(1)}) custom-call(s32[17]{0:T(128)S(1)} %stack.63.scalars, s32[1]{0:T(128)} %collective-permute-done.other_length, bf16[128,512]{1,0:T(8,128)(2,1)S(1)} %get-tuple-element.22.refs_0_, ...), custom_call_target="tpu_custom_call" | custom-call | flops 1610612736 | bytes 4194304 | tf_op jit(solution)/shard_map/pallas_call | solution.py:269
  79.0 0.5 collective-permute-start.18
  79.6 9.4 %collective-permute-done.21.refs_2_ = bf16[1024,512]{1,0:T(8,128)(2,1)} collective-permute-done((bf16[1024,512]{1,0:T(8,128)(2,1)}, bf16[1024,512]{1,0:T(8,128)(2,1)}, u32[]{:S(2)}, u32[]{:S(2)}) %collective-permute-start.21) | collective-permute-done | bytes 1048608 | tf_op jit(solution)/shard_map/ppermute | solution.py:604
  89.0 0.5 collective-permute-start.22
  89.6 2.2 %shard_map.109 = bf16[256,1024]{1,0:T(8,128)(2,1)} custom-call(s32[17]{0:T(128)S(1)} %stack.63.scalars, f32[128,1024]{1,0:T(8,128)S(1)} %copy-done.9, f32[128,128]{1,0:T(8,128)S(1)} %copy-done.17, bf16[256,128]{1,0:T(8,128)(2,1)S(1)} %copy-done.19, f32[128,256]{1,0:T(8,128)S(1)} %get-tuple-element.38.refs_0_, f32[128,256]{1,0:T(8,128)S(1)} %get-tuple-element.39.refs_1_, ...), custom_call_target="tpu_custom_call" | custom-call | flops 536870912 | bytes 3145728 | tf_op jit(solution)/shard_map/pallas_call | solution.py:269
  91.8 5.8 %all-to-all-start.1 = ((bf16[8,32,1024]{2,1,0:T(8,128)(2,1)}), bf16[8,32,1024]{2,1,0:T(8,128)(2,1)S(1)}, u32[]{:S(2)}, u32[]{:S(2)}) async-start(bf16[8,32,1024]{2,1,0:T(8,128)(2,1)} %bitcast.25), calls=%async_computation.1 | async-start | bytes 1048576 | tf_op jit(solution)/shard_map/all_to_all | solution.py:612
  97.6 0.5 collective-permute-start.15
  98.1 1.2 %collective-permute-done.14.refs_2_ = bf16[512,256]{1,0:T(8,128)(2,1)S(1)} collective-permute-done((bf16[512,256]{1,0:T(8,128)(2,1)}, bf16[512,256]{1,0:T(8,128)(2,1)S(1)}, u32[]{:S(2)}, u32[]{:S(2)}) %collective-permute-start.14) | collective-permute-done | bytes 262176 | tf_op jit(solution)/shard_map/ppermute | solution.py:604
  99.4 0.4 collective-permute-done.15.refs_3_
  99.8 1.0 copy-done.7
  100.8 0.9 copy-done.15
  101.8 3.4 %shard_map.108 = bf16[512,1024]{1,0:T(8,128)(2,1)} custom-call(s32[17]{0:T(128)S(1)} %stack.63.scalars, bf16[512,256]{1,0:T(8,128)(2,1)S(1)} %copy-done.13, bf16[512,256]{1,0:T(8,128)(2,1)S(1)} %copy-done.15, bf16[512,256]{1,0:T(8,128)(2,1)S(1)} %collective-permute-done.14.refs_2_, bf16[512,256]{1,0:T(8,128)(2,1)S(1)} %collective-permute-done.15.refs_3_, ...), custom_call_target="tpu_custom_call" | custom-call | flops 1073741824 | bytes 3145728 | tf_op jit(solution)/shard_map/pallas_call | solution.py:269
  105.2 7.1 %all-to-all-done.1 = bf16[8,32,1024]{2,1,0:T(8,128)(2,1)S(1)} async-done(((bf16[8,32,1024]{2,1,0:T(8,128)(2,1)}), bf16[8,32,1024]{2,1,0:T(8,128)(2,1)S(1)}, u32[]{:S(2)}, u32[]{:S(2)}) %all-to-all-start.1) | async-done | bytes 524320 | tf_op jit(solution)/shard_map/all_to_all | solution.py:612
  112.3 4.3 %shard_map.110 = bf16[256,2048]{1,0:T(8,128)(2,1)} custom-call(s32[17]{0:T(128)S(1)} %stack.63.scalars, bf16[256,1024]{1,0:T(8,128)(2,1)S(1)} %bitcast.34, bf16[1024,512]{1,0:T(8,128)(2,1)} %refs_0_.1, bf16[1024,512]{1,0:T(8,128)(2,1)} %collective-permute-done.20.refs_1_, bf16[1024,512]{1,0:T(8,128)(2,1)} %collective-permute-done.21.refs_2_, ...), custom_call_target="tpu_custom_call" | custom-call | flops 1073741824 | bytes 4194304 | tf_op jit(solution)/shard_map/pallas_call | solution.py:269
  (70 shorter events, 0.7 us)
Async XLA Ops:
  0.7 4.2 %copy-start.26 = (bf16[3,1024,128]{2,1,0:T(8,128)(2,1)S(1)}, bf16[3,1024,128]{2,1,0:T(8,128)(2,1)}, u32[]{:S(2)}) copy-start(bf16[3,1024,128]{2,1,0:T(8,128)(2,1)} %param.13) | copy-start | bytes 2359300
  0.7 4.2 %copy-start.27 = (bf16[1024,128]{1,0:T(8,128)(2,1)S(1)}, bf16[1024,128]{1,0:T(8,128)(2,1)}, u32[]{:S(2)}) copy-start(bf16[1024,128]{1,0:T(8,128)(2,1)} %param.14) | copy-start | bytes 786436
  1.8 10.3 %collective-permute-start.6 = (bf16[4,512,128]{2,1,0:T(8,128)(2,1)S(1)}, bf16[4,512,128]{2,1,0:T(8,128)(2,1)}, u32[]{:S(2)}, u32[]{:S(2)}) collective-permute-start(bf16[4,512,128]{2,1,0:T(8,128)(2,1)S(1)} %fusion.1.refs_8_), channel_id=1, source_target_pairs={{0,1},{1,0},{2,3},{3,2},{4,5},{5,4},{6,7},{7,6},{8,10},{9,11},{10,... | collective-permute-start | bytes 1572872 | tf_op jit(solution)/shard_map/ppermute | solution.py:604
  4.9 11.6 %copy-start = (bf16[1,512,1024]{2,1,0:T(8,128)(2,1)S(1)}, bf16[1,512,1024]{2,1,0:T(8,128)(2,1)}, u32[]{:S(2)}) copy-start(bf16[1,512,1024]{2,1,0:T(8,128)(2,1)} %param.9) | copy-start | bytes 3145732
  6.0 21.1 %collective-permute-start.7 = (bf16[4,512,128]{2,1,0:T(8,128)(2,1)}, bf16[4,512,128]{2,1,0:T(8,128)(2,1)S(1)}, u32[]{:S(2)}, u32[]{:S(2)}) collective-permute-start(bf16[4,512,128]{2,1,0:T(8,128)(2,1)} %get-tuple-element.42), channel_id=1, source_target_pairs={{0,6},{1,7},{2,0},{3,1},{4,2},{5,3},{6,4},{7,5},{8,10},{9,11},{10,... | collective-permute-start | bytes 1572872 | tf_op jit(solution)/shard_map/ppermute | solution.py:604
  12.1 32.8 %collective-permute-start.8 = (bf16[4,512,128]{2,1,0:T(8,128)(2,1)}, bf16[4,512,128]{2,1,0:T(8,128)(2,1)}, u32[]{:S(2)}, u32[]{:S(2)}) collective-permute-start(bf16[4,512,128]{2,1,0:T(8,128)(2,1)} %collective-permute-done.6.refs_9_.refs_12_), channel_id=1, source_target_pairs={{0,16},{1,17},{2,18},{3,19},{4,20},{5,21},{6,22},{7,23},{8,9},{9,8... | collective-permute-start | bytes 1572872 | tf_op jit(solution)/shard_map/ppermute | solution.py:604
  14.2 30.8 %collective-permute-start.10 = (bf16[4,512,128]{2,1,0:T(8,128)(2,1)}, bf16[4,512,128]{2,1,0:T(8,128)(2,1)}, u32[]{:S(2)}, u32[]{:S(2)}) collective-permute-start(bf16[4,512,128]{2,1,0:T(8,128)(2,1)} %collective-permute-done.6.refs_9_.refs_12_), channel_id=1, source_target_pairs={{8,10},{9,11},{10,12},{11,13},{12,14},{13,15},{14,8},{15,9},{24,26... | collective-permute-start | bytes 1572872 | tf_op jit(solution)/shard_map/ppermute | solution.py:604
  18.6 0.7 copy-start.11
  19.3 25.6 %all-to-all-start = ((bf16[8,16,1024]{2,1,0:T(8,128)(2,1)}), bf16[8,16,1024]{2,1,0:T(8,128)(2,1)S(1)}, u32[]{:S(2)}, u32[]{:S(2)}) async-start(bf16[8,16,1024]{2,1,0:T(8,128)(2,1)} %copy-done.11), calls=%async_computation | async-start | bytes 524288 | tf_op jit(solution)/shard_map/all_to_all | solution.py:612
  25.1 24.5 %collective-permute-start.3 = (bf16[512,1024]{1,0:T(8,128)(2,1)S(1)}, bf16[512,1024]{1,0:T(8,128)(2,1)}, u32[]{:S(2)}, u32[]{:S(2)}) collective-permute-start(bf16[512,1024]{1,0:T(8,128)(2,1)S(1)} %get-tuple-element.23.refs_2_), channel_id=1, source_target_pairs={{0,8},{1,9},{2,10},{3,11},{4,12},{5,13},{6,14},{7,15},{8,0},{9,1},... | collective-permute-start | bytes 3145736 | tf_op jit(solution)/shard_map/ppermute | solution.py:604
  27.1 20.5 %collective-permute-start.12 = (bf16[4,512,128]{2,1,0:T(8,128)(2,1)S(1)}, bf16[4,512,128]{2,1,0:T(8,128)(2,1)}, u32[]{:S(2)}, u32[]{:S(2)}) collective-permute-start(bf16[4,512,128]{2,1,0:T(8,128)(2,1)S(1)} %collective-permute-done.7.refs_11_.refs_8_), channel_id=1, source_target_pairs={{0,1},{1,0},{2,3},{3,2},{4,5},{5,4},{6,7},{7,6},{8,10},{9,11},{10,... | collective-permute-start | bytes 1572872 | tf_op jit(solution)/shard_map/ppermute | solution.py:604
  28.8 1.3 %collective-permute-start = (s32[1]{0:T(128)}, s32[1]{0:T(128)}, u32[]{:S(2)}, u32[]{:S(2)}) collective-permute-start(s32[1]{0:T(128)} %param.10), channel_id=1, source_target_pairs={{0,8},{1,9},{2,10},{3,11},{4,12},{5,13},{6,14},{7,15},{8,0},{9,1},... | collective-permute-start | bytes 20 | tf_op jit(solution)/shard_map/ppermute | solution.py:604
  30.1 9.1 %copy-start.22 = (s32[1,1,128,1]{2,3,1,0:T(1,128)S(1)}, s32[1,1,128,1]{2,3,1,0:T(1,128)}, u32[]{:S(2)}) copy-start(s32[1,1,128,1]{2,3,1,0:T(1,128)} %param.16) | copy-start | bytes 1540
  30.1 9.1 %collective-permute-start.2 = (bf16[16,1024]{1,0:T(8,128)(2,1)S(1)}, bf16[16,1024]{1,0:T(8,128)(2,1)}, u32[]{:S(2)}, u32[]{:S(2)}) collective-permute-start(bf16[16,1024]{1,0:T(8,128)(2,1)S(1)} %get-tuple-element.24), channel_id=1, source_target_pairs={{1,0},{2,1},{3,2},{4,3},{5,4},{6,5},{7,6},{9,8},{10,9},{11,10},{12... | collective-permute-start | bytes 98312 | tf_op jit(solution)/shard_map/ppermute | solution.py:27
  39.2 5.2 %collective-permute-start.4 = (bf16[16,1024]{1,0:T(8,128)(2,1)}, bf16[16,1024]{1,0:T(8,128)(2,1)}, u32[]{:S(2)}, u32[]{:S(2)}) collective-permute-start(bf16[16,1024]{1,0:T(8,128)(2,1)} %collective-permute-done.2.refs_3_), channel_id=1, source_target_pairs={{0,8},{1,9},{2,10},{3,11},{4,12},{5,13},{6,14},{7,15},{8,0},{9,1},... | collective-permute-start | bytes 98312 | tf_op jit(solution)/shard_map/ppermute | solution.py:604
  40.6 0.8 copy-start.10
  42.3 0.8 copy-start.8
  44.4 1.6 %collective-permute-start.1 = (bf16[128,512]{1,0:T(8,128)(2,1)S(1)}, bf16[128,512]{1,0:T(8,128)(2,1)}, u32[]{:S(2)}, u32[]{:S(2)}) collective-permute-start(bf16[128,512]{1,0:T(8,128)(2,1)S(1)} %get-tuple-element.22.refs_0_), channel_id=1, source_target_pairs={{0,8},{1,9},{2,10},{3,11},{4,12},{5,13},{6,14},{7,15},{8,0},{9,1},... | collective-permute-start | bytes 393224 | tf_op jit(solution)/shard_map/ppermute | solution.py:604
  44.9 4.7 %copy-start.1 = (bf16[4,512,128]{2,1,0:T(8,128)(2,1)S(1)}, bf16[4,512,128]{2,1,0:T(8,128)(2,1)}, u32[]{:S(2)}) copy-start(bf16[4,512,128]{2,1,0:T(8,128)(2,1)} %get-tuple-element.43.refs_10_) | copy-start | bytes 1572868
  44.9 3.1 %collective-permute-start.5 = (bf16[128,1024]{1,0:T(8,128)(2,1)S(1)}, bf16[128,1024]{1,0:T(8,128)(2,1)S(1)}, u32[]{:S(2)}, u32[]{:S(2)}) collective-permute-start(bf16[128,1024]{1,0:T(8,128)(2,1)S(1)} %bitcast.31), channel_id=1, source_target_pairs={{0,8},{1,9},{2,10},{3,11},{4,12},{5,13},{6,14},{7,15},{8,0},{9,1},... | collective-permute-start | bytes 786440 | tf_op jit(solution)/shard_map/ppermute | solution.py:604
  45.0 4.6 %collective-permute-start.9 = (bf16[4,512,128]{2,1,0:T(8,128)(2,1)}, bf16[4,512,128]{2,1,0:T(8,128)(2,1)S(1)}, u32[]{:S(2)}, u32[]{:S(2)}) collective-permute-start(bf16[4,512,128]{2,1,0:T(8,128)(2,1)} %collective-permute-done.8.refs_13_.refs_14_), channel_id=1, source_target_pairs={{8,24},{9,25},{10,26},{11,27},{12,28},{13,29},{14,30},{15,31},{24,... | collective-permute-start | bytes 1572872 | tf_op jit(solution)/shard_map/ppermute | solution.py:604
  46.0 24.6 %collective-permute-start.11 = (bf16[4,512,128]{2,1,0:T(8,128)(2,1)S(1)}, bf16[4,512,128]{2,1,0:T(8,128)(2,1)S(1)}, u32[]{:S(2)}, u32[]{:S(2)}) collective-permute-start(bf16[4,512,128]{2,1,0:T(8,128)(2,1)S(1)} %broadcast_select_fusion), channel_id=1, source_target_pairs={{0,16},{1,17},{2,18},{3,19},{4,20},{5,21},{6,22},{7,23},{8,9},{9,8... | collective-permute-start | bytes 1572872 | tf_op jit(solution)/shard_map/ppermute | solution.py:604
  47.5 23.9 %collective-permute-start.13 = (bf16[4,512,128]{2,1,0:T(8,128)(2,1)}, bf16[4,512,128]{2,1,0:T(8,128)(2,1)S(1)}, u32[]{:S(2)}, u32[]{:S(2)}) collective-permute-start(bf16[4,512,128]{2,1,0:T(8,128)(2,1)} %collective-permute-done.12.refs_11_.refs_12_), channel_id=1, source_target_pairs={{0,16},{1,17},{2,18},{3,19},{4,20},{5,21},{6,22},{7,23},{8,9},{9,8... | collective-permute-start | bytes 1572872 | tf_op jit(solution)/shard_map/ppermute | solution.py:604
  48.0 41.0 %collective-permute-start.21 = (bf16[1024,512]{1,0:T(8,128)(2,1)}, bf16[1024,512]{1,0:T(8,128)(2,1)}, u32[]{:S(2)}, u32[]{:S(2)}) collective-permute-start(bf16[1024,512]{1,0:T(8,128)(2,1)} %refs_0_.1), channel_id=1, source_target_pairs={{0,16},{1,17},{2,18},{3,19},{4,20},{5,21},{6,22},{7,23},{8,24},{9,... | collective-permute-start | bytes 3145736 | tf_op jit(solution)/shard_map/ppermute | solution.py:604
  57.2 0.7 copy-start.12
  57.9 0.7 copy-start.24
  58.6 31.0 %copy-start.2 = (bf16[1024,256]{1,0:T(8,128)(2,1)}, bf16[1024,256]{1,0:T(8,128)(2,1)S(1)}, u32[]{:S(2)}) copy-start(bf16[1024,256]{1,0:T(8,128)(2,1)S(1)} %get-tuple-element.33.refs_4_) | copy-start | bytes 1572868
  58.6 31.0 %copy-start.9 = (f32[128,1024]{1,0:T(8,128)S(1)}, f32[128,1024]{1,0:T(8,128)}, u32[]{:S(2)}) copy-start(f32[128,1024]{1,0:T(8,128)} %copy-done.8) | copy-start | bytes 1572868
  58.6 31.0 %copy-start.17 = (f32[128,128]{1,0:T(8,128)S(1)}, f32[128,128]{1,0:T(8,128)}, u32[]{:S(2)}) copy-start(f32[128,128]{1,0:T(8,128)} %copy-done.16) | copy-start | bytes 196612
  58.6 31.0 %copy-start.19 = (bf16[256,128]{1,0:T(8,128)(2,1)S(1)}, bf16[256,128]{1,0:T(8,128)(2,1)}, u32[]{:S(2)}) copy-start(bf16[256,128]{1,0:T(8,128)(2,1)} %copy-done.18) | copy-start | bytes 196612
  58.6 30.9 %collective-permute-start.16 = (bf16[1024,256]{1,0:T(8,128)(2,1)S(1)}, bf16[1024,256]{1,0:T(8,128)(2,1)S(1)}, u32[]{:S(2)}, u32[]{:S(2)}) collective-permute-start(bf16[1024,256]{1,0:T(8,128)(2,1)S(1)} %get-tuple-element.33.refs_4_), channel_id=1, source_target_pairs={{0,8},{1,9},{2,10},{3,11},{4,12},{5,13},{6,14},{7,15},{8,0},{9,1},... | collective-permute-start | bytes 1572872 | tf_op jit(solution)/shard_map/ppermute | solution.py:604
  78.9 12.8 %copy-start.6 = (bf16[1024,256]{1,0:T(8,128)(2,1)}, bf16[1024,256]{1,0:T(8,128)(2,1)S(1)}, u32[]{:S(2)}) copy-start(bf16[1024,256]{1,0:T(8,128)(2,1)S(1)} %get-tuple-element.34.refs_5_) | copy-start | bytes 1572868
  78.9 12.8 %copy-start.14 = (bf16[512,256]{1,0:T(8,128)(2,1)}, bf16[512,256]{1,0:T(8,128)(2,1)S(1)}, u32[]{:S(2)}) copy-start(bf16[512,256]{1,0:T(8,128)(2,1)S(1)} %get-tuple-element.30.refs_1_) | copy-start | bytes 786436
  78.9 12.8 %copy-start.25 = (bf16[512,256]{1,0:T(8,128)(2,1)}, bf16[512,256]{1,0:T(8,128)(2,1)S(1)}, u32[]{:S(2)}) copy-start(bf16[512,256]{1,0:T(8,128)(2,1)S(1)} %get-tuple-element.32) | copy-start | bytes 786436
  79.0 10.6 %collective-permute-start.17 = (bf16[1024,256]{1,0:T(8,128)(2,1)S(1)}, bf16[1024,256]{1,0:T(8,128)(2,1)S(1)}, u32[]{:S(2)}, u32[]{:S(2)}) collective-permute-start(bf16[1024,256]{1,0:T(8,128)(2,1)S(1)} %get-tuple-element.34.refs_5_), channel_id=1, source_target_pairs={{0,8},{1,9},{2,10},{3,11},{4,12},{5,13},{6,14},{7,15},{8,0},{9,1},... | collective-permute-start | bytes 1572872 | tf_op jit(solution)/shard_map/ppermute | solution.py:604
  79.0 10.0 %collective-permute-start.18 = (f32[128,256]{1,0:T(8,128)S(1)}, f32[128,256]{1,0:T(8,128)S(1)}, u32[]{:S(2)}, u32[]{:S(2)}) collective-permute-start(f32[128,256]{1,0:T(8,128)S(1)} %get-tuple-element.40), channel_id=1, source_target_pairs={{0,8},{1,9},{2,10},{3,11},{4,12},{5,13},{6,14},{7,15},{8,0},{9,1},... | collective-permute-start | bytes 393224 | tf_op jit(solution)/shard_map/ppermute | solution.py:604
  79.5 10.0 %collective-permute-start.19 = (f32[128,256]{1,0:T(8,128)S(1)}, f32[128,256]{1,0:T(8,128)S(1)}, u32[]{:S(2)}, u32[]{:S(2)}) collective-permute-start(f32[128,256]{1,0:T(8,128)S(1)} %get-tuple-element.41), channel_id=1, source_target_pairs={{0,8},{1,9},{2,10},{3,11},{4,12},{5,13},{6,14},{7,15},{8,0},{9,1},... | collective-permute-start | bytes 393224 | tf_op jit(solution)/shard_map/ppermute | solution.py:604
  89.0 16.2 %collective-permute-start.20 = (bf16[1024,512]{1,0:T(8,128)(2,1)}, bf16[1024,512]{1,0:T(8,128)(2,1)}, u32[]{:S(2)}, u32[]{:S(2)}) collective-permute-start(bf16[1024,512]{1,0:T(8,128)(2,1)} %refs_0_.1), channel_id=1, source_target_pairs={{0,8},{1,9},{2,10},{3,11},{4,12},{5,13},{6,14},{7,15},{8,0},{9,1},... | collective-permute-start | bytes 3145736 | tf_op jit(solution)/shard_map/ppermute | solution.py:604
  89.0 16.2 %collective-permute-start.22 = (bf16[1024,512]{1,0:T(8,128)(2,1)}, bf16[1024,512]{1,0:T(8,128)(2,1)}, u32[]{:S(2)}, u32[]{:S(2)}) collective-permute-start(bf16[1024,512]{1,0:T(8,128)(2,1)} %collective-permute-done.21.refs_2_), channel_id=1, source_target_pairs={{0,8},{1,9},{2,10},{3,11},{4,12},{5,13},{6,14},{7,15},{8,0},{9,1},... | collective-permute-start | bytes 3145736 | tf_op jit(solution)/shard_map/ppermute | solution.py:604
  89.5 2.2 %copy-start.4 = (bf16[1024,256]{1,0:T(8,128)(2,1)}, bf16[1024,256]{1,0:T(8,128)(2,1)S(1)}, u32[]{:S(2)}) copy-start(bf16[1024,256]{1,0:T(8,128)(2,1)S(1)} %collective-permute-done.16.refs_6_) | copy-start | bytes 1572868
  89.6 10.2 %copy-start.13 = (bf16[512,256]{1,0:T(8,128)(2,1)S(1)}, bf16[512,256]{1,0:T(8,128)(2,1)}, u32[]{:S(2)}) copy-start(bf16[512,256]{1,0:T(8,128)(2,1)} %copy-done.12) | copy-start | bytes 786436
  91.8 8.0 %copy-start.3 = (bf16[1024,256]{1,0:T(8,128)(2,1)S(1)}, bf16[1024,256]{1,0:T(8,128)(2,1)}, u32[]{:S(2)}) copy-start(bf16[1024,256]{1,0:T(8,128)(2,1)} %copy-done.2) | copy-start | bytes 1572868
  91.8 8.0 %copy-start.5 = (bf16[1024,256]{1,0:T(8,128)(2,1)S(1)}, bf16[1024,256]{1,0:T(8,128)(2,1)}, u32[]{:S(2)}) copy-start(bf16[1024,256]{1,0:T(8,128)(2,1)} %copy-done.4) | copy-start | bytes 1572868
  91.8 20.5 %all-to-all-start.1 = ((bf16[8,32,1024]{2,1,0:T(8,128)(2,1)}), bf16[8,32,1024]{2,1,0:T(8,128)(2,1)S(1)}, u32[]{:S(2)}, u32[]{:S(2)}) async-start(bf16[8,32,1024]{2,1,0:T(8,128)(2,1)} %bitcast.25), calls=%async_computation.1 | async-start | bytes 1048576 | tf_op jit(solution)/shard_map/all_to_all | solution.py:612
  97.6 1.7 %collective-permute-start.14 = (bf16[512,256]{1,0:T(8,128)(2,1)}, bf16[512,256]{1,0:T(8,128)(2,1)S(1)}, u32[]{:S(2)}, u32[]{:S(2)}) collective-permute-start(bf16[512,256]{1,0:T(8,128)(2,1)} %copy-done.24), channel_id=1, source_target_pairs={{0,8},{1,9},{2,10},{3,11},{4,12},{5,13},{6,14},{7,15},{8,0},{9,1},... | collective-permute-start | bytes 786440 | tf_op jit(solution)/shard_map/ppermute | solution.py:604
  97.6 2.1 %collective-permute-start.15 = (bf16[512,256]{1,0:T(8,128)(2,1)}, bf16[512,256]{1,0:T(8,128)(2,1)S(1)}, u32[]{:S(2)}, u32[]{:S(2)}) collective-permute-start(bf16[512,256]{1,0:T(8,128)(2,1)} %copy-done.25), channel_id=1, source_target_pairs={{0,8},{1,9},{2,10},{3,11},{4,12},{5,13},{6,14},{7,15},{8,0},{9,1},... | collective-permute-start | bytes 786440 | tf_op jit(solution)/shard_map/ppermute | solution.py:604
  99.8 1.0 copy-start.7
  100.8 0.9 copy-start.15
  (5 other events, 3.3 us)

commit v10 on v9

--- a/solution.py
+++ b/solution.py
@@ -331,25 +331,15 @@
     )
 
 
-def attend_kernel(span_len, right_len, head_size, starts_here, scalars, other_length, *refs):
-    members, sources, pieces = refs[:2], refs[2:8], refs[8:16]
-    out_refs, sums_out, projection = refs[16:18], refs[18:20], refs[20]
-    outs, rows_in, weight, query, key, value, bias, scores, peaks, weights, sems = refs[21:]
-    first_frame, core, y_half = scalars[0], scalars[2], scalars[3]
-    frame_count, model_width = sources[0].shape
+def project_kernel(head_size, scalars, *refs):
+    sources, pieces = refs[:4], refs[4:12]
+    query, key, value, pair_weight, projection = refs[12:17]
+    rows_in, query_weight, sems = refs[17:]
+    core, y_half = scalars[2], scalars[3]
+    model_width, width = query_weight.shape
     half = model_width // 2
-    width = out_refs[0].shape[1]
-    out_copies = [
-        pltpu.make_async_copy(outs.at[rec], out_refs[rec], sems.at[22 + rec]) for rec in range(2)
-    ]
-    heads = width // head_size
-    block = 2 * span_len
-    blocks = frame_count // block
-    near = bias.shape[0]
-    memory_at = frame_count + near - block
     row_count = rows_in.shape[0] // 2
-    memory_count = row_count - memory_at
-    lanes = heads * block
+    frame_count = sources[0].shape[0]
 
     def piece_copies(of_core, projected):
         places = (y_half * half, (1 - y_half) * half)
@@ -358,37 +348,31 @@
             place = pl.ds(pl.multiple_of(places[side], half), half)
             for shard in range(2):
                 piece = pieces[4 * shard + 2 * side + of_core]
-                raw = starts_here and of_core == 0 and shard == 0
-                shard_width = pieces[-1].shape[2]
-                index = 2 * side + shard
+                shard_width = piece.shape[2]
                 for part in (3,) if projected else (0, 1, 2):
-                    target = projection if projected else weight
-                    start = shard * shard_width + (0 if projected else part * width)
-                    if raw:
-                        source = pieces[2].at[place] if projected else pieces[0].at[part, place]
-                    else:
-                        source = piece.at[part]
+                    target = (query_weight, pair_weight, pair_weight, projection)[part]
+                    start = shard * shard_width + (width if part == 2 else 0)
                     copies.append(
                         pltpu.make_async_copy(
-                            source,
+                            piece.at[part],
                             target.at[place, pl.ds(start, shard_width)],
-                            sems.at[4 * part + index],
+                            sems.at[4 * part + 2 * side + shard],
                         )
                     )
         return copies
 
     row_copies = []
     for rec in range(2):
-        at = rec * row_count
         for i, (start, size) in enumerate(
-            ((0, frame_count), (frame_count, near - block), (memory_at, memory_count))
+            ((0, frame_count), (frame_count, row_count - frame_count))
         ):
             row_copies.append(
                 pltpu.make_async_copy(
-                    sources[3 * rec + i], rows_in.at[pl.ds(at + start, size)], sems.at[16 + 3 * rec + i]
+                    sources[2 * rec + i],
+                    rows_in.at[pl.ds(rec * row_count + start, size)],
+                    sems.at[16 + 2 * rec + i],
                 )
             )
-
     for copy in row_copies:
         copy.start()
     for of_core in range(2):
@@ -397,6 +381,40 @@
         def _():
             for copy in piece_copies(of_core, False) + piece_copies(of_core, True):
                 copy.start()
+
+    for copy in row_copies + piece_copies(1, False):
+        copy.wait()
+    scale = head_size ** (-0.5) * LOG2_E
+    query[...] = (
+        jnp.dot(rows_in[...], query_weight[...], preferred_element_type=jnp.float32) * scale
+    ).astype(jnp.bfloat16)
+    for part, target in enumerate((key, value)):
+        target[...] = jnp.dot(
+            rows_in[...],
+            pair_weight[:, part * width : (part + 1) * width],
+            preferred_element_type=jnp.float32,
+        ).astype(jnp.bfloat16)
+    for copy in piece_copies(1, True):
+        copy.wait()
+
+
+def attend_kernel(span_len, right_len, head_size, scalars, other_length, *refs):
+    members, query, key, value = refs[:2], refs[2], refs[3], refs[4]
+    memories, pair_weight = refs[5:7], refs[7]
+    out_refs, sums_out = refs[8:10], refs[10:12]
+    outs, memory_key, memory_value, bias, scores, peaks, weights, sems = refs[12:]
+    first_frame = scalars[0]
+    frame_count, width = out_refs[0].shape
+    out_copies = [
+        pltpu.make_async_copy(outs.at[rec], out_refs[rec], sems.at[rec]) for rec in range(2)
+    ]
+    heads = width // head_size
+    block = 2 * span_len
+    blocks = frame_count // block
+    near = bias.shape[0]
+    row_count = query.shape[0] // 2
+    memory_count = memories[0].shape[0]
+    lanes = heads * block
 
     rows = lax.broadcasted_iota(jnp.int32, (near, lanes), 0)
     spans = (lax.broadcasted_iota(jnp.int32, (near, lanes), 1) % block) // span_len
@@ -406,17 +424,10 @@
     memory_rows = lax.broadcasted_iota(jnp.int32, (memory_count, lanes), 0)
     feature_head = lax.broadcasted_iota(jnp.int32, (1, width), 1) // head_size
     head_masks = [(feature_head == h).astype(jnp.bfloat16) for h in range(heads)]
-    scale = head_size ** (-0.5) * LOG2_E
-
-    for copy in row_copies + piece_copies(1, False):
-        copy.wait()
-    for part, target in enumerate((query, key, value)):
-        mixed = jnp.dot(
-            rows_in[...],
-            weight[:, part * width : (part + 1) * width],
-            preferred_element_type=jnp.float32,
-        )
-        target[...] = (mixed * scale if part == 0 else mixed).astype(jnp.bfloat16)
+    for rec in range(2):
+        mixed = jnp.dot(memories[rec][...], pair_weight[...], preferred_element_type=jnp.float32)
+        memory_key[rec] = mixed[:, :width].astype(jnp.bfloat16)
+        memory_value[rec] = mixed[:, width:].astype(jnp.bfloat16)
 
     def score_block(i):
         rec, b = divmod(i, blocks)
@@ -425,7 +436,7 @@
         q_now = query[at + start : at + start + block]
         stacked = jnp.concatenate([q_now * m for m in head_masks], axis=0)
         keys = jnp.concatenate(
-            [key[at + start : at + start + near], key[at + memory_at : at + row_count]], axis=0
+            [key[at + start : at + start + near], memory_key[rec]], axis=0
         )
         raw = lax.dot_general(
             keys, stacked, (((1,), (1,)), ((), ())), preferred_element_type=jnp.float32
@@ -453,7 +464,7 @@
         rec, b = divmod(i, blocks)
         at, start = rec * row_count, b * block
         values = jnp.concatenate(
-            [value[at + start : at + start + near], value[at + memory_at : at + row_count]], axis=0
+            [value[at + start : at + start + near], memory_value[rec]], axis=0
         )
         for pair in range(width // LANES):
             columns = slice(pair * LANES, (pair + 1) * LANES)
@@ -482,7 +493,7 @@
         sums_out[rec][...] = jnp.dot(
             members[rec][...], outs[rec], preferred_element_type=jnp.float32
         )
-    for copy in piece_copies(1, True) + out_copies:
+    for copy in out_copies:
         copy.wait()
 
 
@@ -717,41 +728,58 @@
     )
     block = 2 * C
     width = 2 * shard
-    row_count = frame_count + pad + memories.shape[0]
-    keys_seen = block + pad + memories.shape[0]
+    row_count = frame_count + pad
+    memory_count = memories.shape[0]
+    keys_seen = block + pad + memory_count
     lanes = width // head_size * block
     attended, sums, outs = [], [], []
     for pieces in slot_pieces:
         flat = [p for pair in pieces for p in pair]
-        *results, out_piece = local_call(
-            functools.partial(attend_kernel, C, RC, head_size, False),
+        *rows, pair_weight, out_piece = local_call(
+            functools.partial(project_kernel, head_size),
+            (
+                shape_of(2 * row_count, width),
+                shape_of(2 * row_count, width),
+                shape_of(2 * row_count, width),
+                shape_of(model_width, 2 * width),
+                shape_of(model_width, width),
+            ),
+            (scalars,),
+            (normed, ahead, other_normed, other_ahead, *flat),
+            in_place=4 + len(flat),
+            scratch=(
+                pltpu.VMEM((2 * row_count, model_width), bf16),
+                pltpu.VMEM((model_width, width), bf16),
+                pltpu.SemaphoreType.DMA((20,)),
+            ),
+            vmem_mib=16,
+            flops=12 * frame_count * model_width * width,
+            moved=8 * frame_count * model_width,
+        )
+        results = local_call(
+            functools.partial(attend_kernel, C, RC, head_size),
             (
                 shape_of(frame_count, width),
                 shape_of(frame_count, width),
                 shape_of(token_count, width, dtype=jnp.float32),
                 shape_of(token_count, width, dtype=jnp.float32),
-                shape_of(model_width, width),
             ),
             (scalars, other_length),
-            (member, other_member, normed, ahead, memories, other_normed, other_ahead, other_memories, *flat),
-            in_place=6 + len(flat),
-            out_in_place=(True, True, False, False, False),
+            (member, other_member, *rows, memories, other_memories, pair_weight),
+            out_in_place=(True, True, False, False),
             scratch=(
                 pltpu.VMEM((2, frame_count, width), bf16),
-                pltpu.VMEM((2 * row_count, model_width), bf16),
-                pltpu.VMEM((model_width, 3 * width), bf16),
-                pltpu.VMEM((2 * row_count, width), bf16),
-                pltpu.VMEM((2 * row_count, width), bf16),
-                pltpu.VMEM((2 * row_count, width), bf16),
+                pltpu.VMEM((2, memory_count, width), bf16),
+                pltpu.VMEM((2, memory_count, width), bf16),
                 pltpu.VMEM((block + pad, lanes), jnp.float32),
                 pltpu.VMEM((RING, keys_seen, lanes), jnp.float32),
                 pltpu.VMEM((RING, 1, lanes), jnp.float32),
                 pltpu.VMEM((RING, keys_seen, lanes), bf16),
-                pltpu.SemaphoreType.DMA((24,)),
+                pltpu.SemaphoreType.DMA((2,)),
             ),
             vmem_mib=20,
-            flops=12 * frame_count * model_width * width,
-            moved=8 * frame_count * model_width,
+            flops=4 * frame_count * keys_seen * width,
+            moved=8 * frame_count * width,
         )
         attended.append(results[:2])
         sums.append(results[2:])

time: 118 us -> 117 us (level)
  starting transfers between devices: 45.5 us -> 40.8 us
  waiting for transfers between devices: 30.6 us -> 26.2 us
  Pallas kernels: 27.4 us -> 31.6 us
  local copies, waits for them, and re-layouts: 9.19 us -> 12.3 us
    pallas_call x7 -> x9, Pallas kernels: 27.4 us -> 31.6 us  [local_call(): pl.pallas_call(kernel, out_shape=out_shapes, in_specs=[smem_spec()] * len...]
    unnamed x56 -> x68, local copies, waits for them, and re-layouts: 8.36 us -> 12.1 us
    ppermute x22, waiting for transfers between devices: 15.8 us -> 12.5 us  [relocate(): return lax.ppermute(value, ('rec', 'tm'), pairs)]
    ppermute x22, starting transfers between devices: 32.5 us -> 29.6 us  [relocate(): return lax.ppermute(value, ('rec', 'tm'), pairs)]
    ppermute x1, waiting for transfers between devices: 7.66 us -> 4.86 us  [shifted(): return lax.ppermute(block, axis, route)]
    all_to_all x2, starting transfers between devices: 11.6 us -> 9.84 us  [exchange_blocks(): return lax.all_to_all(blocks, 'tm', split_axis=0, concat_axis=0, tiled=True)]
    all_to_all x2, waiting for transfers between devices: 7.12 us -> 8.91 us  [exchange_blocks(): return lax.all_to_all(blocks, 'tm', split_axis=0, concat_axis=0, tiled=True)]
  transfers between devices with their start and end apart: 25 -> 25, of which waited for: 9 -> 10; matrix products, arithmetic and copies ran while one was open for 2% -> 2% of each run, Pallas kernels for 20% -> 24%
where the time goes in v10:
time: 117 us; the launch traced here: 116 us
  starting transfers between devices  40.8 us (35%)
  Pallas kernels  31.6 us (27%)
  waiting for transfers between devices  26.2 us (22%)
  local copies, waits for them, and re-layouts  12.3 us (11%)
  other arithmetic  3.12 us (3%)
  between operations  1.8 us (2%)
    pallas_call x9, Pallas kernels, local_call(): pl.pallas_call(kernel, out_shape=out_shapes, in_specs=[smem_spec()] * len...  31.6 us
    ppermute x22, starting transfers between devices, relocate(): return lax.ppermute(value, ('rec', 'tm'), pairs)  29.6 us
    ppermute x22, waiting for transfers between devices, relocate(): return lax.ppermute(value, ('rec', 'tm'), pairs)  12.5 us
    unnamed x68, local copies, waits for them, and re-layouts  12.1 us
    all_to_all x2, starting transfers between devices, exchange_blocks(): return lax.all_to_all(blocks, 'tm', split_axis=0, concat_axis=0, tiled=True)  9.84 us
    all_to_all x2, waiting for transfers between devices, exchange_blocks(): return lax.all_to_all(blocks, 'tm', split_axis=0, concat_axis=0, tiled=True)  8.91 us
    ppermute x1, waiting for transfers between devices, shifted(): return lax.ppermute(block, axis, route)  4.86 us
  transfers between devices with their start and end apart: 25, of which 10 were waited for; matrix products, arithmetic and copies ran while one was open for 2% of the time, Pallas kernels for 24%

profile of v10, /device:TPU:0, one launch (start us, length us, event | category | flops | bytes accessed | tf_op | source)
XLA Modules:
  0.0 115.9 jit_solution(3943911851472091200)
XLA Ops:
  0.7 1.2 fusion.1.refs_4_
  1.8 3.0 %collective-permute-start.5 = (bf16[4,512,128]{2,1,0:T(8,128)(2,1)S(1)}, bf16[4,512,128]{2,1,0:T(8,128)(2,1)}, u32[]{:S(2)}, u32[]{:S(2)}) collective-permute-start(bf16[4,512,128]{2,1,0:T(8,128)(2,1)S(1)} %fusion.1.refs_4_), channel_id=1, source_target_pairs={{0,1},{1,0},{2,3},{3,2},{4,5},{5,4},{6,7},{7,6},{8,10},{9,11},{10,... | collective-permute-start | bytes 1572872 | tf_op jit(solution)/shard_map/ppermute | solution.py:615
  4.9 1.1 broadcast_select_fusion.1
  6.0 3.6 %collective-permute-start.6 = (bf16[4,512,128]{2,1,0:T(8,128)(2,1)}, bf16[4,512,128]{2,1,0:T(8,128)(2,1)S(1)}, u32[]{:S(2)}, u32[]{:S(2)}) collective-permute-start(bf16[4,512,128]{2,1,0:T(8,128)(2,1)} %get-tuple-element.58), channel_id=1, source_target_pairs={{0,6},{1,7},{2,0},{3,1},{4,2},{5,3},{6,4},{7,5},{8,10},{9,11},{10,... | collective-permute-start | bytes 1572872 | tf_op jit(solution)/shard_map/ppermute | solution.py:615
  9.6 2.6 %collective-permute-done.5.refs_5_.refs_8_ = bf16[4,512,128]{2,1,0:T(8,128)(2,1)} collective-permute-done((bf16[4,512,128]{2,1,0:T(8,128)(2,1)S(1)}, bf16[4,512,128]{2,1,0:T(8,128)(2,1)}, u32[]{:S(2)}, u32[]{:S(2)}) %collective-permute-start.5) | collective-permute-done | bytes 524320 | tf_op jit(solution)/shard_map/ppermute | solution.py:615
  12.1 2.0 %collective-permute-start.7 = (bf16[4,512,128]{2,1,0:T(8,128)(2,1)}, bf16[4,512,128]{2,1,0:T(8,128)(2,1)}, u32[]{:S(2)}, u32[]{:S(2)}) collective-permute-start(bf16[4,512,128]{2,1,0:T(8,128)(2,1)} %collective-permute-done.5.refs_5_.refs_8_), channel_id=1, source_target_pairs={{0,16},{1,17},{2,18},{3,19},{4,20},{5,21},{6,22},{7,23},{8,9},{9,8... | collective-permute-start | bytes 1572872 | tf_op jit(solution)/shard_map/ppermute | solution.py:615
  14.2 1.5 %collective-permute-start.10 = (bf16[4,512,128]{2,1,0:T(8,128)(2,1)}, bf16[4,512,128]{2,1,0:T(8,128)(2,1)}, u32[]{:S(2)}, u32[]{:S(2)}) collective-permute-start(bf16[4,512,128]{2,1,0:T(8,128)(2,1)} %collective-permute-done.5.refs_5_.refs_8_), channel_id=1, source_target_pairs={{8,10},{9,11},{10,12},{11,13},{12,14},{13,15},{14,8},{15,9},{24,26... | collective-permute-start | bytes 1572872 | tf_op jit(solution)/shard_map/ppermute | solution.py:615
  16.4 0.6 copy-done.26
  17.1 1.5 %shard_map.105 = (bf16[512,1024]{1,0:T(8,128)(2,1)S(1)}, bf16[16,1024]{1,0:T(8,128)(2,1)S(1)}, bf16[8,16,1024]{2,1,0:T(8,128)(2,1)S(1)}) custom-call(s32[17]{0:T(128)S(1)} %stack.63.scalars, bf16[512,1024]{1,0:T(8,128)(2,1)S(1)} %bitcast.28, f32[1,1024]{1,0:T(1,128)S(1)} %bitcast.35, f32[1,1024]{1,0:T(1,128)S(1)} %bitcast.36), custom_call_target="tpu_custom_call" | custom-call | flops 5242880 | bytes 2097152 | tf_op jit(solution)/shard_map/pallas_call | solution.py:269
  18.6 3.3 %collective-permute-start.3 = (bf16[512,1024]{1,0:T(8,128)(2,1)S(1)}, bf16[512,1024]{1,0:T(8,128)(2,1)}, u32[]{:S(2)}, u32[]{:S(2)}) collective-permute-start(bf16[512,1024]{1,0:T(8,128)(2,1)S(1)} %get-tuple-element.31.refs_0_), channel_id=1, source_target_pairs={{0,8},{1,9},{2,10},{3,11},{4,12},{5,13},{6,14},{7,15},{8,0},{9,1},... | collective-permute-start | bytes 3145736 | tf_op jit(solution)/shard_map/ppermute | solution.py:615
  21.9 1.1 collective-permute-done.6.refs_7_.refs_4_
  23.5 1.5 %collective-permute-start.8 = (bf16[4,512,128]{2,1,0:T(8,128)(2,1)}, bf16[4,512,128]{2,1,0:T(8,128)(2,1)}, u32[]{:S(2)}, u32[]{:S(2)}) collective-permute-start(bf16[4,512,128]{2,1,0:T(8,128)(2,1)} %collective-permute-done.7.refs_9_.refs_10_), channel_id=1, source_target_pairs={{8,24},{9,25},{10,26},{11,27},{12,28},{13,29},{14,30},{15,31},{24,... | collective-permute-start | bytes 1572872 | tf_op jit(solution)/shard_map/ppermute | solution.py:615
  25.0 0.9 broadcast_select_fusion
  25.9 1.5 %collective-permute-start.11 = (bf16[4,512,128]{2,1,0:T(8,128)(2,1)}, bf16[4,512,128]{2,1,0:T(8,128)(2,1)}, u32[]{:S(2)}, u32[]{:S(2)}) collective-permute-start(bf16[4,512,128]{2,1,0:T(8,128)(2,1)} %broadcast_select_fusion), channel_id=1, source_target_pairs={{0,16},{1,17},{2,18},{3,19},{4,20},{5,21},{6,22},{7,23},{8,9},{9,8... | collective-permute-start | bytes 1572872 | tf_op jit(solution)/shard_map/ppermute | solution.py:615
  27.4 4.9 %collective-permute-done.12.refs_7_.refs_8_ = bf16[4,512,128]{2,1,0:T(8,128)(2,1)} collective-permute-done((bf16[4,512,128]{2,1,0:T(8,128)(2,1)S(1)}, bf16[4,512,128]{2,1,0:T(8,128)(2,1)}, u32[]{:S(2)}, u32[]{:S(2)}) %collective-permute-start.12) | collective-permute-done | bytes 524320 | tf_op jit(solution)/shard_map/ppermute | solution.py:615
  32.3 1.5 %collective-permute-start.13 = (bf16[4,512,128]{2,1,0:T(8,128)(2,1)}, bf16[4,512,128]{2,1,0:T(8,128)(2,1)}, u32[]{:S(2)}, u32[]{:S(2)}) collective-permute-start(bf16[4,512,128]{2,1,0:T(8,128)(2,1)} %collective-permute-done.12.refs_7_.refs_8_), channel_id=1, source_target_pairs={{0,16},{1,17},{2,18},{3,19},{4,20},{5,21},{6,22},{7,23},{8,9},{9,8... | collective-permute-start | bytes 1572872 | tf_op jit(solution)/shard_map/ppermute | solution.py:615
  33.8 1.3 %collective-permute-start.2 = (bf16[16,1024]{1,0:T(8,128)(2,1)S(1)}, bf16[16,1024]{1,0:T(8,128)(2,1)S(1)}, u32[]{:S(2)}, u32[]{:S(2)}) collective-permute-start(bf16[16,1024]{1,0:T(8,128)(2,1)S(1)} %get-tuple-element.32), channel_id=1, source_target_pairs={{1,0},{2,1},{3,2},{4,3},{5,4},{6,5},{7,6},{9,8},{10,9},{11,10},{12... | collective-permute-start | bytes 98312 | tf_op jit(solution)/shard_map/ppermute | solution.py:27
  35.1 4.9 %collective-permute-done.2.refs_1_ = bf16[16,1024]{1,0:T(8,128)(2,1)S(1)} collective-permute-done((bf16[16,1024]{1,0:T(8,128)(2,1)S(1)}, bf16[16,1024]{1,0:T(8,128)(2,1)S(1)}, u32[]{:S(2)}, u32[]{:S(2)}) %collective-permute-start.2) | collective-permute-done | bytes 32800 | tf_op jit(solution)/shard_map/ppermute | solution.py:27
  40.0 6.6 %collective-permute-start.4 = (bf16[16,1024]{1,0:T(8,128)(2,1)S(1)}, bf16[16,1024]{1,0:T(8,128)(2,1)S(1)}, u32[]{:S(2)}, u32[]{:S(2)}) collective-permute-start(bf16[16,1024]{1,0:T(8,128)(2,1)S(1)} %collective-permute-done.2.refs_1_), channel_id=1, source_target_pairs={{0,8},{1,9},{2,10},{3,11},{4,12},{5,13},{6,14},{7,15},{8,0},{9,1},... | collective-permute-start | bytes 98312 | tf_op jit(solution)/shard_map/ppermute | solution.py:615
  46.5 0.9 collective-permute-done.4.refs_3_
  47.4 1.5 %collective-permute-start.21 = (bf16[1024,512]{1,0:T(8,128)(2,1)}, bf16[1024,512]{1,0:T(8,128)(2,1)}, u32[]{:S(2)}, u32[]{:S(2)}) collective-permute-start(bf16[1024,512]{1,0:T(8,128)(2,1)} %refs_0_.1), channel_id=1, source_target_pairs={{0,16},{1,17},{2,18},{3,19},{4,20},{5,21},{6,22},{7,23},{8,24},{9,... | collective-permute-start | bytes 3145736 | tf_op jit(solution)/shard_map/ppermute | solution.py:615
  48.9 3.7 %all-to-all-start = ((bf16[8,16,1024]{2,1,0:T(8,128)(2,1)}), bf16[8,16,1024]{2,1,0:T(8,128)(2,1)S(1)}, u32[]{:S(2)}, u32[]{:S(2)}) async-start(bf16[8,16,1024]{2,1,0:T(8,128)(2,1)} %copy-done.20), calls=%async_computation | async-start | bytes 524288 | tf_op jit(solution)/shard_map/all_to_all | solution.py:623
  52.6 1.0 copy-done.1
  53.7 4.9 %shard_map.106 = (bf16[1056,256]{1,0:T(8,128)(2,1)S(1)}, bf16[1056,256]{1,0:T(8,128)(2,1)S(1)}, bf16[1056,256]{1,0:T(8,128)(2,1)S(1)}, bf16[1024,512]{1,0:T(8,128)(2,1)S(1)}, bf16[1024,256]{1,0:T(8,128)(2,1)}) custom-call(s32[17]{0:T(128)S(1)} %stack.63.scalars, bf16[512,1024]{1,0:T(8,128)(2,1)S(1)} %get-tuple-element.31.refs_0_, ...), custom_call_target="tpu_custom_call" | custom-call | flops 1610612736 | bytes 4194304 | tf_op jit(solution)/shard_map/pallas_call | solution.py:269
  58.6 0.8 copy-done.8
  59.4 0.8 copy-done.10
  60.2 0.8 copy-done.12
  61.0 5.1 %shard_map.108 = (bf16[1056,256]{1,0:T(8,128)(2,1)S(1)}, bf16[1056,256]{1,0:T(8,128)(2,1)S(1)}, bf16[1056,256]{1,0:T(8,128)(2,1)S(1)}, bf16[1024,512]{1,0:T(8,128)(2,1)S(1)}, bf16[1024,256]{1,0:T(8,128)(2,1)}) custom-call(s32[17]{0:T(128)S(1)} %stack.63.scalars, bf16[512,1024]{1,0:T(8,128)(2,1)S(1)} %get-tuple-element.31.refs_0_, ...), custom_call_target="tpu_custom_call" | custom-call | flops 1610612736 | bytes 4194304 | tf_op jit(solution)/shard_map/pallas_call | solution.py:269
  66.1 1.0 copy-done.6
  67.1 0.8 copy-done.14
  67.9 0.8 copy-done.16
  68.7 0.8 copy-done.18
  69.5 0.6 collective-permute-start.17
  70.9 0.6 copy-done.28
  71.5 0.9 shard_map.104
  72.7 1.2 %collective-permute-done.1.refs_1_ = bf16[128,512]{1,0:T(8,128)(2,1)S(1)} collective-permute-done((bf16[128,512]{1,0:T(8,128)(2,1)S(1)}, bf16[128,512]{1,0:T(8,128)(2,1)S(1)}, u32[]{:S(2)}, u32[]{:S(2)}) %collective-permute-start.1) | collective-permute-done | bytes 131104 | tf_op jit(solution)/shard_map/ppermute | solution.py:615
  73.8 1.0 copy-done.9
  74.9 1.0 copy-done.11
  75.9 1.0 copy-done.13
  77.0 4.0 %shard_map.107 = (bf16[512,256]{1,0:T(8,128)(2,1)S(1)}, bf16[512,256]{1,0:T(8,128)(2,1)S(1)}, f32[128,256]{1,0:T(8,128)S(1)}, f32[128,256]{1,0:T(8,128)S(1)}) custom-call(s32[17]{0:T(128)S(1)} %stack.63.scalars, s32[1]{0:T(128)} %collective-permute-done.other_length, bf16[128,512]{1,0:T(8,128)(2,1)S(1)} %get-tuple-element.30.refs_0_, ...), custom_call_target="tpu_custom_call" | custom-call | flops 109051904 | bytes 1048576 | tf_op jit(solution)/shard_map/pallas_call | solution.py:269
  81.0 0.7 copy-done.29
  81.9 3.8 %shard_map.109 = (bf16[512,256]{1,0:T(8,128)(2,1)S(1)}, bf16[512,256]{1,0:T(8,128)(2,1)S(1)}, f32[128,256]{1,0:T(8,128)S(1)}, f32[128,256]{1,0:T(8,128)S(1)}) custom-call(s32[17]{0:T(128)S(1)} %stack.63.scalars, s32[1]{0:T(128)} %collective-permute-done.other_length, bf16[128,512]{1,0:T(8,128)(2,1)S(1)} %get-tuple-element.30.refs_0_, ...), custom_call_target="tpu_custom_call" | custom-call | flops 109051904 | bytes 1048576 | tf_op jit(solution)/shard_map/pallas_call | solution.py:269
  87.1 3.1 %shard_map.111 = bf16[256,1024]{1,0:T(8,128)(2,1)} custom-call(s32[17]{0:T(128)S(1)} %stack.63.scalars, f32[128,1024]{1,0:T(8,128)S(1)} %get-tuple-element.51.base, f32[128,128]{1,0:T(8,128)S(1)} %get-tuple-element.52.inverse, bf16[256,128]{1,0:T(8,128)(2,1)S(1)} %get-tuple-element.53.route, f32[128,256]{1,0:T(8,128)S(1)} %get-tuple-element.54.refs_0_, ...), custom_call_target="tpu_custom_call" | custom-call | flops 536870912 | bytes 3145728 | tf_op jit(solution)/shard_map/pallas_call | solution.py:269
  90.2 6.1 %all-to-all-start.1 = ((bf16[8,32,1024]{2,1,0:T(8,128)(2,1)}), bf16[8,32,1024]{2,1,0:T(8,128)(2,1)S(1)}, u32[]{:S(2)}, u32[]{:S(2)}) async-start(bf16[8,32,1024]{2,1,0:T(8,128)(2,1)} %bitcast.25), calls=%async_computation.1 | async-start | bytes 1048576 | tf_op jit(solution)/shard_map/all_to_all | solution.py:623
  97.0 1.0 collective-permute-done.14.refs_2_
  98.4 4.1 %shard_map.110 = bf16[512,1024]{1,0:T(8,128)(2,1)} custom-call(s32[17]{0:T(128)S(1)} %stack.63.scalars, bf16[512,256]{1,0:T(8,128)(2,1)S(1)} %copy-done.22, bf16[512,256]{1,0:T(8,128)(2,1)S(1)} %copy-done.24, bf16[512,256]{1,0:T(8,128)(2,1)S(1)} %collective-permute-done.14.refs_2_, bf16[512,256]{1,0:T(8,128)(2,1)S(1)} %collective-permute-done.15.refs_3_, ...), custom_call_target="tpu_custom_call" | custom-call | flops 1073741824 | bytes 3145728 | tf_op jit(solution)/shard_map/pallas_call | solution.py:269
  102.5 8.9 %all-to-all-done.1 = bf16[8,32,1024]{2,1,0:T(8,128)(2,1)S(1)} async-done(((bf16[8,32,1024]{2,1,0:T(8,128)(2,1)}), bf16[8,32,1024]{2,1,0:T(8,128)(2,1)S(1)}, u32[]{:S(2)}, u32[]{:S(2)}) %all-to-all-start.1) | async-done | bytes 524320 | tf_op jit(solution)/shard_map/all_to_all | solution.py:623
  111.4 4.3 %shard_map.112 = bf16[256,2048]{1,0:T(8,128)(2,1)} custom-call(s32[17]{0:T(128)S(1)} %stack.63.scalars, bf16[256,1024]{1,0:T(8,128)(2,1)S(1)} %bitcast.34, bf16[1024,512]{1,0:T(8,128)(2,1)} %refs_0_.1, bf16[1024,512]{1,0:T(8,128)(2,1)} %collective-permute-done.20.refs_1_, bf16[1024,512]{1,0:T(8,128)(2,1)} %collective-permute-done.21.refs_2_, ...), custom_call_target="tpu_custom_call" | custom-call | flops 1073741824 | bytes 4194304 | tf_op jit(solution)/shard_map/pallas_call | solution.py:269
  (84 shorter events, 4.5 us)
Async XLA Ops:
  0.7 4.2 %copy-start.32 = (bf16[3,1024,128]{2,1,0:T(8,128)(2,1)S(1)}, bf16[3,1024,128]{2,1,0:T(8,128)(2,1)}, u32[]{:S(2)}) copy-start(bf16[3,1024,128]{2,1,0:T(8,128)(2,1)} %param.13) | copy-start | bytes 2359300
  0.7 4.2 %copy-start.33 = (bf16[1024,128]{1,0:T(8,128)(2,1)S(1)}, bf16[1024,128]{1,0:T(8,128)(2,1)}, u32[]{:S(2)}) copy-start(bf16[1024,128]{1,0:T(8,128)(2,1)} %param.14) | copy-start | bytes 786436
  1.8 10.3 %collective-permute-start.5 = (bf16[4,512,128]{2,1,0:T(8,128)(2,1)S(1)}, bf16[4,512,128]{2,1,0:T(8,128)(2,1)}, u32[]{:S(2)}, u32[]{:S(2)}) collective-permute-start(bf16[4,512,128]{2,1,0:T(8,128)(2,1)S(1)} %fusion.1.refs_4_), channel_id=1, source_target_pairs={{0,1},{1,0},{2,3},{3,2},{4,5},{5,4},{6,7},{7,6},{8,10},{9,11},{10,... | collective-permute-start | bytes 1572872 | tf_op jit(solution)/shard_map/ppermute | solution.py:615
  4.9 11.6 %copy-start = (bf16[1,512,1024]{2,1,0:T(8,128)(2,1)S(1)}, bf16[1,512,1024]{2,1,0:T(8,128)(2,1)}, u32[]{:S(2)}) copy-start(bf16[1,512,1024]{2,1,0:T(8,128)(2,1)} %param.9) | copy-start | bytes 3145732
  6.0 17.0 %collective-permute-start.6 = (bf16[4,512,128]{2,1,0:T(8,128)(2,1)}, bf16[4,512,128]{2,1,0:T(8,128)(2,1)S(1)}, u32[]{:S(2)}, u32[]{:S(2)}) collective-permute-start(bf16[4,512,128]{2,1,0:T(8,128)(2,1)} %get-tuple-element.58), channel_id=1, source_target_pairs={{0,6},{1,7},{2,0},{3,1},{4,2},{5,3},{6,4},{7,5},{8,10},{9,11},{10,... | collective-permute-start | bytes 1572872 | tf_op jit(solution)/shard_map/ppermute | solution.py:615
  12.1 11.4 %collective-permute-start.7 = (bf16[4,512,128]{2,1,0:T(8,128)(2,1)}, bf16[4,512,128]{2,1,0:T(8,128)(2,1)}, u32[]{:S(2)}, u32[]{:S(2)}) collective-permute-start(bf16[4,512,128]{2,1,0:T(8,128)(2,1)} %collective-permute-done.5.refs_5_.refs_8_), channel_id=1, source_target_pairs={{0,16},{1,17},{2,18},{3,19},{4,20},{5,21},{6,22},{7,23},{8,9},{9,8... | collective-permute-start | bytes 1572872 | tf_op jit(solution)/shard_map/ppermute | solution.py:615
  14.2 10.8 %collective-permute-start.10 = (bf16[4,512,128]{2,1,0:T(8,128)(2,1)}, bf16[4,512,128]{2,1,0:T(8,128)(2,1)}, u32[]{:S(2)}, u32[]{:S(2)}) collective-permute-start(bf16[4,512,128]{2,1,0:T(8,128)(2,1)} %collective-permute-done.5.refs_5_.refs_8_), channel_id=1, source_target_pairs={{8,10},{9,11},{10,12},{11,13},{12,14},{13,15},{14,8},{15,9},{24,26... | collective-permute-start | bytes 1572872 | tf_op jit(solution)/shard_map/ppermute | solution.py:615
  18.6 7.3 %copy-start.20 = (bf16[8,16,1024]{2,1,0:T(8,128)(2,1)}, bf16[8,16,1024]{2,1,0:T(8,128)(2,1)S(1)}, u32[]{:S(2)}) copy-start(bf16[8,16,1024]{2,1,0:T(8,128)(2,1)S(1)} %get-tuple-element.39) | copy-start | bytes 786436
  18.6 34.0 %collective-permute-start.3 = (bf16[512,1024]{1,0:T(8,128)(2,1)S(1)}, bf16[512,1024]{1,0:T(8,128)(2,1)}, u32[]{:S(2)}, u32[]{:S(2)}) collective-permute-start(bf16[512,1024]{1,0:T(8,128)(2,1)S(1)} %get-tuple-element.31.refs_0_), channel_id=1, source_target_pairs={{0,8},{1,9},{2,10},{3,11},{4,12},{5,13},{6,14},{7,15},{8,0},{9,1},... | collective-permute-start | bytes 3145736 | tf_op jit(solution)/shard_map/ppermute | solution.py:615
  23.0 9.3 %collective-permute-start.12 = (bf16[4,512,128]{2,1,0:T(8,128)(2,1)S(1)}, bf16[4,512,128]{2,1,0:T(8,128)(2,1)}, u32[]{:S(2)}, u32[]{:S(2)}) collective-permute-start(bf16[4,512,128]{2,1,0:T(8,128)(2,1)S(1)} %collective-permute-done.6.refs_7_.refs_4_), channel_id=1, source_target_pairs={{0,1},{1,0},{2,3},{3,2},{4,5},{5,4},{6,7},{7,6},{8,10},{9,11},{10,... | collective-permute-start | bytes 1572872 | tf_op jit(solution)/shard_map/ppermute | solution.py:615
  23.5 29.1 %collective-permute-start.8 = (bf16[4,512,128]{2,1,0:T(8,128)(2,1)}, bf16[4,512,128]{2,1,0:T(8,128)(2,1)}, u32[]{:S(2)}, u32[]{:S(2)}) collective-permute-start(bf16[4,512,128]{2,1,0:T(8,128)(2,1)} %collective-permute-done.7.refs_9_.refs_10_), channel_id=1, source_target_pairs={{8,24},{9,25},{10,26},{11,27},{12,28},{13,29},{14,30},{15,31},{24,... | collective-permute-start | bytes 1572872 | tf_op jit(solution)/shard_map/ppermute | solution.py:615
  25.9 35.1 %collective-permute-start.11 = (bf16[4,512,128]{2,1,0:T(8,128)(2,1)}, bf16[4,512,128]{2,1,0:T(8,128)(2,1)}, u32[]{:S(2)}, u32[]{:S(2)}) collective-permute-start(bf16[4,512,128]{2,1,0:T(8,128)(2,1)} %broadcast_select_fusion), channel_id=1, source_target_pairs={{0,16},{1,17},{2,18},{3,19},{4,20},{5,21},{6,22},{7,23},{8,9},{9,8... | collective-permute-start | bytes 1572872 | tf_op jit(solution)/shard_map/ppermute | solution.py:615
  32.3 28.7 %collective-permute-start.13 = (bf16[4,512,128]{2,1,0:T(8,128)(2,1)}, bf16[4,512,128]{2,1,0:T(8,128)(2,1)}, u32[]{:S(2)}, u32[]{:S(2)}) collective-permute-start(bf16[4,512,128]{2,1,0:T(8,128)(2,1)} %collective-permute-done.12.refs_7_.refs_8_), channel_id=1, source_target_pairs={{0,16},{1,17},{2,18},{3,19},{4,20},{5,21},{6,22},{7,23},{8,9},{9,8... | collective-permute-start | bytes 1572872 | tf_op jit(solution)/shard_map/ppermute | solution.py:615
  33.8 6.1 %collective-permute-start.2 = (bf16[16,1024]{1,0:T(8,128)(2,1)S(1)}, bf16[16,1024]{1,0:T(8,128)(2,1)S(1)}, u32[]{:S(2)}, u32[]{:S(2)}) collective-permute-start(bf16[16,1024]{1,0:T(8,128)(2,1)S(1)} %get-tuple-element.32), channel_id=1, source_target_pairs={{1,0},{2,1},{3,2},{4,3},{5,4},{6,5},{7,6},{9,8},{10,9},{11,10},{12... | collective-permute-start | bytes 98312 | tf_op jit(solution)/shard_map/ppermute | solution.py:27
  40.0 7.4 %collective-permute-start.4 = (bf16[16,1024]{1,0:T(8,128)(2,1)S(1)}, bf16[16,1024]{1,0:T(8,128)(2,1)S(1)}, u32[]{:S(2)}, u32[]{:S(2)}) collective-permute-start(bf16[16,1024]{1,0:T(8,128)(2,1)S(1)} %collective-permute-done.2.refs_1_), channel_id=1, source_target_pairs={{0,8},{1,9},{2,10},{3,11},{4,12},{5,13},{6,14},{7,15},{8,0},{9,1},... | collective-permute-start | bytes 98312 | tf_op jit(solution)/shard_map/ppermute | solution.py:615
  47.4 38.7 %collective-permute-start.21 = (bf16[1024,512]{1,0:T(8,128)(2,1)}, bf16[1024,512]{1,0:T(8,128)(2,1)}, u32[]{:S(2)}, u32[]{:S(2)}) collective-permute-start(bf16[1024,512]{1,0:T(8,128)(2,1)} %refs_0_.1), channel_id=1, source_target_pairs={{0,16},{1,17},{2,18},{3,19},{4,20},{5,21},{6,22},{7,23},{8,24},{9,... | collective-permute-start | bytes 3145736 | tf_op jit(solution)/shard_map/ppermute | solution.py:615
  48.9 21.3 %all-to-all-start = ((bf16[8,16,1024]{2,1,0:T(8,128)(2,1)}), bf16[8,16,1024]{2,1,0:T(8,128)(2,1)S(1)}, u32[]{:S(2)}, u32[]{:S(2)}) async-start(bf16[8,16,1024]{2,1,0:T(8,128)(2,1)} %copy-done.20), calls=%async_computation | async-start | bytes 524288 | tf_op jit(solution)/shard_map/all_to_all | solution.py:623
  52.6 1.0 copy-start.1
  61.0 5.1 %copy-start.4 = (bf16[1024,512]{1,0:T(8,128)(2,1)}, bf16[1024,512]{1,0:T(8,128)(2,1)S(1)}, u32[]{:S(2)}) copy-start(bf16[1024,512]{1,0:T(8,128)(2,1)S(1)} %get-tuple-element.40.refs_7_) | copy-start | bytes 3145732
  61.0 26.1 %collective-permute-start.16 = (bf16[1024,256]{1,0:T(8,128)(2,1)}, bf16[1024,256]{1,0:T(8,128)(2,1)S(1)}, u32[]{:S(2)}, u32[]{:S(2)}) collective-permute-start(bf16[1024,256]{1,0:T(8,128)(2,1)} %get-tuple-element.49.refs_4_), channel_id=1, source_target_pairs={{0,8},{1,9},{2,10},{3,11},{4,12},{5,13},{6,14},{7,15},{8,0},{9,1},... | collective-permute-start | bytes 1572872 | tf_op jit(solution)/shard_map/ppermute | solution.py:615
  66.1 1.0 copy-start.6
  69.5 17.6 %collective-permute-start.17 = (bf16[1024,256]{1,0:T(8,128)(2,1)}, bf16[1024,256]{1,0:T(8,128)(2,1)S(1)}, u32[]{:S(2)}, u32[]{:S(2)}) collective-permute-start(bf16[1024,256]{1,0:T(8,128)(2,1)} %get-tuple-element.50.refs_5_), channel_id=1, source_target_pairs={{0,8},{1,9},{2,10},{3,11},{4,12},{5,13},{6,14},{7,15},{8,0},{9,1},... | collective-permute-start | bytes 1572872 | tf_op jit(solution)/shard_map/ppermute | solution.py:615
  70.2 3.7 %collective-permute-start.9 = (bf16[128,1024]{1,0:T(8,128)(2,1)S(1)}, bf16[128,1024]{1,0:T(8,128)(2,1)S(1)}, u32[]{:S(2)}, u32[]{:S(2)}) collective-permute-start(bf16[128,1024]{1,0:T(8,128)(2,1)S(1)} %bitcast.31), channel_id=1, source_target_pairs={{0,8},{1,9},{2,10},{3,11},{4,12},{5,13},{6,14},{7,15},{8,0},{9,1},... | collective-permute-start | bytes 786440 | tf_op jit(solution)/shard_map/ppermute | solution.py:615
  70.2 2.2 %collective-permute-start = (s32[1]{0:T(128)}, s32[1]{0:T(128)}, u32[]{:S(2)}, u32[]{:S(2)}) collective-permute-start(s32[1]{0:T(128)} %param.10), channel_id=1, source_target_pairs={{0,8},{1,9},{2,10},{3,11},{4,12},{5,13},{6,14},{7,15},{8,0},{9,1},... | collective-permute-start | bytes 20 | tf_op jit(solution)/shard_map/ppermute | solution.py:615
  70.9 2.9 %copy-start.5 = (bf16[1024,512]{1,0:T(8,128)(2,1)S(1)}, bf16[1024,512]{1,0:T(8,128)(2,1)}, u32[]{:S(2)}) copy-start(bf16[1024,512]{1,0:T(8,128)(2,1)} %copy-done.4) | copy-start | bytes 3145732
  72.4 1.4 %collective-permute-start.1 = (bf16[128,512]{1,0:T(8,128)(2,1)S(1)}, bf16[128,512]{1,0:T(8,128)(2,1)S(1)}, u32[]{:S(2)}, u32[]{:S(2)}) collective-permute-start(bf16[128,512]{1,0:T(8,128)(2,1)S(1)} %get-tuple-element.30.refs_0_), channel_id=1, source_target_pairs={{0,8},{1,9},{2,10},{3,11},{4,12},{5,13},{6,14},{7,15},{8,0},{9,1},... | collective-permute-start | bytes 393224 | tf_op jit(solution)/shard_map/ppermute | solution.py:615
  73.8 1.0 copy-start.9
  74.9 1.0 copy-start.11
  75.9 1.0 copy-start.13
  77.0 4.9 %copy-start.7 = (bf16[1024,512]{1,0:T(8,128)(2,1)S(1)}, bf16[1024,512]{1,0:T(8,128)(2,1)}, u32[]{:S(2)}) copy-start(bf16[1024,512]{1,0:T(8,128)(2,1)} %copy-done.6) | copy-start | bytes 3145732
  77.0 4.9 %copy-start.15 = (bf16[1056,256]{1,0:T(8,128)(2,1)S(1)}, bf16[1056,256]{1,0:T(8,128)(2,1)}, u32[]{:S(2)}) copy-start(bf16[1056,256]{1,0:T(8,128)(2,1)} %copy-done.14) | copy-start | bytes 1622020
  77.0 4.9 %copy-start.17 = (bf16[1056,256]{1,0:T(8,128)(2,1)S(1)}, bf16[1056,256]{1,0:T(8,128)(2,1)}, u32[]{:S(2)}) copy-start(bf16[1056,256]{1,0:T(8,128)(2,1)} %copy-done.16) | copy-start | bytes 1622020
  77.0 4.9 %copy-start.19 = (bf16[1056,256]{1,0:T(8,128)(2,1)S(1)}, bf16[1056,256]{1,0:T(8,128)(2,1)}, u32[]{:S(2)}) copy-start(bf16[1056,256]{1,0:T(8,128)(2,1)} %copy-done.18) | copy-start | bytes 1622020
  81.7 4.0 %copy-start.21 = (bf16[512,256]{1,0:T(8,128)(2,1)}, bf16[512,256]{1,0:T(8,128)(2,1)S(1)}, u32[]{:S(2)}) copy-start(bf16[512,256]{1,0:T(8,128)(2,1)S(1)} %get-tuple-element.41.refs_0_) | copy-start | bytes 786436
  81.7 4.6 %collective-permute-start.18 = (f32[128,256]{1,0:T(8,128)S(1)}, f32[128,256]{1,0:T(8,128)S(1)}, u32[]{:S(2)}, u32[]{:S(2)}) collective-permute-start(f32[128,256]{1,0:T(8,128)S(1)} %get-tuple-element.56), channel_id=1, source_target_pairs={{0,8},{1,9},{2,10},{3,11},{4,12},{5,13},{6,14},{7,15},{8,0},{9,1},... | collective-permute-start | bytes 393224 | tf_op jit(solution)/shard_map/ppermute | solution.py:615
  85.7 4.5 %copy-start.23 = (bf16[512,256]{1,0:T(8,128)(2,1)}, bf16[512,256]{1,0:T(8,128)(2,1)S(1)}, u32[]{:S(2)}) copy-start(bf16[512,256]{1,0:T(8,128)(2,1)S(1)} %get-tuple-element.46.refs_1_) | copy-start | bytes 786436
  85.7 4.5 %copy-start.31 = (bf16[512,256]{1,0:T(8,128)(2,1)}, bf16[512,256]{1,0:T(8,128)(2,1)S(1)}, u32[]{:S(2)}) copy-start(bf16[512,256]{1,0:T(8,128)(2,1)S(1)} %get-tuple-element.48) | copy-start | bytes 786436
  85.7 1.4 %collective-permute-start.19 = (f32[128,256]{1,0:T(8,128)S(1)}, f32[128,256]{1,0:T(8,128)S(1)}, u32[]{:S(2)}, u32[]{:S(2)}) collective-permute-start(f32[128,256]{1,0:T(8,128)S(1)} %get-tuple-element.57), channel_id=1, source_target_pairs={{0,8},{1,9},{2,10},{3,11},{4,12},{5,13},{6,14},{7,15},{8,0},{9,1},... | collective-permute-start | bytes 393224 | tf_op jit(solution)/shard_map/ppermute | solution.py:615
  86.1 16.4 %collective-permute-start.20 = (bf16[1024,512]{1,0:T(8,128)(2,1)}, bf16[1024,512]{1,0:T(8,128)(2,1)}, u32[]{:S(2)}, u32[]{:S(2)}) collective-permute-start(bf16[1024,512]{1,0:T(8,128)(2,1)} %refs_0_.1), channel_id=1, source_target_pairs={{0,8},{1,9},{2,10},{3,11},{4,12},{5,13},{6,14},{7,15},{8,0},{9,1},... | collective-permute-start | bytes 3145736 | tf_op jit(solution)/shard_map/ppermute | solution.py:615
  86.3 16.2 %collective-permute-start.22 = (bf16[1024,512]{1,0:T(8,128)(2,1)}, bf16[1024,512]{1,0:T(8,128)(2,1)}, u32[]{:S(2)}, u32[]{:S(2)}) collective-permute-start(bf16[1024,512]{1,0:T(8,128)(2,1)} %collective-permute-done.21.refs_2_), channel_id=1, source_target_pairs={{0,8},{1,9},{2,10},{3,11},{4,12},{5,13},{6,14},{7,15},{8,0},{9,1},... | collective-permute-start | bytes 3145736 | tf_op jit(solution)/shard_map/ppermute | solution.py:615
  87.1 3.1 %copy-start.2 = (bf16[1024,256]{1,0:T(8,128)(2,1)}, bf16[1024,256]{1,0:T(8,128)(2,1)S(1)}, u32[]{:S(2)}) copy-start(bf16[1024,256]{1,0:T(8,128)(2,1)S(1)} %collective-permute-done.16.refs_6_) | copy-start | bytes 1572868
  87.1 9.2 %copy-start.30 = (bf16[512,256]{1,0:T(8,128)(2,1)S(1)}, bf16[512,256]{1,0:T(8,128)(2,1)}, u32[]{:S(2)}) copy-start(bf16[512,256]{1,0:T(8,128)(2,1)} %copy-done.29) | copy-start | bytes 786436
  90.2 8.1 %copy-start.3 = (bf16[1024,256]{1,0:T(8,128)(2,1)S(1)}, bf16[1024,256]{1,0:T(8,128)(2,1)}, u32[]{:S(2)}) copy-start(bf16[1024,256]{1,0:T(8,128)(2,1)} %copy-done.2) | copy-start | bytes 1572868
  90.2 8.1 %copy-start.22 = (bf16[512,256]{1,0:T(8,128)(2,1)S(1)}, bf16[512,256]{1,0:T(8,128)(2,1)}, u32[]{:S(2)}) copy-start(bf16[512,256]{1,0:T(8,128)(2,1)} %copy-done.21) | copy-start | bytes 786436
  90.2 8.1 %copy-start.24 = (bf16[512,256]{1,0:T(8,128)(2,1)S(1)}, bf16[512,256]{1,0:T(8,128)(2,1)}, u32[]{:S(2)}) copy-start(bf16[512,256]{1,0:T(8,128)(2,1)} %copy-done.23) | copy-start | bytes 786436
  90.2 21.1 %all-to-all-start.1 = ((bf16[8,32,1024]{2,1,0:T(8,128)(2,1)}), bf16[8,32,1024]{2,1,0:T(8,128)(2,1)S(1)}, u32[]{:S(2)}, u32[]{:S(2)}) async-start(bf16[8,32,1024]{2,1,0:T(8,128)(2,1)} %bitcast.25), calls=%async_computation.1 | async-start | bytes 1048576 | tf_op jit(solution)/shard_map/all_to_all | solution.py:623
  96.4 1.6 %collective-permute-start.14 = (bf16[512,256]{1,0:T(8,128)(2,1)S(1)}, bf16[512,256]{1,0:T(8,128)(2,1)S(1)}, u32[]{:S(2)}, u32[]{:S(2)}) collective-permute-start(bf16[512,256]{1,0:T(8,128)(2,1)S(1)} %copy-done.30), channel_id=1, source_target_pairs={{0,8},{1,9},{2,10},{3,11},{4,12},{5,13},{6,14},{7,15},{8,0},{9,1},... | collective-permute-start | bytes 786440 | tf_op jit(solution)/shard_map/ppermute | solution.py:615
  96.5 1.8 %collective-permute-start.15 = (bf16[512,256]{1,0:T(8,128)(2,1)}, bf16[512,256]{1,0:T(8,128)(2,1)S(1)}, u32[]{:S(2)}, u32[]{:S(2)}) collective-permute-start(bf16[512,256]{1,0:T(8,128)(2,1)} %copy-done.31), channel_id=1, source_target_pairs={{0,8},{1,9},{2,10},{3,11},{4,12},{5,13},{6,14},{7,15},{8,0},{9,1},... | collective-permute-start | bytes 786440 | tf_op jit(solution)/shard_map/ppermute | solution.py:615
  (11 other events, 8.3 us)

commit v11 on v9

--- a/solution.py
+++ b/solution.py
@@ -549,17 +549,25 @@
     pieces, out = refs[:-6], refs[-6]
     rows, weights, product, sems, out_sems = refs[-5:]
     count, width = len(pieces), pieces[0].shape[1]
-    row_copy = pltpu.make_async_copy(received, rows, sems.at[count])
+    row_copy = pltpu.make_async_copy(received, rows, sems.at[4 * count])
     row_copy.start()
-    copies = [
-        pltpu.make_async_copy(piece, weights.at[i], sems.at[i]) for i, piece in enumerate(pieces)
-    ]
+    quarter = pieces[0].shape[0] // 4
+    copies = []
+    for i, piece in enumerate(pieces):
+        for part in range(4):
+            part_rows = pl.ds(part * quarter, quarter)
+            copies.append(
+                pltpu.make_async_copy(
+                    piece.at[part_rows], weights.at[i, part_rows], sems.at[4 * i + part]
+                )
+            )
     for copy in copies:
         copy.start()
     row_copy.wait()
     out_copies = []
     for i in range(count):
-        copies[i].wait()
+        for copy in copies[4 * i : 4 * i + 4]:
+            copy.wait()
         product[i] = jnp.dot(
             rows[...], weights[i], preferred_element_type=jnp.float32
         ).astype(jnp.bfloat16)
@@ -798,7 +806,7 @@
             pltpu.VMEM((slot_count, model_width), bf16),
             pltpu.VMEM((rec_count, model_width, language_shard), bf16),
             pltpu.VMEM((rec_count, slot_count, language_shard), bf16),
-            pltpu.SemaphoreType.DMA((rec_count + 1,)),
+            pltpu.SemaphoreType.DMA((4 * rec_count + 1,)),
             pltpu.SemaphoreType.DMA((rec_count,)),
         ),
         flops=2 * slot_count * model_width * rec_count * language_shard,

time: 118 us -> 118 us (level)
  no operation moved by 1% of the time
where the time goes in v11:
time: 118 us; the launch traced here: 117 us
  starting transfers between devices  45.5 us (39%)
  waiting for transfers between devices  30.6 us (26%)
  Pallas kernels  27.4 us (23%)
  local copies, waits for them, and re-layouts  9.19 us (8%)
  other arithmetic  2.32 us (2%)
  between operations  1.79 us (2%)
    ppermute x22, starting transfers between devices, relocate(): return lax.ppermute(value, ('rec', 'tm'), pairs)  32.5 us
    pallas_call x7, Pallas kernels, local_call(): pl.pallas_call(kernel, out_shape=out_shapes, in_specs=[smem_spec()] * len...  27.4 us
    ppermute x22, waiting for transfers between devices, relocate(): return lax.ppermute(value, ('rec', 'tm'), pairs)  15.8 us
    all_to_all x2, starting transfers between devices, exchange_blocks(): return lax.all_to_all(blocks, 'tm', split_axis=0, concat_axis=0, tiled=True)  11.6 us
    unnamed x56, local copies, waits for them, and re-layouts  8.36 us
    ppermute x1, waiting for transfers between devices, shifted(): return lax.ppermute(block, axis, route)  7.66 us
    all_to_all x2, waiting for transfers between devices, exchange_blocks(): return lax.all_to_all(blocks, 'tm', split_axis=0, concat_axis=0, tiled=True)  7.12 us
  transfers between devices with their start and end apart: 25, of which 9 were waited for; matrix products, arithmetic and copies ran while one was open for 2% of the time, Pallas kernels for 20%

profile of v11, /device:TPU:0, one launch (start us, length us, event | category | flops | bytes accessed | tf_op | source)
XLA Modules:
  0.0 116.9 jit_solution(8429804974787772171)
XLA Ops:
  0.7 1.2 fusion.1.refs_8_
  1.8 3.0 %collective-permute-start.6 = (bf16[4,512,128]{2,1,0:T(8,128)(2,1)S(1)}, bf16[4,512,128]{2,1,0:T(8,128)(2,1)}, u32[]{:S(2)}, u32[]{:S(2)}) collective-permute-start(bf16[4,512,128]{2,1,0:T(8,128)(2,1)S(1)} %fusion.1.refs_8_), channel_id=1, source_target_pairs={{0,1},{1,0},{2,3},{3,2},{4,5},{5,4},{6,7},{7,6},{8,10},{9,11},{10,... | collective-permute-start | bytes 1572872 | tf_op jit(solution)/shard_map/ppermute | solution.py:612
  4.9 1.1 broadcast_select_fusion.1
  6.0 3.6 %collective-permute-start.7 = (bf16[4,512,128]{2,1,0:T(8,128)(2,1)}, bf16[4,512,128]{2,1,0:T(8,128)(2,1)S(1)}, u32[]{:S(2)}, u32[]{:S(2)}) collective-permute-start(bf16[4,512,128]{2,1,0:T(8,128)(2,1)} %get-tuple-element.42), channel_id=1, source_target_pairs={{0,6},{1,7},{2,0},{3,1},{4,2},{5,3},{6,4},{7,5},{8,10},{9,11},{10,... | collective-permute-start | bytes 1572872 | tf_op jit(solution)/shard_map/ppermute | solution.py:612
  9.6 2.6 %collective-permute-done.6.refs_9_.refs_12_ = bf16[4,512,128]{2,1,0:T(8,128)(2,1)} collective-permute-done((bf16[4,512,128]{2,1,0:T(8,128)(2,1)S(1)}, bf16[4,512,128]{2,1,0:T(8,128)(2,1)}, u32[]{:S(2)}, u32[]{:S(2)}) %collective-permute-start.6) | collective-permute-done | bytes 524320 | tf_op jit(solution)/shard_map/ppermute | solution.py:612
  12.1 2.0 %collective-permute-start.8 = (bf16[4,512,128]{2,1,0:T(8,128)(2,1)}, bf16[4,512,128]{2,1,0:T(8,128)(2,1)}, u32[]{:S(2)}, u32[]{:S(2)}) collective-permute-start(bf16[4,512,128]{2,1,0:T(8,128)(2,1)} %collective-permute-done.6.refs_9_.refs_12_), channel_id=1, source_target_pairs={{0,16},{1,17},{2,18},{3,19},{4,20},{5,21},{6,22},{7,23},{8,9},{9,8... | collective-permute-start | bytes 1572872 | tf_op jit(solution)/shard_map/ppermute | solution.py:612
  14.2 1.5 %collective-permute-start.10 = (bf16[4,512,128]{2,1,0:T(8,128)(2,1)}, bf16[4,512,128]{2,1,0:T(8,128)(2,1)}, u32[]{:S(2)}, u32[]{:S(2)}) collective-permute-start(bf16[4,512,128]{2,1,0:T(8,128)(2,1)} %collective-permute-done.6.refs_9_.refs_12_), channel_id=1, source_target_pairs={{8,10},{9,11},{10,12},{11,13},{12,14},{13,15},{14,8},{15,9},{24,26... | collective-permute-start | bytes 1572872 | tf_op jit(solution)/shard_map/ppermute | solution.py:612
  16.4 0.6 copy-done.21
  17.0 0.1 copy-done.20
  17.1 1.5 %shard_map.105 = (bf16[512,1024]{1,0:T(8,128)(2,1)S(1)}, bf16[16,1024]{1,0:T(8,128)(2,1)S(1)}, bf16[8,16,1024]{2,1,0:T(8,128)(2,1)S(1)}) custom-call(s32[17]{0:T(128)S(1)} %stack.63.scalars, bf16[512,1024]{1,0:T(8,128)(2,1)S(1)} %bitcast.28, f32[1,1024]{1,0:T(1,128)S(1)} %bitcast.35, f32[1,1024]{1,0:T(1,128)S(1)} %bitcast.36), custom_call_target="tpu_custom_call" | custom-call | flops 5242880 | bytes 2097152 | tf_op jit(solution)/shard_map/pallas_call | solution.py:269
  18.6 0.7 copy-done.11
  19.3 5.8 %all-to-all-start = ((bf16[8,16,1024]{2,1,0:T(8,128)(2,1)}), bf16[8,16,1024]{2,1,0:T(8,128)(2,1)S(1)}, u32[]{:S(2)}, u32[]{:S(2)}) async-start(bf16[8,16,1024]{2,1,0:T(8,128)(2,1)} %copy-done.11), calls=%async_computation | async-start | bytes 524288 | tf_op jit(solution)/shard_map/all_to_all | solution.py:620
  25.1 2.0 %collective-permute-start.3 = (bf16[512,1024]{1,0:T(8,128)(2,1)S(1)}, bf16[512,1024]{1,0:T(8,128)(2,1)}, u32[]{:S(2)}, u32[]{:S(2)}) collective-permute-start(bf16[512,1024]{1,0:T(8,128)(2,1)S(1)} %get-tuple-element.23.refs_2_), channel_id=1, source_target_pairs={{0,8},{1,9},{2,10},{3,11},{4,12},{5,13},{6,14},{7,15},{8,0},{9,1},... | collective-permute-start | bytes 3145736 | tf_op jit(solution)/shard_map/ppermute | solution.py:612
  27.1 1.7 %collective-permute-start.12 = (bf16[4,512,128]{2,1,0:T(8,128)(2,1)S(1)}, bf16[4,512,128]{2,1,0:T(8,128)(2,1)}, u32[]{:S(2)}, u32[]{:S(2)}) collective-permute-start(bf16[4,512,128]{2,1,0:T(8,128)(2,1)S(1)} %collective-permute-done.7.refs_11_.refs_8_), channel_id=1, source_target_pairs={{0,1},{1,0},{2,3},{3,2},{4,5},{5,4},{6,7},{7,6},{8,10},{9,11},{10,... | collective-permute-start | bytes 1572872 | tf_op jit(solution)/shard_map/ppermute | solution.py:612
  28.8 1.3 %collective-permute-done.other_length = s32[1]{0:T(128)} collective-permute-done((s32[1]{0:T(128)}, s32[1]{0:T(128)}, u32[]{:S(2)}, u32[]{:S(2)}) %collective-permute-start) | collective-permute-done | bytes 36 | tf_op jit(solution)/shard_map/ppermute | solution.py:612
  30.1 1.4 %collective-permute-start.2 = (bf16[16,1024]{1,0:T(8,128)(2,1)S(1)}, bf16[16,1024]{1,0:T(8,128)(2,1)}, u32[]{:S(2)}, u32[]{:S(2)}) collective-permute-start(bf16[16,1024]{1,0:T(8,128)(2,1)S(1)} %get-tuple-element.24), channel_id=1, source_target_pairs={{1,0},{2,1},{3,2},{4,3},{5,4},{6,5},{7,6},{9,8},{10,9},{11,10},{12... | collective-permute-start | bytes 98312 | tf_op jit(solution)/shard_map/ppermute | solution.py:27
  31.5 7.7 %collective-permute-done.2.refs_3_ = bf16[16,1024]{1,0:T(8,128)(2,1)} collective-permute-done((bf16[16,1024]{1,0:T(8,128)(2,1)S(1)}, bf16[16,1024]{1,0:T(8,128)(2,1)}, u32[]{:S(2)}, u32[]{:S(2)}) %collective-permute-start.2) | collective-permute-done | bytes 32800 | tf_op jit(solution)/shard_map/ppermute | solution.py:27
  39.2 0.7 copy.11.owners_col
  39.9 0.7 copy-done.23
  40.6 0.8 copy-done.10
  41.4 0.9 shard_map.104
  42.3 0.8 copy-done.8
  43.1 0.6 copy-done.16
  43.7 0.6 copy-done.18
  44.4 0.5 collective-permute-start.1
  45.0 0.8 collective-permute-start.9
  46.0 1.5 %collective-permute-start.11 = (bf16[4,512,128]{2,1,0:T(8,128)(2,1)S(1)}, bf16[4,512,128]{2,1,0:T(8,128)(2,1)S(1)}, u32[]{:S(2)}, u32[]{:S(2)}) collective-permute-start(bf16[4,512,128]{2,1,0:T(8,128)(2,1)S(1)} %broadcast_select_fusion), channel_id=1, source_target_pairs={{0,16},{1,17},{2,18},{3,19},{4,20},{5,21},{6,22},{7,23},{8,9},{9,8... | collective-permute-start | bytes 1572872 | tf_op jit(solution)/shard_map/ppermute | solution.py:612
  47.5 0.5 collective-permute-start.13
  48.0 1.5 %collective-permute-start.21 = (bf16[1024,512]{1,0:T(8,128)(2,1)}, bf16[1024,512]{1,0:T(8,128)(2,1)}, u32[]{:S(2)}, u32[]{:S(2)}) collective-permute-start(bf16[1024,512]{1,0:T(8,128)(2,1)} %refs_0_.1), channel_id=1, source_target_pairs={{0,16},{1,17},{2,18},{3,19},{4,20},{5,21},{6,22},{7,23},{8,24},{9,... | collective-permute-start | bytes 3145736 | tf_op jit(solution)/shard_map/ppermute | solution.py:612
  49.6 7.6 %shard_map.106 = (bf16[512,256]{1,0:T(8,128)(2,1)S(1)}, bf16[512,256]{1,0:T(8,128)(2,1)S(1)}, f32[128,256]{1,0:T(8,128)S(1)}, f32[128,256]{1,0:T(8,128)S(1)}, bf16[1024,256]{1,0:T(8,128)(2,1)S(1)}) custom-call(s32[17]{0:T(128)S(1)} %stack.63.scalars, s32[1]{0:T(128)} %collective-permute-done.other_length, bf16[128,512]{1,0:T(8,128)(2,1)S(1)} %get-tuple-element.22.refs_0_, ...), custom_call_target="tpu_custom_call" | custom-call | flops 1610612736 | bytes 4194304 | tf_op jit(solution)/shard_map/pallas_call | solution.py:269
  57.2 0.7 copy-done.12
  57.9 0.7 copy-done.24
  58.6 12.0 %collective-permute-start.16 = (bf16[1024,256]{1,0:T(8,128)(2,1)S(1)}, bf16[1024,256]{1,0:T(8,128)(2,1)S(1)}, u32[]{:S(2)}, u32[]{:S(2)}) collective-permute-start(bf16[1024,256]{1,0:T(8,128)(2,1)S(1)} %get-tuple-element.33.refs_4_), channel_id=1, source_target_pairs={{0,8},{1,9},{2,10},{3,11},{4,12},{5,13},{6,14},{7,15},{8,0},{9,1},... | collective-permute-start | bytes 1572872 | tf_op jit(solution)/shard_map/ppermute | solution.py:612
  70.6 0.9 collective-permute-done.13.refs_14_.refs_15_
  71.4 7.5 %shard_map.107 = (bf16[512,256]{1,0:T(8,128)(2,1)S(1)}, bf16[512,256]{1,0:T(8,128)(2,1)S(1)}, f32[128,256]{1,0:T(8,128)S(1)}, f32[128,256]{1,0:T(8,128)S(1)}, bf16[1024,256]{1,0:T(8,128)(2,1)S(1)}) custom-call(s32[17]{0:T(128)S(1)} %stack.63.scalars, s32[1]{0:T(128)} %collective-permute-done.other_length, bf16[128,512]{1,0:T(8,128)(2,1)S(1)} %get-tuple-element.22.refs_0_, ...), custom_call_target="tpu_custom_call" | custom-call | flops 1610612736 | bytes 4194304 | tf_op jit(solution)/shard_map/pallas_call | solution.py:269
  79.0 0.5 collective-permute-start.18
  79.6 9.4 %collective-permute-done.21.refs_2_ = bf16[1024,512]{1,0:T(8,128)(2,1)} collective-permute-done((bf16[1024,512]{1,0:T(8,128)(2,1)}, bf16[1024,512]{1,0:T(8,128)(2,1)}, u32[]{:S(2)}, u32[]{:S(2)}) %collective-permute-start.21) | collective-permute-done | bytes 1048608 | tf_op jit(solution)/shard_map/ppermute | solution.py:612
  89.0 0.5 collective-permute-start.22
  89.6 2.2 %shard_map.109 = bf16[256,1024]{1,0:T(8,128)(2,1)} custom-call(s32[17]{0:T(128)S(1)} %stack.63.scalars, f32[128,1024]{1,0:T(8,128)S(1)} %copy-done.9, f32[128,128]{1,0:T(8,128)S(1)} %copy-done.17, bf16[256,128]{1,0:T(8,128)(2,1)S(1)} %copy-done.19, f32[128,256]{1,0:T(8,128)S(1)} %get-tuple-element.38.refs_0_, f32[128,256]{1,0:T(8,128)S(1)} %get-tuple-element.39.refs_1_, ...), custom_call_target="tpu_custom_call" | custom-call | flops 536870912 | bytes 3145728 | tf_op jit(solution)/shard_map/pallas_call | solution.py:269
  91.8 5.8 %all-to-all-start.1 = ((bf16[8,32,1024]{2,1,0:T(8,128)(2,1)}), bf16[8,32,1024]{2,1,0:T(8,128)(2,1)S(1)}, u32[]{:S(2)}, u32[]{:S(2)}) async-start(bf16[8,32,1024]{2,1,0:T(8,128)(2,1)} %bitcast.25), calls=%async_computation.1 | async-start | bytes 1048576 | tf_op jit(solution)/shard_map/all_to_all | solution.py:620
  97.6 0.5 collective-permute-start.15
  98.1 1.2 %collective-permute-done.14.refs_2_ = bf16[512,256]{1,0:T(8,128)(2,1)S(1)} collective-permute-done((bf16[512,256]{1,0:T(8,128)(2,1)}, bf16[512,256]{1,0:T(8,128)(2,1)S(1)}, u32[]{:S(2)}, u32[]{:S(2)}) %collective-permute-start.14) | collective-permute-done | bytes 262176 | tf_op jit(solution)/shard_map/ppermute | solution.py:612
  99.4 0.4 collective-permute-done.15.refs_3_
  99.8 1.0 copy-done.7
  100.8 0.9 copy-done.15
  101.8 3.4 %shard_map.108 = bf16[512,1024]{1,0:T(8,128)(2,1)} custom-call(s32[17]{0:T(128)S(1)} %stack.63.scalars, bf16[512,256]{1,0:T(8,128)(2,1)S(1)} %copy-done.13, bf16[512,256]{1,0:T(8,128)(2,1)S(1)} %copy-done.15, bf16[512,256]{1,0:T(8,128)(2,1)S(1)} %collective-permute-done.14.refs_2_, bf16[512,256]{1,0:T(8,128)(2,1)S(1)} %collective-permute-done.15.refs_3_, ...), custom_call_target="tpu_custom_call" | custom-call | flops 1073741824 | bytes 3145728 | tf_op jit(solution)/shard_map/pallas_call | solution.py:269
  105.2 7.1 %all-to-all-done.1 = bf16[8,32,1024]{2,1,0:T(8,128)(2,1)S(1)} async-done(((bf16[8,32,1024]{2,1,0:T(8,128)(2,1)}), bf16[8,32,1024]{2,1,0:T(8,128)(2,1)S(1)}, u32[]{:S(2)}, u32[]{:S(2)}) %all-to-all-start.1) | async-done | bytes 524320 | tf_op jit(solution)/shard_map/all_to_all | solution.py:620
  112.3 4.4 %shard_map.110 = bf16[256,2048]{1,0:T(8,128)(2,1)} custom-call(s32[17]{0:T(128)S(1)} %stack.63.scalars, bf16[256,1024]{1,0:T(8,128)(2,1)S(1)} %bitcast.34, bf16[1024,512]{1,0:T(8,128)(2,1)} %refs_0_.1, bf16[1024,512]{1,0:T(8,128)(2,1)} %collective-permute-done.20.refs_1_, bf16[1024,512]{1,0:T(8,128)(2,1)} %collective-permute-done.21.refs_2_, ...), custom_call_target="tpu_custom_call" | custom-call | flops 1073741824 | bytes 4194304 | tf_op jit(solution)/shard_map/pallas_call | solution.py:269
  (70 shorter events, 0.7 us)
Async XLA Ops:
  0.7 4.2 %copy-start.26 = (bf16[3,1024,128]{2,1,0:T(8,128)(2,1)S(1)}, bf16[3,1024,128]{2,1,0:T(8,128)(2,1)}, u32[]{:S(2)}) copy-start(bf16[3,1024,128]{2,1,0:T(8,128)(2,1)} %param.13) | copy-start | bytes 2359300
  0.7 4.2 %copy-start.27 = (bf16[1024,128]{1,0:T(8,128)(2,1)S(1)}, bf16[1024,128]{1,0:T(8,128)(2,1)}, u32[]{:S(2)}) copy-start(bf16[1024,128]{1,0:T(8,128)(2,1)} %param.14) | copy-start | bytes 786436
  1.8 10.3 %collective-permute-start.6 = (bf16[4,512,128]{2,1,0:T(8,128)(2,1)S(1)}, bf16[4,512,128]{2,1,0:T(8,128)(2,1)}, u32[]{:S(2)}, u32[]{:S(2)}) collective-permute-start(bf16[4,512,128]{2,1,0:T(8,128)(2,1)S(1)} %fusion.1.refs_8_), channel_id=1, source_target_pairs={{0,1},{1,0},{2,3},{3,2},{4,5},{5,4},{6,7},{7,6},{8,10},{9,11},{10,... | collective-permute-start | bytes 1572872 | tf_op jit(solution)/shard_map/ppermute | solution.py:612
  4.9 11.6 %copy-start = (bf16[1,512,1024]{2,1,0:T(8,128)(2,1)S(1)}, bf16[1,512,1024]{2,1,0:T(8,128)(2,1)}, u32[]{:S(2)}) copy-start(bf16[1,512,1024]{2,1,0:T(8,128)(2,1)} %param.9) | copy-start | bytes 3145732
  6.0 21.1 %collective-permute-start.7 = (bf16[4,512,128]{2,1,0:T(8,128)(2,1)}, bf16[4,512,128]{2,1,0:T(8,128)(2,1)S(1)}, u32[]{:S(2)}, u32[]{:S(2)}) collective-permute-start(bf16[4,512,128]{2,1,0:T(8,128)(2,1)} %get-tuple-element.42), channel_id=1, source_target_pairs={{0,6},{1,7},{2,0},{3,1},{4,2},{5,3},{6,4},{7,5},{8,10},{9,11},{10,... | collective-permute-start | bytes 1572872 | tf_op jit(solution)/shard_map/ppermute | solution.py:612
  12.1 32.8 %collective-permute-start.8 = (bf16[4,512,128]{2,1,0:T(8,128)(2,1)}, bf16[4,512,128]{2,1,0:T(8,128)(2,1)}, u32[]{:S(2)}, u32[]{:S(2)}) collective-permute-start(bf16[4,512,128]{2,1,0:T(8,128)(2,1)} %collective-permute-done.6.refs_9_.refs_12_), channel_id=1, source_target_pairs={{0,16},{1,17},{2,18},{3,19},{4,20},{5,21},{6,22},{7,23},{8,9},{9,8... | collective-permute-start | bytes 1572872 | tf_op jit(solution)/shard_map/ppermute | solution.py:612
  14.2 30.8 %collective-permute-start.10 = (bf16[4,512,128]{2,1,0:T(8,128)(2,1)}, bf16[4,512,128]{2,1,0:T(8,128)(2,1)}, u32[]{:S(2)}, u32[]{:S(2)}) collective-permute-start(bf16[4,512,128]{2,1,0:T(8,128)(2,1)} %collective-permute-done.6.refs_9_.refs_12_), channel_id=1, source_target_pairs={{8,10},{9,11},{10,12},{11,13},{12,14},{13,15},{14,8},{15,9},{24,26... | collective-permute-start | bytes 1572872 | tf_op jit(solution)/shard_map/ppermute | solution.py:612
  18.6 0.7 copy-start.11
  19.3 25.6 %all-to-all-start = ((bf16[8,16,1024]{2,1,0:T(8,128)(2,1)}), bf16[8,16,1024]{2,1,0:T(8,128)(2,1)S(1)}, u32[]{:S(2)}, u32[]{:S(2)}) async-start(bf16[8,16,1024]{2,1,0:T(8,128)(2,1)} %copy-done.11), calls=%async_computation | async-start | bytes 524288 | tf_op jit(solution)/shard_map/all_to_all | solution.py:620
  25.1 24.5 %collective-permute-start.3 = (bf16[512,1024]{1,0:T(8,128)(2,1)S(1)}, bf16[512,1024]{1,0:T(8,128)(2,1)}, u32[]{:S(2)}, u32[]{:S(2)}) collective-permute-start(bf16[512,1024]{1,0:T(8,128)(2,1)S(1)} %get-tuple-element.23.refs_2_), channel_id=1, source_target_pairs={{0,8},{1,9},{2,10},{3,11},{4,12},{5,13},{6,14},{7,15},{8,0},{9,1},... | collective-permute-start | bytes 3145736 | tf_op jit(solution)/shard_map/ppermute | solution.py:612
  27.1 20.5 %collective-permute-start.12 = (bf16[4,512,128]{2,1,0:T(8,128)(2,1)S(1)}, bf16[4,512,128]{2,1,0:T(8,128)(2,1)}, u32[]{:S(2)}, u32[]{:S(2)}) collective-permute-start(bf16[4,512,128]{2,1,0:T(8,128)(2,1)S(1)} %collective-permute-done.7.refs_11_.refs_8_), channel_id=1, source_target_pairs={{0,1},{1,0},{2,3},{3,2},{4,5},{5,4},{6,7},{7,6},{8,10},{9,11},{10,... | collective-permute-start | bytes 1572872 | tf_op jit(solution)/shard_map/ppermute | solution.py:612
  28.8 1.3 %collective-permute-start = (s32[1]{0:T(128)}, s32[1]{0:T(128)}, u32[]{:S(2)}, u32[]{:S(2)}) collective-permute-start(s32[1]{0:T(128)} %param.10), channel_id=1, source_target_pairs={{0,8},{1,9},{2,10},{3,11},{4,12},{5,13},{6,14},{7,15},{8,0},{9,1},... | collective-permute-start | bytes 20 | tf_op jit(solution)/shard_map/ppermute | solution.py:612
  30.1 9.1 %copy-start.22 = (s32[1,1,128,1]{2,3,1,0:T(1,128)S(1)}, s32[1,1,128,1]{2,3,1,0:T(1,128)}, u32[]{:S(2)}) copy-start(s32[1,1,128,1]{2,3,1,0:T(1,128)} %param.16) | copy-start | bytes 1540
  30.1 9.1 %collective-permute-start.2 = (bf16[16,1024]{1,0:T(8,128)(2,1)S(1)}, bf16[16,1024]{1,0:T(8,128)(2,1)}, u32[]{:S(2)}, u32[]{:S(2)}) collective-permute-start(bf16[16,1024]{1,0:T(8,128)(2,1)S(1)} %get-tuple-element.24), channel_id=1, source_target_pairs={{1,0},{2,1},{3,2},{4,3},{5,4},{6,5},{7,6},{9,8},{10,9},{11,10},{12... | collective-permute-start | bytes 98312 | tf_op jit(solution)/shard_map/ppermute | solution.py:27
  39.2 5.2 %collective-permute-start.4 = (bf16[16,1024]{1,0:T(8,128)(2,1)}, bf16[16,1024]{1,0:T(8,128)(2,1)}, u32[]{:S(2)}, u32[]{:S(2)}) collective-permute-start(bf16[16,1024]{1,0:T(8,128)(2,1)} %collective-permute-done.2.refs_3_), channel_id=1, source_target_pairs={{0,8},{1,9},{2,10},{3,11},{4,12},{5,13},{6,14},{7,15},{8,0},{9,1},... | collective-permute-start | bytes 98312 | tf_op jit(solution)/shard_map/ppermute | solution.py:612
  40.6 0.8 copy-start.10
  42.3 0.8 copy-start.8
  44.4 1.6 %collective-permute-start.1 = (bf16[128,512]{1,0:T(8,128)(2,1)S(1)}, bf16[128,512]{1,0:T(8,128)(2,1)}, u32[]{:S(2)}, u32[]{:S(2)}) collective-permute-start(bf16[128,512]{1,0:T(8,128)(2,1)S(1)} %get-tuple-element.22.refs_0_), channel_id=1, source_target_pairs={{0,8},{1,9},{2,10},{3,11},{4,12},{5,13},{6,14},{7,15},{8,0},{9,1},... | collective-permute-start | bytes 393224 | tf_op jit(solution)/shard_map/ppermute | solution.py:612
  44.9 4.7 %copy-start.1 = (bf16[4,512,128]{2,1,0:T(8,128)(2,1)S(1)}, bf16[4,512,128]{2,1,0:T(8,128)(2,1)}, u32[]{:S(2)}) copy-start(bf16[4,512,128]{2,1,0:T(8,128)(2,1)} %get-tuple-element.43.refs_10_) | copy-start | bytes 1572868
  44.9 3.1 %collective-permute-start.5 = (bf16[128,1024]{1,0:T(8,128)(2,1)S(1)}, bf16[128,1024]{1,0:T(8,128)(2,1)S(1)}, u32[]{:S(2)}, u32[]{:S(2)}) collective-permute-start(bf16[128,1024]{1,0:T(8,128)(2,1)S(1)} %bitcast.31), channel_id=1, source_target_pairs={{0,8},{1,9},{2,10},{3,11},{4,12},{5,13},{6,14},{7,15},{8,0},{9,1},... | collective-permute-start | bytes 786440 | tf_op jit(solution)/shard_map/ppermute | solution.py:612
  45.0 4.6 %collective-permute-start.9 = (bf16[4,512,128]{2,1,0:T(8,128)(2,1)}, bf16[4,512,128]{2,1,0:T(8,128)(2,1)S(1)}, u32[]{:S(2)}, u32[]{:S(2)}) collective-permute-start(bf16[4,512,128]{2,1,0:T(8,128)(2,1)} %collective-permute-done.8.refs_13_.refs_14_), channel_id=1, source_target_pairs={{8,24},{9,25},{10,26},{11,27},{12,28},{13,29},{14,30},{15,31},{24,... | collective-permute-start | bytes 1572872 | tf_op jit(solution)/shard_map/ppermute | solution.py:612
  46.0 24.6 %collective-permute-start.11 = (bf16[4,512,128]{2,1,0:T(8,128)(2,1)S(1)}, bf16[4,512,128]{2,1,0:T(8,128)(2,1)S(1)}, u32[]{:S(2)}, u32[]{:S(2)}) collective-permute-start(bf16[4,512,128]{2,1,0:T(8,128)(2,1)S(1)} %broadcast_select_fusion), channel_id=1, source_target_pairs={{0,16},{1,17},{2,18},{3,19},{4,20},{5,21},{6,22},{7,23},{8,9},{9,8... | collective-permute-start | bytes 1572872 | tf_op jit(solution)/shard_map/ppermute | solution.py:612
  47.5 23.9 %collective-permute-start.13 = (bf16[4,512,128]{2,1,0:T(8,128)(2,1)}, bf16[4,512,128]{2,1,0:T(8,128)(2,1)S(1)}, u32[]{:S(2)}, u32[]{:S(2)}) collective-permute-start(bf16[4,512,128]{2,1,0:T(8,128)(2,1)} %collective-permute-done.12.refs_11_.refs_12_), channel_id=1, source_target_pairs={{0,16},{1,17},{2,18},{3,19},{4,20},{5,21},{6,22},{7,23},{8,9},{9,8... | collective-permute-start | bytes 1572872 | tf_op jit(solution)/shard_map/ppermute | solution.py:612
  48.0 41.0 %collective-permute-start.21 = (bf16[1024,512]{1,0:T(8,128)(2,1)}, bf16[1024,512]{1,0:T(8,128)(2,1)}, u32[]{:S(2)}, u32[]{:S(2)}) collective-permute-start(bf16[1024,512]{1,0:T(8,128)(2,1)} %refs_0_.1), channel_id=1, source_target_pairs={{0,16},{1,17},{2,18},{3,19},{4,20},{5,21},{6,22},{7,23},{8,24},{9,... | collective-permute-start | bytes 3145736 | tf_op jit(solution)/shard_map/ppermute | solution.py:612
  57.2 0.7 copy-start.12
  57.9 0.7 copy-start.24
  58.6 31.0 %copy-start.2 = (bf16[1024,256]{1,0:T(8,128)(2,1)}, bf16[1024,256]{1,0:T(8,128)(2,1)S(1)}, u32[]{:S(2)}) copy-start(bf16[1024,256]{1,0:T(8,128)(2,1)S(1)} %get-tuple-element.33.refs_4_) | copy-start | bytes 1572868
  58.6 31.0 %copy-start.9 = (f32[128,1024]{1,0:T(8,128)S(1)}, f32[128,1024]{1,0:T(8,128)}, u32[]{:S(2)}) copy-start(f32[128,1024]{1,0:T(8,128)} %copy-done.8) | copy-start | bytes 1572868
  58.6 31.0 %copy-start.17 = (f32[128,128]{1,0:T(8,128)S(1)}, f32[128,128]{1,0:T(8,128)}, u32[]{:S(2)}) copy-start(f32[128,128]{1,0:T(8,128)} %copy-done.16) | copy-start | bytes 196612
  58.6 31.0 %copy-start.19 = (bf16[256,128]{1,0:T(8,128)(2,1)S(1)}, bf16[256,128]{1,0:T(8,128)(2,1)}, u32[]{:S(2)}) copy-start(bf16[256,128]{1,0:T(8,128)(2,1)} %copy-done.18) | copy-start | bytes 196612
  58.6 30.9 %collective-permute-start.16 = (bf16[1024,256]{1,0:T(8,128)(2,1)S(1)}, bf16[1024,256]{1,0:T(8,128)(2,1)S(1)}, u32[]{:S(2)}, u32[]{:S(2)}) collective-permute-start(bf16[1024,256]{1,0:T(8,128)(2,1)S(1)} %get-tuple-element.33.refs_4_), channel_id=1, source_target_pairs={{0,8},{1,9},{2,10},{3,11},{4,12},{5,13},{6,14},{7,15},{8,0},{9,1},... | collective-permute-start | bytes 1572872 | tf_op jit(solution)/shard_map/ppermute | solution.py:612
  78.9 12.8 %copy-start.6 = (bf16[1024,256]{1,0:T(8,128)(2,1)}, bf16[1024,256]{1,0:T(8,128)(2,1)S(1)}, u32[]{:S(2)}) copy-start(bf16[1024,256]{1,0:T(8,128)(2,1)S(1)} %get-tuple-element.34.refs_5_) | copy-start | bytes 1572868
  78.9 12.8 %copy-start.14 = (bf16[512,256]{1,0:T(8,128)(2,1)}, bf16[512,256]{1,0:T(8,128)(2,1)S(1)}, u32[]{:S(2)}) copy-start(bf16[512,256]{1,0:T(8,128)(2,1)S(1)} %get-tuple-element.30.refs_1_) | copy-start | bytes 786436
  78.9 12.8 %copy-start.25 = (bf16[512,256]{1,0:T(8,128)(2,1)}, bf16[512,256]{1,0:T(8,128)(2,1)S(1)}, u32[]{:S(2)}) copy-start(bf16[512,256]{1,0:T(8,128)(2,1)S(1)} %get-tuple-element.32) | copy-start | bytes 786436
  79.0 10.6 %collective-permute-start.17 = (bf16[1024,256]{1,0:T(8,128)(2,1)S(1)}, bf16[1024,256]{1,0:T(8,128)(2,1)S(1)}, u32[]{:S(2)}, u32[]{:S(2)}) collective-permute-start(bf16[1024,256]{1,0:T(8,128)(2,1)S(1)} %get-tuple-element.34.refs_5_), channel_id=1, source_target_pairs={{0,8},{1,9},{2,10},{3,11},{4,12},{5,13},{6,14},{7,15},{8,0},{9,1},... | collective-permute-start | bytes 1572872 | tf_op jit(solution)/shard_map/ppermute | solution.py:612
  79.0 10.0 %collective-permute-start.18 = (f32[128,256]{1,0:T(8,128)S(1)}, f32[128,256]{1,0:T(8,128)S(1)}, u32[]{:S(2)}, u32[]{:S(2)}) collective-permute-start(f32[128,256]{1,0:T(8,128)S(1)} %get-tuple-element.40), channel_id=1, source_target_pairs={{0,8},{1,9},{2,10},{3,11},{4,12},{5,13},{6,14},{7,15},{8,0},{9,1},... | collective-permute-start | bytes 393224 | tf_op jit(solution)/shard_map/ppermute | solution.py:612
  79.5 10.0 %collective-permute-start.19 = (f32[128,256]{1,0:T(8,128)S(1)}, f32[128,256]{1,0:T(8,128)S(1)}, u32[]{:S(2)}, u32[]{:S(2)}) collective-permute-start(f32[128,256]{1,0:T(8,128)S(1)} %get-tuple-element.41), channel_id=1, source_target_pairs={{0,8},{1,9},{2,10},{3,11},{4,12},{5,13},{6,14},{7,15},{8,0},{9,1},... | collective-permute-start | bytes 393224 | tf_op jit(solution)/shard_map/ppermute | solution.py:612
  89.0 16.2 %collective-permute-start.20 = (bf16[1024,512]{1,0:T(8,128)(2,1)}, bf16[1024,512]{1,0:T(8,128)(2,1)}, u32[]{:S(2)}, u32[]{:S(2)}) collective-permute-start(bf16[1024,512]{1,0:T(8,128)(2,1)} %refs_0_.1), channel_id=1, source_target_pairs={{0,8},{1,9},{2,10},{3,11},{4,12},{5,13},{6,14},{7,15},{8,0},{9,1},... | collective-permute-start | bytes 3145736 | tf_op jit(solution)/shard_map/ppermute | solution.py:612
  89.0 16.2 %collective-permute-start.22 = (bf16[1024,512]{1,0:T(8,128)(2,1)}, bf16[1024,512]{1,0:T(8,128)(2,1)}, u32[]{:S(2)}, u32[]{:S(2)}) collective-permute-start(bf16[1024,512]{1,0:T(8,128)(2,1)} %collective-permute-done.21.refs_2_), channel_id=1, source_target_pairs={{0,8},{1,9},{2,10},{3,11},{4,12},{5,13},{6,14},{7,15},{8,0},{9,1},... | collective-permute-start | bytes 3145736 | tf_op jit(solution)/shard_map/ppermute | solution.py:612
  89.5 2.2 %copy-start.4 = (bf16[1024,256]{1,0:T(8,128)(2,1)}, bf16[1024,256]{1,0:T(8,128)(2,1)S(1)}, u32[]{:S(2)}) copy-start(bf16[1024,256]{1,0:T(8,128)(2,1)S(1)} %collective-permute-done.16.refs_6_) | copy-start | bytes 1572868
  89.6 10.2 %copy-start.13 = (bf16[512,256]{1,0:T(8,128)(2,1)S(1)}, bf16[512,256]{1,0:T(8,128)(2,1)}, u32[]{:S(2)}) copy-start(bf16[512,256]{1,0:T(8,128)(2,1)} %copy-done.12) | copy-start | bytes 786436
  91.8 8.0 %copy-start.3 = (bf16[1024,256]{1,0:T(8,128)(2,1)S(1)}, bf16[1024,256]{1,0:T(8,128)(2,1)}, u32[]{:S(2)}) copy-start(bf16[1024,256]{1,0:T(8,128)(2,1)} %copy-done.2) | copy-start | bytes 1572868
  91.8 8.0 %copy-start.5 = (bf16[1024,256]{1,0:T(8,128)(2,1)S(1)}, bf16[1024,256]{1,0:T(8,128)(2,1)}, u32[]{:S(2)}) copy-start(bf16[1024,256]{1,0:T(8,128)(2,1)} %copy-done.4) | copy-start | bytes 1572868
  91.8 20.5 %all-to-all-start.1 = ((bf16[8,32,1024]{2,1,0:T(8,128)(2,1)}), bf16[8,32,1024]{2,1,0:T(8,128)(2,1)S(1)}, u32[]{:S(2)}, u32[]{:S(2)}) async-start(bf16[8,32,1024]{2,1,0:T(8,128)(2,1)} %bitcast.25), calls=%async_computation.1 | async-start | bytes 1048576 | tf_op jit(solution)/shard_map/all_to_all | solution.py:620
  97.6 1.7 %collective-permute-start.14 = (bf16[512,256]{1,0:T(8,128)(2,1)}, bf16[512,256]{1,0:T(8,128)(2,1)S(1)}, u32[]{:S(2)}, u32[]{:S(2)}) collective-permute-start(bf16[512,256]{1,0:T(8,128)(2,1)} %copy-done.24), channel_id=1, source_target_pairs={{0,8},{1,9},{2,10},{3,11},{4,12},{5,13},{6,14},{7,15},{8,0},{9,1},... | collective-permute-start | bytes 786440 | tf_op jit(solution)/shard_map/ppermute | solution.py:612
  97.6 2.1 %collective-permute-start.15 = (bf16[512,256]{1,0:T(8,128)(2,1)}, bf16[512,256]{1,0:T(8,128)(2,1)S(1)}, u32[]{:S(2)}, u32[]{:S(2)}) collective-permute-start(bf16[512,256]{1,0:T(8,128)(2,1)} %copy-done.25), channel_id=1, source_target_pairs={{0,8},{1,9},{2,10},{3,11},{4,12},{5,13},{6,14},{7,15},{8,0},{9,1},... | collective-permute-start | bytes 786440 | tf_op jit(solution)/shard_map/ppermute | solution.py:612
  99.8 1.0 copy-start.7
  100.8 0.9 copy-start.15
  (5 other events, 3.3 us)
